TPU v7x, 32 devices: a whole 2x2x4 slice. The times are simulated.
32 devices in a mesh: dp: 16 (over z, y, x), head: 2 (over core).
Axes of the slice: x: 2, y: 2, z: 4, core: 2. Of those that a mesh axis runs over, the one named last changes fastest.
Arguments:
- tokens: bfloat16 [8192, 2048], P('dp'), may hold values from -6 to 6
- seq_count: int32 [16], P('dp'), may hold values from 1 to 2
- valid_len: int32 [32], P('dp'), may hold values from 128 to 256
- attn_gain: bfloat16 [2048], P('dp'), may hold values from 0.5 to 1.5
- ffn_gain: bfloat16 [2048], P('dp'), may hold values from 0.5 to 1.5
- q_weight: bfloat16 [2048, 2048], P('dp', 'head'), may hold values from -0.25 to 0.25
- k_weight: bfloat16 [2048, 2048], P('dp', 'head'), may hold values from -0.25 to 0.25
- v_weight: bfloat16 [2048, 2048], P('dp', 'head'), may hold values from -0.125 to 0.125
- forget_weight: bfloat16 [2048, 256], P('dp', 'head'), may hold values from -0.125 to 0.125
- out_weight: bfloat16 [2048, 2048], P('dp', 'head'), may hold values from -1.5 to 1.5
- gate_weight: bfloat16 [2048, 5632], P('dp', 'head'), may hold values from -0.125 to 0.125
- up_weight: bfloat16 [2048, 5632], P('dp', 'head'), may hold values from -0.125 to 0.125
- down_weight: bfloat16 [2048, 5632], P('dp', 'head'), may hold values from -0.078125 to 0.078125
- cotangent: float32 [8192, 2048], P('dp'), may hold values from -6 to 6
Outputs:
- block_out: bfloat16 [8192, 2048], P('dp')
- input_grad: float32 [8192, 2048], P('dp')
- attn_gain_grad: float32 [2048], P('dp')
- ffn_gain_grad: float32 [2048], P('dp')
- q_grad: float32 [2048, 2048], P('dp', 'head')
- k_grad: float32 [2048, 2048], P('dp', 'head')
- v_grad: float32 [2048, 2048], P('dp', 'head')
- forget_grad: float32 [2048, 256], P('dp', 'head')
- out_grad: float32 [2048, 2048], P('dp', 'head')
- gate_grad: float32 [2048, 5632], P('dp', 'head')
- up_grad: float32 [2048, 5632], P('dp', 'head')
- down_grad: float32 [2048, 5632], P('dp', 'head')
All inputs are finite; a program needn't handle non-finite values.
Results may differ from a plain program's by a relative error of at most 0.0089.
Values may be sent and summed in bfloat16 or wider, within the bound.
A program may use at most 256 MiB of HBM per device.

v0:
```python
import jax
import jax.numpy as jnp
from jax import lax
from jax.sharding import PartitionSpec as P

SLOTS = 64
KDIM = 512
SEQ_LEN = 256


def einsum_high(form, left, right):
    return jnp.einsum(form, left, right, precision=lax.Precision.HIGHEST)


def times_trans(left, right):
    return lax.dot_general(
        left, right, (((1,), (1,)), ((), ())), preferred_element_type=jnp.float32
    )


def outer_sum(left, right):
    return lax.dot_general(
        left, right, (((0,), (0,)), ((), ())), preferred_element_type=jnp.float32
    )


def rms_norm(values, gain):
    return values * lax.rsqrt(jnp.mean(values * values, axis=-1, keepdims=True) + 1e-06) * gain


def swiglu(gate_vals, up_vals):
    return jax.nn.silu(gate_vals) * up_vals


def block_step(states, block):
    key_state, value_state = states
    query_block, key_block, value_block, forget_block = block
    width = query_block.shape[0]
    totals = jnp.cumsum(forget_block, axis=0)
    writes = -jnp.expm1(forget_block)
    order = jnp.arange(width, dtype=jnp.int32)
    lower = (order[:, None] >= order[None, :])[:, :, None]
    spread = jnp.where(lower, totals[:, None, :] - totals[None, :, :], 0.0)
    decays = jnp.where(lower, jnp.exp(spread), 0.0) * writes[None, :, :]
    products = einsum_high("td,id->ti", query_block, key_block)
    carried = jnp.exp(totals)
    scores = einsum_high("ti,tim->tm", products, decays) + carried * einsum_high(
        "td,md->tm", query_block, key_state
    )
    weights = jax.nn.softmax(scores, axis=-1)
    mixing = einsum_high("tm,tim->ti", weights, decays)
    result = einsum_high("ti,id->td", mixing, value_block) + einsum_high(
        "tm,md->td", weights * carried, value_state
    )
    final = totals[-1]
    tails = jnp.exp(final[None, :] - totals) * writes
    key_next = jnp.exp(final)[:, None] * key_state + einsum_high("im,id->md", tails, key_block)
    value_next = jnp.exp(final)[:, None] * value_state + einsum_high(
        "im,id->md", tails, value_block
    )
    return ((key_next, value_next), result)


def scan_slots(query, keys, values_in, forget):
    width = min(64, SEQ_LEN)
    count = SEQ_LEN // width
    pieces = (
        query.reshape(count, width, KDIM),
        keys.reshape(count, width, KDIM),
        values_in.reshape(count, width, KDIM),
        forget.reshape(count, width, SLOTS),
    )
    start = (jnp.zeros((SLOTS, KDIM), jnp.float32), jnp.zeros((SLOTS, KDIM), jnp.float32))
    ignored, outputs = lax.scan(jax.checkpoint(block_step), start, pieces)
    return outputs.reshape(SEQ_LEN, KDIM)


def mixer(query_proj, key_proj, value_proj, forget_proj):
    rows = query_proj.shape[0]
    seq_total = rows // SEQ_LEN
    head_total = forget_proj.shape[1] // SLOTS

    def split(values, width):
        shaped = values.reshape(seq_total, SEQ_LEN, head_total, width).transpose(0, 2, 1, 3)
        return shaped.reshape(seq_total * head_total, SEQ_LEN, width)

    query = split(jax.nn.silu(query_proj), KDIM) * KDIM ** (-0.5)
    keys = split(jax.nn.silu(key_proj), KDIM)
    values_in = split(value_proj, KDIM)
    forget = split(jax.nn.log_sigmoid(forget_proj) / 8.0, SLOTS)
    outputs = jax.vmap(scan_slots)(query, keys, values_in, forget)
    outputs = outputs.reshape(seq_total, head_total, SEQ_LEN, KDIM).transpose(0, 2, 1, 3)
    return outputs.reshape(rows, head_total * KDIM)


def body(
    tokens,
    seq_count,
    valid_len,
    attn_gain,
    ffn_gain,
    q_weight,
    k_weight,
    v_weight,
    forget_weight,
    out_weight,
    gate_weight,
    up_weight,
    down_weight,
    cotangent,
):
    shards = (
        attn_gain,
        ffn_gain,
        q_weight,
        k_weight,
        v_weight,
        forget_weight,
        out_weight,
        gate_weight,
        up_weight,
        down_weight,
    )
    whole = (
        lax.all_gather(shards[0], "dp", axis=0, tiled=True),
        lax.all_gather(shards[1], "dp", axis=0, tiled=True),
        lax.all_gather(shards[2], "dp", axis=0, tiled=True),
        lax.all_gather(shards[3], "dp", axis=0, tiled=True),
        lax.all_gather(shards[4], "dp", axis=0, tiled=True),
        lax.all_gather(shards[5], "dp", axis=0, tiled=True),
        lax.all_gather(shards[6], "dp", axis=0, tiled=True),
        lax.all_gather(shards[7], "dp", axis=0, tiled=True),
        lax.all_gather(shards[8], "dp", axis=0, tiled=True),
        lax.all_gather(shards[9], "dp", axis=0, tiled=True),
    )
    gain_attn, gain_ffn, w_query, w_key, w_value, w_forget, w_out, w_gate, w_up, w_down = whole
    rows = tokens.shape[0]
    places = jnp.arange(rows, dtype=jnp.int32)
    slot_ids = places // SEQ_LEN
    inside = places % SEQ_LEN
    slot_range = jnp.arange(valid_len.shape[0], dtype=jnp.int32)
    lengths = jnp.sum(
        jnp.where(slot_ids[:, None] == slot_range[None, :], valid_len[None, :], 0), axis=1
    )
    live = ((slot_ids < seq_count[0]) & (inside < lengths)).astype(jnp.float32)[:, None]
    inputs = tokens.astype(jnp.float32)
    normed_attn, attn_norm_back = jax.vjp(rms_norm, inputs, gain_attn.astype(jnp.float32))
    attn_in = normed_attn.astype(jnp.bfloat16)
    query_proj = jnp.dot(attn_in, w_query, preferred_element_type=jnp.float32)
    key_proj = jnp.dot(attn_in, w_key, preferred_element_type=jnp.float32)
    value_proj = jnp.dot(attn_in, w_value, preferred_element_type=jnp.float32)
    forget_proj = jnp.dot(attn_in, w_forget, preferred_element_type=jnp.float32)
    mixed_full, mixer_back = jax.vjp(mixer, query_proj, key_proj, value_proj, forget_proj)
    mixed = mixed_full.astype(jnp.bfloat16)
    attn = lax.psum(times_trans(mixed, w_out), "head")
    resid = inputs + attn
    normed_ffn, ffn_norm_back = jax.vjp(rms_norm, resid, gain_ffn.astype(jnp.float32))
    ffn_in = normed_ffn.astype(jnp.bfloat16)
    gate_vals = jnp.dot(ffn_in, w_gate, preferred_element_type=jnp.float32)
    up_vals = jnp.dot(ffn_in, w_up, preferred_element_type=jnp.float32)
    hidden_full, glu_back = jax.vjp(swiglu, gate_vals, up_vals)
    hidden = hidden_full.astype(jnp.bfloat16)
    ffn = lax.psum(times_trans(hidden, w_down), "head")
    block_out = (live * (resid + ffn)).astype(jnp.bfloat16)
    again = (
        lax.all_gather(shards[0], "dp", axis=0, tiled=True),
        lax.all_gather(shards[1], "dp", axis=0, tiled=True),
        lax.all_gather(shards[2], "dp", axis=0, tiled=True),
        lax.all_gather(shards[3], "dp", axis=0, tiled=True),
        lax.all_gather(shards[4], "dp", axis=0, tiled=True),
        lax.all_gather(shards[5], "dp", axis=0, tiled=True),
        lax.all_gather(shards[6], "dp", axis=0, tiled=True),
        lax.all_gather(shards[7], "dp", axis=0, tiled=True),
        lax.all_gather(shards[8], "dp", axis=0, tiled=True),
        lax.all_gather(shards[9], "dp", axis=0, tiled=True),
    )
    gain_attn, gain_ffn, w_query, w_key, w_value, w_forget, w_out, w_gate, w_up, w_down = again
    grad_res = live * cotangent
    grad_ffn = grad_res.astype(jnp.bfloat16)
    grad_down = outer_sum(grad_ffn, hidden)
    grad_hidden = jnp.dot(grad_ffn, w_down, preferred_element_type=jnp.float32)
    grad_gate_vals, grad_up_vals = glu_back(grad_hidden)
    gate_low = grad_gate_vals.astype(jnp.bfloat16)
    up_low = grad_up_vals.astype(jnp.bfloat16)
    grad_gate = outer_sum(ffn_in, gate_low)
    grad_up = outer_sum(ffn_in, up_low)
    grad_ffn_in = lax.psum(times_trans(gate_low, w_gate) + times_trans(up_low, w_up), "head")
    grad_resid_norm, grad_gain_ffn = ffn_norm_back(grad_ffn_in)
    grad_resid = grad_res + grad_resid_norm
    grad_attn = grad_resid.astype(jnp.bfloat16)
    grad_out = outer_sum(grad_attn, mixed)
    grad_mixed = jnp.dot(grad_attn, w_out, preferred_element_type=jnp.float32)
    grad_qproj, grad_kproj, grad_vproj, grad_fproj = mixer_back(grad_mixed)
    query_low = grad_qproj.astype(jnp.bfloat16)
    key_low = grad_kproj.astype(jnp.bfloat16)
    value_low = grad_vproj.astype(jnp.bfloat16)
    forget_low = grad_fproj.astype(jnp.bfloat16)
    grad_query = outer_sum(attn_in, query_low)
    grad_key = outer_sum(attn_in, key_low)
    grad_value = outer_sum(attn_in, value_low)
    grad_forget = outer_sum(attn_in, forget_low)
    local_in = (
        times_trans(query_low, w_query)
        + times_trans(key_low, w_key)
        + times_trans(value_low, w_value)
        + times_trans(forget_low, w_forget)
    )
    grad_attn_in = lax.psum(local_in, "head")
    grad_input_norm, grad_gain_attn = attn_norm_back(grad_attn_in)
    input_grad = grad_resid + grad_input_norm
    reduced = (
        lax.psum_scatter(grad_gain_attn, "dp", scatter_dimension=0, tiled=True),
        lax.psum_scatter(grad_gain_ffn, "dp", scatter_dimension=0, tiled=True),
        lax.psum_scatter(grad_query, "dp", scatter_dimension=0, tiled=True),
        lax.psum_scatter(grad_key, "dp", scatter_dimension=0, tiled=True),
        lax.psum_scatter(grad_value, "dp", scatter_dimension=0, tiled=True),
        lax.psum_scatter(grad_forget, "dp", scatter_dimension=0, tiled=True),
        lax.psum_scatter(grad_out, "dp", scatter_dimension=0, tiled=True),
        lax.psum_scatter(grad_gate, "dp", scatter_dimension=0, tiled=True),
        lax.psum_scatter(grad_up, "dp", scatter_dimension=0, tiled=True),
        lax.psum_scatter(grad_down, "dp", scatter_dimension=0, tiled=True),
    )
    return (
        block_out,
        input_grad,
        reduced[0],
        reduced[1],
        reduced[2],
        reduced[3],
        reduced[4],
        reduced[5],
        reduced[6],
        reduced[7],
        reduced[8],
        reduced[9],
    )


def solution(mesh):
    in_specs = (
        P("dp", None),
        P("dp"),
        P("dp"),
        P("dp"),
        P("dp"),
        P("dp", "head"),
        P("dp", "head"),
        P("dp", "head"),
        P("dp", "head"),
        P("dp", "head"),
        P("dp", "head"),
        P("dp", "head"),
        P("dp", "head"),
        P("dp", None),
    )
    out_specs = (
        P("dp", None),
        P("dp", None),
        P("dp"),
        P("dp"),
        P("dp", "head"),
        P("dp", "head"),
        P("dp", "head"),
        P("dp", "head"),
        P("dp", "head"),
        P("dp", "head"),
        P("dp", "head"),
        P("dp", "head"),
    )
    return jax.shard_map(body, mesh=mesh, in_specs=in_specs, out_specs=out_specs, check_vma=False)
```

profile of v0, /device:TPU:0, one launch (start us, length us, event | category | flops | bytes accessed | tf_op | source)
XLA Modules:
  0.0 3712.4 jit_solution(2996730783707626634)
XLA Ops:
  14.0 47.9 %all_gather.39 = bf16[2048,128]{1,0:T(8,128)(2,1)S(1)} all-gather(bf16[128,128]{1,0:T(8,128)(2,1)S(1)} %copy-done.48), channel_id=1, replica_groups=mesh['dp'=16,'head'=2] {'dp'}, dimensions={0}, use_global_device_ids=true | all-gather | bytes 557056 | tf_op jit(solution)/shard_map/all_gather | solution.py:130
  62.0 35.5 all-gather
  118.0 52.0 %all-gather.12.cloned.1.call-done = bf16[2048,1024]{1,0:T(8,128)(2,1)} async-done(((bf16[128,1024]{1,0:T(8,128)(2,1)}), bf16[2048,1024]{1,0:T(8,128)(2,1)}) %all-gather.12.cloned.1.call-update) | async-done | bytes 4194320 | tf_op jit(solution)/shard_map/all_gather | solution.py:129
  183.5 64.0 %all-gather.14.cloned.1.call-done = bf16[2048,1024]{1,0:T(8,128)(2,1)} async-done(((bf16[128,1024]{1,0:T(8,128)(2,1)}), bf16[2048,1024]{1,0:T(8,128)(2,1)}) %all-gather.14.cloned.1.call-update) | async-done | bytes 4194320 | tf_op jit(solution)/shard_map/all_gather | solution.py:127
  261.8 175.8 %while.48 = (s32[]{:T(128)}, f32[4,64,512]{2,1,0:T(8,128)S(1)}, f32[4,64,512]{2,1,0:T(8,128)S(1)}, bf16[4,4,64,512]{3,2,0,1:T(8,128)(2,1)}, f32[4,4,64,512]{3,2,...) while((s32[]{:T(128)}, f32[4,64,512]{2,1,0:T(8,128)S(1)}, ...), condition=%wide.region_6.7_spmd.clone.clone, body=%wide.region_2.6_spmd.clone.clone.sunk | while | flops 640237632 | bytes 21779780 | solution.py:74
  285.8 15.7 fusion.406
  329.6 15.7 fusion.406
  373.4 15.7 fusion.406
  417.2 15.7 fusion.406
  449.3 38.2 %all-gather.1 = bf16[16,1,128]{2,1,0:T(2,128)(2,1)S(1)} all-gather(bf16[1,1,128]{2,1,0:T(2,128)(2,1)S(1)} %bitcast.438), channel_id=1, replica_groups=mesh['dp'=16,'head'=2] {'dp'}, dimensions={0}, use_global_device_ids=true | all-gather | bytes 4352 | tf_op jit(solution)/shard_map/all_gather | solution.py:126
  493.6 127.2 %all-gather.18.cloned.1.call-done = bf16[2048,2816]{1,0:T(8,128)(2,1)} async-done(((bf16[128,2816]{1,0:T(8,128)(2,1)}), bf16[2048,2816]{1,0:T(8,128)(2,1)}) %all-gather.18.cloned.1.call-update) | async-done | bytes 11534352 | tf_op jit(solution)/shard_map/all_gather | solution.py:132
  632.1 132.2 %all-gather.20.cloned.1.call-done = bf16[2048,2816]{1,0:T(8,128)(2,1)} async-done(((bf16[128,2816]{1,0:T(8,128)(2,1)}), bf16[2048,2816]{1,0:T(8,128)(2,1)}) %all-gather.20.cloned.1.call-update) | async-done | bytes 11534352 | tf_op jit(solution)/shard_map/all_gather | solution.py:133
  775.4 132.4 %all-gather.22.cloned.1.call-done = bf16[2048,2816]{1,0:T(8,128)(2,1)} async-done(((bf16[128,2816]{1,0:T(8,128)(2,1)}), bf16[2048,2816]{1,0:T(8,128)(2,1)}) %all-gather.22.cloned.1.call-update) | async-done | bytes 11534352 | tf_op jit(solution)/shard_map/all_gather | solution.py:134
  907.8 16.3 multiply_convert_fusion
  957.3 15.3 all-reduce.11.cloned.1.call-done
  996.6 389.0 %while.47 = (s32[]{:T(128)}, f32[4,64,512]{2,1,0:T(8,128)S(1)}, f32[4,64,512]{2,1,0:T(8,128)}, f32[4,4,64,512]{3,2,0,1:T(8,128)}, f32[4,4,64,512]{3,2,0,1:T(8,12...) while((s32[]{:T(128)}, f32[4,64,512]{2,1,0:T(8,128)S(1)}, ...), condition=%wide.region_24.25_spmd.clone, body=%wide.region_12.24_spmd.clone.sunk | while | flops 1495470592 | bytes 52910904 | solution.py:74
  1044.5 15.4 fusion.380
  1064.4 14.9 fusion.385
  1139.9 15.4 fusion.380
  1159.5 15.1 fusion.385
  1235.2 15.4 fusion.380
  1254.9 14.9 fusion.385
  1330.4 15.4 fusion.380
  1350.3 14.9 fusion.385
  1493.3 77.7 %all-reduce.3 = (f32[2048]{0:T(1024)S(1)}, f32[2048]{0:T(1024)S(1)}) all-reduce(f32[2048]{0:T(1024)S(1)} %get-tuple-element.678, f32[2048]{0:T(1024)S(1)} %copy-done.49), channel_id=2, replica_groups=mesh['dp'=16,'head'=2] {'dp'}, use_global_device_ids=true, to_apply=%region_28.29.clone | all-reduce | flops 4096 | bytes 32768
  1581.7 130.1 %reduce-scatter.9.cloned.1.call-done = f32[128,1024]{1,0:T(8,128)} async-done(((f32[2048,1024]{1,0:T(8,128)}), f32[128,1024]{1,0:T(8,128)}) %reduce-scatter.9.cloned.1.call-update) | async-done | bytes 524304 | tf_op jit(solution)/shard_map/reduce_scatter | solution.py:214
  1711.8 183.7 %reduce-scatter.11.cloned.1.call-done = f32[128,1024]{1,0:T(8,128)} async-done(((f32[2048,1024]{1,0:T(8,128)}), f32[128,1024]{1,0:T(8,128)}) %reduce-scatter.11.cloned.1.call-update) | async-done | bytes 524304 | tf_op jit(solution)/shard_map/reduce_scatter | solution.py:215
  1895.5 183.1 %reduce-scatter.13.cloned.1.call-done = f32[128,1024]{1,0:T(8,128)} async-done(((f32[2048,1024]{1,0:T(8,128)}), f32[128,1024]{1,0:T(8,128)}) %reduce-scatter.13.cloned.1.call-update) | async-done | bytes 524304 | tf_op jit(solution)/shard_map/reduce_scatter | solution.py:216
  2078.7 183.1 %reduce-scatter.17.cloned.1.call-done = f32[128,1024]{1,0:T(8,128)} async-done(((f32[2048,1024]{1,0:T(8,128)}), f32[128,1024]{1,0:T(8,128)}) %reduce-scatter.17.cloned.1.call-update) | async-done | bytes 524304 | tf_op jit(solution)/shard_map/reduce_scatter | solution.py:218
  2261.7 478.3 %reduce-scatter.19.cloned.1.call-done = f32[128,2816]{1,0:T(8,128)} async-done(((f32[2048,2816]{1,0:T(8,128)}), f32[128,2816]{1,0:T(8,128)}) %reduce-scatter.19.cloned.1.call-update) | async-done | bytes 1441808 | tf_op jit(solution)/shard_map/reduce_scatter | solution.py:219
  2740.0 482.7 %reduce-scatter.21.cloned.1.call-done = f32[128,2816]{1,0:T(8,128)} async-done(((f32[2048,2816]{1,0:T(8,128)}), f32[128,2816]{1,0:T(8,128)}) %reduce-scatter.21.cloned.1.call-update) | async-done | bytes 1441808 | tf_op jit(solution)/shard_map/reduce_scatter | solution.py:220
  3222.6 482.7 %reduce-scatter.23.cloned.1.call-done = f32[128,2816]{1,0:T(8,128)} async-done(((f32[2048,2816]{1,0:T(8,128)}), f32[128,2816]{1,0:T(8,128)}) %reduce-scatter.23.cloned.1.call-update) | async-done | bytes 1441808 | tf_op jit(solution)/shard_map/reduce_scatter | solution.py:221
  (689 shorter events, 636.3 us)
Async XLA Ops:
  7.2 54.8 %copy-start.56 = (bf16[128]{0:T(256)(128)(2,1)S(1)}, bf16[128]{0:T(256)(128)(2,1)}, u32[]{:S(2)}) copy-start(bf16[128]{0:T(256)(128)(2,1)} %param.21) | copy-start | bytes 772
  7.2 90.3 %copy-start.5 = (bf16[512,2048]{1,0:T(8,128)(2,1)S(1)}, bf16[512,2048]{1,0:T(8,128)(2,1)}, u32[]{:S(2)}) copy-start(bf16[512,2048]{1,0:T(8,128)(2,1)} %param.18) | copy-start | bytes 6291460
  7.2 96.4 %all-gather.10.cloned.1.call-start = ((), (), s32[]{:S(2)}) async-start(), calls=%async_computation.8 | async-start | bytes 4456448 | tf_op jit(solution)/shard_map/all_gather | solution.py:128
  7.9 162.1 %all-gather.12.cloned.1.call-start = ((), (), s32[]{:S(2)}) async-start(), calls=%async_computation.9 | async-start | bytes 4456448 | tf_op jit(solution)/shard_map/all_gather | solution.py:129
  8.7 238.8 %all-gather.14.cloned.1.call-start = ((), (), s32[]{:S(2)}) async-start(), calls=%async_computation.10 | async-start | bytes 4456448 | tf_op jit(solution)/shard_map/all_gather | solution.py:127
  9.4 430.7 %all-gather.16.cloned.1.call-start = ((), (), s32[]{:S(2)}) async-start(), calls=%async_computation.11 | async-start | bytes 4456448 | tf_op jit(solution)/shard_map/all_gather | solution.py:131
  10.0 478.3 %all-reduce.9.cloned.1.call-start = ((), (), s32[]{:S(2)}) async-start(), calls=%async_computation.12 | async-start | bytes 8388608 | tf_op jit(solution)/shard_map/psum | solution.py:155
  62.0 36.0 copy-start.36
  97.5 150.0 %copy-start.46 = (f32[16,1,128]{2,1,0:T(1,128)}, f32[16,1,128]{2,1,0:T(1,128)S(1)}, u32[]{:S(2)}) copy-start(f32[16,1,128]{2,1,0:T(1,128)S(1)} %convert_element_type.104) | copy-start | bytes 24580
  98.0 149.5 %copy-start.50 = (f32[512]{0:T(512)}, f32[512]{0:T(512)S(1)}, u32[]{:S(2)}) copy-start(f32[512]{0:T(512)S(1)} %fusion.151) | copy-start | bytes 6148
  285.8 17.4 copy-start.25
  329.6 17.3 copy-start.25
  373.4 17.3 copy-start.25
  447.1 41.0 %copy-start.58 = (s32[2]{0:T(128)S(1)}, s32[2]{0:T(128)}, u32[]{:S(2)}) copy-start(s32[2]{0:T(128)} %param.20) | copy-start | bytes 28
  447.1 173.6 %all-gather.18.cloned.1.call-start = ((), (), s32[]{:S(2)}) async-start(), calls=%async_computation.13 | async-start | bytes 12255232 | tf_op jit(solution)/shard_map/all_gather | solution.py:132
  447.7 316.6 %all-gather.20.cloned.1.call-start = ((), (), s32[]{:S(2)}) async-start(), calls=%async_computation.14 | async-start | bytes 12255232 | tf_op jit(solution)/shard_map/all_gather | solution.py:133
  448.5 459.3 %all-gather.22.cloned.1.call-start = ((), (), s32[]{:S(2)}) async-start(), calls=%async_computation.15 | async-start | bytes 12255232 | tf_op jit(solution)/shard_map/all_gather | solution.py:134
  449.2 523.3 %all-reduce.11.cloned.1.call-start = ((), (), s32[]{:S(2)}) async-start(), calls=%async_computation.16 | async-start | bytes 8388608 | tf_op jit(solution)/shard_map/psum | solution.py:187
  488.2 489.6 %copy-start.52 = (f32[512]{0:T(512)}, f32[512]{0:T(512)S(1)}, u32[]{:S(2)}) copy-start(f32[512]{0:T(512)S(1)} %and_convert_fusion) | copy-start | bytes 6148
  493.6 270.7 %copy-start.35 = (bf16[512,2048]{1,0:T(8,128)(2,1)}, bf16[512,2048]{1,0:T(8,128)(2,1)S(1)}, u32[]{:S(2)}) copy-start(bf16[512,2048]{1,0:T(8,128)(2,1)S(1)} %multiply_convert_fusion.3) | copy-start | bytes 6291460
  907.8 28.7 slice-start
  907.8 28.7 slice-start.1
  945.8 543.9 %all-reduce.13.cloned.1.call-start = ((), (), s32[]{:S(2)}) async-start(), calls=%async_computation.25 | async-start | bytes 16777216 | tf_op jit(solution)/shard_map/psum | solution.py:163
  1411.8 169.9 %reduce-scatter.15.cloned.1.call-start = ((), (), s32[]{:S(2)}) async-start(), calls=%async_computation.20 | async-start | bytes 1114112 | tf_op jit(solution)/shard_map/reduce_scatter | solution.py:217
  1415.4 296.4 %reduce-scatter.9.cloned.1.call-start = ((), (), s32[]{:S(2)}) async-start(), calls=%async_computation.17 | async-start | bytes 8912896 | tf_op jit(solution)/shard_map/reduce_scatter | solution.py:214
  1423.3 472.3 %reduce-scatter.11.cloned.1.call-start = ((), (), s32[]{:S(2)}) async-start(), calls=%async_computation.18 | async-start | bytes 8912896 | tf_op jit(solution)/shard_map/reduce_scatter | solution.py:215
  1429.5 649.2 %reduce-scatter.13.cloned.1.call-start = ((), (), s32[]{:S(2)}) async-start(), calls=%async_computation.19 | async-start | bytes 8912896 | tf_op jit(solution)/shard_map/reduce_scatter | solution.py:216
  1436.5 825.2 %reduce-scatter.17.cloned.1.call-start = ((), (), s32[]{:S(2)}) async-start(), calls=%async_computation.21 | async-start | bytes 8912896 | tf_op jit(solution)/shard_map/reduce_scatter | solution.py:218
  1446.9 1293.1 %reduce-scatter.19.cloned.1.call-start = ((), (), s32[]{:S(2)}) async-start(), calls=%async_computation.22 | async-start | bytes 24510464 | tf_op jit(solution)/shard_map/reduce_scatter | solution.py:219
  1460.6 1762.0 %reduce-scatter.21.cloned.1.call-start = ((), (), s32[]{:S(2)}) async-start(), calls=%async_computation.23 | async-start | bytes 24510464 | tf_op jit(solution)/shard_map/reduce_scatter | solution.py:220
  1473.8 2231.5 %reduce-scatter.23.cloned.1.call-start = ((), (), s32[]{:S(2)}) async-start(), calls=%async_computation.24 | async-start | bytes 24510464 | tf_op jit(solution)/shard_map/reduce_scatter | solution.py:221
  1487.8 84.3 %copy-start.55 = (f32[512]{0:T(512)S(1)}, f32[512]{0:T(512)}, u32[]{:S(2)}) copy-start(f32[512]{0:T(512)} %copy-done.54) | copy-start | bytes 6148
  (133 other events, 1011.4 us)
Sparse Core Ops, SparseCore 0:
  10.8 81.6 all-gather.9
  95.3 74.7 all-gather.11
  172.8 74.6 all-gather.13
  250.1 74.6 all-gather.15
  447.3 27.1 all-reduce.8
  477.4 143.3 all-gather.17
  623.9 140.3 all-gather.19
  767.4 140.3 all-gather.21
  945.9 26.6 all-reduce.10
  1412.0 40.0 all-reduce.12
  1454.9 79.0 reduce-scatter.14
  1536.8 174.9 reduce-scatter.8
  1714.8 180.7 reduce-scatter.10
  1898.4 180.2 reduce-scatter.12
  2081.5 180.1 reduce-scatter.16
  2264.6 475.3 reduce-scatter.18
  2742.8 479.7 reduce-scatter.20
  3225.5 479.7 reduce-scatter.22
where the time goes:
time: 3730 us; the launch traced here: 3710 us
  waiting for transfers between devices  2650 us (71%)
  matrix products  590 us (16%)
  blocking collectives  199 us (5%)
  local copies, waits for them, and re-layouts  127 us (3%)
  other arithmetic  114 us (3%)
    reduce_scatter x1, waiting for transfers between devices, body(): lax.psum_scatter(grad_down, 'dp', scatter_dimension=0, tiled=True)  483 us
    reduce_scatter x1, waiting for transfers between devices, body(): lax.psum_scatter(grad_up, 'dp', scatter_dimension=0, tiled=True)  483 us
    reduce_scatter x1, waiting for transfers between devices, body(): lax.psum_scatter(grad_gate, 'dp', scatter_dimension=0, tiled=True)  478 us
    dot_general x104, matrix products, einsum_high(): return jnp.einsum(form, left, right, precision=lax.Precision.HIGHEST)  406 us
    reduce_scatter x1, waiting for transfers between devices, body(): lax.psum_scatter(grad_key, 'dp', scatter_dimension=0, tiled=True)  184 us
    reduce_scatter x1, waiting for transfers between devices, body(): lax.psum_scatter(grad_value, 'dp', scatter_dimension=0, tiled=True)  183 us
    reduce_scatter x1, waiting for transfers between devices, body(): lax.psum_scatter(grad_out, 'dp', scatter_dimension=0, tiled=True)  183 us
    all_gather x1, waiting for transfers between devices, body(): lax.all_gather(shards[9], 'dp', axis=0, tiled=True)  132 us
  transfers between devices with their start and end apart: 18, of which 13 were waited for; matrix products, arithmetic and copies ran while one was open for 9% of the time, Pallas kernels for 0%

commit v1 on v0

v1 whole, which is shorter than its diff:
```python
import functools
import jax
import jax.numpy as jnp
from jax import lax
from jax.experimental import pallas as pl
from jax.experimental.pallas import tpu as pltpu
from jax.sharding import PartitionSpec as P

SLOTS = 64
KDIM = 512
SEQ_LEN = 256
HALF = 128
F32, BF16 = jnp.float32, jnp.bfloat16
WIDE = 3 * KDIM + 128
NT = (((1,), (1,)), ((), ()))
NN = (((1,), (0,)), ((), ()))
TN = (((0,), (0,)), ((), ()))
LEVELS = (8, 16, 32, 64)


def split(value):
    high = value.astype(BF16)
    return high, (value - high.astype(F32)).astype(BF16)


def dot3(left, right, dims):
    one = functools.partial(lax.dot_general, dimension_numbers=dims, preferred_element_type=F32)
    return one(left[0], right[0]) + (one(left[0], right[1]) + one(left[1], right[0]))


def silu_parts(value):
    gate = 1.0 / (1.0 + jnp.exp(-value))
    return gate, value * gate


def level_mask(size):
    row = lax.broadcasted_iota(jnp.int32, (HALF, HALF), 0) // size
    col = lax.broadcasted_iota(jnp.int32, (HALF, HALF), 1) // size
    return (row == col + 1) & (row % 2 == 1)


def band_mask(back):
    row = lax.broadcasted_iota(jnp.int32, (HALF, HALF), 0)
    col = lax.broadcasted_iota(jnp.int32, (HALF, HALF), 1)
    return (row == col + back) & (row // 8 == col // 8)


def down(value, back):
    return value if back == 0 else pltpu.roll(value, back, 0)


def up(value, back):
    return value if back == 0 else pltpu.roll(value, SEQ_LEN - back, 0)


def gates(forget):
    lane = lax.broadcasted_iota(jnp.int32, forget.shape, 1) < SLOTS
    place = lax.broadcasted_iota(jnp.int32, forget.shape, 0)
    forget = jnp.where(lane, forget, 0.0)
    tail = jnp.exp(-jnp.abs(forget))
    log_decay = (jnp.minimum(forget, 0.0) - jnp.log1p(tail)) * 0.125
    log_decay = jnp.where(lane, log_decay, 0.0)
    g = log_decay
    series = 1.0 + g * (1.0 / 7.0)
    for n in (6.0, 5.0, 4.0, 3.0, 2.0):
        series = 1.0 + g * (1.0 / n) * series
    writes = jnp.where(g > -0.3, -g * series, 1.0 - jnp.exp(g))
    writes = jnp.where(lane, writes, 0.0)
    ahead, behind = g, g
    for step in (1, 2, 4):
        ahead = ahead + jnp.where(place % 8 >= step, down(ahead, step), 0.0)
        behind = behind + jnp.where(place % 8 < 8 - step, up(behind, step), 0.0)
    behind = jnp.where(place % 8 < 7, up(behind, 1), 0.0)
    aheads, behinds = {8: ahead}, {8: behind}
    size = 8
    while size < HALF:
        first = ahead.reshape(SEQ_LEN // (2 * size), 2, size, 128)
        last = behind.reshape(SEQ_LEN // (2 * size), 2, size, 128)
        left, right = first[:, 0:1], first[:, 1:2]
        left_sum, right_sum = left[:, :, size - 1 :], right[:, :, size - 1 :]
        ahead = jnp.concatenate([left, right + left_sum], axis=1).reshape(SEQ_LEN, 128)
        behind = jnp.concatenate([last[:, 0:1] + right_sum, last[:, 1:2]], axis=1).reshape(SEQ_LEN, 128)
        size *= 2
        aheads[size], behinds[size] = ahead, behind
    return lane, place, g, writes, aheads, behinds


def near_decays(place, aheads, back):
    ahead = aheads[8]
    gap = jnp.where(place % 8 >= back, ahead - down(ahead, back), 0.0)
    return jnp.where(place % 8 >= back, jnp.exp(gap), 0.0)


def halves(value):
    return value[:HALF], value[HALF:]


def to_slots(blocks, cross, place, writes, aheads, behinds, nears):
    grow = {size: jnp.exp(aheads[size]) for size in LEVELS}
    keep = {size: split(jnp.exp(behinds[size]) * writes) for size in LEVELS}
    outs = []
    for half in range(2):
        here = slice(half * HALF, (half + 1) * HALF)
        block = blocks[half]
        parts = split(block)
        total = None
        for size in LEVELS:
            mask = level_mask(size)
            masked = tuple(jnp.where(mask, part, jnp.zeros_like(part)) for part in parts)
            term = grow[size][here] * dot3(masked, tuple(k[here] for k in keep[size]), NN)
            total = term if total is None else total + term
        for back in range(8):
            near = jnp.sum(jnp.where(band_mask(back), block, 0.0), axis=1, keepdims=True)
            total = total + near * nears[back][here]
        if half == 1:
            far = split((jnp.exp(behinds[HALF]) * writes)[:HALF])
            total = total + jnp.exp(aheads[HALF])[HALF:] * dot3(split(cross), far, NN)
        outs.append(total)
    return jnp.concatenate(outs, axis=0)


def to_tokens(slots, writes, aheads, behinds, nears):
    blocks = []
    for half in range(2):
        here = slice(half * HALF, (half + 1) * HALF)
        total = jnp.zeros((HALF, HALF), F32)
        for size in LEVELS:
            left = split((slots * jnp.exp(aheads[size]))[here])
            right = split((jnp.exp(behinds[size]) * writes)[here])
            total = jnp.where(level_mask(size), dot3(left, right, NT), total)
        for back in range(8):
            near = jnp.sum(slots[here] * nears[back][here], axis=1, keepdims=True)
            total = jnp.where(band_mask(back), near, total)
        blocks.append(total)
    left = split((slots * jnp.exp(aheads[HALF]))[HALF:])
    right = split((jnp.exp(behinds[HALF]) * writes)[:HALF])
    return blocks, dot3(left, right, NT)


def forward_kernel(q_ref, k_ref, v_ref, f_ref, o_ref, p_ref, s_ref, a_ref, b_ref):
    query = split(silu_parts(q_ref[...])[1] * KDIM ** (-0.5))
    keys = split(silu_parts(k_ref[...])[1])
    values = split(v_ref[...])
    lane, place, g, writes, aheads, behinds = gates(f_ref[...])
    nears = [near_decays(place, aheads, back) * down(writes, back) for back in range(8)]
    q0, q1 = tuple(x[:HALF] for x in query), tuple(x[HALF:] for x in query)
    k0, k1 = tuple(x[:HALF] for x in keys), tuple(x[HALF:] for x in keys)
    blocks = (dot3(q0, k0, NT), dot3(q1, k1, NT))
    cross = dot3(q1, k0, NT)
    scores = to_slots(blocks, cross, place, writes, aheads, behinds, nears)
    shown = jnp.where(lane, scores, -1e30)
    weights = jnp.exp(shown - jnp.max(shown, axis=1, keepdims=True))
    weights = jnp.where(lane, weights, 0.0)
    weights = weights / jnp.sum(weights, axis=1, keepdims=True)
    mixes, mix_cross = to_tokens(weights, writes, aheads, behinds, nears)
    v0 = tuple(x[:HALF] for x in values)
    o_ref[:HALF, :] = dot3(split(mixes[0]), v0, NN).astype(o_ref.dtype)
    row = jnp.concatenate([mix_cross, mixes[1]], axis=1)
    o_ref[HALF:, :] = dot3(split(row), values, NN).astype(o_ref.dtype)
    p_ref[...] = weights
    s_ref[...] = scores
    a_ref[:HALF, :] = jnp.concatenate([blocks[0], jnp.zeros_like(cross)], axis=1)
    a_ref[HALF:, :] = jnp.concatenate([cross, blocks[1]], axis=1)
    b_ref[:HALF, :] = jnp.concatenate([mixes[0], jnp.zeros_like(cross)], axis=1)
    b_ref[HALF:, :] = row


def backward_kernel(q_ref, k_ref, v_ref, f_ref, p_ref, s_ref, a_ref, b_ref, d_ref, out_ref):
    lane, place, g, writes, aheads, behinds = gates(f_ref[...])
    spans = [near_decays(place, aheads, back) for back in range(8)]
    nears = [spans[back] * down(writes, back) for back in range(8)]
    weights, scores = p_ref[...], s_ref[...]
    products, mixing = a_ref[...], b_ref[...]
    grad = split(d_ref[...])
    g0, g1 = tuple(x[:HALF] for x in grad), tuple(x[HALF:] for x in grad)
    values = split(v_ref[...])
    v0, v1 = tuple(x[:HALF] for x in values), tuple(x[HALF:] for x in values)
    m_parts = split(mixing)
    dv0 = dot3(tuple(x[:, :HALF] for x in m_parts), grad, TN)
    dv1 = dot3(tuple(x[HALF:, HALF:] for x in m_parts), g1, TN)
    out_ref[:HALF, 2 * KDIM : 3 * KDIM] = dv0.astype(BF16)
    out_ref[HALF:, 2 * KDIM : 3 * KDIM] = dv1.astype(BF16)
    mix_blocks = (dot3(g0, v0, NT), dot3(g1, v1, NT))
    mix_cross = dot3(g1, v0, NT)
    d_weights = to_slots(mix_blocks, mix_cross, place, writes, aheads, behinds, nears)
    inner = jnp.sum(weights * d_weights, axis=1, keepdims=True)
    d_scores = weights * (d_weights - inner)
    d_blocks, d_cross = to_tokens(d_scores, writes, aheads, behinds, nears)
    q_gate, q_act = silu_parts(q_ref[...])
    k_gate, k_act = silu_parts(k_ref[...])
    scale = KDIM ** (-0.5)
    query, keys = split(q_act * scale), split(k_act)
    k0 = tuple(x[:HALF] for x in keys)
    low = split(jnp.concatenate([d_cross, d_blocks[1]], axis=1))
    top = split(d_blocks[0])
    dq = jnp.concatenate([dot3(top, k0, NN), dot3(low, keys, NN)], axis=0)
    first = tuple(jnp.concatenate([t, l[:, :HALF]], axis=0) for t, l in zip(top, low))
    dk0 = dot3(first, query, TN)
    dk1 = dot3(tuple(x[:, HALF:] for x in low), tuple(x[HALF:] for x in query), TN)
    dk = jnp.concatenate([dk0, dk1], axis=0)
    out_ref[:, :KDIM] = (dq * scale * (q_gate + q_act * (1.0 - q_gate))).astype(BF16)
    out_ref[:, KDIM : 2 * KDIM] = (dk * (k_gate + k_act * (1.0 - k_gate))).astype(BF16)
    parts = []
    for half in range(2):
        here = slice(half * HALF, (half + 1) * HALF)
        both = jnp.concatenate([mix_blocks[half], products[here, here]], axis=0)
        both_parts = split(both)
        total = None
        for size in LEVELS:
            mask = level_mask(size)
            mask = jnp.concatenate([mask, mask], axis=0)
            grow = jnp.exp(aheads[size][here])
            right = split(jnp.concatenate([weights[here] * grow, d_scores[here] * grow], axis=0))
            left = tuple(jnp.where(mask, part, jnp.zeros_like(part)) for part in both_parts)
            term = jnp.exp(behinds[size][here]) * dot3(left, right, TN)
            total = term if total is None else total + term
        parts.append(total)
    grow = jnp.exp(aheads[HALF][HALF:])
    left = split(jnp.concatenate([mix_cross, products[HALF:, :HALF]], axis=0))
    right = split(jnp.concatenate([weights[HALF:] * grow, d_scores[HALF:] * grow], axis=0))
    parts[0] = parts[0] + jnp.exp(behinds[HALF][:HALF]) * dot3(left, right, TN)
    reach = jnp.concatenate(parts, axis=0)
    for back in range(8):
        mask = band_mask(back)
        near_mix = jnp.concatenate([jnp.sum(jnp.where(mask, mix_blocks[h], 0.0), axis=1, keepdims=True) for h in range(2)], axis=0)
        near_pro = jnp.concatenate(
            [jnp.sum(jnp.where(mask, products[h * HALF : (h + 1) * HALF, h * HALF : (h + 1) * HALF], 0.0), axis=1, keepdims=True) for h in range(2)],
            axis=0,
        )
        reach = reach + up((near_mix * weights + near_pro * d_scores) * spans[back], back)
    d_sum = weights * d_weights + d_scores * scores - writes * reach
    step = 1
    while step < SEQ_LEN:
        d_sum = d_sum + jnp.where(place < SEQ_LEN - step, up(d_sum, step), 0.0)
        step *= 2
    d_log = d_sum - reach * jnp.exp(g)
    d_forget = d_log * 0.125 / (1.0 + jnp.exp(f_ref[...]))
    out_ref[:, 3 * KDIM :] = jnp.where(lane, d_forget, 0.0).astype(BF16)


def spec(width, column):
    return pl.BlockSpec((SEQ_LEN, width), lambda i: (i, column))


IN_SPECS = [spec(KDIM, 0), spec(KDIM, 1), spec(KDIM, 2), spec(128, 3 * KDIM // 128)]


def mixer_forward(proj):
    rows = proj.shape[0]
    shape = lambda width, kind: jax.ShapeDtypeStruct((rows, width), kind)
    return pl.pallas_call(
        forward_kernel,
        grid=(rows // SEQ_LEN,),
        in_specs=IN_SPECS,
        out_specs=[spec(KDIM, 0), spec(128, 0), spec(128, 0), spec(SEQ_LEN, 0), spec(SEQ_LEN, 0)],
        out_shape=[shape(KDIM, BF16), shape(128, F32), shape(128, F32), shape(SEQ_LEN, F32), shape(SEQ_LEN, F32)],
        compiler_params=pltpu.CompilerParams(vmem_limit_bytes=48 << 20),
        cost_estimate=pl.CostEstimate(flops=rows * 3000000, bytes_accessed=rows * 10000, transcendentals=rows * 3000),
        name="mixer_forward",
    )(proj, proj, proj, proj)


def mixer_backward(proj, saved, grad):
    rows = proj.shape[0]
    weights, scores, products, mixing = saved
    return pl.pallas_call(
        backward_kernel,
        grid=(rows // SEQ_LEN,),
        in_specs=IN_SPECS + [spec(128, 0), spec(128, 0), spec(SEQ_LEN, 0), spec(SEQ_LEN, 0), spec(KDIM, 0)],
        out_specs=spec(WIDE, 0),
        out_shape=jax.ShapeDtypeStruct((rows, WIDE), BF16),
        compiler_params=pltpu.CompilerParams(vmem_limit_bytes=48 << 20),
        cost_estimate=pl.CostEstimate(flops=rows * 9000000, bytes_accessed=rows * 16000, transcendentals=rows * 5000),
        name="mixer_backward",
    )(proj, proj, proj, proj, weights, scores, products, mixing, grad)


PAD = 128 - SLOTS


class Ring:
    def __init__(self, count):
        self.count = count
        self.stages = []
        left, stride = count // 2, count
        while left > 1:
            size = 4 if left % 4 == 0 else 2
            stride //= size
            left //= size
            self.stages.append((stride, size))

    def perm(self, stride, size, shift):
        moves = []
        for source in range(self.count):
            digit = source // stride % size
            moves.append((source, source + ((digit + shift) % size - digit) * stride))
        return moves

    def send(self, value, stage, shift):
        stride, size = stage
        return lax.ppermute(value, "dp", self.perm(stride, size, shift % size))

    def swap(self, value):
        return lax.ppermute(value, "dp", self.perm(1, 2, 1))

    def digit(self, stage):
        return lax.axis_index("dp") // stage[0] % stage[1]

    def gather(self, block):
        blocks = [block]
        for stage in self.stages:
            more = list(blocks)
            for shift in range(1, stage[1]):
                more += [self.send(one, stage, -shift) for one in blocks]
            blocks = more
        return blocks

    def scatter(self, make):
        def level(depth, offset, width):
            if depth == len(self.stages):
                return lambda inner: make(offset + inner)
            return None

        widths = [1]
        for stage in self.stages:
            widths.append(widths[-1] * stage[1])

        def total(depth, index):
            if depth == len(self.stages):
                return make(index)
            stage = self.stages[depth]
            parts = []
            for shift in range(1, stage[1]):
                sent = total(depth + 1, index + shift * widths[depth]).astype(BF16)
                parts.append(self.send(sent, stage, shift))
            mine = total(depth + 1, index)
            for part in parts:
                mine = mine + part.astype(F32)
            return mine

        return total(0, 0)

    def order(self, value, width, back=False):
        parts = [value[:, i * width : (i + 1) * width] for i in range(self.count // 2)]
        stages = self.stages
        if back:
            parts = self.turn_digits(parts, [s[1] for s in stages[::-1]])
        inner = len(parts)
        for stage in stages:
            size = stage[1]
            inner //= size
            digit = self.digit(stage)
            new = []
            for place in range(len(parts)):
                at = place // inner % size
                base = place - at * inner
                picks = []
                for k in range(size):
                    picks.append(parts[base + ((at - k) % size if back else (at + k) % size) * inner])
                one = picks[0]
                for k in range(1, size):
                    one = jnp.where(digit == k, picks[k], one)
                new.append(one)
            parts = new
        if not back:
            parts = self.turn_digits(parts, [s[1] for s in stages])
        return jnp.concatenate(parts, axis=1)

    def turn_digits(self, parts, sizes):
        count = len(parts)
        out = [None] * count
        for index in range(count):
            rest, digits = index, []
            for size in reversed(sizes):
                digits.append(rest % size)
                rest //= size
            new = 0
            for digit, size in zip(digits, reversed(sizes)):
                new = new * size + digit
            out[new] = parts[index]
        return out


def mm(left, right, dims=NN, kind=F32):
    return lax.dot_general(left, right, dims, preferred_element_type=F32).astype(kind)


def rms(values):
    return lax.rsqrt(jnp.mean(values * values, axis=-1, keepdims=True) + 1e-06)


def norm_back(values, gain, grad):
    scale = rms(values)
    scaled = gain * grad
    inner = jnp.mean(scaled * values, axis=-1, keepdims=True)
    return scale * scaled - values * (scale * scale * scale * inner), jnp.sum(grad * values * scale, axis=0)


def body(
    tokens,
    seq_count,
    valid_len,
    attn_gain,
    ffn_gain,
    q_weight,
    k_weight,
    v_weight,
    forget_weight,
    out_weight,
    gate_weight,
    up_weight,
    down_weight,
    cotangent,
    *,
    ring,
):
    shard = q_weight.shape[0]
    width = 2 * shard
    core = lax.axis_index("head")
    even = lax.axis_index("dp") % 2 == 0
    first = core == 0
    rows = tokens.shape[0]

    def other_core(value):
        return lax.ppermute(value, "head", [(0, 1), (1, 0)])

    def pair_rows(mine, theirs, axis=0):
        return jnp.where(
            even, jnp.concatenate([mine, theirs], axis=axis), jnp.concatenate([theirs, mine], axis=axis)
        )

    def gather(parts):
        left = jnp.concatenate([p[0] for p in parts], axis=1)
        right = jnp.concatenate([p[1] for p in parts], axis=1)
        mine, theirs = jnp.where(even, left, right), jnp.where(even, right, left)
        return jnp.concatenate(ring.gather(pair_rows(mine, ring.swap(theirs))), axis=0)

    def cut(weight):
        half = weight.shape[1] // 2
        return (weight[:, :half], weight[:, half:])

    def quad_gather(mine):
        chips = jnp.concatenate([mine, ring.swap(mine)], axis=0)
        return jnp.concatenate([chips, other_core(chips)], axis=0)

    def quad_scatter(make):
        theirs = other_core(make(slice(2 * SEQ_LEN, 4 * SEQ_LEN)))
        far = make(slice(SEQ_LEN, 2 * SEQ_LEN)) + theirs[SEQ_LEN:]
        near = make(slice(0, SEQ_LEN)) + theirs[:SEQ_LEN]
        return near + ring.swap(far.astype(BF16)).astype(F32)

    def whole_rows(mine):
        theirs = other_core(mine)
        return jnp.where(
            first, jnp.concatenate([mine, theirs], axis=0), jnp.concatenate([theirs, mine], axis=0)
        )

    def weight_sum(act, grads):
        def make(index):
            return mm(act[:, index * width : (index + 1) * width], grads, TN)

        done = ring.scatter(make)
        mine = jnp.where(even, done[:shard], done[shard:])
        theirs = ring.swap(jnp.where(even, done[shard:], done[:shard]))
        return (jnp.where(even, mine, theirs), jnp.where(even, theirs, mine))

    gains = jnp.concatenate(
        [attn_gain[:, None], ffn_gain[:, None], jnp.zeros((shard, PAD - 2), BF16)], axis=1
    )
    w_in = gather([cut(q_weight), cut(k_weight), cut(v_weight), cut(forget_weight), (gains, gains)])
    w_out = gather([cut(out_weight)])
    w_gate = gather([cut(gate_weight)])
    w_up = gather([cut(up_weight)])
    w_down = gather([cut(down_weight)])
    gain_attn = w_in[:, WIDE - PAD].astype(F32)[None, :]
    gain_ffn = w_in[:, WIDE - PAD + 1].astype(F32)[None, :]

    def own(value):
        return ring.order(jnp.where(first, value[:SEQ_LEN], value[SEQ_LEN:]), width)

    places = lax.broadcasted_iota(jnp.int32, (SEQ_LEN, 1), 0)
    length = jnp.where(first, valid_len[0], valid_len[1])
    live = ((core < seq_count[0]) & (places < length)).astype(F32)
    own_tokens = own(tokens)
    d_res = live * own(cotangent)
    d_ffn = quad_gather(d_res.astype(BF16))
    inputs = quad_gather(own_tokens).astype(F32)
    attn_in = (inputs * rms(inputs) * gain_attn).astype(BF16)
    proj = mm(attn_in, w_in)
    mixed, *saved = mixer_forward(proj)
    own_inputs = own_tokens.astype(F32)
    resid = own_inputs + quad_scatter(lambda r: mm(mixed[r], w_out, NT))
    ffn_in = quad_gather((resid * rms(resid) * gain_ffn).astype(BF16))
    gate, up_vals = mm(ffn_in, w_gate), mm(ffn_in, w_up)
    sig = jax.nn.sigmoid(gate)
    hidden = (gate * sig * up_vals).astype(BF16)
    down_sum = weight_sum(d_ffn, hidden)
    d_hidden = mm(d_ffn, w_down)
    d_gate = (d_hidden * up_vals * (sig * (1.0 + gate * (1.0 - sig)))).astype(BF16)
    d_up = (d_hidden * (gate * sig)).astype(BF16)
    d_ffn_in = quad_scatter(lambda r: mm(d_gate[r], w_gate, NT) + mm(d_up[r], w_up, NT))
    gate_sum = weight_sum(ffn_in, d_gate)
    up_sum = weight_sum(ffn_in, d_up)
    ffn = quad_scatter(lambda r: mm(hidden[r], w_down, NT))
    block_out = whole_rows(ring.order((live * (resid + ffn)).astype(BF16), width, back=True))
    d_norm, ffn_gain_part = norm_back(resid, gain_ffn, d_ffn_in)
    d_h = d_res + d_norm
    d_attn = quad_gather(d_h.astype(BF16))
    d_mixed = mm(d_attn, w_out)
    d_proj = mixer_backward(proj, saved, d_mixed)
    d_attn_in = quad_scatter(lambda r: mm(d_proj[r], w_in, NT))
    out_sum = weight_sum(d_attn, mixed)
    in_sum = weight_sum(attn_in, d_proj)
    d_input, attn_gain_part = norm_back(own_inputs, gain_attn, d_attn_in)
    input_grad = whole_rows(ring.order(d_h + d_input, width, back=True))

    both = jnp.stack([attn_gain_part, ffn_gain_part], axis=0)
    both = both + other_core(both)
    both = both.reshape(2, ring.count // 2, width)
    for stage in ring.stages[::-1]:
        size = stage[1]
        both = both.reshape(2, size, -1, width)
        parts = [ring.send(both[:, shift], stage, shift) for shift in range(1, size)]
        both = both[:, 0]
        for part in parts:
            both = both + part
    both = both.reshape(2, 2, shard)
    both = jnp.where(even, both[:, 0], both[:, 1]) + ring.swap(jnp.where(even, both[:, 1], both[:, 0]))

    def columns(pieces, start, stop):
        return jnp.concatenate([p[:, start:stop] for p in pieces], axis=1)

    return (
        block_out,
        input_grad,
        both[0],
        both[1],
        columns(in_sum, 0, KDIM),
        columns(in_sum, KDIM, 2 * KDIM),
        columns(in_sum, 2 * KDIM, 3 * KDIM),
        columns(in_sum, 3 * KDIM, 3 * KDIM + SLOTS),
        columns(out_sum, 0, KDIM),
        jnp.concatenate(gate_sum, axis=1),
        jnp.concatenate(up_sum, axis=1),
        jnp.concatenate(down_sum, axis=1),
    )


def solution(mesh):
    ring = Ring(mesh.shape["dp"])
    split_one, split_two = P("dp"), P("dp", "head")
    row = P("dp", None)
    in_specs = (row, split_one, split_one, split_one, split_one) + (split_two,) * 8 + (row,)
    out_specs = (row, row, split_one, split_one) + (split_two,) * 8
    return jax.shard_map(
        functools.partial(body, ring=ring),
        mesh=mesh,
        in_specs=in_specs,
        out_specs=out_specs,
        check_vma=False,
    )
```

time: 3730 us -> 1340 us (0.36)
  waiting for transfers between devices: 2650 us -> 792 us
  matrix products: 590 us -> 186 us
  starting transfers between devices: 1.19 us -> 239 us
  blocking collectives: 199 us -> 0 us
  local copies, waits for them, and re-layouts: 127 us -> 25.3 us
  other arithmetic: 114 us -> 58.3 us
    reduce_scatter x8 -> x0, waiting for transfers between devices: 2120 us -> none  [the longest x1 483 us: body(): lax.psum_scatter(grad_down, 'dp', scatter_dimension=0, tiled=True)]
    ppermute x0 -> x104, waiting for transfers between devices: none -> 792 us  [the longest x74 686 us: send(): return lax.ppermute(value, 'dp', self.perm(stride, size, shift % size))]
    all_gather x7 -> x0, waiting for transfers between devices: 508 us -> none  [the longest x1 132 us: body(): lax.all_gather(shards[9], 'dp', axis=0, tiled=True)]
    dot_general x128 -> x60, matrix products: 590 us -> 186 us  [mm(): lax.dot_general(left, right, dims, preferred_element_type=F32).astype(kind)]
    ppermute x0 -> x104, starting transfers between devices: none -> 239 us  [the longest x74 218 us: send(): return lax.ppermute(value, 'dp', self.perm(stride, size, shift % size))]
    all_gather x3 -> x0, blocking collectives: 122 us -> none  [the longest x1 47.9 us: body(): lax.all_gather(shards[5], 'dp', axis=0, tiled=True)]
    unnamed x1 -> x0, blocking collectives: 77.7 us -> none
    reduce_sum x25 -> x2, other arithmetic: 48.3 us -> 2.76 us  [rms(): return lax.rsqrt(jnp.mean(values * values, axis=-1, keepdims=True) + 1e-06)]
  transfers between devices with their start and end apart: 18 -> 104, of which waited for: 13 -> 58; matrix products, arithmetic and copies ran while one was open for 9% -> 11% of each run, Pallas kernels for 0% -> 1%
where the time goes in v1:
time: 1340 us
  waiting for transfers between devices  792 us (59%)
  starting transfers between devices  239 us (18%)
  matrix products  186 us (14%)
  other arithmetic  58.3 us (4%)
  Pallas kernels  31.1 us (2%)
  local copies, waits for them, and re-layouts  25.3 us (2%)
    ppermute x74, waiting for transfers between devices, send(): return lax.ppermute(value, 'dp', self.perm(stride, size, shift % size))  686 us
    ppermute x74, starting transfers between devices, send(): return lax.ppermute(value, 'dp', self.perm(stride, size, shift % size))  218 us
    dot_general x60, matrix products, mm(): lax.dot_general(left, right, dims, preferred_element_type=F32).astype(kind)  186 us
    ppermute x19, waiting for transfers between devices, swap(): return lax.ppermute(value, 'dp', self.perm(1, 2, 1))  105 us
  transfers between devices with their start and end apart: 104, of which 58 were waited for; matrix products, arithmetic and copies ran while one was open for 11% of the time, Pallas kernels for 1%

profile of v1, /device:TPU:0, one launch (start us, length us, event | category | flops | bytes accessed | tf_op | source)
XLA Modules:
  0.0 1336.5 jit_solution(3292106956072869619)
XLA Ops:
  26.6 14.9 %collective-permute-done.10 = bf16[128,512]{1,0:T(8,128)(2,1)} collective-permute-done((bf16[128,512]{1,0:T(8,128)(2,1)}, bf16[128,512]{1,0:T(8,128)(2,1)}, u32[]{:S(2)}, u32[]{:S(2)}) %collective-permute-start.10) | collective-permute-done | bytes 131104 | tf_op jit(solution)/shard_map/ppermute | solution.py:304
  92.5 51.3 %collective-permute-done.4 = bf16[256,1664]{1,0:T(8,128)(2,1)S(1)} collective-permute-done((bf16[256,1664]{1,0:T(8,128)(2,1)S(1)}, bf16[256,1664]{1,0:T(8,128)(2,1)S(1)}, u32[]{:S(2)}, u32[]{:S(2)}) %collective-permute-start.4) | collective-permute-done | bytes 852000 | tf_op jit(solution)/shard_map/ppermute | solution.py:301
  148.5 17.2 %collective-permute-done.8 = bf16[256,1664]{1,0:T(8,128)(2,1)S(1)} collective-permute-done((bf16[256,1664]{1,0:T(8,128)(2,1)S(1)}, bf16[256,1664]{1,0:T(8,128)(2,1)S(1)}, u32[]{:S(2)}, u32[]{:S(2)}) %collective-permute-start.8) | collective-permute-done | bytes 852000 | tf_op jit(solution)/shard_map/ppermute | solution.py:301
  167.3 13.7 %collective-permute-done.9 = bf16[256,1664]{1,0:T(8,128)(2,1)S(1)} collective-permute-done((bf16[256,1664]{1,0:T(8,128)(2,1)S(1)}, bf16[256,1664]{1,0:T(8,128)(2,1)S(1)}, u32[]{:S(2)}, u32[]{:S(2)}) %collective-permute-start.9) | collective-permute-done | bytes 852000 | tf_op jit(solution)/shard_map/ppermute | solution.py:301
  221.0 14.5 %collective-permute-done.31 = bf16[256,1408]{1,0:T(8,128)(2,1)S(1)} collective-permute-done((bf16[256,1408]{1,0:T(8,128)(2,1)S(1)}, bf16[256,1408]{1,0:T(8,128)(2,1)S(1)}, u32[]{:S(2)}, u32[]{:S(2)}) %collective-permute-start.31) | collective-permute-done | bytes 720928 | tf_op jit(solution)/shard_map/ppermute | solution.py:301
  237.5 41.1 %collective-permute-done.32 = bf16[256,1408]{1,0:T(8,128)(2,1)S(1)} collective-permute-done((bf16[256,1408]{1,0:T(8,128)(2,1)S(1)}, bf16[256,1408]{1,0:T(8,128)(2,1)S(1)}, u32[]{:S(2)}, u32[]{:S(2)}) %collective-permute-start.32) | collective-permute-done | bytes 720928 | tf_op jit(solution)/shard_map/ppermute | solution.py:301
  279.5 31.3 %collective-permute-start.41 = (bf16[256,1408]{1,0:T(8,128)(2,1)S(1)}, bf16[256,1408]{1,0:T(8,128)(2,1)S(1)}, u32[]{:S(2)}, u32[]{:S(2)}) collective-permute-start(bf16[256,1408]{1,0:T(8,128)(2,1)S(1)} %get-tuple-element.71), channel_id=1, source_target_pairs={{0,8},{2,10},{4,12},{6,14},{8,16},{10,18},{12,20},{14,22},{16,24},... | collective-permute-start | bytes 2162696 | tf_op jit(solution)/shard_map/ppermute | solution.py:301
  315.3 25.1 %collective-permute-done.40 = bf16[256,1408]{1,0:T(8,128)(2,1)S(1)} collective-permute-done((bf16[256,1408]{1,0:T(8,128)(2,1)S(1)}, bf16[256,1408]{1,0:T(8,128)(2,1)S(1)}, u32[]{:S(2)}, u32[]{:S(2)}) %collective-permute-start.40) | collective-permute-done | bytes 720928 | tf_op jit(solution)/shard_map/ppermute | solution.py:301
  341.4 31.7 %collective-permute-start.25 = (bf16[256,1408]{1,0:T(8,128)(2,1)S(1)}, bf16[256,1408]{1,0:T(8,128)(2,1)S(1)}, u32[]{:S(2)}, u32[]{:S(2)}) collective-permute-start(bf16[256,1408]{1,0:T(8,128)(2,1)S(1)} %get-tuple-element.67), channel_id=1, source_target_pairs={{0,8},{2,10},{4,12},{6,14},{8,16},{10,18},{12,20},{14,22},{16,24},... | collective-permute-start | bytes 2162696 | tf_op jit(solution)/shard_map/ppermute | solution.py:301
  376.8 25.2 %collective-permute-done.24 = bf16[256,1408]{1,0:T(8,128)(2,1)S(1)} collective-permute-done((bf16[256,1408]{1,0:T(8,128)(2,1)S(1)}, bf16[256,1408]{1,0:T(8,128)(2,1)S(1)}, u32[]{:S(2)}, u32[]{:S(2)}) %collective-permute-start.24) | collective-permute-done | bytes 720928 | tf_op jit(solution)/shard_map/ppermute | solution.py:301
  407.6 13.4 %collective-permute-done.35 = bf16[256,1408]{1,0:T(8,128)(2,1)S(1)} collective-permute-done((bf16[256,1408]{1,0:T(8,128)(2,1)S(1)}, bf16[256,1408]{1,0:T(8,128)(2,1)S(1)}, u32[]{:S(2)}, u32[]{:S(2)}) %collective-permute-start.35) | collective-permute-done | bytes 720928 | tf_op jit(solution)/shard_map/ppermute | solution.py:301
  484.3 14.0 %collective-permute-done.45 = bf16[256,1408]{1,0:T(8,128)(2,1)S(1)} collective-permute-done((bf16[256,1408]{1,0:T(8,128)(2,1)S(1)}, bf16[256,1408]{1,0:T(8,128)(2,1)S(1)}, u32[]{:S(2)}, u32[]{:S(2)}) %collective-permute-start.45) | collective-permute-done | bytes 720928 | tf_op jit(solution)/shard_map/ppermute | solution.py:301
  513.8 15.4 %collective-permute-done.28 = bf16[256,1408]{1,0:T(8,128)(2,1)S(1)} collective-permute-done((bf16[256,1408]{1,0:T(8,128)(2,1)S(1)}, bf16[256,1408]{1,0:T(8,128)(2,1)S(1)}, u32[]{:S(2)}, u32[]{:S(2)}) %collective-permute-start.28) | collective-permute-done | bytes 720928 | tf_op jit(solution)/shard_map/ppermute | solution.py:301
  529.3 14.3 %collective-permute-done.29 = bf16[256,1408]{1,0:T(8,128)(2,1)S(1)} collective-permute-done((bf16[256,1408]{1,0:T(8,128)(2,1)S(1)}, bf16[256,1408]{1,0:T(8,128)(2,1)S(1)}, u32[]{:S(2)}, u32[]{:S(2)}) %collective-permute-start.29) | collective-permute-done | bytes 720928 | tf_op jit(solution)/shard_map/ppermute | solution.py:301
  572.7 16.6 %multiply_convert_fusion.1 = (bf16[1024,1408]{1,0:T(8,128)(2,1)}, bf16[1024,1408]{1,0:T(8,128)(2,1)}, bf16[1024,1408]{1,0:T(8,128)(2,1)}) fusion(f32[1024,1408]{1,0:T(8,128)} %fusion.126, f32[1024,1408]{1,0:T(8,128)} %fusion.127, bf16[2048,1408]{1,0:T(8,128)(2,1)} %copy-done.4, bf16[512,2048]{1,0:T(8,128)(2,1)} %copy-done.18, ...), kind=kOutput, calls=%fused_computation.6 | convolution fusion | flops 5939789824 | bytes 30146560 | tf_op jit(solution)/shard_map/dot_general | solution.py:385
  657.1 18.6 %collective-permute-done.97 = bf16[256,1408]{1,0:T(8,128)(2,1)} collective-permute-done((bf16[256,1408]{1,0:T(8,128)(2,1)}, bf16[256,1408]{1,0:T(8,128)(2,1)}, u32[]{:S(2)}, u32[]{:S(2)}) %collective-permute-start.97) | collective-permute-done | bytes 720928 | tf_op jit(solution)/shard_map/ppermute | solution.py:301
  723.8 13.6 %collective-permute-done.91 = bf16[256,1408]{1,0:T(8,128)(2,1)S(1)} collective-permute-done((bf16[256,1408]{1,0:T(8,128)(2,1)S(1)}, bf16[256,1408]{1,0:T(8,128)(2,1)S(1)}, u32[]{:S(2)}, u32[]{:S(2)}) %collective-permute-start.91) | collective-permute-done | bytes 720928 | tf_op jit(solution)/shard_map/ppermute | solution.py:301
  742.4 25.9 %collective-permute-done.93 = bf16[256,1408]{1,0:T(8,128)(2,1)S(1)} collective-permute-done((bf16[256,1408]{1,0:T(8,128)(2,1)S(1)}, bf16[256,1408]{1,0:T(8,128)(2,1)S(1)}, u32[]{:S(2)}, u32[]{:S(2)}) %collective-permute-start.93) | collective-permute-done | bytes 720928 | tf_op jit(solution)/shard_map/ppermute | solution.py:301
  783.8 15.4 %collective-permute-done.83 = bf16[256,1408]{1,0:T(8,128)(2,1)S(1)} collective-permute-done((bf16[256,1408]{1,0:T(8,128)(2,1)S(1)}, bf16[256,1408]{1,0:T(8,128)(2,1)S(1)}, u32[]{:S(2)}, u32[]{:S(2)}) %collective-permute-start.83) | collective-permute-done | bytes 720928 | tf_op jit(solution)/shard_map/ppermute | solution.py:301
  823.1 20.7 %collective-permute-done.102 = bf16[256,1408]{1,0:T(8,128)(2,1)S(1)} collective-permute-done((bf16[256,1408]{1,0:T(8,128)(2,1)S(1)}, bf16[256,1408]{1,0:T(8,128)(2,1)S(1)}, u32[]{:S(2)}, u32[]{:S(2)}) %collective-permute-start.102) | collective-permute-done | bytes 720928 | tf_op jit(solution)/shard_map/ppermute | solution.py:301
  846.3 34.3 %collective-permute-start.82 = (bf16[256,1408]{1,0:T(8,128)(2,1)S(1)}, bf16[256,1408]{1,0:T(8,128)(2,1)S(1)}, u32[]{:S(2)}, u32[]{:S(2)}) collective-permute-start(bf16[256,1408]{1,0:T(8,128)(2,1)S(1)} %fusion.24), channel_id=1, source_target_pairs={{0,8},{2,10},{4,12},{6,14},{8,16},{10,18},{12,20},{14,22},{16,24},... | collective-permute-start | bytes 2162696 | tf_op jit(solution)/shard_map/ppermute | solution.py:301
  884.4 30.8 %collective-permute-done.94 = bf16[256,1408]{1,0:T(8,128)(2,1)S(1)} collective-permute-done((bf16[256,1408]{1,0:T(8,128)(2,1)S(1)}, bf16[256,1408]{1,0:T(8,128)(2,1)S(1)}, u32[]{:S(2)}, u32[]{:S(2)}) %collective-permute-start.94) | collective-permute-done | bytes 720928 | tf_op jit(solution)/shard_map/ppermute | solution.py:301
  917.3 28.9 %collective-permute-done.84 = bf16[256,1408]{1,0:T(8,128)(2,1)S(1)} collective-permute-done((bf16[256,1408]{1,0:T(8,128)(2,1)S(1)}, bf16[256,1408]{1,0:T(8,128)(2,1)S(1)}, u32[]{:S(2)}, u32[]{:S(2)}) %collective-permute-start.84) | collective-permute-done | bytes 720928 | tf_op jit(solution)/shard_map/ppermute | solution.py:301
  946.8 14.8 %collective-permute-done.86 = bf16[256,1408]{1,0:T(8,128)(2,1)S(1)} collective-permute-done((bf16[256,1408]{1,0:T(8,128)(2,1)S(1)}, bf16[256,1408]{1,0:T(8,128)(2,1)S(1)}, u32[]{:S(2)}, u32[]{:S(2)}) %collective-permute-start.86) | collective-permute-done | bytes 720928 | tf_op jit(solution)/shard_map/ppermute | solution.py:301
  979.9 25.6 %collective-permute-done.52 = bf16[256,2048]{1,0:T(8,128)(2,1)} collective-permute-done((bf16[256,2048]{1,0:T(8,128)(2,1)S(1)}, bf16[256,2048]{1,0:T(8,128)(2,1)}, u32[]{:S(2)}, u32[]{:S(2)}) %collective-permute-start.52) | collective-permute-done | bytes 1048608 | tf_op jit(solution)/shard_map/ppermute | solution.py:304
  1011.0 17.0 %collective-permute-done.47 = bf16[256,2048]{1,0:T(8,128)(2,1)} collective-permute-done((bf16[256,2048]{1,0:T(8,128)(2,1)}, bf16[256,2048]{1,0:T(8,128)(2,1)}, u32[]{:S(2)}, u32[]{:S(2)}) %collective-permute-start.47) | collective-permute-done | bytes 1048608 | tf_op jit(solution)/shard_map/ppermute | solution.py:304
  1034.2 15.4 %collective-permute-done.53 = bf16[256,2048]{1,0:T(8,128)(2,1)S(1)} collective-permute-done((bf16[256,2048]{1,0:T(8,128)(2,1)S(1)}, bf16[256,2048]{1,0:T(8,128)(2,1)S(1)}, u32[]{:S(2)}, u32[]{:S(2)}) %collective-permute-start.53) | collective-permute-done | bytes 1048608 | tf_op jit(solution)/shard_map/ppermute | solution.py:304
  1065.1 18.4 %mixer_backward.1 = bf16[1024,1664]{1,0:T(8,128)(2,1)} custom-call(f32[1024,1664]{1,0:T(8,128)} %fusion.138.q_ref.k_ref.v_ref.f_ref, f32[1024,1664]{1,0:T(8,128)} %fusion.138.q_ref.k_ref.v_ref.f_ref, f32[1024,1664]{1,0:T(8,128)} %fusion.138.q_ref.k_ref.v_ref.f_ref, f32[1024,1664]{1,0:T(8,128)} %fusion.138.q_ref.k_ref.v_ref.f_ref, ...), custom_call_target="tpu_custom_call" | custom-call | flops 9216000000 | bytes 16384000 | tf_op jit(solution)/shard_map/mixer_backward/pallas_call | solution.py:266
  1107.7 29.0 %collective-permute-done.75 = bf16[256,512]{1,0:T(8,128)(2,1)S(1)} collective-permute-done((bf16[256,512]{1,0:T(8,128)(2,1)S(1)}, bf16[256,512]{1,0:T(8,128)(2,1)S(1)}, u32[]{:S(2)}, u32[]{:S(2)}) %collective-permute-start.75) | collective-permute-done | bytes 262176 | tf_op jit(solution)/shard_map/ppermute | solution.py:301
  1214.9 34.9 %collective-permute-done.68 = bf16[256,1664]{1,0:T(8,128)(2,1)S(1)} collective-permute-done((bf16[256,1664]{1,0:T(8,128)(2,1)S(1)}, bf16[256,1664]{1,0:T(8,128)(2,1)S(1)}, u32[]{:S(2)}, u32[]{:S(2)}) %collective-permute-start.68) | collective-permute-done | bytes 852000 | tf_op jit(solution)/shard_map/ppermute | solution.py:301
  1273.5 18.6 %collective-permute-done.56 = bf16[256,2048]{1,0:T(8,128)(2,1)S(1)} collective-permute-done((bf16[256,2048]{1,0:T(8,128)(2,1)}, bf16[256,2048]{1,0:T(8,128)(2,1)S(1)}, u32[]{:S(2)}, u32[]{:S(2)}) %collective-permute-start.56) | collective-permute-done | bytes 1048608 | tf_op jit(solution)/shard_map/ppermute | solution.py:304
  1300.4 19.7 %collective-permute-start.60 = (f32[2,1,256]{2,0,1:T(2,128)S(1)}, f32[2,1,256]{2,0,1:T(2,128)S(1)}, u32[]{:S(2)}, u32[]{:S(2)}) collective-permute-start(f32[2,1,256]{2,0,1:T(2,128)S(1)} %get-tuple-element.125), channel_id=1, source_target_pairs={{0,8},{2,10},{4,12},{6,14},{8,16},{10,18},{12,20},{14,22},{16,24},... | collective-permute-start | bytes 6152 | tf_op jit(solution)/shard_map/ppermute | solution.py:301
  (505 shorter events, 611.0 us)
Async XLA Ops:
  3.3 74.9 %collective-permute-start = (bf16[256,2048]{1,0:T(8,128)(2,1)S(1)}, bf16[256,2048]{1,0:T(8,128)(2,1)}, u32[]{:S(2)}, u32[]{:S(2)}) collective-permute-start(bf16[256,2048]{1,0:T(8,128)(2,1)S(1)} %constant_dynamic-update-slice_fusion), channel_id=1, source_target_pairs={{0,2},{2,0},{4,6},{6,4},{8,10},{10,8},{12,14},{14,12},{16,18},{18,... | collective-permute-start | bytes 3145736 | tf_op jit(solution)/shard_map/ppermute | solution.py:304
  77.1 66.7 %collective-permute-start.4 = (bf16[256,1664]{1,0:T(8,128)(2,1)S(1)}, bf16[256,1664]{1,0:T(8,128)(2,1)S(1)}, u32[]{:S(2)}, u32[]{:S(2)}) collective-permute-start(bf16[256,1664]{1,0:T(8,128)(2,1)S(1)} %get-tuple-element.73), channel_id=1, source_target_pairs={{0,16},{2,18},{4,20},{6,22},{8,24},{10,26},{12,28},{14,30},{16,0},... | collective-permute-start | bytes 2555912 | tf_op jit(solution)/shard_map/ppermute | solution.py:301
  78.2 67.3 %collective-permute-start.5 = (bf16[256,1664]{1,0:T(8,128)(2,1)S(1)}, bf16[256,1664]{1,0:T(8,128)(2,1)S(1)}, u32[]{:S(2)}, u32[]{:S(2)}) collective-permute-start(bf16[256,1664]{1,0:T(8,128)(2,1)S(1)} %get-tuple-element.73), channel_id=1, source_target_pairs={{0,8},{2,10},{4,12},{6,14},{8,16},{10,18},{12,20},{14,22},{16,24},... | collective-permute-start | bytes 2555912 | tf_op jit(solution)/shard_map/ppermute | solution.py:301
  82.6 100.7 %collective-permute-start.1 = (bf16[512,2048]{1,0:T(8,128)(2,1)S(1)}, bf16[512,2048]{1,0:T(8,128)(2,1)S(1)}, u32[]{:S(2)}, u32[]{:S(2)}) collective-permute-start(bf16[512,2048]{1,0:T(8,128)(2,1)S(1)} %pad_maximum_fusion.4), channel_id=1, source_target_pairs={{0,1},{1,0},{2,3},{3,2},{4,5},{5,4},{6,7},{7,6},{8,9},{9,8},{10,11... | collective-permute-start | bytes 6291464 | tf_op jit(solution)/shard_map/ppermute | solution.py:425
  146.1 72.8 %collective-permute-start.49 = (bf16[256,2048]{1,0:T(8,128)(2,1)S(1)}, bf16[256,2048]{1,0:T(8,128)(2,1)S(1)}, u32[]{:S(2)}, u32[]{:S(2)}) collective-permute-start(bf16[256,2048]{1,0:T(8,128)(2,1)S(1)} %multiply_convert_fusion.4), channel_id=1, source_target_pairs={{0,2},{2,0},{4,6},{6,4},{8,10},{10,8},{12,14},{14,12},{16,18},{18,... | collective-permute-start | bytes 3145736 | tf_op jit(solution)/shard_map/ppermute | solution.py:304
  147.8 66.8 %collective-permute-start.30 = (bf16[128,1408]{1,0:T(8,128)(2,1)}, bf16[128,1408]{1,0:T(8,128)(2,1)S(1)}, u32[]{:S(2)}, u32[]{:S(2)}) collective-permute-start(bf16[128,1408]{1,0:T(8,128)(2,1)} %get-tuple-element.111), channel_id=1, source_target_pairs={{0,2},{2,0},{4,6},{6,4},{8,10},{10,8},{12,14},{14,12},{16,18},{18,... | collective-permute-start | bytes 1081352 | tf_op jit(solution)/shard_map/ppermute | solution.py:304
  213.7 190.7 %collective-permute-start.18 = (f32[512,2048]{1,0:T(8,128)S(1)}, f32[512,2048]{1,0:T(8,128)S(1)}, u32[]{:S(2)}, u32[]{:S(2)}) collective-permute-start(f32[512,2048]{1,0:T(8,128)S(1)} %fusion.98), channel_id=1, source_target_pairs={{0,1},{1,0},{2,3},{3,2},{4,5},{5,4},{6,7},{7,6},{8,9},{9,8},{10,11... | collective-permute-start | bytes 12582920 | tf_op jit(solution)/shard_map/ppermute | solution.py:425
  215.7 62.9 %collective-permute-start.32 = (bf16[256,1408]{1,0:T(8,128)(2,1)S(1)}, bf16[256,1408]{1,0:T(8,128)(2,1)S(1)}, u32[]{:S(2)}, u32[]{:S(2)}) collective-permute-start(bf16[256,1408]{1,0:T(8,128)(2,1)S(1)} %get-tuple-element.69), channel_id=1, source_target_pairs={{0,16},{2,18},{4,20},{6,22},{8,24},{10,26},{12,28},{14,30},{16,0},... | collective-permute-start | bytes 2162696 | tf_op jit(solution)/shard_map/ppermute | solution.py:301
  216.7 62.8 %collective-permute-start.33 = (bf16[256,1408]{1,0:T(8,128)(2,1)S(1)}, bf16[256,1408]{1,0:T(8,128)(2,1)S(1)}, u32[]{:S(2)}, u32[]{:S(2)}) collective-permute-start(bf16[256,1408]{1,0:T(8,128)(2,1)S(1)} %get-tuple-element.69), channel_id=1, source_target_pairs={{0,8},{2,10},{4,12},{6,14},{8,16},{10,18},{12,20},{14,22},{16,24},... | collective-permute-start | bytes 2162696 | tf_op jit(solution)/shard_map/ppermute | solution.py:301
  218.9 92.8 %collective-permute-start.34 = (bf16[256,1408]{1,0:T(8,128)(2,1)S(1)}, bf16[256,1408]{1,0:T(8,128)(2,1)S(1)}, u32[]{:S(2)}, u32[]{:S(2)}) collective-permute-start(bf16[256,1408]{1,0:T(8,128)(2,1)S(1)} %get-tuple-element.69), channel_id=1, source_target_pairs={{0,4},{2,6},{4,0},{6,2},{8,12},{10,14},{12,8},{14,10},{16,20},{18,... | collective-permute-start | bytes 2162696 | tf_op jit(solution)/shard_map/ppermute | solution.py:301
  235.5 78.9 %collective-permute-start.39 = (bf16[256,1408]{1,0:T(8,128)(2,1)S(1)}, bf16[256,1408]{1,0:T(8,128)(2,1)S(1)}, u32[]{:S(2)}, u32[]{:S(2)}) collective-permute-start(bf16[256,1408]{1,0:T(8,128)(2,1)S(1)} %get-tuple-element.71), channel_id=1, source_target_pairs={{0,24},{2,26},{4,28},{6,30},{8,0},{10,2},{12,4},{14,6},{16,8},{18,... | collective-permute-start | bytes 2162696 | tf_op jit(solution)/shard_map/ppermute | solution.py:301
  278.6 61.8 %collective-permute-start.40 = (bf16[256,1408]{1,0:T(8,128)(2,1)S(1)}, bf16[256,1408]{1,0:T(8,128)(2,1)S(1)}, u32[]{:S(2)}, u32[]{:S(2)}) collective-permute-start(bf16[256,1408]{1,0:T(8,128)(2,1)S(1)} %get-tuple-element.71), channel_id=1, source_target_pairs={{0,16},{2,18},{4,20},{6,22},{8,24},{10,26},{12,28},{14,30},{16,0},... | collective-permute-start | bytes 2162696 | tf_op jit(solution)/shard_map/ppermute | solution.py:301
  279.5 61.8 %collective-permute-start.41 = (bf16[256,1408]{1,0:T(8,128)(2,1)S(1)}, bf16[256,1408]{1,0:T(8,128)(2,1)S(1)}, u32[]{:S(2)}, u32[]{:S(2)}) collective-permute-start(bf16[256,1408]{1,0:T(8,128)(2,1)S(1)} %get-tuple-element.71), channel_id=1, source_target_pairs={{0,8},{2,10},{4,12},{6,14},{8,16},{10,18},{12,20},{14,22},{16,24},... | collective-permute-start | bytes 2162696 | tf_op jit(solution)/shard_map/ppermute | solution.py:301
  311.7 62.3 %collective-permute-start.42 = (bf16[256,1408]{1,0:T(8,128)(2,1)S(1)}, bf16[256,1408]{1,0:T(8,128)(2,1)S(1)}, u32[]{:S(2)}, u32[]{:S(2)}) collective-permute-start(bf16[256,1408]{1,0:T(8,128)(2,1)S(1)} %get-tuple-element.71), channel_id=1, source_target_pairs={{0,4},{2,6},{4,0},{6,2},{8,12},{10,14},{12,8},{14,10},{16,20},{18,... | collective-permute-start | bytes 2162696 | tf_op jit(solution)/shard_map/ppermute | solution.py:301
  314.4 62.3 %collective-permute-start.23 = (bf16[256,1408]{1,0:T(8,128)(2,1)S(1)}, bf16[256,1408]{1,0:T(8,128)(2,1)S(1)}, u32[]{:S(2)}, u32[]{:S(2)}) collective-permute-start(bf16[256,1408]{1,0:T(8,128)(2,1)S(1)} %get-tuple-element.67), channel_id=1, source_target_pairs={{0,24},{2,26},{4,28},{6,30},{8,0},{10,2},{12,4},{14,6},{16,8},{18,... | collective-permute-start | bytes 2162696 | tf_op jit(solution)/shard_map/ppermute | solution.py:301
  341.4 62.5 %collective-permute-start.25 = (bf16[256,1408]{1,0:T(8,128)(2,1)S(1)}, bf16[256,1408]{1,0:T(8,128)(2,1)S(1)}, u32[]{:S(2)}, u32[]{:S(2)}) collective-permute-start(bf16[256,1408]{1,0:T(8,128)(2,1)S(1)} %get-tuple-element.67), channel_id=1, source_target_pairs={{0,8},{2,10},{4,12},{6,14},{8,16},{10,18},{12,20},{14,22},{16,24},... | collective-permute-start | bytes 2162696 | tf_op jit(solution)/shard_map/ppermute | solution.py:301
  376.7 169.7 %collective-permute-start.50 = (bf16[512,2048]{1,0:T(8,128)(2,1)S(1)}, bf16[512,2048]{1,0:T(8,128)(2,1)S(1)}, u32[]{:S(2)}, u32[]{:S(2)}) collective-permute-start(bf16[512,2048]{1,0:T(8,128)(2,1)S(1)} %pad_maximum_fusion.6), channel_id=1, source_target_pairs={{0,1},{1,0},{2,3},{3,2},{4,5},{5,4},{6,7},{7,6},{8,9},{9,8},{10,11... | collective-permute-start | bytes 6291464 | tf_op jit(solution)/shard_map/ppermute | solution.py:425
  406.9 63.1 %collective-permute-start.19 = (bf16[256,2048]{1,0:T(8,128)(2,1)S(1)}, bf16[256,2048]{1,0:T(8,128)(2,1)S(1)}, u32[]{:S(2)}, u32[]{:S(2)}) collective-permute-start(bf16[256,2048]{1,0:T(8,128)(2,1)S(1)} %fusion.23), channel_id=1, source_target_pairs={{0,2},{2,0},{4,6},{6,4},{8,10},{10,8},{12,14},{14,12},{16,18},{18,... | collective-permute-start | bytes 3145736 | tf_op jit(solution)/shard_map/ppermute | solution.py:304
  640.9 130.2 %collective-permute-start.96 = (bf16[256,1408]{1,0:T(8,128)(2,1)}, bf16[256,1408]{1,0:T(8,128)(2,1)S(1)}, u32[]{:S(2)}, u32[]{:S(2)}) collective-permute-start(bf16[256,1408]{1,0:T(8,128)(2,1)} %convolution_convert_fusion.3), channel_id=1, source_target_pairs={{0,4},{2,6},{4,0},{6,2},{8,12},{10,14},{12,8},{14,10},{16,20},{18,... | collective-permute-start | bytes 2162696 | tf_op jit(solution)/shard_map/ppermute | solution.py:301
  644.7 62.0 %collective-permute-start.101 = (bf16[256,1408]{1,0:T(8,128)(2,1)}, bf16[256,1408]{1,0:T(8,128)(2,1)}, u32[]{:S(2)}, u32[]{:S(2)}) collective-permute-start(bf16[256,1408]{1,0:T(8,128)(2,1)} %convolution_convert_fusion), channel_id=1, source_target_pairs={{0,4},{2,6},{4,0},{6,2},{8,12},{10,14},{12,8},{14,10},{16,20},{18,... | collective-permute-start | bytes 2162696 | tf_op jit(solution)/shard_map/ppermute | solution.py:301
  644.9 77.1 %collective-permute-start.89 = (bf16[256,1408]{1,0:T(8,128)(2,1)}, bf16[256,1408]{1,0:T(8,128)(2,1)}, u32[]{:S(2)}, u32[]{:S(2)}) collective-permute-start(bf16[256,1408]{1,0:T(8,128)(2,1)} %convolution_convert_fusion.6), channel_id=1, source_target_pairs={{0,4},{2,6},{4,0},{6,2},{8,12},{10,14},{12,8},{14,10},{16,20},{18,... | collective-permute-start | bytes 2162696 | tf_op jit(solution)/shard_map/ppermute | solution.py:301
  691.2 80.0 %collective-permute-start.88 = (bf16[256,1408]{1,0:T(8,128)(2,1)S(1)}, bf16[256,1408]{1,0:T(8,128)(2,1)S(1)}, u32[]{:S(2)}, u32[]{:S(2)}) collective-permute-start(bf16[256,1408]{1,0:T(8,128)(2,1)S(1)} %copy-done.46), channel_id=1, source_target_pairs={{0,4},{2,6},{4,0},{6,2},{8,12},{10,14},{12,8},{14,10},{16,20},{18,... | collective-permute-start | bytes 2162696 | tf_op jit(solution)/shard_map/ppermute | solution.py:301
  706.6 61.7 %collective-permute-start.93 = (bf16[256,1408]{1,0:T(8,128)(2,1)S(1)}, bf16[256,1408]{1,0:T(8,128)(2,1)S(1)}, u32[]{:S(2)}, u32[]{:S(2)}) collective-permute-start(bf16[256,1408]{1,0:T(8,128)(2,1)S(1)} %convolution_convert_fusion.4), channel_id=1, source_target_pairs={{0,4},{2,6},{4,0},{6,2},{8,12},{10,14},{12,8},{14,10},{16,20},{18,... | collective-permute-start | bytes 2162696 | tf_op jit(solution)/shard_map/ppermute | solution.py:301
  737.4 61.8 %collective-permute-start.83 = (bf16[256,1408]{1,0:T(8,128)(2,1)S(1)}, bf16[256,1408]{1,0:T(8,128)(2,1)S(1)}, u32[]{:S(2)}, u32[]{:S(2)}) collective-permute-start(bf16[256,1408]{1,0:T(8,128)(2,1)S(1)} %convolution_convert_fusion.9), channel_id=1, source_target_pairs={{0,4},{2,6},{4,0},{6,2},{8,12},{10,14},{12,8},{14,10},{16,20},{18,... | collective-permute-start | bytes 2162696 | tf_op jit(solution)/shard_map/ppermute | solution.py:301
  771.1 193.4 %collective-permute-start.51 = (f32[512,2048]{1,0:T(8,128)S(1)}, f32[512,2048]{1,0:T(8,128)}, u32[]{:S(2)}, u32[]{:S(2)}) collective-permute-start(f32[512,2048]{1,0:T(8,128)S(1)} %copy-done.40), channel_id=1, source_target_pairs={{0,1},{1,0},{2,3},{3,2},{4,5},{5,4},{6,7},{7,6},{8,9},{9,8},{10,11... | collective-permute-start | bytes 12582920 | tf_op jit(solution)/shard_map/ppermute | solution.py:425
  843.8 71.4 %collective-permute-start.94 = (bf16[256,1408]{1,0:T(8,128)(2,1)S(1)}, bf16[256,1408]{1,0:T(8,128)(2,1)S(1)}, u32[]{:S(2)}, u32[]{:S(2)}) collective-permute-start(bf16[256,1408]{1,0:T(8,128)(2,1)S(1)} %fusion.29), channel_id=1, source_target_pairs={{0,24},{2,26},{4,28},{6,30},{8,0},{10,2},{12,4},{14,6},{16,8},{18,... | collective-permute-start | bytes 2162696 | tf_op jit(solution)/shard_map/ppermute | solution.py:301
  846.1 126.7 %collective-permute-start.46 = (f32[512,2048]{1,0:T(8,128)}, f32[512,2048]{1,0:T(8,128)}, u32[]{:S(2)}, u32[]{:S(2)}) collective-permute-start(f32[512,2048]{1,0:T(8,128)} %fusion.46), channel_id=1, source_target_pairs={{0,1},{1,0},{2,3},{3,2},{4,5},{5,4},{6,7},{7,6},{8,9},{9,8},{10,11... | collective-permute-start | bytes 12582920 | tf_op jit(solution)/shard_map/ppermute | solution.py:425
  846.3 70.5 %collective-permute-start.82 = (bf16[256,1408]{1,0:T(8,128)(2,1)S(1)}, bf16[256,1408]{1,0:T(8,128)(2,1)S(1)}, u32[]{:S(2)}, u32[]{:S(2)}) collective-permute-start(bf16[256,1408]{1,0:T(8,128)(2,1)S(1)} %fusion.24), channel_id=1, source_target_pairs={{0,8},{2,10},{4,12},{6,14},{8,16},{10,18},{12,20},{14,22},{16,24},... | collective-permute-start | bytes 2162696 | tf_op jit(solution)/shard_map/ppermute | solution.py:301
  884.4 61.8 %collective-permute-start.84 = (bf16[256,1408]{1,0:T(8,128)(2,1)S(1)}, bf16[256,1408]{1,0:T(8,128)(2,1)S(1)}, u32[]{:S(2)}, u32[]{:S(2)}) collective-permute-start(bf16[256,1408]{1,0:T(8,128)(2,1)S(1)} %fusion.25), channel_id=1, source_target_pairs={{0,16},{2,18},{4,20},{6,22},{8,24},{10,26},{12,28},{14,30},{16,0},... | collective-permute-start | bytes 2162696 | tf_op jit(solution)/shard_map/ppermute | solution.py:301
  963.8 88.1 %collective-permute-start.87 = (f32[128,1408]{1,0:T(8,128)}, f32[128,1408]{1,0:T(8,128)}, u32[]{:S(2)}, u32[]{:S(2)}) collective-permute-start(f32[128,1408]{1,0:T(8,128)} %slice_select_fusion.8), channel_id=1, source_target_pairs={{0,2},{2,0},{4,6},{6,4},{8,10},{10,8},{12,14},{14,12},{16,18},{18,... | collective-permute-start | bytes 2162696 | tf_op jit(solution)/shard_map/ppermute | solution.py:304
  1100.4 90.0 %collective-permute-start.72 = (bf16[256,512]{1,0:T(8,128)(2,1)S(1)}, bf16[256,512]{1,0:T(8,128)(2,1)S(1)}, u32[]{:S(2)}, u32[]{:S(2)}) collective-permute-start(bf16[256,512]{1,0:T(8,128)(2,1)S(1)} %copy-done.48), channel_id=1, source_target_pairs={{0,4},{2,6},{4,0},{6,2},{8,12},{10,14},{12,8},{14,10},{16,20},{18,... | collective-permute-start | bytes 786440 | tf_op jit(solution)/shard_map/ppermute | solution.py:301
  1107.3 144.6 %collective-permute-start.55 = (f32[512,2048]{1,0:T(8,128)}, f32[512,2048]{1,0:T(8,128)S(1)}, u32[]{:S(2)}, u32[]{:S(2)}) collective-permute-start(f32[512,2048]{1,0:T(8,128)} %fusion.41), channel_id=1, source_target_pairs={{0,1},{1,0},{2,3},{3,2},{4,5},{5,4},{6,7},{7,6},{8,9},{9,8},{10,11... | collective-permute-start | bytes 12582920 | tf_op jit(solution)/shard_map/ppermute | solution.py:425
  (131 other events, 3717.9 us)

commit v2 on v1

--- a/solution.py
+++ b/solution.py
@@ -275,6 +275,231 @@
     )(proj, proj, proj, proj, weights, scores, products, mixing, grad)
 
 
+MESH = pl.DeviceIdType.MESH
+ANY = pl.BlockSpec(memory_space=pl.ANY)
+
+
+def places():
+    dp, core = lax.axis_index("dp"), lax.axis_index("head")
+    x, y, z = dp % 2, dp // 2 % 2, dp // 4
+    rest = dp % 4
+    return {
+        "x": (dp + 1 - 2 * x, core),
+        "y": (dp + 2 - 4 * y, core),
+        "up": ((z + 1) % 4 * 4 + rest, core),
+        "down": ((z + 3) % 4 * 4 + rest, core),
+        "core": (dp, 1 - core),
+    }, x
+
+
+def greet(peers):
+    ready = pltpu.get_barrier_semaphore()
+    for peer in peers:
+        pl.semaphore_signal(ready, inc=1, device_id=peer, device_id_type=MESH)
+    pl.semaphore_wait(ready, len(peers))
+
+
+def remote(source, target, sends, recvs, peer):
+    return pltpu.make_async_remote_copy(
+        src_ref=source, dst_ref=target, send_sem=sends, recv_sem=recvs, device_id=peer, device_id_type=MESH
+    )
+
+
+def gather_kernel(chunks, count, *refs):
+    total = len(chunks)
+    mine, theirs = refs[:total], refs[total : 2 * total]
+    full = refs[2 * total : 2 * total + count]
+    local, xs, xr, zs, zr, ys, yr = refs[2 * total + count :]
+    peers, x = places()
+    half = mine[0].shape[0]
+    rows = pl.ds(pl.multiple_of(x * half, half), half)
+    greet([peers[name] for name in ("x", "y", "up", "down")])
+
+    def block(c, index):
+        array, start, width, _ = chunks[c]
+        return full[array].at[index, :, pl.ds(start, width)]
+
+    def keep(c):
+        array, start, width, _ = chunks[c]
+        return pltpu.make_async_copy(mine[c], full[array].at[0, rows, pl.ds(start, width)], local.at[c])
+
+    def swap(c):
+        array, start, width, _ = chunks[c]
+        return remote(theirs[c], full[array].at[0, rows, pl.ds(start, width)], xs.at[c], xr.at[c], peers["x"])
+
+    def rise(c, step, upper):
+        source = (5 - step) % 4
+        return remote(
+            block(c, source + 4 * upper), block(c, 4 - step + 4 * upper), zs.at[c, upper, step - 1], zr.at[c, upper, step - 1], peers["up"]
+        )
+
+    def cross(c, index):
+        return remote(block(c, index), block(c, 4 + index), ys.at[c, index], yr.at[c, index], peers["y"])
+
+    order = range(total)
+    for c in order:
+        swap(c).start()
+        keep(c).start()
+    for c in order:
+        keep(c).wait()
+        swap(c).wait_recv()
+        rise(c, 1, 0).start()
+        cross(c, 0).start()
+    for step in (1, 2, 3):
+        if step == 1:
+            for c in order:
+                if chunks[c][3]:
+                    cross(c, 0).wait_recv()
+                    rise(c, 1, 1).start()
+        for c in order:
+            for upper in (0, 1) if chunks[c][3] else (0,):
+                rise(c, step, upper).wait_recv()
+                if step < 3:
+                    rise(c, step + 1, upper).start()
+            if not chunks[c][3]:
+                cross(c, 4 - step).start()
+    for c in order:
+        swap(c).wait_send()
+        for index in range(1 if chunks[c][3] else 4):
+            copy = cross(c, index)
+            copy.wait_send()
+            if not chunks[c][3]:
+                copy.wait_recv()
+        for upper in (0, 1) if chunks[c][3] else (0,):
+            for step in (1, 2, 3):
+                rise(c, step, upper).wait_send()
+
+
+def gather_call(chunks, widths, mine, theirs, ident):
+    total = len(chunks)
+    half = mine[0].shape[0]
+    sems = pltpu.SemaphoreType.DMA
+    full = pl.pallas_call(
+        functools.partial(gather_kernel, chunks, len(widths)),
+        in_specs=[ANY] * (2 * total),
+        out_specs=[ANY] * len(widths),
+        out_shape=[jax.ShapeDtypeStruct((8, 2 * half, width), BF16) for width in widths],
+        scratch_shapes=[
+            sems((total,)),
+            sems((total,)),
+            sems((total,)),
+            sems((total, 2, 3)),
+            sems((total, 2, 3)),
+            sems((total, 4)),
+            sems((total, 4)),
+        ],
+        compiler_params=pltpu.CompilerParams(collective_id=ident, has_side_effects=True),
+        name="gather_weights",
+    )(*mine, *theirs)
+    return [one.reshape(16 * half, one.shape[2]) for one in full]
+
+
+def scatter_kernel(chunks, count, *refs):
+    total = len(chunks)
+    terms = refs[:count]
+    outs = refs[count : count + total]
+    others = refs[count + total : count + 2 * total]
+    scratch = refs[count + 2 * total :]
+    own, from_y, from_z, to_z, final = (scratch[i * total : (i + 1) * total] for i in range(5))
+    local, ys, yr, zs, zr, xs, xr, last = scratch[5 * total :]
+    peers, x = places()
+    rows = terms[0].shape[1]
+    half = rows // 2
+    greet([peers[name] for name in ("x", "y", "up", "down")])
+
+    def block(c, index):
+        array, start, width = chunks[c]
+        return terms[array].at[index, :, pl.ds(start, width)]
+
+    def cross(c, index):
+        return remote(block(c, 4 + index), from_y[c].at[index], ys.at[c, index], yr.at[c, index], peers["y"])
+
+    def load(c, index):
+        return pltpu.make_async_copy(block(c, index), own[c].at[index], local.at[c, index])
+
+    def rise(c, step):
+        return remote(to_z[c].at[step], from_z[c].at[step], zs.at[c, step], zr.at[c, step], peers["up"])
+
+    mine = pl.ds(pl.multiple_of(x * half, half), half)
+    away = pl.ds(pl.multiple_of((1 - x) * half, half), half)
+
+    def swap(c):
+        return remote(final[c].at[away], others[c], xs.at[c], xr.at[c], peers["x"])
+
+    def leave(c):
+        return pltpu.make_async_copy(final[c].at[mine], outs[c], last.at[c])
+
+    order = range(total)
+    for index in (3, 2, 1, 0):
+        for c in order:
+            cross(c, index).start()
+            load(c, index).start()
+    for step in range(4):
+        index = 3 - step
+        for c in order:
+            cross(c, index).wait_recv()
+            load(c, index).wait()
+            if step:
+                rise(c, step - 1).wait_recv()
+            piece = 32
+
+            def add(i, carry, c=c, step=step, index=index):
+                part = pl.ds(pl.multiple_of(i * piece, piece), piece)
+                value = own[c][index, part].astype(F32) + from_y[c][index, part].astype(F32)
+                if step:
+                    value = value + from_z[c][step - 1, part].astype(F32)
+                if step < 3:
+                    to_z[c][step, part] = value.astype(BF16)
+                else:
+                    final[c][part] = value
+                return carry
+
+            lax.fori_loop(0, rows // piece, add, 0)
+            if step < 3:
+                rise(c, step).start()
+            else:
+                swap(c).start()
+                leave(c).start()
+    for c in order:
+        for index in range(4):
+            cross(c, index).wait_send()
+        for step in range(3):
+            rise(c, step).wait_send()
+        leave(c).wait()
+        swap(c).wait()
+
+
+def scatter_call(chunks, terms, ident):
+    total = len(chunks)
+    rows = terms[0].shape[0] // 8
+    terms = [term.reshape(8, rows, term.shape[1]) for term in terms]
+    sems = pltpu.SemaphoreType.DMA
+    scratch = []
+    for depth, kind in ((4, BF16), (4, BF16), (3, BF16), (3, BF16)):
+        scratch += [pltpu.VMEM((depth, rows, width), kind) for _, _, width in chunks]
+    scratch += [pltpu.VMEM((rows, width), F32) for _, _, width in chunks]
+    outs = pl.pallas_call(
+        functools.partial(scatter_kernel, chunks, len(terms)),
+        in_specs=[ANY] * len(terms),
+        out_specs=[ANY] * (2 * total),
+        out_shape=[jax.ShapeDtypeStruct((rows // 2, width), F32) for _, _, width in chunks] * 2,
+        scratch_shapes=scratch
+        + [
+            sems((total, 4)),
+            sems((total, 4)),
+            sems((total, 4)),
+            sems((total, 3)),
+            sems((total, 3)),
+            sems((total,)),
+            sems((total,)),
+            sems((total,)),
+        ],
+        compiler_params=pltpu.CompilerParams(collective_id=ident, has_side_effects=True, vmem_limit_bytes=56 << 20),
+        name="sum_gradients",
+    )(*terms)
+    return outs[:total], outs[total:]
+
+
 PAD = 128 - SLOTS
 
 
@@ -435,6 +660,27 @@
         mine, theirs = jnp.where(even, left, right), jnp.where(even, right, left)
         return jnp.concatenate(ring.gather(pair_rows(mine, ring.swap(theirs))), axis=0)
 
+    def gather_all(groups, layout, ident):
+        if ring.count != 16:
+            arrays = {}
+            for group, chunk in zip(groups, layout):
+                arrays.setdefault(chunk[0], []).append((chunk[1], group))
+            return [gather([g for _, g in sorted(arrays[i], key=lambda one: one[0])]) for i in sorted(arrays)]
+        mine = [jnp.where(even, left, right) for left, right in groups]
+        theirs = [jnp.where(even, right, left) for left, right in groups]
+        widths = {}
+        for array, start, size, _ in layout:
+            widths[array] = max(widths.get(array, 0), start + size)
+        return gather_call(layout, [widths[i] for i in sorted(widths)], mine, theirs, ident)
+
+    def scatter_all(pairs, layout, ident):
+        if ring.count != 16:
+            sums = [weight_sum(act, grads) for act, grads in pairs]
+            return [tuple(p[:, start : start + size] for p in sums[array]) for array, start, size in layout]
+        terms = [mm(act, grads, TN, BF16) for act, grads in pairs]
+        mine, theirs = scatter_call(layout, terms, ident)
+        return [(jnp.where(even, m, t), jnp.where(even, t, m)) for m, t in zip(mine, theirs)]
+
     def cut(weight):
         half = weight.shape[1] // 2
         return (weight[:, :half], weight[:, half:])
@@ -467,11 +713,20 @@
     gains = jnp.concatenate(
         [attn_gain[:, None], ffn_gain[:, None], jnp.zeros((shard, PAD - 2), BF16)], axis=1
     )
-    w_in = gather([cut(q_weight), cut(k_weight), cut(v_weight), cut(forget_weight), (gains, gains)])
-    w_out = gather([cut(out_weight)])
-    w_gate = gather([cut(gate_weight)])
-    w_up = gather([cut(up_weight)])
-    w_down = gather([cut(down_weight)])
+    small = tuple(jnp.concatenate([part, gains], axis=1) for part in cut(forget_weight))
+    w_in, w_out = gather_all(
+        [small, cut(q_weight), cut(k_weight), cut(v_weight), cut(out_weight)],
+        ((0, 3 * KDIM, 128, False), (0, 0, KDIM, False), (0, KDIM, KDIM, False), (0, 2 * KDIM, KDIM, False), (1, 0, KDIM, True)),
+        0,
+    )
+    hid = gate_weight.shape[1] // 2
+    low, high = hid // 256 * 128, hid - hid // 256 * 128
+    down_left, down_right = cut(down_weight)
+    w_gate, w_up, w_down = gather_all(
+        [cut(gate_weight), cut(up_weight), (down_left[:, :low], down_right[:, :low]), (down_left[:, low:], down_right[:, low:])],
+        ((0, 0, hid, False), (1, 0, hid, False), (2, 0, low, False), (2, low, high, True)),
+        1,
+    )
     gain_attn = w_in[:, WIDE - PAD].astype(F32)[None, :]
     gain_ffn = w_in[:, WIDE - PAD + 1].astype(F32)[None, :]
 
@@ -494,13 +749,13 @@
     gate, up_vals = mm(ffn_in, w_gate), mm(ffn_in, w_up)
     sig = jax.nn.sigmoid(gate)
     hidden = (gate * sig * up_vals).astype(BF16)
-    down_sum = weight_sum(d_ffn, hidden)
     d_hidden = mm(d_ffn, w_down)
     d_gate = (d_hidden * up_vals * (sig * (1.0 + gate * (1.0 - sig)))).astype(BF16)
     d_up = (d_hidden * (gate * sig)).astype(BF16)
     d_ffn_in = quad_scatter(lambda r: mm(d_gate[r], w_gate, NT) + mm(d_up[r], w_up, NT))
-    gate_sum = weight_sum(ffn_in, d_gate)
-    up_sum = weight_sum(ffn_in, d_up)
+    down_sum, gate_sum, up_sum = scatter_all(
+        [(d_ffn, hidden), (ffn_in, d_gate), (ffn_in, d_up)], tuple((i, 0, hid) for i in range(3)), 2
+    )
     ffn = quad_scatter(lambda r: mm(hidden[r], w_down, NT))
     block_out = whole_rows(ring.order((live * (resid + ffn)).astype(BF16), width, back=True))
     d_norm, ffn_gain_part = norm_back(resid, gain_ffn, d_ffn_in)
@@ -509,8 +764,11 @@
     d_mixed = mm(d_attn, w_out)
     d_proj = mixer_backward(proj, saved, d_mixed)
     d_attn_in = quad_scatter(lambda r: mm(d_proj[r], w_in, NT))
-    out_sum = weight_sum(d_attn, mixed)
-    in_sum = weight_sum(attn_in, d_proj)
+    out_sum, *in_sum = scatter_all(
+        [(d_attn, mixed), (attn_in, d_proj)],
+        ((0, 0, KDIM), (1, 0, KDIM), (1, KDIM, KDIM), (1, 2 * KDIM, KDIM), (1, 3 * KDIM, 128)),
+        3,
+    )
     d_input, attn_gain_part = norm_back(own_inputs, gain_attn, d_attn_in)
     input_grad = whole_rows(ring.order(d_h + d_input, width, back=True))
 
@@ -535,10 +793,10 @@
         input_grad,
         both[0],
         both[1],
-        columns(in_sum, 0, KDIM),
-        columns(in_sum, KDIM, 2 * KDIM),
-        columns(in_sum, 2 * KDIM, 3 * KDIM),
-        columns(in_sum, 3 * KDIM, 3 * KDIM + SLOTS),
+        columns(in_sum[0], 0, KDIM),
+        columns(in_sum[1], 0, KDIM),
+        columns(in_sum[2], 0, KDIM),
+        columns(in_sum[3], 0, SLOTS),
         columns(out_sum, 0, KDIM),
         jnp.concatenate(gate_sum, axis=1),
         jnp.concatenate(up_sum, axis=1),

time: 1340 us -> 1050 us (0.78)
  waiting for transfers between devices: 792 us -> 140 us
  Pallas kernels: 31.1 us -> 645 us
  starting transfers between devices: 239 us -> 14.7 us
  local copies, waits for them, and re-layouts: 25.3 us -> 6.84 us
    ppermute x74 -> x4, waiting for transfers between devices: 686 us -> 4.93 us  [send(): return lax.ppermute(value, 'dp', self.perm(stride, size, shift % size))]
    pallas_call x0 -> x4, Pallas kernels: none -> 614 us  [the longest x2 313 us: scatter_call(): pl.pallas_call(functools.partial(scatter_kernel, chunks, len(terms)), in_...]
    ppermute x74 -> x4, starting transfers between devices: 218 us -> 4.24 us  [send(): return lax.ppermute(value, 'dp', self.perm(stride, size, shift % size))]
    ppermute x19 -> x9, waiting for transfers between devices: 105 us -> 131 us  [swap(): return lax.ppermute(value, 'dp', self.perm(1, 2, 1))]
    unnamed x148 -> x120, local copies, waits for them, and re-layouts: 21.3 us -> 5.28 us
    dot_general x60 -> x25, matrix products: 186 us -> 176 us  [mm(): lax.dot_general(left, right, dims, preferred_element_type=F32).astype(kind)]
  transfers between devices with their start and end apart: 104 -> 24, of which waited for: 58 -> 14; matrix products, arithmetic and copies ran while one was open for 11% -> 14% of each run, Pallas kernels for 1% -> 61%
where the time goes in v2:
time: 1050 us; the launch traced here: 1040 us
  Pallas kernels  645 us (61%)
  matrix products  176 us (17%)
  waiting for transfers between devices  140 us (13%)
  other arithmetic  54.6 us (5%)
  starting transfers between devices  14.7 us (1%)
    pallas_call x2, Pallas kernels, scatter_call(): pl.pallas_call(functools.partial(scatter_kernel, chunks, len(terms)), in_...  313 us
    pallas_call x2, Pallas kernels, gather_call(): pl.pallas_call(functools.partial(gather_kernel, chunks, len(widths)), in_...  300 us
    dot_general x25, matrix products, mm(): lax.dot_general(left, right, dims, preferred_element_type=F32).astype(kind)  176 us
    ppermute x9, waiting for transfers between devices, swap(): return lax.ppermute(value, 'dp', self.perm(1, 2, 1))  131 us
  transfers between devices with their start and end apart: 24, of which 14 were waited for; matrix products, arithmetic and copies ran while one was open for 14% of the time, Pallas kernels for 61%

profile of v2, /device:TPU:0, one launch (start us, length us, event | category | flops | bytes accessed | tf_op | source)
XLA Modules:
  0.0 1041.5 jit_solution(18176671719798416716)
XLA Ops:
  6.6 22.8 %collective-permute-done = bf16[256,2048]{1,0:T(8,128)(2,1)S(1)} collective-permute-done((bf16[256,2048]{1,0:T(8,128)(2,1)S(1)}, bf16[256,2048]{1,0:T(8,128)(2,1)S(1)}, u32[]{:S(2)}, u32[]{:S(2)}) %collective-permute-start) | collective-permute-done | bytes 1048608 | tf_op jit(solution)/shard_map/ppermute | solution.py:529
  35.3 103.4 %gather_weights.2 = (bf16[8,256,1664]{2,1,0:T(8,128)(2,1)}, bf16[8,256,512]{2,1,0:T(8,128)(2,1)}) custom-call(bf16[128,128]{1,0:T(8,128)(2,1)} %broadcast_select_fusion.31.refs_0_, bf16[128,512]{1,0:T(8,128)(2,1)} %get-tuple-element.161.refs_1_, bf16[128,512]{1,0:T(8,128)(2,1)} %get-tuple-element.159.refs_2_, bf16[128,512]{1,0:T(8,128)(2,1)} %get-tuple-element.157.refs_3_, ...), custom_call_target="tpu_custom_call" | custom-call | tf_op jit(solution)/shard_map/gather_weights/pallas_call | solution.py:377
  144.4 14.8 %fusion.71.q_ref.k_ref.v_ref.f_ref = f32[1024,1664]{1,0:T(8,128)} fusion(bf16[2048,1664]{1,0:T(8,128)(2,1)} %bitcast.92, f32[2048]{0:T(1024)S(1)} %bitcast.101, f32[1024]{0:T(1024)S(1)} %add_rsqrt_fusion, bf16[512,2048]{1,0:T(8,128)(2,1)} %collective-permute-done.1, bf16[256,2048]{1,0:T(8,128)(2,1)S(1)} %collective-permute-done, ...), kind=kOutput, calls=%fused_computation.234 | convolution fusion | flops 6998196224 | bytes 17838080 | tf_op jit(solution)/shard_map/dot_general | solution.py:610
  159.2 13.0 %mixer_forward.1 = (bf16[1024,512]{1,0:T(8,128)(2,1)S(1)}, f32[1024,128]{1,0:T(8,128)S(1)}, f32[1024,128]{1,0:T(8,128)S(1)}, f32[1024,256]{1,0:T(8,128)S(1)}, f32[1024,256]{1,0:T(8,128)S(1)}) custom-call(f32[1024,1664]{1,0:T(8,128)} %fusion.71.q_ref.k_ref.v_ref.f_ref, f32[1024,1664]{1,0:T(8,128)} %fusion.71.q_ref.k_ref.v_ref.f_ref, ...), custom_call_target="tpu_custom_call" | custom-call | flops 3072000000 | bytes 10240000 | tf_op jit(solution)/shard_map/mixer_forward/pallas_call | solution.py:251
  187.4 24.3 %collective-permute-done.3 = bf16[256,2048]{1,0:T(8,128)(2,1)S(1)} collective-permute-done((bf16[256,2048]{1,0:T(8,128)(2,1)S(1)}, bf16[256,2048]{1,0:T(8,128)(2,1)S(1)}, u32[]{:S(2)}, u32[]{:S(2)}) %collective-permute-start.3) | collective-permute-done | bytes 1048608 | tf_op jit(solution)/shard_map/ppermute | solution.py:529
  215.4 23.8 %collective-permute-done.4 = bf16[256,2048]{1,0:T(8,128)(2,1)S(1)} collective-permute-done((bf16[256,2048]{1,0:T(8,128)(2,1)S(1)}, bf16[256,2048]{1,0:T(8,128)(2,1)S(1)}, u32[]{:S(2)}, u32[]{:S(2)}) %collective-permute-start.4) | collective-permute-done | bytes 1048608 | tf_op jit(solution)/shard_map/ppermute | solution.py:529
  245.9 196.7 %gather_weights.3 = (bf16[8,256,1408]{2,1,0:T(8,128)(2,1)}, bf16[8,256,1408]{2,1,0:T(8,128)(2,1)}, bf16[8,256,1408]{2,1,0:T(8,128)(2,1)}) custom-call(bf16[128,1408]{1,0:T(8,128)(2,1)} %get-tuple-element.145.refs_0_, bf16[128,1408]{1,0:T(8,128)(2,1)} %get-tuple-element.143.refs_1_, bf16[128,640]{1,0:T(8,128)(2,1)} %get-tuple-element.141.refs_2_, ...), custom_call_target="tpu_custom_call" | custom-call | tf_op jit(solution)/shard_map/gather_weights/pallas_call | solution.py:377
  445.2 12.3 %fusion.74 = f32[1024,1408]{1,0:T(8,128)} fusion(bf16[2048,1408]{1,0:T(8,128)(2,1)} %bitcast.132, bf16[512,2048]{1,0:T(8,128)(2,1)} %collective-permute-done.5, bf16[256,2048]{1,0:T(8,128)(2,1)S(1)} %copy-done.20, bf16[256,2048]{1,0:T(8,128)(2,1)S(1)} %multiply_convert_fusion.3), kind=kOutput, calls=%fused_computation.236 | convolution fusion | flops 5918162944 | bytes 15728640 | tf_op jit(solution)/shard_map/dot_general | solution.py:610
  457.5 9.7 fusion.73
  468.5 15.0 %multiply_convert_fusion = (bf16[1024,1408]{1,0:T(8,128)(2,1)}, bf16[1024,1408]{1,0:T(8,128)(2,1)}, bf16[1024,1408]{1,0:T(8,128)(2,1)}) fusion(f32[1024,1408]{1,0:T(8,128)} %fusion.74, f32[1024,1408]{1,0:T(8,128)} %fusion.73, bf16[2048,1408]{1,0:T(8,128)(2,1)S(1)} %bitcast.120, bf16[512,2048]{1,0:T(8,128)(2,1)} %copy-done.47, ...), kind=kOutput, calls=%fused_computation.9 | convolution fusion | flops 5939789824 | bytes 30146560 | tf_op jit(solution)/shard_map/dot_general | solution.py:610
  483.5 8.5 fusion.26
  492.0 4.8 fusion.42
  496.9 8.5 convolution_add_fusion
  507.7 6.8 fusion.28
  514.6 6.1 fusion.39
  520.7 10.7 %convolution_convert_fusion.2 = bf16[2048,1408]{1,0:T(8,128)(2,1)} fusion(bf16[1024,1408]{1,0:T(8,128)(2,1)} %get-tuple-element.127, bf16[512,2048]{1,0:T(8,128)(2,1)S(1)} %copy-done.48, bf16[256,2048]{1,0:T(8,128)(2,1)} %collective-permute-done.9, bf16[256,2048]{1,0:T(8,128)(2,1)} %multiply_convert_fusion.4), kind=kOutput, calls=%fused_computation.7 | convolution fusion | flops 5921046528 | bytes 12845056 | tf_op jit(solution)/shard_map/dot_general | solution.py:610
  531.4 11.0 %convolution_convert_fusion.1 = bf16[2048,1408]{1,0:T(8,128)(2,1)} fusion(bf16[1024,1408]{1,0:T(8,128)(2,1)} %get-tuple-element.126, bf16[512,2048]{1,0:T(8,128)(2,1)} %collective-permute-done.5, bf16[256,2048]{1,0:T(8,128)(2,1)S(1)} %copy-done.20, bf16[256,2048]{1,0:T(8,128)(2,1)S(1)} %multiply_convert_fusion.3), kind=kOutput, calls=%fused_computation.6 | convolution fusion | flops 5921046528 | bytes 12845056 | tf_op jit(solution)/shard_map/dot_general | solution.py:610
  542.5 4.0 fusion.12
  548.0 4.0 fusion.14
  555.6 17.1 %collective-permute-done.12 = bf16[256,2048]{1,0:T(8,128)(2,1)S(1)} collective-permute-done((bf16[256,2048]{1,0:T(8,128)(2,1)}, bf16[256,2048]{1,0:T(8,128)(2,1)S(1)}, u32[]{:S(2)}, u32[]{:S(2)}) %collective-permute-start.12) | collective-permute-done | bytes 1048608 | tf_op jit(solution)/shard_map/ppermute | solution.py:529
  573.6 21.1 %collective-permute-done.7 = bf16[256,2048]{1,0:T(8,128)(2,1)S(1)} collective-permute-done((bf16[256,2048]{1,0:T(8,128)(2,1)}, bf16[256,2048]{1,0:T(8,128)(2,1)S(1)}, u32[]{:S(2)}, u32[]{:S(2)}) %collective-permute-start.7) | collective-permute-done | bytes 1048608 | tf_op jit(solution)/shard_map/ppermute | solution.py:529
  597.4 10.7 %convolution_convert_fusion = bf16[2048,1408]{1,0:T(8,128)(2,1)} fusion(bf16[1024,1408]{1,0:T(8,128)(2,1)} %get-tuple-element.125, bf16[512,2048]{1,0:T(8,128)(2,1)} %collective-permute-done.5, bf16[256,2048]{1,0:T(8,128)(2,1)S(1)} %copy-done.20, bf16[256,2048]{1,0:T(8,128)(2,1)S(1)} %multiply_convert_fusion.3), kind=kOutput, calls=%fused_computation.5 | convolution fusion | flops 5921046528 | bytes 12845056 | tf_op jit(solution)/shard_map/dot_general | solution.py:610
  608.1 205.1 %sum_gradients.3 = (f32[128,1408]{1,0:T(8,128)}, f32[128,1408]{1,0:T(8,128)}, f32[128,1408]{1,0:T(8,128)}, f32[128,1408]{1,0:T(8,128)}, f32[128,1408]{1,0:T(8,128)}, /*index=5*/f32[128,1408]{1,0:T(8,128)}) custom-call(bf16[8,256,1408]{2,1,0:T(8,128)(2,1)} %bitcast.87, bf16[8,256,1408]{2,1,0:T(8,128)(2,1)} %bitcast.88, bf16[8,256,1408]{2,1,0:T(8,128)(2,1)} %bitcast.89), custom_call_target="tpu_custom_call" | custom-call | tf_op jit(solution)/shard_map/sum_gradients/pallas_call | solution.py:481
  820.9 4.3 fusion.22.d_ref
  825.2 18.5 %mixer_backward.1 = bf16[1024,1664]{1,0:T(8,128)(2,1)} custom-call(f32[1024,1664]{1,0:T(8,128)} %fusion.71.q_ref.k_ref.v_ref.f_ref, f32[1024,1664]{1,0:T(8,128)} %fusion.71.q_ref.k_ref.v_ref.f_ref, f32[1024,1664]{1,0:T(8,128)} %fusion.71.q_ref.k_ref.v_ref.f_ref, f32[1024,1664]{1,0:T(8,128)} %fusion.71.q_ref.k_ref.v_ref.f_ref, f32[1024,128]{1,0:T(8,128)S(1)} %copy-done.3, ...), custom_call_target="tpu_custom_call" | custom-call | flops 9216000000 | bytes 16384000 | tf_op jit(solution)/shard_map/mixer_backward/pallas_call | solution.py:266
  843.8 9.5 fusion.23
  859.3 5.1 convolution_convert_fusion.4
  864.4 11.4 %convolution_convert_fusion.3 = bf16[2048,1664]{1,0:T(8,128)(2,1)} fusion(bf16[1024,1664]{1,0:T(8,128)(2,1)S(1)} %copy-done.18, f32[2048]{0:T(1024)S(1)} %bitcast.102, f32[1024]{0:T(1024)S(1)} %copy-done.41, bf16[512,2048]{1,0:T(8,128)(2,1)} %collective-permute-done.1, bf16[256,2048]{1,0:T(8,128)(2,1)S(1)} %copy-done.17, bf16[256,2048]{1,0:T(8,128)(2,1)S(1)} %copy-done.10), kind=kOutput, calls=%fused_computation.8 | convolution fusion | flops 7001604096 | bytes 14430208 | tf_op jit(solution)/shard_map/dot_general | solution.py:610
  875.8 108.3 %sum_gradients.2 = (f32[128,512]{1,0:T(8,128)}, f32[128,512]{1,0:T(8,128)}, f32[128,512]{1,0:T(8,128)}, f32[128,512]{1,0:T(8,128)}, f32[128,128]{1,0:T(8,128)}, ...) custom-call(bf16[8,256,512]{2,1,0:T(8,128)(2,1)} %bitcast.90, ...), custom_call_target="tpu_custom_call" | custom-call | tf_op jit(solution)/shard_map/sum_gradients/pallas_call | solution.py:481
  986.5 5.8 fusion.10
  996.8 19.1 %collective-permute-done.16 = bf16[256,2048]{1,0:T(8,128)(2,1)S(1)} collective-permute-done((bf16[256,2048]{1,0:T(8,128)(2,1)S(1)}, bf16[256,2048]{1,0:T(8,128)(2,1)S(1)}, u32[]{:S(2)}, u32[]{:S(2)}) %collective-permute-start.16) | collective-permute-done | bytes 1048608 | tf_op jit(solution)/shard_map/ppermute | solution.py:529
  1036.0 5.0 maximum_select_fusion
  (266 shorter events, 96.0 us)
Async XLA Ops:
  3.0 28.0 %copy-start.34 = (bf16[128,128]{1,0:T(8,128)(2,1)S(1)}, bf16[128,128]{1,0:T(8,128)(2,1)}, u32[]{:S(2)}) copy-start(bf16[128,128]{1,0:T(8,128)(2,1)} %param.22) | copy-start | bytes 98308
  3.1 29.3 %copy-start.30 = (bf16[128,1024]{1,0:T(8,128)(2,1)S(1)}, bf16[128,1024]{1,0:T(8,128)(2,1)}, u32[]{:S(2)}) copy-start(bf16[128,1024]{1,0:T(8,128)(2,1)} %param.19) | copy-start | bytes 786436
  3.2 30.0 %copy-start.31 = (bf16[128,1024]{1,0:T(8,128)(2,1)S(1)}, bf16[128,1024]{1,0:T(8,128)(2,1)}, u32[]{:S(2)}) copy-start(bf16[128,1024]{1,0:T(8,128)(2,1)} %param.20) | copy-start | bytes 786436
  3.3 140.6 %copy-start.8 = (bf16[256,2048]{1,0:T(8,128)(2,1)}, bf16[256,2048]{1,0:T(8,128)(2,1)S(1)}, u32[]{:S(2)}) copy-start(bf16[256,2048]{1,0:T(8,128)(2,1)S(1)} %select_dynamic-update-slice_fusion.24) | copy-start | bytes 3145732
  3.3 26.2 %collective-permute-start = (bf16[256,2048]{1,0:T(8,128)(2,1)S(1)}, bf16[256,2048]{1,0:T(8,128)(2,1)S(1)}, u32[]{:S(2)}, u32[]{:S(2)}) collective-permute-start(bf16[256,2048]{1,0:T(8,128)(2,1)S(1)} %select_dynamic-update-slice_fusion.24), channel_id=1, source_target_pairs={{0,2},{2,0},{4,6},{6,4},{8,10},{10,8},{12,14},{14,12},{16,18},{18,... | collective-permute-start | bytes 3145736 | tf_op jit(solution)/shard_map/ppermute | solution.py:529
  6.6 28.0 %copy-start.33 = (bf16[128,1024]{1,0:T(8,128)(2,1)S(1)}, bf16[128,1024]{1,0:T(8,128)(2,1)}, u32[]{:S(2)}) copy-start(bf16[128,1024]{1,0:T(8,128)(2,1)} %param.23) | copy-start | bytes 786436
  29.4 114.4 %copy-start.16 = (bf16[256,2048]{1,0:T(8,128)(2,1)}, bf16[256,2048]{1,0:T(8,128)(2,1)S(1)}, u32[]{:S(2)}) copy-start(bf16[256,2048]{1,0:T(8,128)(2,1)S(1)} %collective-permute-done) | copy-start | bytes 3145732
  31.0 110.6 %collective-permute-start.1 = (bf16[512,2048]{1,0:T(8,128)(2,1)}, bf16[512,2048]{1,0:T(8,128)(2,1)}, u32[]{:S(2)}, u32[]{:S(2)}) collective-permute-start(bf16[512,2048]{1,0:T(8,128)(2,1)} %pad_maximum_fusion.4), channel_id=1, source_target_pairs={{0,1},{1,0},{2,3},{3,2},{4,5},{5,4},{6,7},{7,6},{8,9},{9,8},{10,11... | collective-permute-start | bytes 6291464 | tf_op jit(solution)/shard_map/ppermute | solution.py:650
  175.6 7.5 collective-permute-start.2
  186.1 25.6 %collective-permute-start.3 = (bf16[256,2048]{1,0:T(8,128)(2,1)S(1)}, bf16[256,2048]{1,0:T(8,128)(2,1)S(1)}, u32[]{:S(2)}, u32[]{:S(2)}) collective-permute-start(bf16[256,2048]{1,0:T(8,128)(2,1)S(1)} %fusion.19), channel_id=1, source_target_pairs={{0,2},{2,0},{4,6},{6,4},{8,10},{10,8},{12,14},{14,12},{16,18},{18,... | collective-permute-start | bytes 3145736 | tf_op jit(solution)/shard_map/ppermute | solution.py:529
  214.1 230.5 %copy-start.38 = (f32[256]{0:T(256)}, f32[256]{0:T(256)S(1)}, u32[]{:S(2)}) copy-start(f32[256]{0:T(256)S(1)} %get-tuple-element.137) | copy-start | bytes 3076
  214.3 24.8 %collective-permute-start.4 = (bf16[256,2048]{1,0:T(8,128)(2,1)S(1)}, bf16[256,2048]{1,0:T(8,128)(2,1)S(1)}, u32[]{:S(2)}, u32[]{:S(2)}) collective-permute-start(bf16[256,2048]{1,0:T(8,128)(2,1)S(1)} %multiply_convert_fusion.3), channel_id=1, source_target_pairs={{0,2},{2,0},{4,6},{6,4},{8,10},{10,8},{12,14},{14,12},{16,18},{18,... | collective-permute-start | bytes 3145736 | tf_op jit(solution)/shard_map/ppermute | solution.py:529
  240.8 204.3 %collective-permute-start.5 = (bf16[512,2048]{1,0:T(8,128)(2,1)}, bf16[512,2048]{1,0:T(8,128)(2,1)}, u32[]{:S(2)}, u32[]{:S(2)}) collective-permute-start(bf16[512,2048]{1,0:T(8,128)(2,1)} %pad_maximum_fusion.5), channel_id=1, source_target_pairs={{0,1},{1,0},{2,3},{3,2},{4,5},{5,4},{6,7},{7,6},{8,9},{9,8},{10,11... | collective-permute-start | bytes 6291464 | tf_op jit(solution)/shard_map/ppermute | solution.py:650
  242.0 200.6 %collective-permute-start.9 = (bf16[256,2048]{1,0:T(8,128)(2,1)}, bf16[256,2048]{1,0:T(8,128)(2,1)}, u32[]{:S(2)}, u32[]{:S(2)}) collective-permute-start(bf16[256,2048]{1,0:T(8,128)(2,1)} %multiply_convert_fusion.4), channel_id=1, source_target_pairs={{0,2},{2,0},{4,6},{6,4},{8,10},{10,8},{12,14},{14,12},{16,18},{18,... | collective-permute-start | bytes 3145736 | tf_op jit(solution)/shard_map/ppermute | solution.py:529
  444.5 22.7 %collective-permute-start.10 = (bf16[512,2048]{1,0:T(8,128)(2,1)S(1)}, bf16[512,2048]{1,0:T(8,128)(2,1)S(1)}, u32[]{:S(2)}, u32[]{:S(2)}) collective-permute-start(bf16[512,2048]{1,0:T(8,128)(2,1)S(1)} %pad_maximum_fusion.6), channel_id=1, source_target_pairs={{0,1},{1,0},{2,3},{3,2},{4,5},{5,4},{6,7},{7,6},{8,9},{9,8},{10,11... | collective-permute-start | bytes 6291464 | tf_op jit(solution)/shard_map/ppermute | solution.py:650
  505.4 37.1 %collective-permute-start.11 = (f32[512,2048]{1,0:T(8,128)}, f32[512,2048]{1,0:T(8,128)S(1)}, u32[]{:S(2)}, u32[]{:S(2)}) collective-permute-start(f32[512,2048]{1,0:T(8,128)} %convolution_add_fusion), channel_id=1, source_target_pairs={{0,1},{1,0},{2,3},{3,2},{4,5},{5,4},{6,7},{7,6},{8,9},{9,8},{10,11... | collective-permute-start | bytes 12582920 | tf_op jit(solution)/shard_map/ppermute | solution.py:650
  514.5 33.5 %collective-permute-start.6 = (f32[512,2048]{1,0:T(8,128)}, f32[512,2048]{1,0:T(8,128)S(1)}, u32[]{:S(2)}, u32[]{:S(2)}) collective-permute-start(f32[512,2048]{1,0:T(8,128)} %fusion.28), channel_id=1, source_target_pairs={{0,1},{1,0},{2,3},{3,2},{4,5},{5,4},{6,7},{7,6},{8,9},{9,8},{10,11... | collective-permute-start | bytes 12582920 | tf_op jit(solution)/shard_map/ppermute | solution.py:650
  546.5 26.2 %collective-permute-start.12 = (bf16[256,2048]{1,0:T(8,128)(2,1)}, bf16[256,2048]{1,0:T(8,128)(2,1)S(1)}, u32[]{:S(2)}, u32[]{:S(2)}) collective-permute-start(bf16[256,2048]{1,0:T(8,128)(2,1)} %fusion.12), channel_id=1, source_target_pairs={{0,2},{2,0},{4,6},{6,4},{8,10},{10,8},{12,14},{14,12},{16,18},{18,... | collective-permute-start | bytes 3145736 | tf_op jit(solution)/shard_map/ppermute | solution.py:529
  552.0 42.7 %collective-permute-start.7 = (bf16[256,2048]{1,0:T(8,128)(2,1)}, bf16[256,2048]{1,0:T(8,128)(2,1)S(1)}, u32[]{:S(2)}, u32[]{:S(2)}) collective-permute-start(bf16[256,2048]{1,0:T(8,128)(2,1)} %fusion.14), channel_id=1, source_target_pairs={{0,2},{2,0},{4,6},{6,4},{8,10},{10,8},{12,14},{14,12},{16,18},{18,... | collective-permute-start | bytes 3145736 | tf_op jit(solution)/shard_map/ppermute | solution.py:529
  555.6 39.1 %copy-start.15 = (f32[256,2048]{1,0:T(8,128)S(1)}, f32[256,2048]{1,0:T(8,128)}, u32[]{:S(2)}) copy-start(f32[256,2048]{1,0:T(8,128)} %copy-done.14) | copy-start | bytes 6291460
  595.8 219.4 %collective-permute-start.13 = (bf16[256,2048]{1,0:T(8,128)(2,1)S(1)}, bf16[256,2048]{1,0:T(8,128)(2,1)}, u32[]{:S(2)}, u32[]{:S(2)}) collective-permute-start(bf16[256,2048]{1,0:T(8,128)(2,1)S(1)} %get-tuple-element.81), channel_id=1, source_target_pairs={{0,2},{2,0},{4,6},{6,4},{8,10},{10,8},{12,14},{14,12},{16,18},{18,... | collective-permute-start | bytes 3145736 | tf_op jit(solution)/shard_map/ppermute | solution.py:529
  816.7 4.2 collective-permute-start.14
  817.7 39.2 %collective-permute-start.8 = (bf16[256,2048]{1,0:T(8,128)(2,1)S(1)}, bf16[256,2048]{1,0:T(8,128)(2,1)S(1)}, u32[]{:S(2)}, u32[]{:S(2)}) collective-permute-start(bf16[256,2048]{1,0:T(8,128)(2,1)S(1)} %select_dynamic-update-slice_fusion.16), channel_id=1, source_target_pairs={{0,1},{1,0},{2,3},{3,2},{4,5},{5,4},{6,7},{7,6},{8,9},{9,8},{10,11... | collective-permute-start | bytes 3145736 | tf_op jit(solution)/shard_map/ppermute | solution.py:650
  853.2 133.3 %collective-permute-start.15 = (f32[512,2048]{1,0:T(8,128)}, f32[512,2048]{1,0:T(8,128)}, u32[]{:S(2)}, u32[]{:S(2)}) collective-permute-start(f32[512,2048]{1,0:T(8,128)} %fusion.23), channel_id=1, source_target_pairs={{0,1},{1,0},{2,3},{3,2},{4,5},{5,4},{6,7},{7,6},{8,9},{9,8},{10,11... | collective-permute-start | bytes 12582920 | tf_op jit(solution)/shard_map/ppermute | solution.py:650
  992.3 23.6 %collective-permute-start.16 = (bf16[256,2048]{1,0:T(8,128)(2,1)S(1)}, bf16[256,2048]{1,0:T(8,128)(2,1)S(1)}, u32[]{:S(2)}, u32[]{:S(2)}) collective-permute-start(bf16[256,2048]{1,0:T(8,128)(2,1)S(1)} %fusion.10), channel_id=1, source_target_pairs={{0,2},{2,0},{4,6},{6,4},{8,10},{10,8},{12,14},{14,12},{16,18},{18,... | collective-permute-start | bytes 3145736 | tf_op jit(solution)/shard_map/ppermute | solution.py:529
  1019.7 1.2 collective-permute-start.18
  1019.8 16.2 %collective-permute-start.17 = (f32[256,2048]{1,0:T(8,128)S(1)}, f32[256,2048]{1,0:T(8,128)}, u32[]{:S(2)}, u32[]{:S(2)}) collective-permute-start(f32[256,2048]{1,0:T(8,128)S(1)} %select_dynamic-update-slice_fusion), channel_id=1, source_target_pairs={{0,1},{1,0},{2,3},{3,2},{4,5},{5,4},{6,7},{7,6},{8,9},{9,8},{10,11... | collective-permute-start | bytes 6291464 | tf_op jit(solution)/shard_map/ppermute | solution.py:650
  1020.9 3.7 collective-permute-start.19
  1024.7 3.6 collective-permute-start.22
  1026.4 4.5 collective-permute-start.21
  1026.4 5.4 collective-permute-start.20
  1031.8 3.6 collective-permute-start.23
  (51 other events, 467.8 us)

commit v3 on v1

--- a/solution.py
+++ b/solution.py
@@ -275,6 +275,606 @@
     )(proj, proj, proj, proj, weights, scores, products, mixing, grad)
 
 
+MESH = pl.DeviceIdType.MESH
+ANY = pl.BlockSpec(memory_space=pl.ANY)
+VMEM = pl.BlockSpec(memory_space=pltpu.VMEM)
+DMA = pltpu.SemaphoreType.DMA
+PIECE = 32
+
+
+class Place:
+    def __init__(self):
+        dp = lax.axis_index("dp")
+        self.core = lax.axis_index("head")
+        self.x, self.y, self.z = dp % 2, dp // 2 % 2, dp // 4
+        rest = dp % 4
+        self.peers = {
+            "x": (dp + 1 - 2 * self.x, self.core),
+            "y": (dp + 2 - 4 * self.y, self.core),
+            "up": ((self.z + 1) % 4 * 4 + rest, self.core),
+            "down": ((self.z + 3) % 4 * 4 + rest, self.core),
+            "core": (dp, 1 - self.core),
+        }
+
+    def greet(self):
+        ready = pltpu.get_barrier_semaphore()
+        for peer in self.peers.values():
+            pl.semaphore_signal(ready, inc=1, device_id=peer, device_id_type=MESH)
+        pl.semaphore_wait(ready, len(self.peers))
+
+    def copy(self, name, source, target, sems):
+        return pltpu.make_async_remote_copy(
+            src_ref=source,
+            dst_ref=target,
+            send_sem=sems[0],
+            recv_sem=sems[1],
+            device_id=self.peers[name],
+            device_id_type=MESH,
+        )
+
+    def half(self, size, other=False):
+        place = 1 - self.x if other else self.x
+        return pl.ds(pl.multiple_of(place * size, size), size)
+
+    def columns(self, index, size):
+        natural = (self.z + index % 4) % 4 * 2 + (self.y + index // 4) % 2
+        return pl.ds(pl.multiple_of(natural * size, size), size)
+
+
+class Sems:
+    def __init__(self, ref):
+        self.ref, self.used = ref, 0
+
+    def one(self):
+        self.used += 1
+        return self.ref.at[self.used - 1]
+
+    def two(self):
+        return (self.one(), self.one())
+
+
+def pieces(rows, work):
+    def step(i, carry):
+        work(pl.ds(pl.multiple_of(i * PIECE, PIECE), PIECE))
+        return carry
+
+    lax.fori_loop(0, rows // PIECE, step, 0)
+
+
+class Keep:
+    def __init__(self, sems, source, target, stage):
+        self.load = pltpu.make_async_copy(source, stage, sems.one())
+        self.store = pltpu.make_async_copy(stage, target, sems.one())
+
+    def start(self):
+        self.load.start()
+
+    def turn(self):
+        self.load.wait()
+        self.store.start()
+
+    def wait(self):
+        self.store.wait()
+
+
+class Quad:
+    def __init__(self, place, sems, source, target):
+        near = [pltpu.make_async_copy(source, target.at[0], sems.one())]
+        self.swap = place.copy("x", source, target.at[1], sems.two())
+        self.core = place.copy("core", source, target.at[2], sems.two())
+        self.last = place.copy("core", target.at[1], target.at[3], sems.two())
+        self.near = near
+
+    def start(self):
+        self.swap.start()
+        self.core.start()
+        for copy in self.near:
+            copy.start()
+
+    def forward(self):
+        self.swap.wait_recv()
+        self.last.start()
+
+    def finish(self):
+        self.swap.wait_send()
+        self.core.wait()
+        self.last.wait()
+        for copy in self.near:
+            copy.wait()
+
+
+class QuadSum:
+    def __init__(self, place, sems, terms, scratch):
+        self.near, self.theirs, self.far, self.swapped = scratch
+        self.core = place.copy("core", terms.at[pl.ds(2, 2)], self.theirs, sems.two())
+        self.load = pltpu.make_async_copy(terms.at[pl.ds(0, 2)], self.near, sems.one())
+        self.swap = place.copy("x", self.far, self.swapped, sems.two())
+
+    def start(self):
+        self.core.start()
+        self.load.start()
+
+    def middle(self):
+        self.core.wait()
+        self.load.wait()
+
+        def add(part):
+            self.far[part] = (self.near[1, part] + self.theirs[1, part]).astype(BF16)
+
+        pieces(SEQ_LEN, add)
+        self.swap.start()
+
+    def ready(self):
+        self.swap.wait()
+
+    def read(self, part):
+        return self.near[0, part] + self.theirs[0, part] + self.swapped[part].astype(F32)
+
+
+def quad_scratch(width):
+    return [
+        pltpu.VMEM((2, SEQ_LEN, width), F32),
+        pltpu.VMEM((2, SEQ_LEN, width), F32),
+        pltpu.VMEM((SEQ_LEN, width), BF16),
+        pltpu.VMEM((SEQ_LEN, width), BF16),
+    ]
+
+
+class Leave:
+    def __init__(self, place, sems, source, target):
+        rows = pl.ds(pl.multiple_of(place.core * SEQ_LEN, SEQ_LEN), SEQ_LEN)
+        width = source.shape[1] // 8
+        self.copies, self.here = [], []
+        for index in range(8):
+            part = source.at[:, pl.ds(index * width, width)]
+            there = target.at[rows, place.columns(index, width)]
+            self.copies.append(place.copy("core", part, there, sems.two()))
+            self.here.append(pltpu.make_async_copy(part, there, sems.one()))
+
+    def start(self):
+        for copy in self.copies + self.here:
+            copy.start()
+
+    def finish(self):
+        for copy in self.copies + self.here:
+            copy.wait()
+
+
+def gather_first_kernel(
+    tokens, q_w, k_w, v_w, small, out_w, gate_w, up_w, down_w, w_in, w_out, ffn, seqs, stage, held, sem
+):
+    place, sems = Place(), Sems(sem)
+    shard = q_w.shape[0]
+    rows = place.half(shard)
+    hid = gate_w.shape[1] // 2
+    chunks = [
+        (small, 128, w_in, 3 * KDIM, False, True),
+        (q_w, KDIM, w_in, 0, False, True),
+        (k_w, KDIM, w_in, KDIM, False, True),
+        (v_w, KDIM, w_in, 2 * KDIM, False, True),
+        (out_w, KDIM, w_out, 0, True, True),
+        (gate_w, hid, ffn, 0, False, False),
+        (up_w, hid, ffn, hid, False, False),
+        (down_w, hid, ffn, 2 * hid, False, False),
+    ]
+    place.greet()
+    swaps, keeps, rises, crosses = [], [], [], []
+    used = 0
+    for source, width, target, first, y_first, beyond in chunks:
+        cols = pl.ds(first, width)
+        where = target.at[0, rows, cols] if beyond else target.at[rows, cols]
+        swaps.append(place.copy("x", source.at[:, place.half(width, True)], where, sems.two()))
+        keeps.append(Keep(sems, source.at[:, place.half(width)], where, stage.at[:, pl.ds(used, width)]))
+        used += width
+        if not beyond:
+            continue
+
+        def block(index, target=target, cols=cols):
+            return target.at[index, :, cols]
+
+        rises.append(
+            [
+                [place.copy("up", block((4 - step) % 4 + 4 * u), block(3 - step + 4 * u), sems.two()) for step in range(3)]
+                for u in range(2 if y_first else 1)
+            ]
+        )
+        crosses.append(
+            [place.copy("y", block(i), block(4 + i), sems.two()) for i in range(1 if y_first else 4)]
+        )
+    for swap, keep in zip(swaps[:5], keeps[:5]):
+        swap.start()
+        keep.start()
+    width = tokens.shape[1] // 8
+    mine = pl.ds(pl.multiple_of(place.core * SEQ_LEN, SEQ_LEN), SEQ_LEN)
+    near, far, side, last = [], [], [], []
+    for index in range(8):
+        part = tokens.at[mine, place.columns(index, width)]
+        cols = pl.ds(index * width, width)
+        far.append(place.copy("x", part, seqs.at[1, :, cols], sems.two()))
+        side.append(place.copy("core", part, seqs.at[2, :, cols], sems.two()))
+        near.append(Keep(sems, part, seqs.at[0, :, cols], held.at[:, cols]))
+    last.append(place.copy("core", seqs.at[1], seqs.at[3], sems.two()))
+    for copy in far + side + near:
+        copy.start()
+    for swap, keep in zip(swaps[5:], keeps[5:]):
+        swap.start()
+        keep.start()
+    for keep in keeps + near:
+        keep.turn()
+    for c in range(5):
+        keeps[c].wait()
+        swaps[c].wait_recv()
+        rises[c][0][0].start()
+        crosses[c][0].start()
+    for step in range(3):
+        if step == 0:
+            for c in range(5):
+                if chunks[c][4]:
+                    crosses[c][0].wait_recv()
+                    rises[c][1][0].start()
+        if step == 1:
+            for copy in far:
+                copy.wait_recv()
+            last[0].start()
+        for c in range(5):
+            for rise in rises[c]:
+                rise[step].wait_recv()
+                if step < 2:
+                    rise[step + 1].start()
+            if not chunks[c][4]:
+                crosses[c][3 - step].start()
+    for c in range(5):
+        for cross in crosses[c]:
+            cross.wait_send()
+        if not chunks[c][4]:
+            for cross in crosses[c]:
+                cross.wait_recv()
+        for rise in rises[c]:
+            for copy in rise:
+                copy.wait_send()
+    for swap in swaps[:5]:
+        swap.wait_send()
+    for swap, keep in zip(swaps[5:], keeps[5:]):
+        swap.wait()
+        keep.wait()
+    for copy in far:
+        copy.wait_send()
+    for copy in side + near + last:
+        copy.wait()
+
+
+def gather_ffn_kernel(
+    hid, cut, b0, b3, b4, terms, tokens, gain, d_ffn, w_gate, w_up, w_down, resid, ffn_in, d_all, s0, s1, s2, s3, kept, normed, inputs, low, stage, sem
+):
+    place, sems = Place(), Sems(sem)
+    chunks = [
+        (0, hid, w_gate, 0, False),
+        (hid, hid, w_up, 0, False),
+        (2 * hid, cut, w_down, 0, False),
+        (2 * hid + cut, hid - cut, w_down, cut, True),
+    ]
+    keeps, rises, crosses = [], [], []
+    for first, width, target, start, y_first in chunks:
+        cols, source = pl.ds(start, width), pl.ds(first, width)
+
+        def block(index, target=target, cols=cols):
+            return target.at[index, :, cols]
+
+        keeps += [
+            Keep(sems, b.at[:, source], block(i), stage.at[at, :, source])
+            for at, (b, i) in enumerate(((b0, 0), (b3, 3), (b4, 4)))
+        ]
+        lower = [
+            place.copy("up", b3.at[:, source], block(2), sems.two()),
+            place.copy("up", block(2), block(1), sems.two()),
+        ]
+        high = []
+        if y_first:
+            high = [
+                place.copy("up", b4.at[:, source], block(7), sems.two()),
+                place.copy("up", block(7), block(6), sems.two()),
+                place.copy("up", block(6), block(5), sems.two()),
+            ]
+            crosses.append([])
+        else:
+            crosses.append(
+                [
+                    place.copy("y", b3.at[:, source], block(7), sems.two()),
+                    place.copy("y", block(2), block(6), sems.two()),
+                    place.copy("y", block(1), block(5), sems.two()),
+                ]
+            )
+        rises.append((lower, high))
+    total = QuadSum(place, sems, terms, (s0, s1, s2, s3))
+    cot = Quad(place, sems, low, d_all)
+    fetch_low = pltpu.make_async_copy(d_ffn, low, sems.one())
+    out = Quad(place, sems, normed, ffn_in)
+    fetch = pltpu.make_async_copy(tokens.at[0], inputs, sems.one())
+    save = pltpu.make_async_copy(kept, resid, sems.one())
+    place.greet()
+    total.start()
+    fetch.start()
+    fetch_low.start()
+    for (lower, high), cross in zip(rises, crosses):
+        lower[0].start()
+        for copy in high[:1] + cross[:1]:
+            copy.start()
+    for copy in keeps:
+        copy.start()
+    total.middle()
+    for copy in keeps:
+        copy.turn()
+    fetch.wait()
+    for c, ((lower, high), cross) in enumerate(zip(rises, crosses)):
+        if c == 2:
+            total.ready()
+
+            def norm(part):
+                value = total.read(part) + inputs[part].astype(F32)
+                kept[part] = value
+                normed[part] = (value * rms(value) * gain[...]).astype(BF16)
+
+            pieces(SEQ_LEN, norm)
+            out.start()
+            save.start()
+            fetch_low.wait()
+            cot.start()
+        lower[0].wait_recv()
+        lower[1].start()
+        for copy in cross[1:2]:
+            copy.start()
+        if high:
+            high[0].wait_recv()
+            high[1].start()
+    for c, ((lower, high), cross) in enumerate(zip(rises, crosses)):
+        lower[1].wait_recv()
+        for copy in cross[2:]:
+            copy.start()
+        if high:
+            high[1].wait_recv()
+            high[2].start()
+        if c == 1:
+            out.forward()
+    cot.forward()
+    for (lower, high), cross in zip(rises, crosses):
+        for copy in cross:
+            copy.wait()
+        for copy in high[2:]:
+            copy.wait_recv()
+        for copy in lower + high:
+            copy.wait_send()
+    for copy in keeps:
+        copy.wait()
+    out.finish()
+    cot.finish()
+    save.wait()
+
+
+class Sum:
+    def __init__(self, place, sems, terms, given, result, first, width, scratch):
+        self.own, self.other, self.from_z, self.to_z, self.final = scratch
+        cols = pl.ds(first, width)
+        self.loads, self.crosses = [], []
+        for index in range(4):
+            self.loads.append(pltpu.make_async_copy(terms.at[index, :, cols], self.own.at[index], sems.one()))
+            if given is None:
+                self.crosses.append(place.copy("y", terms.at[4 + index, :, cols], self.other.at[index], sems.two()))
+            else:
+                self.loads.append(pltpu.make_async_copy(given.at[index, :, cols], self.other.at[index], sems.one()))
+        self.per = len(self.loads) // 4
+        self.rises = [place.copy("up", self.to_z.at[i], self.from_z.at[i], sems.two()) for i in range(3)]
+        half = self.final.shape[0] // 2
+        there = result.at[:, place.half(width)]
+        self.leave = pltpu.make_async_copy(self.final.at[place.half(half)], there, sems.one())
+        self.swap = place.copy("x", self.final.at[place.half(half, True)], there, sems.two())
+
+    def start(self, step):
+        index = 3 - step
+        for copy in self.crosses[index : index + 1] + self.loads[index * self.per : (index + 1) * self.per]:
+            copy.start()
+
+    def step(self, step):
+        index = 3 - step
+        for copy in self.loads[index * self.per : (index + 1) * self.per]:
+            copy.wait()
+        for copy in self.crosses[index : index + 1]:
+            copy.wait_recv()
+        if step:
+            self.rises[step - 1].wait_recv()
+
+        def add(part):
+            value = self.own[index, part].astype(F32) + self.other[index, part].astype(F32)
+            if step:
+                value = value + self.from_z[step - 1, part].astype(F32)
+            if step < 3:
+                self.to_z[step, part] = value.astype(BF16)
+            else:
+                self.final[part] = value
+
+        pieces(self.final.shape[0], add)
+        if step < 3:
+            self.rises[step].start()
+        else:
+            self.swap.start()
+            self.leave.start()
+
+    def finish(self):
+        for copy in self.crosses + self.rises:
+            copy.wait_send()
+        self.leave.wait()
+        self.swap.wait()
+
+
+def sum_scratch(rows, width):
+    return [pltpu.VMEM((depth, rows, width), BF16) for depth in (4, 4, 3, 3)] + [pltpu.VMEM((rows, width), F32)]
+
+
+def norm_back_piece(value, gain, grad):
+    scale = rms(value)
+    scaled = gain * grad
+    inner = jnp.mean(scaled * value, axis=-1, keepdims=True)
+    gains = (grad * value * scale).reshape(PIECE // 8, 8, value.shape[1])
+    return scale * scaled - value * (scale * scale * scale * inner), jnp.sum(gains, axis=0)
+
+
+def sum_ffn_kernel(
+    hid, gate, down, given, terms, resid, gain, d_res, out_terms, live, gate_sum, down_sum, d_h, d_attn, gain_sum, block_out, *scratch
+):
+    *scratch, sem = scratch
+    place, sems = Place(), Sems(sem)
+    first = Sum(place, sems, down, given, down_sum, 0, hid, scratch[0:5])
+    second = Sum(place, sems, gate, None, gate_sum, 0, hid, scratch[5:10])
+    back = QuadSum(place, sems, terms, scratch[10:14])
+    ahead = QuadSum(place, sems, out_terms, scratch[14:18])
+    value, res, low, shown = scratch[18:22]
+    quad = Quad(place, sems, low, d_attn)
+    leave = Leave(place, sems, shown, block_out)
+    fetch = [pltpu.make_async_copy(resid, value, sems.one()), pltpu.make_async_copy(d_res, res, sems.one())]
+    save = pltpu.make_async_copy(res, d_h, sems.one())
+    place.greet()
+    back.start()
+    for step in range(4):
+        second.start(step)
+        first.start(step)
+    for copy in fetch:
+        copy.start()
+    ahead.start()
+    first.step(0)
+    back.middle()
+    ahead.middle()
+    second.step(0)
+    for copy in fetch:
+        copy.wait()
+    first.step(1)
+    back.ready()
+    gain_sum[...] = jnp.zeros_like(gain_sum)
+
+    def norm(part):
+        d_norm, gains = norm_back_piece(value[part], gain[...], back.read(part))
+        grad = res[part] + d_norm
+        res[part] = grad
+        low[part] = grad.astype(BF16)
+        gain_sum[...] += gains
+
+    pieces(SEQ_LEN, norm)
+    quad.start()
+    save.start()
+    second.step(1)
+    first.step(2)
+    ahead.ready()
+
+    def show(part):
+        shown[part] = (live[part, :1] * (value[part] + ahead.read(part))).astype(BF16)
+
+    pieces(SEQ_LEN, show)
+    leave.start()
+    second.step(2)
+    quad.forward()
+    first.step(3)
+    second.step(3)
+    quad.finish()
+    save.wait()
+    leave.finish()
+    first.finish()
+    second.finish()
+
+
+def sum_last_kernel(
+    hid, up, given, out_t, in_t, terms, tokens, gain, d_h, ffn_gains, up_sum, out_sum, q_sum, k_sum, v_sum, f_sum, grad, gain_sum, *scratch
+):
+    *scratch, sem = scratch
+    place, sems = Place(), Sems(sem)
+    sums = []
+    for terms_in, given_in, result, start, width in (
+        (up, given, up_sum, 0, hid),
+        (out_t, None, out_sum, 0, KDIM),
+        (in_t, None, q_sum, 0, KDIM),
+        (in_t, None, k_sum, KDIM, KDIM),
+        (in_t, None, v_sum, 2 * KDIM, KDIM),
+        (in_t, None, f_sum, 3 * KDIM, 128),
+    ):
+        sums.append(Sum(place, sems, terms_in, given_in, result, start, width, scratch[: 5]))
+        scratch = scratch[5:]
+    back = QuadSum(place, sems, terms, scratch[0:4])
+    value, res, gains, parts, met, crossed, risen, rising, last, swapped = scratch[4:]
+    leave = Leave(place, sems, res, grad)
+    fetch = [pltpu.make_async_copy(tokens.at[0], value, sems.one()), pltpu.make_async_copy(d_h, res, sems.one())]
+    meet = place.copy("core", parts, met, sems.two())
+    cross = place.copy("y", parts.at[pl.ds(4, 4)], crossed, sems.two())
+    rise = [place.copy("up", rising.at[i], risen.at[i], sems.two()) for i in range(3)]
+    swap = place.copy("x", last.at[1 - place.x], swapped, sems.two())
+    place.greet()
+    back.start()
+    for step in range(4):
+        for one in sums:
+            one.start(step)
+    for copy in fetch:
+        copy.start()
+    sums[0].step(0)
+    back.middle()
+    for one in sums[1:]:
+        one.step(0)
+    for copy in fetch:
+        copy.wait()
+    gains[...] = jnp.zeros_like(gains)
+    back.ready()
+
+    def norm(part):
+        d_norm, added = norm_back_piece(value[part].astype(F32), gain[...], back.read(part))
+        res[part] = res[part] + d_norm
+        gains[...] += added
+
+    pieces(SEQ_LEN, norm)
+    leave.start()
+    width = res.shape[1] // 8
+    parts[...] = jnp.zeros_like(parts)
+    for row, source in enumerate((gains[...], ffn_gains[...])):
+        summed = jnp.sum(source, axis=0, keepdims=True)
+        for index in range(8):
+            parts[index, row : row + 1, :] = summed[:, index * width : (index + 1) * width]
+    meet.start()
+    for one in sums:
+        one.step(1)
+    meet.wait()
+    parts[...] = parts[...] + met[...]
+    cross.start()
+    for one in sums:
+        one.step(2)
+    cross.wait()
+    rising[0] = parts[3] + crossed[3]
+    rise[0].start()
+    for one in sums:
+        one.step(3)
+    for step in (1, 2):
+        rise[step - 1].wait_recv()
+        rising[step] = parts[3 - step] + crossed[3 - step] + risen[step - 1]
+        rise[step].start()
+    rise[2].wait_recv()
+    total = parts[0] + crossed[0] + risen[2]
+    last[0] = total[:, : width // 2]
+    last[1] = total[:, width // 2 :]
+    swap.start()
+    swap.wait()
+    gain_sum[...] = last[place.x] + swapped[...]
+    for copy in rise:
+        copy.wait_send()
+    leave.finish()
+    for one in sums:
+        one.finish()
+
+
+def call(kernel, name, ident, inputs, specs, outputs, out_specs, scratch, sems):
+    return pl.pallas_call(
+        kernel,
+        in_specs=specs,
+        out_specs=out_specs,
+        out_shape=[jax.ShapeDtypeStruct(shape, kind) for shape, kind in outputs],
+        scratch_shapes=scratch + [DMA((sems,))],
+        compiler_params=pltpu.CompilerParams(collective_id=ident, has_side_effects=True, vmem_limit_bytes=60 << 20),
+        name=name,
+    )(*inputs)
+
+
 PAD = 128 - SLOTS
 
 
@@ -396,7 +996,7 @@
     return scale * scaled - values * (scale * scale * scale * inner), jnp.sum(grad * values * scale, axis=0)
 
 
-def body(
+def body_by_permutes(
     tokens,
     seq_count,
     valid_len,
@@ -494,11 +1094,11 @@
     gate, up_vals = mm(ffn_in, w_gate), mm(ffn_in, w_up)
     sig = jax.nn.sigmoid(gate)
     hidden = (gate * sig * up_vals).astype(BF16)
-    down_sum = weight_sum(d_ffn, hidden)
     d_hidden = mm(d_ffn, w_down)
     d_gate = (d_hidden * up_vals * (sig * (1.0 + gate * (1.0 - sig)))).astype(BF16)
     d_up = (d_hidden * (gate * sig)).astype(BF16)
     d_ffn_in = quad_scatter(lambda r: mm(d_gate[r], w_gate, NT) + mm(d_up[r], w_up, NT))
+    down_sum = weight_sum(d_ffn, hidden)
     gate_sum = weight_sum(ffn_in, d_gate)
     up_sum = weight_sum(ffn_in, d_up)
     ffn = quad_scatter(lambda r: mm(hidden[r], w_down, NT))
@@ -546,8 +1146,186 @@
     )
 
 
+def body_by_kernels(
+    tokens,
+    seq_count,
+    valid_len,
+    attn_gain,
+    ffn_gain,
+    q_weight,
+    k_weight,
+    v_weight,
+    forget_weight,
+    out_weight,
+    gate_weight,
+    up_weight,
+    down_weight,
+    cotangent,
+    *,
+    ring,
+):
+    shard, dim = q_weight.shape[0], tokens.shape[1]
+    width, hid = 2 * shard, gate_weight.shape[1] // 2
+    core = lax.axis_index("head")
+    first = core == 0
+    up_z, over_y = (lambda value: ring.send(value, ring.stages[0], 1)), (lambda value: ring.send(value, ring.stages[1], 1))
+    rows4 = (4, SEQ_LEN, dim)
+    blocks = lambda value: value.reshape(-1, width, value.shape[-1])
+    flat = lambda value: value.reshape(-1, value.shape[-1])
+    half = dim // 2
+
+    gains = jnp.concatenate([attn_gain[:, None], ffn_gain[:, None], jnp.zeros((shard, PAD - 2), BF16)], axis=1)
+    small = jnp.concatenate([forget_weight[:, :SLOTS], gains, forget_weight[:, SLOTS:], gains], axis=1)
+    w_in, w_out, part0, seqs = call(
+        gather_first_kernel,
+        "gather_first",
+        0,
+        (tokens, q_weight, k_weight, v_weight, small, out_weight, gate_weight, up_weight, down_weight),
+        [ANY] * 9,
+        [((8, width, WIDE), BF16), ((8, width, KDIM), BF16), ((width, 3 * hid), BF16), (rows4, BF16)],
+        [ANY] * 4,
+        [pltpu.VMEM((shard, 4 * KDIM + 128 + 3 * hid), BF16), pltpu.VMEM((SEQ_LEN, dim), BF16)],
+        200,
+    )
+    part3, part4 = up_z(part0), over_y(part0)
+    w_in, w_out = flat(w_in), flat(w_out)
+    gain_attn = w_in[:, WIDE - PAD].astype(F32)[None, :]
+    gain_ffn = w_in[:, WIDE - PAD + 1].astype(F32)[None, :]
+    inputs = flat(seqs).astype(F32)
+    attn_in = (inputs * rms(inputs) * gain_attn).astype(BF16)
+    proj = mm(attn_in, w_in)
+    mixed, *saved = mixer_forward(proj)
+    attn_terms = mm(mixed, w_out, NT).reshape(rows4)
+    places = lax.broadcasted_iota(jnp.int32, (SEQ_LEN, 1), 0)
+    length = jnp.where(first, valid_len[0], valid_len[1])
+    live = ((core < seq_count[0]) & (places < length)).astype(F32)
+    d_res = live * ring.order(jnp.where(first, cotangent[:SEQ_LEN], cotangent[SEQ_LEN:]), width)
+    cut = hid // 256 * 128 + 128
+    w_gate, w_up, w_down, resid, ffn_in, d_ffn = call(
+        functools.partial(gather_ffn_kernel, hid, cut),
+        "gather_ffn",
+        1,
+        (part0, part3, part4, attn_terms, seqs, gain_ffn, d_res.astype(BF16)),
+        [ANY] * 5 + [VMEM, ANY],
+        [((8, width, hid), BF16)] * 3 + [((SEQ_LEN, dim), F32), (rows4, BF16), (rows4, BF16)],
+        [ANY] * 6,
+        quad_scratch(dim)
+        + [pltpu.VMEM((SEQ_LEN, dim), F32), pltpu.VMEM((SEQ_LEN, dim), BF16)]
+        + [pltpu.VMEM((SEQ_LEN, dim), BF16)] * 2
+        + [pltpu.VMEM((3, width, 3 * hid), BF16)],
+        160,
+    )
+    w_gate, w_up, w_down, ffn_in, d_ffn = map(flat, (w_gate, w_up, w_down, ffn_in, d_ffn))
+    gate, up_vals = mm(ffn_in, w_gate), mm(ffn_in, w_up)
+    sig = jax.nn.sigmoid(gate)
+    hidden = (gate * sig * up_vals).astype(BF16)
+    down_given = over_y(mm(d_ffn[:, half:], hidden, TN, BF16))
+    down_terms = mm(d_ffn[:, :half], hidden, TN, BF16)
+    d_hidden = mm(d_ffn, w_down)
+    d_gate = (d_hidden * up_vals * (sig * (1.0 + gate * (1.0 - sig)))).astype(BF16)
+    d_up = (d_hidden * (gate * sig)).astype(BF16)
+    up_given = over_y(mm(ffn_in[:, half:], d_up, TN, BF16))
+    up_terms = mm(ffn_in[:, :half], d_up, TN, BF16)
+    gate_terms = mm(ffn_in, d_gate, TN, BF16)
+    ffn_terms = mm(hidden, w_down, NT).reshape(rows4)
+    d_ffn_terms = (mm(d_gate, w_gate, NT) + mm(d_up, w_up, NT)).reshape(rows4)
+    gate_sum, down_sum, d_h, d_attn, ffn_gains, block_out = call(
+        functools.partial(sum_ffn_kernel, hid),
+        "sum_ffn",
+        2,
+        (
+            blocks(gate_terms),
+            blocks(down_terms),
+            blocks(down_given),
+            d_ffn_terms,
+            resid,
+            gain_ffn,
+            d_res,
+            ffn_terms,
+            jnp.broadcast_to(live, (SEQ_LEN, 128)),
+        ),
+        [ANY] * 5 + [VMEM, ANY, ANY, VMEM],
+        [
+            ((shard, 2 * hid), F32),
+            ((shard, 2 * hid), F32),
+            ((SEQ_LEN, dim), F32),
+            (rows4, BF16),
+            ((8, dim), F32),
+            ((2 * SEQ_LEN, dim), BF16),
+        ],
+        [ANY] * 4 + [VMEM, ANY],
+        sum_scratch(width, hid) * 2
+        + quad_scratch(dim) * 2
+        + [
+            pltpu.VMEM((SEQ_LEN, dim), F32),
+            pltpu.VMEM((SEQ_LEN, dim), F32),
+            pltpu.VMEM((SEQ_LEN, dim), BF16),
+            pltpu.VMEM((SEQ_LEN, dim), BF16),
+        ],
+        160,
+    )
+    d_attn = flat(d_attn)
+    d_proj = mixer_backward(proj, saved, mm(d_attn, w_out))
+    d_attn_terms = mm(d_proj, w_in, NT).reshape(rows4)
+    tail = width // 2
+    up_sum, out_sum, q_sum, k_sum, v_sum, f_sum, input_grad, gain_sums = call(
+        functools.partial(sum_last_kernel, hid),
+        "sum_last",
+        3,
+        (
+            blocks(up_terms),
+            blocks(up_given),
+            blocks(mm(d_attn, mixed, TN, BF16)),
+            blocks(mm(attn_in, d_proj, TN, BF16)),
+            d_attn_terms,
+            seqs,
+            gain_attn,
+            d_h,
+            ffn_gains,
+        ),
+        [ANY] * 6 + [VMEM, ANY, VMEM],
+        [((shard, 2 * hid), F32)]
+        + [((shard, 2 * KDIM), F32)] * 4
+        + [((shard, 256), F32), ((2 * SEQ_LEN, dim), F32), ((8, tail), F32)],
+        [ANY] * 7 + [VMEM],
+        sum_scratch(width, hid)
+        + sum_scratch(width, KDIM) * 4
+        + sum_scratch(width, 128)
+        + quad_scratch(dim)
+        + [
+            pltpu.VMEM((SEQ_LEN, dim), BF16),
+            pltpu.VMEM((SEQ_LEN, dim), F32),
+            pltpu.VMEM((8, dim), F32),
+            pltpu.VMEM((8, 8, width), F32),
+            pltpu.VMEM((8, 8, width), F32),
+            pltpu.VMEM((4, 8, width), F32),
+            pltpu.VMEM((3, 8, width), F32),
+            pltpu.VMEM((3, 8, width), F32),
+            pltpu.VMEM((2, 8, tail), F32),
+            pltpu.VMEM((8, tail), F32),
+        ],
+        240,
+    )
+    f_grad = jnp.concatenate([f_sum[:, :SLOTS], f_sum[:, 128 : 128 + SLOTS]], axis=1)
+    return (
+        block_out,
+        input_grad,
+        gain_sums[0],
+        gain_sums[1],
+        q_sum,
+        k_sum,
+        v_sum,
+        f_grad,
+        out_sum,
+        gate_sum,
+        up_sum,
+        down_sum,
+    )
+
+
 def solution(mesh):
     ring = Ring(mesh.shape["dp"])
+    body = body_by_kernels if ring.count == 16 else body_by_permutes
     split_one, split_two = P("dp"), P("dp", "head")
     row = P("dp", None)
     in_specs = (row, split_one, split_one, split_one, split_one) + (split_two,) * 8 + (row,)

time: 1340 us -> 810 us (0.60)
  waiting for transfers between devices: 792 us -> 29.4 us
  Pallas kernels: 31.1 us -> 571 us
  starting transfers between devices: 239 us -> 4.03 us
  matrix products: 186 us -> 149 us
  other arithmetic: 58.3 us -> 25.9 us
    ppermute x74 -> x4, waiting for transfers between devices: 686 us -> 29.4 us  [send(): return lax.ppermute(value, 'dp', self.perm(stride, size, shift % size))]
    pallas_call x0 -> x4, Pallas kernels: none -> 539 us  [call(): pl.pallas_call(kernel, in_specs=specs, out_specs=out_specs, out_shape=[ja...]
    ppermute x74 -> x4, starting transfers between devices: 218 us -> 4.03 us  [send(): return lax.ppermute(value, 'dp', self.perm(stride, size, shift % size))]
    ppermute x30 -> x0, waiting for transfers between devices: 106 us -> none  [the longest x19 105 us: swap(): return lax.ppermute(value, 'dp', self.perm(1, 2, 1))]
    dot_general x60 -> x17, matrix products: 186 us -> 149 us  [mm(): lax.dot_general(left, right, dims, preferred_element_type=F32).astype(kind)]
    ppermute x30 -> x0, starting transfers between devices: 20.5 us -> none  [the longest x19 18.9 us: swap(): return lax.ppermute(value, 'dp', self.perm(1, 2, 1))]
    select_n x19 -> x1, other arithmetic: 21.7 us -> 2.48 us  [body_by_kernels(): jnp.where(first, cotangent[:SEQ_LEN], cotangent[SEQ_LEN:])]
  transfers between devices with their start and end apart: 104 -> 4, of which waited for: 58 -> 1; matrix products, arithmetic and copies ran while one was open for 11% -> 14% of each run, Pallas kernels for 1% -> 25%
where the time goes in v3:
time: 810 us; the launch traced here: 805 us
  Pallas kernels  571 us (70%)
  matrix products  149 us (18%)
  waiting for transfers between devices  29.4 us (4%)
  other arithmetic  25.9 us (3%)
  local copies, waits for them, and re-layouts  22.6 us (3%)
    pallas_call x4, Pallas kernels, call(): pl.pallas_call(kernel, in_specs=specs, out_specs=out_specs, out_shape=[ja...  539 us
    dot_general x17, matrix products, mm(): lax.dot_general(left, right, dims, preferred_element_type=F32).astype(kind)  149 us
    ppermute x4, waiting for transfers between devices, send(): return lax.ppermute(value, 'dp', self.perm(stride, size, shift % size))  29.4 us
    pallas_call x1, Pallas kernels, mixer_backward(): pl.pallas_call(backward_kernel, grid=(rows // SEQ_LEN,), in_specs=IN_SPEC...  18.5 us
  transfers between devices with their start and end apart: 4, of which 1 were waited for; matrix products, arithmetic and copies ran while one was open for 14% of the time, Pallas kernels for 25%

profile of v3, /device:TPU:0, one launch (start us, length us, event | category | flops | bytes accessed | tf_op | source)
XLA Modules:
  0.0 805.0 jit_solution(4547013016995543591)
XLA Ops:
  3.9 102.2 %gather_first.1 = (bf16[8,256,1664]{2,1,0:T(8,128)(2,1)}, bf16[8,256,512]{2,1,0:T(8,128)(2,1)}, bf16[256,4224]{1,0:T(8,128)(2,1)}, bf16[4,256,2048]{2,1,0:T(8,128)(2,1)}) custom-call(bf16[512,2048]{1,0:T(8,128)(2,1)} %tokens.1, bf16[128,1024]{1,0:T(8,128)(2,1)} %q_w.1, bf16[128,1024]{1,0:T(8,128)(2,1)} %k_w.1, bf16[128,1024]{1,0:T(8,128)(2,1)} %v_w.1, ...), custom_call_target="tpu_custom_call" | custom-call | tf_op jit(solution)/shard_map/gather_first/pallas_call | solution.py:867
  108.1 2.5 slice_select_fusion
  116.8 2.4 fusion.9
  119.5 3.2 multiply_reduce_fusion
  124.1 13.1 %fusion.13.q_ref.k_ref.v_ref.f_ref = f32[1024,1664]{1,0:T(8,128)} fusion(bf16[1024,2048]{1,0:T(8,128)(2,1)S(1)} %bitcast.84, bf16[2048,1664]{1,0:T(8,128)(2,1)} %bitcast.90), kind=kOutput, calls=%fused_computation.53 | convolution fusion | flops 6979321856 | bytes 17825792 | tf_op jit(solution)/shard_map/dot_general | solution.py:985
  137.2 12.7 %mixer_forward.1 = (bf16[1024,512]{1,0:T(8,128)(2,1)S(1)}, f32[1024,128]{1,0:T(8,128)S(1)}, f32[1024,128]{1,0:T(8,128)S(1)}, f32[1024,256]{1,0:T(8,128)S(1)}, f32[1024,256]{1,0:T(8,128)S(1)}) custom-call(f32[1024,1664]{1,0:T(8,128)} %fusion.13.q_ref.k_ref.v_ref.f_ref, f32[1024,1664]{1,0:T(8,128)} %fusion.13.q_ref.k_ref.v_ref.f_ref, ...), custom_call_target="tpu_custom_call" | custom-call | flops 3072000000 | bytes 10240000 | tf_op jit(solution)/shard_map/mixer_forward/pallas_call | solution.py:251
  153.4 1.7 select_dynamic-update-slice_fusion.3
  160.8 7.8 fusion.14.terms
  168.6 1.9 fusion.8
  171.9 3.0 fusion.1
  174.9 122.0 %gather_ffn.1 = (bf16[8,256,1408]{2,1,0:T(8,128)(2,1)}, bf16[8,256,1408]{2,1,0:T(8,128)(2,1)}, bf16[8,256,1408]{2,1,0:T(8,128)(2,1)}, f32[256,2048]{1,0:T(8,128)...) custom-call(bf16[256,4224]{1,0:T(8,128)(2,1)} %get-tuple-element.41.b0, ...), custom_call_target="tpu_custom_call" | custom-call | tf_op jit(solution)/shard_map/gather_ffn/pallas_call | solution.py:867
  297.0 11.9 %fusion.15 = f32[1024,1408]{1,0:T(8,128)} fusion(bf16[1024,2048]{1,0:T(8,128)(2,1)} %bitcast.110, bf16[2048,1408]{1,0:T(8,128)(2,1)} %bitcast.106), kind=kOutput, calls=%fused_computation.55 | convolution fusion | flops 5905580032 | bytes 15728640 | tf_op jit(solution)/shard_map/dot_general | solution.py:985
  308.9 8.6 %fusion.16 = f32[1024,1408]{1,0:T(8,128)} fusion(bf16[1024,2048]{1,0:T(8,128)(2,1)S(1)} %bitcast.111, bf16[2048,1408]{1,0:T(8,128)(2,1)S(1)} %bitcast.100), kind=kOutput, calls=%fused_computation.56 | convolution fusion | flops 5905580032 | bytes 15728640 | tf_op jit(solution)/shard_map/dot_general | solution.py:985
  317.5 14.9 %multiply_convert_fusion.1 = (bf16[1024,1408]{1,0:T(8,128)(2,1)}, bf16[1024,1408]{1,0:T(8,128)(2,1)}, bf16[1024,1408]{1,0:T(8,128)(2,1)}) fusion(f32[1024,1408]{1,0:T(8,128)} %fusion.16, f32[1024,1408]{1,0:T(8,128)} %fusion.15, bf16[1024,2048]{1,0:T(8,128)(2,1)} %bitcast.117, bf16[2048,1408]{1,0:T(8,128)(2,1)S(1)} %bitcast.104), kind=kOutput, calls=%fused_computation.7 | convolution fusion | flops 5927206912 | bytes 30146560 | tf_op jit(solution)/shard_map/dot_general | solution.py:985
  332.4 6.1 convolution_convert_fusion.4
  338.5 4.9 convolution_convert_fusion.5
  343.4 10.5 %fusion.17 = f32[1024,2048]{1,0:T(8,128)} fusion(bf16[1024,1408]{1,0:T(8,128)(2,1)} %get-tuple-element.84, bf16[2048,1408]{1,0:T(8,128)(2,1)S(1)} %bitcast.109), kind=kOutput, calls=%fused_computation.57 | convolution fusion | flops 5905580032 | bytes 17039360 | tf_op jit(solution)/shard_map/dot_general | solution.py:985
  353.9 6.8 convolution_convert_fusion.2
  360.7 1.9 collective-permute-start.2
  362.6 8.7 %convolution_convert_fusion.1 = bf16[2048,1408]{1,0:T(8,128)(2,1)} fusion(bf16[1024,2048]{1,0:T(8,128)(2,1)S(1)} %bitcast.113, bf16[1024,1408]{1,0:T(8,128)(2,1)S(1)} %copy-done.25), kind=kOutput, calls=%fused_computation.6 | convolution fusion | flops 5908463616 | bytes 12845056 | tf_op jit(solution)/shard_map/dot_general | solution.py:985
  371.5 9.0 %fusion.18.out_terms = f32[4,256,2048]{2,1,0:T(8,128)} fusion(bf16[4,256,1408]{2,1,0:T(8,128)(2,1)S(1)} %bitcast.122, bf16[2048,1408,1]{1,0,2:T(8,128)(2,1)S(1)} %bitcast.105), kind=kOutput, calls=%fused_computation.58 | convolution fusion | flops 5905580032 | bytes 17039360 | tf_op jit(solution)/shard_map/dot_general | solution.py:985
  380.5 4.8 convolution_convert_fusion.3
  385.4 11.4 %convolution_add_fusion = f32[1024,2048]{1,0:T(8,128)} fusion(f32[1024,2048]{1,0:T(8,128)} %fusion.17, bf16[1024,1408]{1,0:T(8,128)(2,1)S(1)} %copy-done.26, bf16[2048,1408]{1,0:T(8,128)(2,1)S(1)} %bitcast.101), kind=kOutput, calls=%fused_computation.12 | convolution fusion | flops 5907677184 | bytes 25427968 | tf_op jit(solution)/shard_map/dot_general | solution.py:985
  396.8 29.4 %collective-permute-done.2 = bf16[1024,1408]{1,0:T(8,128)(2,1)} collective-permute-done((bf16[1024,1408]{1,0:T(8,128)(2,1)S(1)}, bf16[1024,1408]{1,0:T(8,128)(2,1)}, u32[]{:S(2)}, u32[]{:S(2)}) %collective-permute-start.2) | collective-permute-done | bytes 2883616 | tf_op jit(solution)/shard_map/ppermute | solution.py:901
  427.0 171.0 %sum_ffn.1 = (f32[128,2816]{1,0:T(8,128)}, f32[128,2816]{1,0:T(8,128)}, f32[256,2048]{1,0:T(8,128)}, bf16[4,256,2048]{2,1,0:T(8,128)(2,1)}, f32[8,2048]{1,0:T(8,128)}, /*index=5*/bf16[512,2048]{1,0:T(8,128)(2,1)}) custom-call(bf16[8,256,1408]{2,1,0:T(8,128)(2,1)} %bitcast.83, bf16[4,256,1408]{2,1,0:T(8,128)(2,1)} %bitcast.87, ...), custom_call_target="tpu_custom_call" | custom-call | tf_op jit(solution)/shard_map/sum_ffn/pallas_call | solution.py:867
  597.9 5.3 fusion.19.d_ref
  603.3 18.5 %mixer_backward.1 = bf16[1024,1664]{1,0:T(8,128)(2,1)} custom-call(f32[1024,1664]{1,0:T(8,128)} %fusion.13.q_ref.k_ref.v_ref.f_ref, f32[1024,1664]{1,0:T(8,128)} %fusion.13.q_ref.k_ref.v_ref.f_ref, f32[1024,1664]{1,0:T(8,128)} %fusion.13.q_ref.k_ref.v_ref.f_ref, f32[1024,1664]{1,0:T(8,128)} %fusion.13.q_ref.k_ref.v_ref.f_ref, ...), custom_call_target="tpu_custom_call" | custom-call | flops 9216000000 | bytes 16384000 | tf_op jit(solution)/shard_map/mixer_backward/pallas_call | solution.py:266
  621.8 11.6 %fusion.20.terms = f32[4,256,2048]{2,1,0:T(8,128)} fusion(bf16[4,256,1664]{2,1,0:T(8,128)(2,1)} %bitcast.85, bf16[2048,1664,1]{1,0,2:T(8,128)(2,1)S(1)} %bitcast.93), kind=kOutput, calls=%fused_computation.60 | convolution fusion | flops 6979321856 | bytes 18612224 | tf_op jit(solution)/shard_map/dot_general | solution.py:985
  633.4 3.8 convolution_convert_fusion.6
  637.2 10.1 %convolution_convert_fusion = bf16[2048,1664]{1,0:T(8,128)(2,1)} fusion(bf16[1024,2048]{1,0:T(8,128)(2,1)S(1)} %copy-done.4, bf16[1024,1664]{1,0:T(8,128)(2,1)S(1)} %copy-done.6), kind=kOutput, calls=%fused_computation.5 | convolution fusion | flops 6982729728 | bytes 14417920 | tf_op jit(solution)/shard_map/dot_general | solution.py:985
  647.3 144.2 %sum_last.1 = (f32[128,2816]{1,0:T(8,128)}, f32[128,1024]{1,0:T(8,128)}, f32[128,1024]{1,0:T(8,128)}, f32[128,1024]{1,0:T(8,128)}, f32[128,1024]{1,0:T(8,128)}, ...) custom-call(bf16[4,256,1408]{2,1,0:T(8,128)(2,1)} %bitcast.86, bf16[4,256,1408]{2,1,0:T(8,128)(2,1)} %bitcast.24.given, ...), custom_call_target="tpu_custom_call" | custom-call | tf_op jit(solution)/shard_map/sum_last/pallas_call | solution.py:867
  796.1 2.1 copy.58
  (107 shorter events, 33.7 us)
Async XLA Ops:
  106.1 68.8 %collective-permute-start = (bf16[256,4224]{1,0:T(8,128)(2,1)}, bf16[256,4224]{1,0:T(8,128)(2,1)}, u32[]{:S(2)}, u32[]{:S(2)}) collective-permute-start(bf16[256,4224]{1,0:T(8,128)(2,1)} %get-tuple-element.41.b0), channel_id=1, source_target_pairs={{0,8},{2,10},{4,12},{6,14},{8,16},{10,18},{12,20},{14,22},{16,24},... | collective-permute-start | bytes 6488072 | tf_op jit(solution)/shard_map/ppermute | solution.py:901
  107.2 67.7 %collective-permute-start.1 = (bf16[256,4224]{1,0:T(8,128)(2,1)}, bf16[256,4224]{1,0:T(8,128)(2,1)}, u32[]{:S(2)}, u32[]{:S(2)}) collective-permute-start(bf16[256,4224]{1,0:T(8,128)(2,1)} %get-tuple-element.41.b0), channel_id=1, source_target_pairs={{0,4},{2,6},{4,0},{6,2},{8,12},{10,14},{12,8},{14,10},{16,20},{18,... | collective-permute-start | bytes 6488072 | tf_op jit(solution)/shard_map/ppermute | solution.py:901
  111.5 4.0 copy-start.18
  119.5 50.9 %copy-start.17 = (f32[2048,1]{0,1:T(1,128)}, f32[2048,1]{0,1:T(1,128)S(1)}, u32[]{:S(2)}) copy-start(f32[2048,1]{0,1:T(1,128)S(1)} %copy.39) | copy-start | bytes 24580
  119.5 3.5 copy-start.2
  160.8 7.8 copy-start.8
  168.6 3.3 copy-start.3
  297.0 12.0 %copy-start.19 = (bf16[8,256,1408]{2,1,0:T(8,128)(2,1)S(1)}, bf16[8,256,1408]{2,1,0:T(8,128)(2,1)}, u32[]{:S(2)}) copy-start(bf16[8,256,1408]{2,1,0:T(8,128)(2,1)} %get-tuple-element.50) | copy-start | bytes 17301508
  297.0 12.0 %copy-start.20 = (bf16[4,256,2048]{2,1,0:T(8,128)(2,1)S(1)}, bf16[4,256,2048]{2,1,0:T(8,128)(2,1)}, u32[]{:S(2)}) copy-start(bf16[4,256,2048]{2,1,0:T(8,128)(2,1)} %get-tuple-element.46) | copy-start | bytes 12582916
  297.0 20.5 %slice-start.2 = ((s8[5767168]{0:T(1024)(128)(4,1)}), s8[4194304]{0:T(1024)(128)(4,1)S(1)}, s32[]{:S(2)}) async-start(s8[5767168]{0:T(1024)(128)(4,1)} %bitcast.102), calls=%async_computation.2 | async-start | bytes 8388608
  308.9 8.6 %slice-start.3 = ((s8[5767168]{0:T(1024)(128)(4,1)}), s8[1572864]{0:T(1024)(128)(4,1)S(1)}, s32[]{:S(2)}) async-start(s8[5767168]{0:T(1024)(128)(4,1)} %bitcast.102), calls=%async_computation.3 | async-start | bytes 3145728
  332.4 6.1 copy-start.22
  332.4 6.1 copy-start.23
  332.4 11.0 %slice-start.4 = ((s8[5767168]{0:T(1024)(128)(4,1)}), s8[4194304]{0:T(1024)(128)(4,1)S(1)}, s32[]{:S(2)}) async-start(s8[5767168]{0:T(1024)(128)(4,1)} %bitcast.107), calls=%async_computation.4 | async-start | bytes 8388608
  338.5 4.9 slice-start.5
  353.9 8.6 %copy-start.25 = (bf16[1024,1408]{1,0:T(8,128)(2,1)S(1)}, bf16[1024,1408]{1,0:T(8,128)(2,1)}, u32[]{:S(2)}) copy-start(bf16[1024,1408]{1,0:T(8,128)(2,1)} %get-tuple-element.85) | copy-start | bytes 8650756
  360.7 65.5 %collective-permute-start.2 = (bf16[1024,1408]{1,0:T(8,128)(2,1)S(1)}, bf16[1024,1408]{1,0:T(8,128)(2,1)}, u32[]{:S(2)}, u32[]{:S(2)}) collective-permute-start(bf16[1024,1408]{1,0:T(8,128)(2,1)S(1)} %convolution_convert_fusion.4), channel_id=1, source_target_pairs={{0,4},{2,6},{4,0},{6,2},{8,12},{10,14},{12,8},{14,10},{16,20},{18,... | collective-permute-start | bytes 8650760 | tf_op jit(solution)/shard_map/ppermute | solution.py:901
  371.3 276.0 %collective-permute-start.3 = (bf16[1024,1408]{1,0:T(8,128)(2,1)}, bf16[1024,1408]{1,0:T(8,128)(2,1)}, u32[]{:S(2)}, u32[]{:S(2)}) collective-permute-start(bf16[1024,1408]{1,0:T(8,128)(2,1)} %convolution_convert_fusion.2), channel_id=1, source_target_pairs={{0,4},{2,6},{4,0},{6,2},{8,12},{10,14},{12,8},{14,10},{16,20},{18,... | collective-permute-start | bytes 8650760 | tf_op jit(solution)/shard_map/ppermute | solution.py:901
  371.5 9.1 %copy-start.24 = (bf16[1024,1408]{1,0:T(8,128)(2,1)S(1)}, bf16[1024,1408]{1,0:T(8,128)(2,1)}, u32[]{:S(2)}) copy-start(bf16[1024,1408]{1,0:T(8,128)(2,1)} %get-tuple-element.84) | copy-start | bytes 8650756
  380.5 4.9 copy-start.26
  597.9 23.8 %slice-start = ((s8[6815744]{0:T(1024)(128)(4,1)}), s8[4194304]{0:T(1024)(128)(4,1)S(1)}, s32[]{:S(2)}) async-start(s8[6815744]{0:T(1024)(128)(4,1)} %bitcast.91), calls=%async_computation | async-start | bytes 8388608
  603.3 18.5 %slice-start.1 = ((s8[6815744]{0:T(1024)(128)(4,1)}), s8[2621440]{0:T(1024)(128)(4,1)S(1)}, s32[]{:S(2)}) async-start(s8[6815744]{0:T(1024)(128)(4,1)} %bitcast.91), calls=%async_computation.1 | async-start | bytes 5242880
  621.8 11.6 %copy-start.1 = (bf16[1024,512]{1,0:T(8,128)(2,1)S(1)}, bf16[1024,512]{1,0:T(8,128)(2,1)}, u32[]{:S(2)}) copy-start(bf16[1024,512]{1,0:T(8,128)(2,1)} %copy-done) | copy-start | bytes 3145732
  621.8 11.6 %copy-start.21 = (bf16[4,256,2048]{2,1,0:T(8,128)(2,1)S(1)}, bf16[4,256,2048]{2,1,0:T(8,128)(2,1)}, u32[]{:S(2)}) copy-start(bf16[4,256,2048]{2,1,0:T(8,128)(2,1)} %get-tuple-element.53) | copy-start | bytes 12582916
  633.4 3.8 copy-start.4
  633.4 3.8 copy-start.6
  647.3 147.5 %copy-start.9 = (bf16[512,2048]{1,0:T(8,128)(2,1)S(1)}, bf16[512,2048]{1,0:T(8,128)(2,1)}, u32[]{:S(2)}) copy-start(bf16[512,2048]{1,0:T(8,128)(2,1)} %get-tuple-element.111) | copy-start | bytes 6291460
  791.6 4.5 copy-start.5
  796.1 3.7 copy-start.14
  796.1 4.5 copy-start.13
  798.3 4.3 copy-start.12
  799.9 3.8 copy-start.10
  (5 other events, 10.6 us)

commit v4 on v3

--- a/solution.py
+++ b/solution.py
@@ -441,32 +441,36 @@
 
 
 def gather_first_kernel(
-    tokens, q_w, k_w, v_w, small, out_w, gate_w, up_w, down_w, w_in, w_out, ffn, seqs, stage, held, sem
+    tokens, cot, live, q_w, k_w, v_w, small, out_w, gate_w, up_w, down_w, w_in, w_out, ffn, own, attn_in, d_res, d_ffn, gains,
+    stage, seqs, normed, scales, turned, grads, low, sem
 ):
     place, sems = Place(), Sems(sem)
     shard = q_w.shape[0]
     rows = place.half(shard)
     hid = gate_w.shape[1] // 2
     chunks = [
-        (small, 128, w_in, 3 * KDIM, False, True),
-        (q_w, KDIM, w_in, 0, False, True),
-        (k_w, KDIM, w_in, KDIM, False, True),
-        (v_w, KDIM, w_in, 2 * KDIM, False, True),
-        (out_w, KDIM, w_out, 0, True, True),
-        (gate_w, hid, ffn, 0, False, False),
-        (up_w, hid, ffn, hid, False, False),
-        (down_w, hid, ffn, 2 * hid, False, False),
+        (small, 0, 128, w_in, 3 * KDIM, True),
+        (q_w, 0, KDIM, w_in, 0, False),
+        (k_w, 0, KDIM, w_in, KDIM, False),
+        (v_w, 0, KDIM, w_in, 2 * KDIM, False),
+        (out_w, 0, KDIM // 2, w_out, 0, True),
+        (out_w, KDIM // 2, KDIM // 2, w_out, KDIM // 2, False),
+        (gate_w, 0, hid, ffn, 0, False),
+        (up_w, 0, hid, ffn, hid, False),
+        (down_w, 0, hid, ffn, 2 * hid, False),
     ]
-    place.greet()
+    full = len(chunks) - 3
     swaps, keeps, rises, crosses = [], [], [], []
     used = 0
-    for source, width, target, first, y_first, beyond in chunks:
+    for c, (source, offset, width, target, first, y_first) in enumerate(chunks):
         cols = pl.ds(first, width)
-        where = target.at[0, rows, cols] if beyond else target.at[rows, cols]
-        swaps.append(place.copy("x", source.at[:, place.half(width, True)], where, sems.two()))
-        keeps.append(Keep(sems, source.at[:, place.half(width)], where, stage.at[:, pl.ds(used, width)]))
+        where = target.at[0, rows, cols] if c < full else target.at[rows, cols]
+        span = source.shape[1] // 2
+        here, there = (pl.ds(pl.multiple_of(at * span + offset, 128), width) for at in (place.x, 1 - place.x))
+        swaps.append(place.copy("x", source.at[:, there], where, sems.two()))
+        keeps.append(Keep(sems, source.at[:, here], where, stage.at[:, pl.ds(used, width)]))
         used += width
-        if not beyond:
+        if c >= full:
             continue
 
         def block(index, target=target, cols=cols):
@@ -481,70 +485,125 @@
         crosses.append(
             [place.copy("y", block(i), block(4 + i), sems.two()) for i in range(1 if y_first else 4)]
         )
-    for swap, keep in zip(swaps[:5], keeps[:5]):
-        swap.start()
-        keep.start()
     width = tokens.shape[1] // 8
     mine = pl.ds(pl.multiple_of(place.core * SEQ_LEN, SEQ_LEN), SEQ_LEN)
-    near, far, side, last = [], [], [], []
+    far, side, fetch, fetch_cot = [], [], [], []
     for index in range(8):
         part = tokens.at[mine, place.columns(index, width)]
         cols = pl.ds(index * width, width)
         far.append(place.copy("x", part, seqs.at[1, :, cols], sems.two()))
         side.append(place.copy("core", part, seqs.at[2, :, cols], sems.two()))
-        near.append(Keep(sems, part, seqs.at[0, :, cols], held.at[:, cols]))
-    last.append(place.copy("core", seqs.at[1], seqs.at[3], sems.two()))
-    for copy in far + side + near:
-        copy.start()
-    for swap, keep in zip(swaps[5:], keeps[5:]):
+        fetch.append(pltpu.make_async_copy(part, seqs.at[0, :, cols], sems.one()))
+        fetch_cot.append(
+            pltpu.make_async_copy(cot.at[mine, place.columns(index, width)], grads.at[:, cols], sems.one())
+        )
+    last = place.copy("core", seqs.at[1], seqs.at[3], sems.two())
+    quad = Quad(place, sems, low, d_ffn)
+    save_own = pltpu.make_async_copy(seqs.at[0], own, sems.one())
+    save_res = pltpu.make_async_copy(grads, d_res, sems.one())
+    save_in = [pltpu.make_async_copy(normed.at[i], attn_in.at[i], sems.one()) for i in range(4)]
+    load_gains = [pltpu.make_async_copy(w_in.at[i, :, pl.ds(3 * KDIM, 128)], turned.at[i], sems.one()) for i in range(8)]
+    place.greet()
+    for swap, keep in zip(swaps[:full], keeps[:full]):
         swap.start()
         keep.start()
-    for keep in keeps + near:
+    for copy in far + side + fetch + fetch_cot:
+        copy.start()
+    for swap, keep in zip(swaps[full:], keeps[full:]):
+        swap.start()
+        keep.start()
+    for keep in keeps:
         keep.turn()
-    for c in range(5):
+    for c in range(full):
         keeps[c].wait()
         swaps[c].wait_recv()
         rises[c][0][0].start()
         crosses[c][0].start()
+    for copy in fetch + fetch_cot:
+        copy.wait()
+    save_own.start()
+
+    def mask(part):
+        value = grads[part] * live[part, :1]
+        grads[part] = value
+        low[part] = value.astype(BF16)
+
+    pieces(SEQ_LEN, mask)
+    save_res.start()
+    quad.start()
+    for c in range(full):
+        if chunks[c][5]:
+            crosses[c][0].wait_recv()
+            rises[c][1][0].start()
+
+    def measure(slot):
+        def one(part):
+            scales[slot, part] = jnp.broadcast_to(rms(seqs[slot, part].astype(F32)), (PIECE, 128))
+
+        pieces(SEQ_LEN, one)
+
+    def norm(slot):
+        def one(part):
+            value = seqs[slot, part].astype(F32) * scales[slot, part, :1] * gains[0:1, :]
+            normed[slot, part] = value.astype(BF16)
+
+        pieces(SEQ_LEN, one)
+        save_in[slot].start()
+
     for step in range(3):
-        if step == 0:
-            for c in range(5):
-                if chunks[c][4]:
-                    crosses[c][0].wait_recv()
-                    rises[c][1][0].start()
-        if step == 1:
-            for copy in far:
-                copy.wait_recv()
-            last[0].start()
-        for c in range(5):
+        for c in range(full):
             for rise in rises[c]:
                 rise[step].wait_recv()
                 if step < 2:
                     rise[step + 1].start()
-            if not chunks[c][4]:
+            if not chunks[c][5]:
                 crosses[c][3 - step].start()
-    for c in range(5):
+            if step == 0 and c == 1:
+                measure(0)
+            if step == 0 and c == full - 1:
+                for copy in far:
+                    copy.wait_recv()
+                last.start()
+            if step == 1:
+                if c == 0:
+                    for copy in side:
+                        copy.wait_recv()
+                    last.wait_recv()
+                if 1 <= c <= 3:
+                    measure(c)
+            if step == 2:
+                if c == 0:
+                    for copy in load_gains:
+                        copy.start()
+                    for index, copy in enumerate(load_gains):
+                        copy.wait()
+                        flipped = turned[index].astype(F32).T
+                        gains[0:8, index * width : (index + 1) * width] = flipped[SLOTS : SLOTS + 8]
+                if 1 <= c <= 4:
+                    norm(c - 1)
+    quad.forward()
+    for c in range(full):
         for cross in crosses[c]:
             cross.wait_send()
-        if not chunks[c][4]:
-            for cross in crosses[c]:
+            if not chunks[c][5]:
                 cross.wait_recv()
         for rise in rises[c]:
             for copy in rise:
                 copy.wait_send()
-    for swap in swaps[:5]:
+    for swap in swaps[:full]:
         swap.wait_send()
-    for swap, keep in zip(swaps[5:], keeps[5:]):
+    for swap, keep in zip(swaps[full:], keeps[full:]):
         swap.wait()
         keep.wait()
-    for copy in far:
+    for copy in far + side + [last]:
         copy.wait_send()
-    for copy in side + near + last:
+    for copy in save_in + [save_own, save_res]:
         copy.wait()
+    quad.finish()
 
 
 def gather_ffn_kernel(
-    hid, cut, b0, b3, b4, terms, tokens, gain, d_ffn, w_gate, w_up, w_down, resid, ffn_in, d_all, s0, s1, s2, s3, kept, normed, inputs, low, stage, sem
+    hid, cut, b0, b3, b4, terms, tokens, gains, w_gate, w_up, w_down, resid, ffn_in, s0, s1, s2, s3, kept, normed, inputs, stage, sem
 ):
     place, sems = Place(), Sems(sem)
     chunks = [
@@ -586,15 +645,12 @@
             )
         rises.append((lower, high))
     total = QuadSum(place, sems, terms, (s0, s1, s2, s3))
-    cot = Quad(place, sems, low, d_all)
-    fetch_low = pltpu.make_async_copy(d_ffn, low, sems.one())
     out = Quad(place, sems, normed, ffn_in)
-    fetch = pltpu.make_async_copy(tokens.at[0], inputs, sems.one())
+    fetch = pltpu.make_async_copy(tokens, inputs, sems.one())
     save = pltpu.make_async_copy(kept, resid, sems.one())
     place.greet()
     total.start()
     fetch.start()
-    fetch_low.start()
     for (lower, high), cross in zip(rises, crosses):
         lower[0].start()
         for copy in high[:1] + cross[:1]:
@@ -612,13 +668,11 @@
             def norm(part):
                 value = total.read(part) + inputs[part].astype(F32)
                 kept[part] = value
-                normed[part] = (value * rms(value) * gain[...]).astype(BF16)
+                normed[part] = (value * rms(value) * gains[1:2, :]).astype(BF16)
 
             pieces(SEQ_LEN, norm)
             out.start()
             save.start()
-            fetch_low.wait()
-            cot.start()
         lower[0].wait_recv()
         lower[1].start()
         for copy in cross[1:2]:
@@ -635,7 +689,6 @@
             high[2].start()
         if c == 1:
             out.forward()
-    cot.forward()
     for (lower, high), cross in zip(rises, crosses):
         for copy in cross:
             copy.wait()
@@ -646,12 +699,11 @@
     for copy in keeps:
         copy.wait()
     out.finish()
-    cot.finish()
     save.wait()
 
 
 class Sum:
-    def __init__(self, place, sems, terms, given, result, first, width, scratch):
+    def __init__(self, place, sems, terms, given, result, first, width, scratch, span=None, start=0):
         self.own, self.other, self.from_z, self.to_z, self.final = scratch
         cols = pl.ds(first, width)
         self.loads, self.crosses = [], []
@@ -664,7 +716,7 @@
         self.per = len(self.loads) // 4
         self.rises = [place.copy("up", self.to_z.at[i], self.from_z.at[i], sems.two()) for i in range(3)]
         half = self.final.shape[0] // 2
-        there = result.at[:, place.half(width)]
+        there = result.at[:, pl.ds(pl.multiple_of(place.x * (span or width) + start, 128), width)]
         self.leave = pltpu.make_async_copy(self.final.at[place.half(half)], there, sems.one())
         self.swap = place.copy("x", self.final.at[place.half(half, True)], there, sems.two())
 
@@ -717,92 +769,20 @@
     return scale * scaled - value * (scale * scale * scale * inner), jnp.sum(gains, axis=0)
 
 
-def sum_ffn_kernel(
-    hid, gate, down, given, terms, resid, gain, d_res, out_terms, live, gate_sum, down_sum, d_h, d_attn, gain_sum, block_out, *scratch
-):
+def sum_ffn_kernel(hid, part_hid, gate, down, given, down_rest, terms, resid, gains, d_res, gate_sum, down_sum, d_h, d_attn, gain_sum, *scratch):
     *scratch, sem = scratch
     place, sems = Place(), Sems(sem)
-    first = Sum(place, sems, down, given, down_sum, 0, hid, scratch[0:5])
-    second = Sum(place, sems, gate, None, gate_sum, 0, hid, scratch[5:10])
-    back = QuadSum(place, sems, terms, scratch[10:14])
-    ahead = QuadSum(place, sems, out_terms, scratch[14:18])
-    value, res, low, shown = scratch[18:22]
+    sums = [
+        Sum(place, sems, down, given, down_sum, 0, part_hid, scratch[0:5], hid),
+        Sum(place, sems, down_rest, None, down_sum, 0, hid - part_hid, scratch[5:10], hid, part_hid),
+        Sum(place, sems, gate, None, gate_sum, 0, part_hid, scratch[10:15], hid),
+        Sum(place, sems, gate, None, gate_sum, part_hid, hid - part_hid, scratch[15:20], hid, part_hid),
+    ]
+    back = QuadSum(place, sems, terms, scratch[20:24])
+    value, res, low = scratch[24:27]
     quad = Quad(place, sems, low, d_attn)
-    leave = Leave(place, sems, shown, block_out)
     fetch = [pltpu.make_async_copy(resid, value, sems.one()), pltpu.make_async_copy(d_res, res, sems.one())]
     save = pltpu.make_async_copy(res, d_h, sems.one())
-    place.greet()
-    back.start()
-    for step in range(4):
-        second.start(step)
-        first.start(step)
-    for copy in fetch:
-        copy.start()
-    ahead.start()
-    first.step(0)
-    back.middle()
-    ahead.middle()
-    second.step(0)
-    for copy in fetch:
-        copy.wait()
-    first.step(1)
-    back.ready()
-    gain_sum[...] = jnp.zeros_like(gain_sum)
-
-    def norm(part):
-        d_norm, gains = norm_back_piece(value[part], gain[...], back.read(part))
-        grad = res[part] + d_norm
-        res[part] = grad
-        low[part] = grad.astype(BF16)
-        gain_sum[...] += gains
-
-    pieces(SEQ_LEN, norm)
-    quad.start()
-    save.start()
-    second.step(1)
-    first.step(2)
-    ahead.ready()
-
-    def show(part):
-        shown[part] = (live[part, :1] * (value[part] + ahead.read(part))).astype(BF16)
-
-    pieces(SEQ_LEN, show)
-    leave.start()
-    second.step(2)
-    quad.forward()
-    first.step(3)
-    second.step(3)
-    quad.finish()
-    save.wait()
-    leave.finish()
-    first.finish()
-    second.finish()
-
-
-def sum_last_kernel(
-    hid, up, given, out_t, in_t, terms, tokens, gain, d_h, ffn_gains, up_sum, out_sum, q_sum, k_sum, v_sum, f_sum, grad, gain_sum, *scratch
-):
-    *scratch, sem = scratch
-    place, sems = Place(), Sems(sem)
-    sums = []
-    for terms_in, given_in, result, start, width in (
-        (up, given, up_sum, 0, hid),
-        (out_t, None, out_sum, 0, KDIM),
-        (in_t, None, q_sum, 0, KDIM),
-        (in_t, None, k_sum, KDIM, KDIM),
-        (in_t, None, v_sum, 2 * KDIM, KDIM),
-        (in_t, None, f_sum, 3 * KDIM, 128),
-    ):
-        sums.append(Sum(place, sems, terms_in, given_in, result, start, width, scratch[: 5]))
-        scratch = scratch[5:]
-    back = QuadSum(place, sems, terms, scratch[0:4])
-    value, res, gains, parts, met, crossed, risen, rising, last, swapped = scratch[4:]
-    leave = Leave(place, sems, res, grad)
-    fetch = [pltpu.make_async_copy(tokens.at[0], value, sems.one()), pltpu.make_async_copy(d_h, res, sems.one())]
-    meet = place.copy("core", parts, met, sems.two())
-    cross = place.copy("y", parts.at[pl.ds(4, 4)], crossed, sems.two())
-    rise = [place.copy("up", rising.at[i], risen.at[i], sems.two()) for i in range(3)]
-    swap = place.copy("x", last.at[1 - place.x], swapped, sems.two())
     place.greet()
     back.start()
     for step in range(4):
@@ -816,11 +796,81 @@
         one.step(0)
     for copy in fetch:
         copy.wait()
+    sums[0].step(1)
+    back.ready()
+    gain_sum[...] = jnp.zeros_like(gain_sum)
+
+    def norm(part):
+        d_norm, added = norm_back_piece(value[part], gains[1:2, :], back.read(part))
+        grad = res[part] + d_norm
+        res[part] = grad
+        low[part] = grad.astype(BF16)
+        gain_sum[...] += added
+
+    pieces(SEQ_LEN, norm)
+    quad.start()
+    save.start()
+    for one in sums[1:]:
+        one.step(1)
+    for one in sums:
+        one.step(2)
+    quad.forward()
+    for one in sums:
+        one.step(3)
+    quad.finish()
+    save.wait()
+    for one in sums:
+        one.finish()
+
+
+def sum_last_kernel(
+    hid, part_hid, up, given, up_rest, out_t, in_t, terms, tokens, gain_rows, d_h, ffn_gains, out_terms, resid, live,
+    up_sum, out_sum, q_sum, k_sum, v_sum, f_sum, grad, block_out, gain_sum, *scratch
+):
+    *scratch, sem = scratch
+    place, sems = Place(), Sems(sem)
+    sums = []
+    for terms_in, given_in, result, first, width, span, start in (
+        (up, given, up_sum, 0, part_hid, hid, 0),
+        (up_rest, None, up_sum, 0, hid - part_hid, hid, part_hid),
+        (out_t, None, out_sum, 0, KDIM, None, 0),
+        (in_t, None, q_sum, 0, KDIM, None, 0),
+        (in_t, None, k_sum, KDIM, KDIM, None, 0),
+        (in_t, None, v_sum, 2 * KDIM, KDIM, None, 0),
+        (in_t, None, f_sum, 3 * KDIM, 128, None, 0),
+    ):
+        sums.append(Sum(place, sems, terms_in, given_in, result, first, width, scratch[:5], span, start))
+        scratch = scratch[5:]
+    back = QuadSum(place, sems, terms, scratch[0:4])
+    ahead = QuadSum(place, sems, out_terms, scratch[4:8])
+    value, res, kept, shown, gains, parts, met, crossed, risen, rising, last, swapped = scratch[8:]
+    leave = Leave(place, sems, res, grad)
+    leave_out = Leave(place, sems, shown, block_out)
+    fetch = [pltpu.make_async_copy(tokens, value, sems.one()), pltpu.make_async_copy(d_h, res, sems.one())]
+    fetch.append(pltpu.make_async_copy(resid, kept, sems.one()))
+    meet = place.copy("core", parts, met, sems.two())
+    cross = place.copy("y", parts.at[pl.ds(4, 4)], crossed, sems.two())
+    rise = [place.copy("up", rising.at[i], risen.at[i], sems.two()) for i in range(3)]
+    swap = place.copy("x", last.at[1 - place.x], swapped, sems.two())
+    place.greet()
+    back.start()
+    for step in range(3):
+        for one in sums:
+            one.start(step)
+    for copy in fetch:
+        copy.start()
+    ahead.start()
+    sums[0].step(0)
+    back.middle()
+    for one in sums[1:]:
+        one.step(0)
+    for copy in fetch:
+        copy.wait()
     gains[...] = jnp.zeros_like(gains)
     back.ready()
 
     def norm(part):
-        d_norm, added = norm_back_piece(value[part].astype(F32), gain[...], back.read(part))
+        d_norm, added = norm_back_piece(value[part].astype(F32), gain_rows[0:1, :], back.read(part))
         res[part] = res[part] + d_norm
         gains[...] += added
 
@@ -833,16 +883,27 @@
         for index in range(8):
             parts[index, row : row + 1, :] = summed[:, index * width : (index + 1) * width]
     meet.start()
-    for one in sums:
-        one.step(1)
+    sums[0].step(1)
     meet.wait()
     parts[...] = parts[...] + met[...]
     cross.start()
+    for one in sums:
+        one.start(3)
+    for one in sums[1:]:
+        one.step(1)
+    ahead.middle()
     for one in sums:
         one.step(2)
     cross.wait()
     rising[0] = parts[3] + crossed[3]
     rise[0].start()
+    ahead.ready()
+
+    def show(part):
+        shown[part] = (live[part, :1] * (kept[part] + ahead.read(part))).astype(BF16)
+
+    pieces(SEQ_LEN, show)
+    leave_out.start()
     for one in sums:
         one.step(3)
     for step in (1, 2):
@@ -859,6 +920,7 @@
     for copy in rise:
         copy.wait_send()
     leave.finish()
+    leave_out.finish()
     for one in sums:
         one.finish()
 
@@ -876,6 +938,8 @@
 
 
 PAD = 128 - SLOTS
+DOWN_EARLY = 768
+UP_EARLY = 896
 
 
 class Ring:
@@ -1176,135 +1240,134 @@
 
     gains = jnp.concatenate([attn_gain[:, None], ffn_gain[:, None], jnp.zeros((shard, PAD - 2), BF16)], axis=1)
     small = jnp.concatenate([forget_weight[:, :SLOTS], gains, forget_weight[:, SLOTS:], gains], axis=1)
-    w_in, w_out, part0, seqs = call(
+    places = lax.broadcasted_iota(jnp.int32, (SEQ_LEN, 128), 0)
+    length = jnp.where(first, valid_len[0], valid_len[1])
+    live = ((core < seq_count[0]) & (places < length)).astype(F32)
+    row = (SEQ_LEN, dim)
+    vmem = lambda shape, kind=F32: pltpu.VMEM(shape, kind)
+    w_in, w_out, part0, own, attn_in, d_res, d_ffn, gain_rows = call(
         gather_first_kernel,
         "gather_first",
         0,
-        (tokens, q_weight, k_weight, v_weight, small, out_weight, gate_weight, up_weight, down_weight),
-        [ANY] * 9,
-        [((8, width, WIDE), BF16), ((8, width, KDIM), BF16), ((width, 3 * hid), BF16), (rows4, BF16)],
-        [ANY] * 4,
-        [pltpu.VMEM((shard, 4 * KDIM + 128 + 3 * hid), BF16), pltpu.VMEM((SEQ_LEN, dim), BF16)],
-        200,
+        (tokens, cotangent, live, q_weight, k_weight, v_weight, small, out_weight, gate_weight, up_weight, down_weight),
+        [ANY, ANY, VMEM] + [ANY] * 8,
+        [
+            ((8, width, WIDE), BF16),
+            ((8, width, KDIM), BF16),
+            ((width, 3 * hid), BF16),
+            (row, BF16),
+            (rows4, BF16),
+            (row, F32),
+            (rows4, BF16),
+            ((8, dim), F32),
+        ],
+        [ANY] * 7 + [VMEM],
+        [
+            vmem((shard, 4 * KDIM + 128 + 3 * hid), BF16),
+            vmem(rows4, BF16),
+            vmem(rows4, BF16),
+            vmem((4, SEQ_LEN, 128)),
+            vmem((8, width, 128), BF16),
+            vmem(row),
+            vmem(row, BF16),
+        ],
+        240,
     )
     part3, part4 = up_z(part0), over_y(part0)
-    w_in, w_out = flat(w_in), flat(w_out)
-    gain_attn = w_in[:, WIDE - PAD].astype(F32)[None, :]
-    gain_ffn = w_in[:, WIDE - PAD + 1].astype(F32)[None, :]
-    inputs = flat(seqs).astype(F32)
-    attn_in = (inputs * rms(inputs) * gain_attn).astype(BF16)
+    w_in, w_out, attn_in, d_ffn = map(flat, (w_in, w_out, attn_in, d_ffn))
     proj = mm(attn_in, w_in)
     mixed, *saved = mixer_forward(proj)
     attn_terms = mm(mixed, w_out, NT).reshape(rows4)
-    places = lax.broadcasted_iota(jnp.int32, (SEQ_LEN, 1), 0)
-    length = jnp.where(first, valid_len[0], valid_len[1])
-    live = ((core < seq_count[0]) & (places < length)).astype(F32)
-    d_res = live * ring.order(jnp.where(first, cotangent[:SEQ_LEN], cotangent[SEQ_LEN:]), width)
     cut = hid // 256 * 128 + 128
-    w_gate, w_up, w_down, resid, ffn_in, d_ffn = call(
+    w_gate, w_up, w_down, resid, ffn_in = call(
         functools.partial(gather_ffn_kernel, hid, cut),
         "gather_ffn",
         1,
-        (part0, part3, part4, attn_terms, seqs, gain_ffn, d_res.astype(BF16)),
-        [ANY] * 5 + [VMEM, ANY],
-        [((8, width, hid), BF16)] * 3 + [((SEQ_LEN, dim), F32), (rows4, BF16), (rows4, BF16)],
-        [ANY] * 6,
-        quad_scratch(dim)
-        + [pltpu.VMEM((SEQ_LEN, dim), F32), pltpu.VMEM((SEQ_LEN, dim), BF16)]
-        + [pltpu.VMEM((SEQ_LEN, dim), BF16)] * 2
-        + [pltpu.VMEM((3, width, 3 * hid), BF16)],
+        (part0, part3, part4, attn_terms, own, gain_rows),
+        [ANY] * 5 + [VMEM],
+        [((8, width, hid), BF16)] * 3 + [(row, F32), (rows4, BF16)],
+        [ANY] * 5,
+        quad_scratch(dim) + [vmem(row), vmem(row, BF16), vmem(row, BF16), vmem((3, width, 3 * hid), BF16)],
         160,
     )
-    w_gate, w_up, w_down, ffn_in, d_ffn = map(flat, (w_gate, w_up, w_down, ffn_in, d_ffn))
+    w_gate, w_up, w_down, ffn_in = map(flat, (w_gate, w_up, w_down, ffn_in))
     gate, up_vals = mm(ffn_in, w_gate), mm(ffn_in, w_up)
     sig = jax.nn.sigmoid(gate)
     hidden = (gate * sig * up_vals).astype(BF16)
-    down_given = over_y(mm(d_ffn[:, half:], hidden, TN, BF16))
-    down_terms = mm(d_ffn[:, :half], hidden, TN, BF16)
+    down_given = over_y(mm(d_ffn[:, half:], hidden[:, :DOWN_EARLY], TN, BF16))
+    down_terms = mm(d_ffn[:, :half], hidden[:, :DOWN_EARLY], TN, BF16)
+    down_rest = mm(d_ffn, hidden[:, DOWN_EARLY:], TN, BF16)
     d_hidden = mm(d_ffn, w_down)
     d_gate = (d_hidden * up_vals * (sig * (1.0 + gate * (1.0 - sig)))).astype(BF16)
     d_up = (d_hidden * (gate * sig)).astype(BF16)
-    up_given = over_y(mm(ffn_in[:, half:], d_up, TN, BF16))
-    up_terms = mm(ffn_in[:, :half], d_up, TN, BF16)
     gate_terms = mm(ffn_in, d_gate, TN, BF16)
-    ffn_terms = mm(hidden, w_down, NT).reshape(rows4)
     d_ffn_terms = (mm(d_gate, w_gate, NT) + mm(d_up, w_up, NT)).reshape(rows4)
-    gate_sum, down_sum, d_h, d_attn, ffn_gains, block_out = call(
-        functools.partial(sum_ffn_kernel, hid),
+    gate_sum, down_sum, d_h, d_attn, ffn_gains = call(
+        functools.partial(sum_ffn_kernel, hid, DOWN_EARLY),
         "sum_ffn",
         2,
         (
             blocks(gate_terms),
             blocks(down_terms),
             blocks(down_given),
+            blocks(down_rest),
             d_ffn_terms,
             resid,
-            gain_ffn,
+            gain_rows,
             d_res,
-            ffn_terms,
-            jnp.broadcast_to(live, (SEQ_LEN, 128)),
         ),
-        [ANY] * 5 + [VMEM, ANY, ANY, VMEM],
-        [
-            ((shard, 2 * hid), F32),
-            ((shard, 2 * hid), F32),
-            ((SEQ_LEN, dim), F32),
-            (rows4, BF16),
-            ((8, dim), F32),
-            ((2 * SEQ_LEN, dim), BF16),
-        ],
-        [ANY] * 4 + [VMEM, ANY],
-        sum_scratch(width, hid) * 2
-        + quad_scratch(dim) * 2
-        + [
-            pltpu.VMEM((SEQ_LEN, dim), F32),
-            pltpu.VMEM((SEQ_LEN, dim), F32),
-            pltpu.VMEM((SEQ_LEN, dim), BF16),
-            pltpu.VMEM((SEQ_LEN, dim), BF16),
-        ],
-        160,
+        [ANY] * 6 + [VMEM, ANY],
+        [((shard, 2 * hid), F32), ((shard, 2 * hid), F32), (row, F32), (rows4, BF16), ((8, dim), F32)],
+        [ANY] * 4 + [VMEM],
+        sum_scratch(width, DOWN_EARLY)
+        + sum_scratch(width, hid - DOWN_EARLY)
+        + sum_scratch(width, DOWN_EARLY)
+        + sum_scratch(width, hid - DOWN_EARLY)
+        + quad_scratch(dim)
+        + [vmem(row), vmem(row), vmem(row, BF16)],
+        200,
     )
-    d_attn = flat(d_attn)
+    d_attn, d_up, hidden, ffn_in = lax.optimization_barrier((flat(d_attn), d_up, hidden, ffn_in))
+    up_given = over_y(mm(ffn_in[:, half:], d_up[:, :UP_EARLY], TN, BF16))
     d_proj = mixer_backward(proj, saved, mm(d_attn, w_out))
     d_attn_terms = mm(d_proj, w_in, NT).reshape(rows4)
+    up_terms = mm(ffn_in[:, :half], d_up[:, :UP_EARLY], TN, BF16)
+    up_rest = mm(ffn_in, d_up[:, UP_EARLY:], TN, BF16)
+    ffn_terms = mm(hidden, w_down, NT).reshape(rows4)
     tail = width // 2
-    up_sum, out_sum, q_sum, k_sum, v_sum, f_sum, input_grad, gain_sums = call(
-        functools.partial(sum_last_kernel, hid),
+    up_sum, out_sum, q_sum, k_sum, v_sum, f_sum, input_grad, block_out, gain_sums = call(
+        functools.partial(sum_last_kernel, hid, UP_EARLY),
         "sum_last",
         3,
         (
             blocks(up_terms),
             blocks(up_given),
+            blocks(up_rest),
             blocks(mm(d_attn, mixed, TN, BF16)),
             blocks(mm(attn_in, d_proj, TN, BF16)),
             d_attn_terms,
-            seqs,
-            gain_attn,
+            own,
+            gain_rows,
             d_h,
             ffn_gains,
+            ffn_terms,
+            resid,
+            live,
         ),
-        [ANY] * 6 + [VMEM, ANY, VMEM],
+        [ANY] * 7 + [VMEM, ANY, VMEM, ANY, ANY, VMEM],
         [((shard, 2 * hid), F32)]
         + [((shard, 2 * KDIM), F32)] * 4
-        + [((shard, 256), F32), ((2 * SEQ_LEN, dim), F32), ((8, tail), F32)],
-        [ANY] * 7 + [VMEM],
-        sum_scratch(width, hid)
+        + [((shard, 256), F32), ((2 * SEQ_LEN, dim), F32), ((2 * SEQ_LEN, dim), BF16), ((8, tail), F32)],
+        [ANY] * 8 + [VMEM],
+        sum_scratch(width, UP_EARLY)
+        + sum_scratch(width, hid - UP_EARLY)
         + sum_scratch(width, KDIM) * 4
         + sum_scratch(width, 128)
-        + quad_scratch(dim)
-        + [
-            pltpu.VMEM((SEQ_LEN, dim), BF16),
-            pltpu.VMEM((SEQ_LEN, dim), F32),
-            pltpu.VMEM((8, dim), F32),
-            pltpu.VMEM((8, 8, width), F32),
-            pltpu.VMEM((8, 8, width), F32),
-            pltpu.VMEM((4, 8, width), F32),
-            pltpu.VMEM((3, 8, width), F32),
-            pltpu.VMEM((3, 8, width), F32),
-            pltpu.VMEM((2, 8, tail), F32),
-            pltpu.VMEM((8, tail), F32),
-        ],
-        240,
+        + quad_scratch(dim) * 2
+        + [vmem(row, BF16), vmem(row), vmem(row), vmem(row, BF16), vmem((8, dim))]
+        + [vmem((depth, 8, width)) for depth in (8, 8, 4, 3, 3)]
+        + [vmem((2, 8, tail)), vmem((8, tail))],
+        280,
     )
     f_grad = jnp.concatenate([f_sum[:, :SLOTS], f_sum[:, 128 : 128 + SLOTS]], axis=1)
     return (

time: 810 us -> 717 us (0.89)
  Pallas kernels: 571 us -> 506 us
  other arithmetic: 25.9 us -> 0.73 us
  waiting for transfers between devices: 29.4 us -> 15.4 us
    pallas_call x4, Pallas kernels: 539 us -> 475 us  [call(): pl.pallas_call(kernel, in_specs=specs, out_specs=out_specs, out_shape=[ja...]
    ppermute x4, waiting for transfers between devices: 29.4 us -> 15.4 us  [send(): return lax.ppermute(value, 'dp', self.perm(stride, size, shift % size))]
    unnamed x11 -> x4, other arithmetic: 8.69 us -> 0.01 us
    dot_general x17 -> x19, matrix products: 149 us -> 155 us  [mm(): lax.dot_general(left, right, dims, preferred_element_type=F32).astype(kind)]
  transfers between devices with their start and end apart: 4 -> 4, of which waited for: 1 -> 2; matrix products, arithmetic and copies ran while one was open for 14% -> 13% of each run, Pallas kernels for 25% -> 4%
where the time goes in v4:
time: 717 us; the launch traced here: 707 us
  Pallas kernels  506 us (71%)
  matrix products  155 us (22%)
  local copies, waits for them, and re-layouts  22.1 us (3%)
  waiting for transfers between devices  15.4 us (2%)
    pallas_call x4, Pallas kernels, call(): pl.pallas_call(kernel, in_specs=specs, out_specs=out_specs, out_shape=[ja...  475 us
    dot_general x19, matrix products, mm(): lax.dot_general(left, right, dims, preferred_element_type=F32).astype(kind)  155 us
    pallas_call x1, Pallas kernels, mixer_backward(): pl.pallas_call(backward_kernel, grid=(rows // SEQ_LEN,), in_specs=IN_SPEC...  18.3 us
    ppermute x4, waiting for transfers between devices, send(): return lax.ppermute(value, 'dp', self.perm(stride, size, shift % size))  15.4 us
    unnamed x79, local copies, waits for them, and re-layouts  14.6 us
  transfers between devices with their start and end apart: 4, of which 2 were waited for; matrix products, arithmetic and copies ran while one was open for 13% of the time, Pallas kernels for 4%

profile of v4, /device:TPU:0, one launch (start us, length us, event | category | flops | bytes accessed | tf_op | source)
XLA Modules:
  0.0 706.5 jit_solution(2231575094409700060)
XLA Ops:
  8.0 103.7 %gather_first.1 = (bf16[8,256,1664]{2,1,0:T(8,128)(2,1)}, bf16[8,256,512]{2,1,0:T(8,128)(2,1)}, bf16[256,4224]{1,0:T(8,128)(2,1)}, bf16[256,2048]{1,0:T(8,128)(2...) custom-call(bf16[512,2048]{1,0:T(8,128)(2,1)} %tokens.1, ...), custom_call_target="tpu_custom_call" | custom-call | tf_op jit(solution)/shard_map/gather_first/pallas_call | solution.py:929
  111.7 1.4 collective-permute-start.1
  113.5 13.3 %fusion.30.q_ref.k_ref.v_ref.f_ref = f32[1024,1664]{1,0:T(8,128)} fusion(bf16[1024,2048]{1,0:T(8,128)(2,1)} %bitcast.94, bf16[2048,1664]{1,0:T(8,128)(2,1)} %bitcast.78), kind=kOutput, calls=%fused_computation.36 | convolution fusion | flops 6979321856 | bytes 17825792 | tf_op jit(solution)/shard_map/dot_general | solution.py:1049
  126.8 12.8 %mixer_forward.1 = (bf16[1024,512]{1,0:T(8,128)(2,1)S(1)}, f32[1024,128]{1,0:T(8,128)S(1)}, f32[1024,128]{1,0:T(8,128)S(1)}, f32[1024,256]{1,0:T(8,128)S(1)}, f32[1024,256]{1,0:T(8,128)S(1)}) custom-call(f32[1024,1664]{1,0:T(8,128)} %fusion.30.q_ref.k_ref.v_ref.f_ref, f32[1024,1664]{1,0:T(8,128)} %fusion.30.q_ref.k_ref.v_ref.f_ref, ...), custom_call_target="tpu_custom_call" | custom-call | flops 3072000000 | bytes 10240000 | tf_op jit(solution)/shard_map/mixer_forward/pallas_call | solution.py:251
  139.7 5.7 fusion.31.terms
  145.3 14.5 %collective-permute-done.1.b4 = bf16[256,4224]{1,0:T(8,128)(2,1)S(1)} collective-permute-done((bf16[256,4224]{1,0:T(8,128)(2,1)}, bf16[256,4224]{1,0:T(8,128)(2,1)S(1)}, u32[]{:S(2)}, u32[]{:S(2)}) %collective-permute-start.1) | collective-permute-done | bytes 2162720 | tf_op jit(solution)/shard_map/ppermute | solution.py:965
  159.8 1.3 copy-done.4
  162.1 1.3 copy-done.5
  163.4 123.3 %gather_ffn.1 = (bf16[8,256,1408]{2,1,0:T(8,128)(2,1)}, bf16[8,256,1408]{2,1,0:T(8,128)(2,1)}, bf16[8,256,1408]{2,1,0:T(8,128)(2,1)}, f32[256,2048]{1,0:T(8,128)}, bf16[4,256,2048]{2,1,0:T(8,128)(2,1)}) custom-call(bf16[256,4224]{1,0:T(8,128)(2,1)} %get-tuple-element.48.b0, bf16[256,4224]{1,0:T(8,128)(2,1)} %copy-done.5, bf16[256,4224]{1,0:T(8,128)(2,1)} %copy-done.4, ...), custom_call_target="tpu_custom_call" | custom-call | tf_op jit(solution)/shard_map/gather_ffn/pallas_call | solution.py:929
  286.8 11.8 %fusion.32 = f32[1024,1408]{1,0:T(8,128)} fusion(bf16[1024,2048]{1,0:T(8,128)(2,1)} %bitcast.100, bf16[2048,1408]{1,0:T(8,128)(2,1)} %bitcast.90), kind=kOutput, calls=%fused_computation.38 | convolution fusion | flops 5905580032 | bytes 15728640 | tf_op jit(solution)/shard_map/dot_general | solution.py:1049
  298.6 8.4 %fusion.33 = f32[1024,1408]{1,0:T(8,128)} fusion(bf16[1024,2048]{1,0:T(8,128)(2,1)S(1)} %bitcast.102, bf16[2048,1408]{1,0:T(8,128)(2,1)S(1)} %bitcast.88), kind=kOutput, calls=%fused_computation.39 | convolution fusion | flops 5905580032 | bytes 15728640 | tf_op jit(solution)/shard_map/dot_general | solution.py:1049
  307.1 13.6 %multiply_convert_fusion = (bf16[1024,1408]{1,0:T(8,128)(2,1)}, bf16[1024,1408]{1,0:T(8,128)(2,1)}, bf16[1024,1408]{1,0:T(8,128)(2,1)}) fusion(f32[1024,1408]{1,0:T(8,128)} %fusion.33, f32[1024,1408]{1,0:T(8,128)} %fusion.32, bf16[1024,2048]{1,0:T(8,128)(2,1)S(1)} %bitcast.96, bf16[2048,1408]{1,0:T(8,128)(2,1)S(1)} %bitcast.84), kind=kOutput, calls=%fused_computation.2 | convolution fusion | flops 5927206912 | bytes 30146560 | tf_op jit(solution)/shard_map/dot_general | solution.py:1049
  320.6 3.5 fusion.18
  324.1 3.1 fusion.15
  327.2 4.9 convolution_convert_fusion.2
  332.8 9.0 %fusion.34 = f32[1024,2048]{1,0:T(8,128)} fusion(bf16[1024,1408]{1,0:T(8,128)(2,1)S(1)} %copy-done.24, bf16[2048,1408]{1,0:T(8,128)(2,1)S(1)} %bitcast.93), kind=kOutput, calls=%fused_computation.40 | convolution fusion | flops 5905580032 | bytes 17039360 | tf_op jit(solution)/shard_map/dot_general | solution.py:1049
  341.9 23.6 %convolution_add_fusion = f32[1024,2048]{1,0:T(8,128)} fusion(f32[1024,2048]{1,0:T(8,128)} %fusion.34, bf16[1024,1408]{1,0:T(8,128)(2,1)} %get-tuple-element.85, bf16[2048,1408]{1,0:T(8,128)(2,1)S(1)} %bitcast.89), kind=kOutput, calls=%fused_computation.7 | convolution fusion | flops 5907677184 | bytes 25427968 | tf_op jit(solution)/shard_map/dot_general | solution.py:1049
  365.4 8.6 %convolution_convert_fusion.1 = bf16[2048,1408]{1,0:T(8,128)(2,1)} fusion(bf16[1024,2048]{1,0:T(8,128)(2,1)S(1)} %bitcast.103, bf16[1024,1408]{1,0:T(8,128)(2,1)S(1)} %copy-done.26), kind=kOutput, calls=%fused_computation.1 | convolution fusion | flops 5908463616 | bytes 12845056 | tf_op jit(solution)/shard_map/dot_general | solution.py:1049
  374.0 111.2 %sum_ffn.1 = (f32[128,2816]{1,0:T(8,128)}, f32[128,2816]{1,0:T(8,128)}, f32[256,2048]{1,0:T(8,128)}, bf16[4,256,2048]{2,1,0:T(8,128)(2,1)}, f32[8,2048]{1,0:T(8,128)}) custom-call(bf16[8,256,1408]{2,1,0:T(8,128)(2,1)} %bitcast.69, bf16[4,256,768]{2,1,0:T(8,128)(2,1)} %bitcast.75, bf16[4,256,768]{2,1,0:T(8,128)(2,1)} %bitcast.17.given, ...), custom_call_target="tpu_custom_call" | custom-call | tf_op jit(solution)/shard_map/sum_ffn/pallas_call | solution.py:929
  485.2 4.7 fusion.12
  489.9 3.6 fusion.9
  493.6 3.8 convolution_convert_fusion.4
  497.3 3.8 convolution_convert_fusion.3
  501.2 2.3 fusion.35.d_ref
  504.7 9.2 %fusion.37.out_terms = f32[4,256,2048]{2,1,0:T(8,128)} fusion(bf16[4,256,1408]{2,1,0:T(8,128)(2,1)S(1)} %bitcast.110, bf16[2048,1408,1]{1,0,2:T(8,128)(2,1)S(1)} %bitcast.87), kind=kOutput, calls=%fused_computation.43 | convolution fusion | flops 5905580032 | bytes 17039360 | tf_op jit(solution)/shard_map/dot_general | solution.py:1049
  513.9 18.3 %mixer_backward.1 = bf16[1024,1664]{1,0:T(8,128)(2,1)} custom-call(f32[1024,1664]{1,0:T(8,128)} %fusion.30.q_ref.k_ref.v_ref.f_ref, f32[1024,1664]{1,0:T(8,128)} %fusion.30.q_ref.k_ref.v_ref.f_ref, f32[1024,1664]{1,0:T(8,128)} %fusion.30.q_ref.k_ref.v_ref.f_ref, f32[1024,1664]{1,0:T(8,128)} %fusion.30.q_ref.k_ref.v_ref.f_ref, ...), custom_call_target="tpu_custom_call" | custom-call | flops 9216000000 | bytes 16384000 | tf_op jit(solution)/shard_map/mixer_backward/pallas_call | solution.py:266
  532.2 11.7 %fusion.36.terms = f32[4,256,2048]{2,1,0:T(8,128)} fusion(bf16[4,256,1664]{2,1,0:T(8,128)(2,1)} %bitcast.70, bf16[2048,1664,1]{1,0,2:T(8,128)(2,1)S(1)} %bitcast.81), kind=kOutput, calls=%fused_computation.42 | convolution fusion | flops 6979321856 | bytes 18612224 | tf_op jit(solution)/shard_map/dot_general | solution.py:1049
  543.9 10.3 %convolution_convert_fusion = bf16[2048,1664]{1,0:T(8,128)(2,1)} fusion(bf16[1024,2048]{1,0:T(8,128)(2,1)S(1)} %bitcast.95, bf16[1024,1664]{1,0:T(8,128)(2,1)S(1)} %copy-done.3), kind=kOutput, calls=%fused_computation | convolution fusion | flops 6982729728 | bytes 14417920 | tf_op jit(solution)/shard_map/dot_general | solution.py:1049
  554.2 137.1 %sum_last.1 = (f32[128,2816]{1,0:T(8,128)}, f32[128,1024]{1,0:T(8,128)}, f32[128,1024]{1,0:T(8,128)}, f32[128,1024]{1,0:T(8,128)}, f32[128,1024]{1,0:T(8,128)}, ...) custom-call(bf16[4,256,896]{2,1,0:T(8,128)(2,1)} %bitcast.74, ...), custom_call_target="tpu_custom_call" | custom-call | tf_op jit(solution)/shard_map/sum_last/pallas_call | solution.py:929
  691.3 1.3 slice_bitcast_fusion
  694.3 3.2 copy.40
  697.4 2.1 copy.41
  (95 shorter events, 17.0 us)
Async XLA Ops:
  111.7 48.1 %collective-permute-start.1 = (bf16[256,4224]{1,0:T(8,128)(2,1)}, bf16[256,4224]{1,0:T(8,128)(2,1)S(1)}, u32[]{:S(2)}, u32[]{:S(2)}) collective-permute-start(bf16[256,4224]{1,0:T(8,128)(2,1)} %get-tuple-element.48.b0), channel_id=1, source_target_pairs={{0,4},{2,6},{4,0},{6,2},{8,12},{10,14},{12,8},{14,10},{16,20},{18,... | collective-permute-start | bytes 6488072 | tf_op jit(solution)/shard_map/ppermute | solution.py:965
  113.0 49.0 %collective-permute-start = (bf16[256,4224]{1,0:T(8,128)(2,1)}, bf16[256,4224]{1,0:T(8,128)(2,1)S(1)}, u32[]{:S(2)}, u32[]{:S(2)}) collective-permute-start(bf16[256,4224]{1,0:T(8,128)(2,1)} %get-tuple-element.48.b0), channel_id=1, source_target_pairs={{0,8},{2,10},{4,12},{6,14},{8,16},{10,18},{12,20},{14,22},{16,24},... | collective-permute-start | bytes 6488072 | tf_op jit(solution)/shard_map/ppermute | solution.py:965
  126.8 12.8 %copy-start.20 = (bf16[8,256,512]{2,1,0:T(8,128)(2,1)S(1)}, bf16[8,256,512]{2,1,0:T(8,128)(2,1)}, u32[]{:S(2)}) copy-start(bf16[8,256,512]{2,1,0:T(8,128)(2,1)} %get-tuple-element.52) | copy-start | bytes 6291460
  139.6 5.7 copy-start
  286.7 11.9 %copy-start.13 = (bf16[8,256,1408]{2,1,0:T(8,128)(2,1)S(1)}, bf16[8,256,1408]{2,1,0:T(8,128)(2,1)}, u32[]{:S(2)}) copy-start(bf16[8,256,1408]{2,1,0:T(8,128)(2,1)} %get-tuple-element.59) | copy-start | bytes 17301508
  286.7 11.9 %copy-start.16 = (bf16[4,256,2048]{2,1,0:T(8,128)(2,1)S(1)}, bf16[4,256,2048]{2,1,0:T(8,128)(2,1)}, u32[]{:S(2)}) copy-start(bf16[4,256,2048]{2,1,0:T(8,128)(2,1)} %get-tuple-element.55) | copy-start | bytes 12582916
  286.7 20.3 %slice-start.2 = ((s8[5767168]{0:T(1024)(128)(4,1)}), s8[4194304]{0:T(1024)(128)(4,1)S(1)}, s32[]{:S(2)}) async-start(s8[5767168]{0:T(1024)(128)(4,1)} %bitcast.82), calls=%async_computation.2 | async-start | bytes 8388608
  298.6 8.5 %slice-start.3 = ((s8[5767168]{0:T(1024)(128)(4,1)}), s8[1572864]{0:T(1024)(128)(4,1)S(1)}, s32[]{:S(2)}) async-start(s8[5767168]{0:T(1024)(128)(4,1)} %bitcast.82), calls=%async_computation.3 | async-start | bytes 3145728
  298.6 8.5 %copy-start.15 = (bf16[4,256,2048]{2,1,0:T(8,128)(2,1)S(1)}, bf16[4,256,2048]{2,1,0:T(8,128)(2,1)}, u32[]{:S(2)}) copy-start(bf16[4,256,2048]{2,1,0:T(8,128)(2,1)} %get-tuple-element.56) | copy-start | bytes 12582916
  324.1 8.7 %slice-start.6 = ((s8[5767168]{0:T(1024)(128)(4,1)}), s8[4194304]{0:T(1024)(128)(4,1)S(1)}, s32[]{:S(2)}) async-start(s8[5767168]{0:T(1024)(128)(4,1)} %bitcast.91), calls=%async_computation.6 | async-start | bytes 8388608
  327.2 5.6 slice-start.7
  327.2 5.6 copy-start.24
  332.1 42.0 %collective-permute-start.2 = (bf16[1024,768]{1,0:T(8,128)(2,1)S(1)}, bf16[1024,768]{1,0:T(8,128)(2,1)}, u32[]{:S(2)}, u32[]{:S(2)}) collective-permute-start(bf16[1024,768]{1,0:T(8,128)(2,1)S(1)} %fusion.18), channel_id=1, source_target_pairs={{0,4},{2,6},{4,0},{6,2},{8,12},{10,14},{12,8},{14,10},{16,20},{18,... | collective-permute-start | bytes 4718600 | tf_op jit(solution)/shard_map/ppermute | solution.py:965
  341.8 23.6 %copy-start.17 = (bf16[4,256,2048]{2,1,0:T(8,128)(2,1)S(1)}, bf16[4,256,2048]{2,1,0:T(8,128)(2,1)}, u32[]{:S(2)}) copy-start(bf16[4,256,2048]{2,1,0:T(8,128)(2,1)} %get-tuple-element.55) | copy-start | bytes 12582916
  341.8 23.6 %copy-start.26 = (bf16[1024,1408]{1,0:T(8,128)(2,1)S(1)}, bf16[1024,1408]{1,0:T(8,128)(2,1)}, u32[]{:S(2)}) copy-start(bf16[1024,1408]{1,0:T(8,128)(2,1)} %get-tuple-element.85) | copy-start | bytes 8650756
  485.2 4.7 copy-start.18
  485.2 4.7 copy-start.25
  493.6 3.8 copy-start.1
  493.6 3.8 copy-start.19
  497.3 3.8 copy-start.21
  497.3 7.4 %slice-start.4 = ((s8[5767168]{0:T(1024)(128)(4,1)}), s8[4194304]{0:T(1024)(128)(4,1)S(1)}, s32[]{:S(2)}) async-start(s8[5767168]{0:T(1024)(128)(4,1)} %bitcast.85), calls=%async_computation.4 | async-start | bytes 8388608
  501.1 3.6 copy-start.23
  501.1 31.1 %slice-start = ((s8[6815744]{0:T(1024)(128)(4,1)}), s8[4194304]{0:T(1024)(128)(4,1)S(1)}, s32[]{:S(2)}) async-start(s8[6815744]{0:T(1024)(128)(4,1)} %bitcast.79), calls=%async_computation | async-start | bytes 8388608
  503.5 50.7 %collective-permute-start.3 = (bf16[1024,896]{1,0:T(8,128)(2,1)S(1)}, bf16[1024,896]{1,0:T(8,128)(2,1)}, u32[]{:S(2)}, u32[]{:S(2)}) collective-permute-start(bf16[1024,896]{1,0:T(8,128)(2,1)S(1)} %fusion.12), channel_id=1, source_target_pairs={{0,4},{2,6},{4,0},{6,2},{8,12},{10,14},{12,8},{14,10},{16,20},{18,... | collective-permute-start | bytes 5505032 | tf_op jit(solution)/shard_map/ppermute | solution.py:965
  504.7 27.5 %slice-start.1 = ((s8[6815744]{0:T(1024)(128)(4,1)}), s8[2621440]{0:T(1024)(128)(4,1)S(1)}, s32[]{:S(2)}) async-start(s8[6815744]{0:T(1024)(128)(4,1)} %bitcast.79), calls=%async_computation.1 | async-start | bytes 5242880
  532.2 11.7 %copy-start.3 = (bf16[1024,1664]{1,0:T(8,128)(2,1)S(1)}, bf16[1024,1664]{1,0:T(8,128)(2,1)}, u32[]{:S(2)}) copy-start(bf16[1024,1664]{1,0:T(8,128)(2,1)} %mixer_backward.1) | copy-start | bytes 10223620
  532.2 11.7 %copy-start.14 = (bf16[4,256,2048]{2,1,0:T(8,128)(2,1)S(1)}, bf16[4,256,2048]{2,1,0:T(8,128)(2,1)}, u32[]{:S(2)}) copy-start(bf16[4,256,2048]{2,1,0:T(8,128)(2,1)} %get-tuple-element.49) | copy-start | bytes 12582916
  691.3 6.1 copy-start.2
  697.4 3.7 copy-start.10
  697.4 4.5 copy-start.9
  699.6 4.3 copy-start.8
  701.2 3.8 copy-start.6
  (7 other events, 18.0 us)

commit v5 on v4

--- a/solution.py
+++ b/solution.py
@@ -332,6 +332,11 @@
     def two(self):
         return (self.one(), self.one())
 
+    def some(self, count):
+        first = self.used
+        self.used += count
+        return lambda index: self.ref.at[first + index]
+
 
 def pieces(rows, work):
     def step(i, carry):
@@ -603,12 +608,12 @@
 
 
 def gather_ffn_kernel(
-    hid, cut, b0, b3, b4, terms, tokens, gains, w_gate, w_up, w_down, resid, ffn_in, s0, s1, s2, s3, kept, normed, inputs, stage, sem
+    hid, cut, b0, b3, b4, terms, tokens, gains, w_wide, w_down, resid, ffn_in, s0, s1, s2, s3, kept, normed, inputs, stage, sem
 ):
     place, sems = Place(), Sems(sem)
     chunks = [
-        (0, hid, w_gate, 0, False),
-        (hid, hid, w_up, 0, False),
+        (0, hid, w_wide, 0, False),
+        (hid, hid, w_wide, hid, False),
         (2 * hid, cut, w_down, 0, False),
         (2 * hid + cut, hid - cut, w_down, cut, True),
     ]
@@ -712,7 +717,7 @@
             if given is None:
                 self.crosses.append(place.copy("y", terms.at[4 + index, :, cols], self.other.at[index], sems.two()))
             else:
-                self.loads.append(pltpu.make_async_copy(given.at[index, :, cols], self.other.at[index], sems.one()))
+                self.loads.append(pltpu.make_async_copy(given.at[index], self.other.at[index], sems.one()))
         self.per = len(self.loads) // 4
         self.rises = [place.copy("up", self.to_z.at[i], self.from_z.at[i], sems.two()) for i in range(3)]
         half = self.final.shape[0] // 2
@@ -757,8 +762,160 @@
         self.swap.wait()
 
 
+class SumGiven:
+    def __init__(self, place, sems, terms, given, result, first, width, scratch, span, start):
+        self.own, self.others, self.to_y, self.from_y, self.final = scratch
+        cols = pl.ds(first, width)
+        self.loads = [
+            pltpu.make_async_copy(terms.at[d * (terms.shape[0] // 2), :, cols], self.own.at[d], sems.one())
+            for d in range(2)
+        ]
+        self.loads += [pltpu.make_async_copy(one, self.others.at[i], sems.one()) for i, one in enumerate(given)]
+        self.cross = place.copy("y", self.to_y, self.from_y, sems.two())
+        half = self.final.shape[0] // 2
+        there = result.at[:, pl.ds(pl.multiple_of(place.x * span + start, 128), width)]
+        self.leave = pltpu.make_async_copy(self.final.at[place.half(half)], there, sems.one())
+        self.swap = place.copy("x", self.final.at[place.half(half, True)], there, sems.two())
+
+    def start(self):
+        for copy in self.loads:
+            copy.start()
+
+    def first(self):
+        for copy in self.loads:
+            copy.wait()
+
+        def add(part):
+            for d in (1, 0):
+                value = self.own[d, part].astype(F32)
+                for i in range(3):
+                    value = value + self.others[i, d, part].astype(F32)
+                if d:
+                    self.to_y[part] = value.astype(BF16)
+                else:
+                    self.final[part] = value
+
+        pieces(self.final.shape[0], add)
+        self.cross.start()
+
+    def second(self):
+        self.cross.wait_recv()
+
+        def add(part):
+            self.final[part] = self.final[part] + self.from_y[part].astype(F32)
+
+        pieces(self.final.shape[0], add)
+        self.swap.start()
+        self.leave.start()
+
+    def finish(self):
+        self.cross.wait_send()
+        self.leave.wait()
+        self.swap.wait()
+
+
+def given_scratch(rows, width):
+    return [
+        pltpu.VMEM((2, rows, width), BF16),
+        pltpu.VMEM((3, 2, rows, width), BF16),
+        pltpu.VMEM((rows, width), BF16),
+        pltpu.VMEM((rows, width), BF16),
+        pltpu.VMEM((rows, width), F32),
+    ]
+
+
 def sum_scratch(rows, width):
     return [pltpu.VMEM((depth, rows, width), BF16) for depth in (4, 4, 3, 3)] + [pltpu.VMEM((rows, width), F32)]
+
+
+class UpTerms:
+    def __init__(self, sems, acts, grads, bufs, over, own, parts):
+        self.acts, self.grads, self.bufs = acts, grads, bufs
+        self.over, self.own, self.parts = over, own, parts
+        self.early = over.shape[2]
+        self.left, self.right = sems.some(2), sems.some(2)
+
+    def copies(self, slot, left, right):
+        early, rest = self.early, self.bufs.shape[2] - self.early
+        return (
+            pltpu.make_async_copy(self.bufs.at[slot, :, pl.ds(0, early)], left, self.left(slot)),
+            pltpu.make_async_copy(self.bufs.at[slot, :, pl.ds(early, rest)], right, self.right(slot)),
+        )
+
+    def wait(self, slot):
+        for copy in self.copies(slot, self.own.at[0], self.parts[0].at[0]):
+            copy.wait()
+
+    def run(self, start, stop):
+        width = self.bufs.shape[1]
+
+        def step(i, carry):
+            slot, side, away = i % 2, i // 4, i % 4
+
+            @pl.when(i >= 2)
+            def _():
+                self.wait(slot)
+
+            cols = pl.ds(pl.multiple_of(i * width, width), width)
+            self.bufs[slot] = mm(self.acts[:, cols], self.grads[...], TN, BF16)
+
+            @pl.when(side == 0)
+            def _():
+                self.copies(slot, self.own.at[away], self.parts[0].at[0])[0].start()
+
+            @pl.when(side == 1)
+            def _():
+                self.copies(slot, self.over.at[away], self.parts[0].at[0])[0].start()
+
+            for place in range(4):
+
+                @pl.when(away == place)
+                def _(place=place):
+                    self.copies(slot, self.own.at[0], self.parts[place].at[side])[1].start()
+
+            return carry
+
+        lax.fori_loop(start, stop, step, 0)
+
+    def finish(self):
+        self.wait(0)
+        self.wait(1)
+
+
+class OutTerms:
+    def __init__(self, sems, hidden, weight, stage, bufs, target):
+        self.hidden, self.weight, self.stage, self.bufs, self.target = hidden, weight, stage, bufs, target
+        self.loads, self.stores = sems.some(2), sems.some(2)
+
+    def load(self, i):
+        return pltpu.make_async_copy(self.weight.at[i], self.stage.at[i % 2], self.loads(i % 2))
+
+    def store(self, i):
+        width = self.bufs.shape[2]
+        cols = pl.ds(pl.multiple_of(i * width, width), width)
+        return pltpu.make_async_copy(self.bufs.at[i % 2], self.target.at[:, cols], self.stores(i % 2))
+
+    def run(self, start, stop):
+        def step(i, carry):
+            self.load(i).wait()
+
+            @pl.when(i < 7)
+            def _():
+                self.load(i + 1).start()
+
+            @pl.when(i >= 2)
+            def _():
+                self.store(i).wait()
+
+            self.bufs[i % 2] = mm(self.hidden[...], self.stage[i % 2], NT)
+            self.store(i).start()
+            return carry
+
+        lax.fori_loop(start, stop, step, 0)
+
+    def finish(self):
+        self.store(6).wait()
+        self.store(7).wait()
 
 
 def norm_back_piece(value, gain, grad):
@@ -769,34 +926,55 @@
     return scale * scaled - value * (scale * scale * scale * inner), jnp.sum(gains, axis=0)
 
 
-def sum_ffn_kernel(hid, part_hid, gate, down, given, down_rest, terms, resid, gains, d_res, gate_sum, down_sum, d_h, d_attn, gain_sum, *scratch):
+def sum_ffn_kernel(
+    hid, early, gate_t, down, given, given1, given2, given3, terms, resid, gains, d_res, ffn_in, d_wide, hidden, w_down,
+    gate_sum, down_sum, d_h, d_attn, gain_sum, up_over, up_own, up0, up1, up2, up3, out_terms, *scratch
+):
     *scratch, sem = scratch
     place, sems = Place(), Sems(sem)
-    sums = [
-        Sum(place, sems, down, given, down_sum, 0, part_hid, scratch[0:5], hid),
-        Sum(place, sems, down_rest, None, down_sum, 0, hid - part_hid, scratch[5:10], hid, part_hid),
-        Sum(place, sems, gate, None, gate_sum, 0, part_hid, scratch[10:15], hid),
-        Sum(place, sems, gate, None, gate_sum, part_hid, hid - part_hid, scratch[15:20], hid, part_hid),
+    rest = hid - early
+    down_y = Sum(place, sems, down, given, down_sum, 0, early, scratch[0:5], hid)
+    down_z = SumGiven(place, sems, down, (given1, given2, given3), down_sum, early, rest, scratch[5:10], hid, early)
+    gate = [
+        Sum(place, sems, gate_t, None, gate_sum, 0, early, scratch[10:15], hid),
+        Sum(place, sems, gate_t, None, gate_sum, early, rest, scratch[15:20], hid, early),
     ]
     back = QuadSum(place, sems, terms, scratch[20:24])
-    value, res, low = scratch[24:27]
+    value, res, low, acts, ups, up_bufs, hid_v, stage, out_bufs = scratch[24:33]
     quad = Quad(place, sems, low, d_attn)
+    up = UpTerms(sems, acts, ups, up_bufs, up_over, up_own, (up0, up1, up2, up3))
+    out = OutTerms(sems, hid_v, w_down, stage, out_bufs, out_terms)
+    ready = [
+        pltpu.make_async_copy(ffn_in, acts, sems.one()),
+        pltpu.make_async_copy(d_wide.at[:, pl.ds(hid, hid)], ups, sems.one()),
+        pltpu.make_async_copy(hidden, hid_v, sems.one()),
+    ]
     fetch = [pltpu.make_async_copy(resid, value, sems.one()), pltpu.make_async_copy(d_res, res, sems.one())]
     save = pltpu.make_async_copy(res, d_h, sems.one())
     place.greet()
     back.start()
-    for step in range(4):
-        for one in sums:
-            one.start(step)
+    for one in (down_y, *gate):
+        one.start(0)
+    down_z.start()
     for copy in fetch:
         copy.start()
-    sums[0].step(0)
+    for one in (down_y, *gate):
+        one.start(1)
+    down_y.step(0)
+    down_z.first()
+    for step in (2, 3):
+        for one in (down_y, *gate):
+            one.start(step)
+    for copy in ready:
+        copy.start()
+    out.load(0).start()
     back.middle()
-    for one in sums[1:]:
+    for one in gate:
         one.step(0)
-    for copy in fetch:
+    for copy in fetch + ready:
         copy.wait()
-    sums[0].step(1)
+    down_y.step(1)
+    up.run(0, 4)
     back.ready()
     gain_sum[...] = jnp.zeros_like(gain_sum)
 
@@ -810,29 +988,35 @@
     pieces(SEQ_LEN, norm)
     quad.start()
     save.start()
-    for one in sums[1:]:
+    for one in gate:
         one.step(1)
-    for one in sums:
+    down_y.step(2)
+    up.run(4, 8)
+    for one in gate:
         one.step(2)
+    down_y.step(3)
+    out.run(0, 8)
+    down_z.second()
     quad.forward()
-    for one in sums:
+    for one in gate:
         one.step(3)
     quad.finish()
     save.wait()
-    for one in sums:
+    up.finish()
+    out.finish()
+    for one in (down_y, down_z, *gate):
         one.finish()
 
 
 def sum_last_kernel(
-    hid, part_hid, up, given, up_rest, out_t, in_t, terms, tokens, gain_rows, d_h, ffn_gains, out_terms, resid, live,
+    hid, early, up, given, up_rest, given1, given2, given3, out_t, in_t, terms, tokens, gain_rows, d_h, ffn_gains, out_terms, resid, live,
     up_sum, out_sum, q_sum, k_sum, v_sum, f_sum, grad, block_out, gain_sum, *scratch
 ):
     *scratch, sem = scratch
     place, sems = Place(), Sems(sem)
     sums = []
     for terms_in, given_in, result, first, width, span, start in (
-        (up, given, up_sum, 0, part_hid, hid, 0),
-        (up_rest, None, up_sum, 0, hid - part_hid, hid, part_hid),
+        (up, given, up_sum, 0, early, hid, 0),
         (out_t, None, out_sum, 0, KDIM, None, 0),
         (in_t, None, q_sum, 0, KDIM, None, 0),
         (in_t, None, k_sum, KDIM, KDIM, None, 0),
@@ -841,6 +1025,8 @@
     ):
         sums.append(Sum(place, sems, terms_in, given_in, result, first, width, scratch[:5], span, start))
         scratch = scratch[5:]
+    up_z = SumGiven(place, sems, up_rest, (given1, given2, given3), up_sum, 0, hid - early, scratch[:5], hid, early)
+    scratch = scratch[5:]
     back = QuadSum(place, sems, terms, scratch[0:4])
     ahead = QuadSum(place, sems, out_terms, scratch[4:8])
     value, res, kept, shown, gains, parts, met, crossed, risen, rising, last, swapped = scratch[8:]
@@ -854,13 +1040,18 @@
     swap = place.copy("x", last.at[1 - place.x], swapped, sems.two())
     place.greet()
     back.start()
-    for step in range(3):
-        for one in sums:
-            one.start(step)
+    for one in sums:
+        one.start(0)
+    up_z.start()
     for copy in fetch:
         copy.start()
+    for one in sums:
+        one.start(1)
     ahead.start()
     sums[0].step(0)
+    up_z.first()
+    for one in sums:
+        one.start(2)
     back.middle()
     for one in sums[1:]:
         one.step(0)
@@ -892,6 +1083,7 @@
     for one in sums[1:]:
         one.step(1)
     ahead.middle()
+    up_z.second()
     for one in sums:
         one.step(2)
     cross.wait()
@@ -921,6 +1113,7 @@
         copy.wait_send()
     leave.finish()
     leave_out.finish()
+    up_z.finish()
     for one in sums:
         one.finish()
 
@@ -938,8 +1131,7 @@
 
 
 PAD = 128 - SLOTS
-DOWN_EARLY = 768
-UP_EARLY = 896
+EARLY = 896
 
 
 class Ring:
@@ -1279,70 +1471,86 @@
     mixed, *saved = mixer_forward(proj)
     attn_terms = mm(mixed, w_out, NT).reshape(rows4)
     cut = hid // 256 * 128 + 128
-    w_gate, w_up, w_down, resid, ffn_in = call(
+    w_wide, w_down, resid, ffn_in = call(
         functools.partial(gather_ffn_kernel, hid, cut),
         "gather_ffn",
         1,
         (part0, part3, part4, attn_terms, own, gain_rows),
         [ANY] * 5 + [VMEM],
-        [((8, width, hid), BF16)] * 3 + [(row, F32), (rows4, BF16)],
-        [ANY] * 5,
+        [((8, width, 2 * hid), BF16), ((8, width, hid), BF16), (row, F32), (rows4, BF16)],
+        [ANY] * 4,
         quad_scratch(dim) + [vmem(row), vmem(row, BF16), vmem(row, BF16), vmem((3, width, 3 * hid), BF16)],
         160,
     )
-    w_gate, w_up, w_down, ffn_in = map(flat, (w_gate, w_up, w_down, ffn_in))
-    gate, up_vals = mm(ffn_in, w_gate), mm(ffn_in, w_up)
+    w_wide, w_down, ffn_in = map(flat, (w_wide, w_down, ffn_in))
+
+    def early_terms(terms, start):
+        over = over_y(terms[half:, start : start + EARLY])
+        rest = blocks(terms)[:, :, start + EARLY : start + hid]
+        given = [ring.send(jnp.stack([rest[d], rest[4 + d]]), ring.stages[0], d) for d in (1, 2, 3)]
+        return [blocks(over), *given]
+
+    wide = mm(ffn_in, w_wide)
+    gate, up_vals = wide[:, :hid], wide[:, hid:]
     sig = jax.nn.sigmoid(gate)
     hidden = (gate * sig * up_vals).astype(BF16)
-    down_given = over_y(mm(d_ffn[:, half:], hidden[:, :DOWN_EARLY], TN, BF16))
-    down_terms = mm(d_ffn[:, :half], hidden[:, :DOWN_EARLY], TN, BF16)
-    down_rest = mm(d_ffn, hidden[:, DOWN_EARLY:], TN, BF16)
+    down_terms = mm(d_ffn, hidden, TN, BF16)
+    down_given = early_terms(down_terms, 0)
     d_hidden = mm(d_ffn, w_down)
     d_gate = (d_hidden * up_vals * (sig * (1.0 + gate * (1.0 - sig)))).astype(BF16)
     d_up = (d_hidden * (gate * sig)).astype(BF16)
-    gate_terms = mm(ffn_in, d_gate, TN, BF16)
-    d_ffn_terms = (mm(d_gate, w_gate, NT) + mm(d_up, w_up, NT)).reshape(rows4)
-    gate_sum, down_sum, d_h, d_attn, ffn_gains = call(
-        functools.partial(sum_ffn_kernel, hid, DOWN_EARLY),
+    d_wide = jnp.concatenate([d_gate, d_up], axis=1)
+    gate_terms = mm(ffn_in, d_wide[:, :hid], TN, BF16)
+    d_ffn_terms = mm(d_wide, w_wide, NT).reshape(rows4)
+    rest = hid - EARLY
+    gate_sum, down_sum, d_h, d_attn, ffn_gains, up_over, up_own, *up_parts, ffn_terms = call(
+        functools.partial(sum_ffn_kernel, hid, EARLY),
         "sum_ffn",
         2,
         (
             blocks(gate_terms),
             blocks(down_terms),
-            blocks(down_given),
-            blocks(down_rest),
+            *down_given,
             d_ffn_terms,
             resid,
             gain_rows,
             d_res,
+            ffn_in,
+            d_wide,
+            hidden,
+            blocks(w_down),
         ),
-        [ANY] * 6 + [VMEM, ANY],
-        [((shard, 2 * hid), F32), ((shard, 2 * hid), F32), (row, F32), (rows4, BF16), ((8, dim), F32)],
-        [ANY] * 4 + [VMEM],
-        sum_scratch(width, DOWN_EARLY)
-        + sum_scratch(width, hid - DOWN_EARLY)
-        + sum_scratch(width, DOWN_EARLY)
-        + sum_scratch(width, hid - DOWN_EARLY)
+        [ANY] * 8 + [VMEM] + [ANY] * 5,
+        [((shard, 2 * hid), F32), ((shard, 2 * hid), F32), (row, F32), (rows4, BF16), ((8, dim), F32)]
+        + [((4, width, EARLY), BF16)] * 2
+        + [((2, width, rest), BF16)] * 4
+        + [((4 * SEQ_LEN, dim), F32)],
+        [ANY] * 4 + [VMEM] + [ANY] * 7,
+        sum_scratch(width, EARLY)
+        + given_scratch(width, rest)
+        + sum_scratch(width, EARLY)
+        + sum_scratch(width, rest)
         + quad_scratch(dim)
-        + [vmem(row), vmem(row), vmem(row, BF16)],
-        200,
+        + [vmem(row), vmem(row), vmem(row, BF16)]
+        + [vmem((4 * SEQ_LEN, dim), BF16), vmem((4 * SEQ_LEN, hid), BF16), vmem((2, width, hid), BF16)]
+        + [vmem((4 * SEQ_LEN, hid), BF16), vmem((2, width, hid), BF16), vmem((2, 4 * SEQ_LEN, width))],
+        220,
     )
-    d_attn, d_up, hidden, ffn_in = lax.optimization_barrier((flat(d_attn), d_up, hidden, ffn_in))
-    up_given = over_y(mm(ffn_in[:, half:], d_up[:, :UP_EARLY], TN, BF16))
+    d_attn = flat(d_attn)
+    up_given = [over_y(up_over)] + [ring.send(up_parts[d], ring.stages[0], d) for d in (1, 2, 3)]
     d_proj = mixer_backward(proj, saved, mm(d_attn, w_out))
     d_attn_terms = mm(d_proj, w_in, NT).reshape(rows4)
-    up_terms = mm(ffn_in[:, :half], d_up[:, :UP_EARLY], TN, BF16)
-    up_rest = mm(ffn_in, d_up[:, UP_EARLY:], TN, BF16)
-    ffn_terms = mm(hidden, w_down, NT).reshape(rows4)
+    ffn_terms = ffn_terms.reshape(rows4)
     tail = width // 2
     up_sum, out_sum, q_sum, k_sum, v_sum, f_sum, input_grad, block_out, gain_sums = call(
-        functools.partial(sum_last_kernel, hid, UP_EARLY),
+        functools.partial(sum_last_kernel, hid, EARLY),
         "sum_last",
         3,
         (
-            blocks(up_terms),
-            blocks(up_given),
-            blocks(up_rest),
+            up_own,
+            up_given[0],
+            up_parts[0],
+            *up_given[1:],
             blocks(mm(d_attn, mixed, TN, BF16)),
             blocks(mm(attn_in, d_proj, TN, BF16)),
             d_attn_terms,
@@ -1354,15 +1562,15 @@
             resid,
             live,
         ),
-        [ANY] * 7 + [VMEM, ANY, VMEM, ANY, ANY, VMEM],
+        [ANY] * 10 + [VMEM, ANY, VMEM, ANY, ANY, VMEM],
         [((shard, 2 * hid), F32)]
         + [((shard, 2 * KDIM), F32)] * 4
         + [((shard, 256), F32), ((2 * SEQ_LEN, dim), F32), ((2 * SEQ_LEN, dim), BF16), ((8, tail), F32)],
         [ANY] * 8 + [VMEM],
-        sum_scratch(width, UP_EARLY)
-        + sum_scratch(width, hid - UP_EARLY)
+        sum_scratch(width, EARLY)
         + sum_scratch(width, KDIM) * 4
         + sum_scratch(width, 128)
+        + given_scratch(width, rest)
         + quad_scratch(dim) * 2
         + [vmem(row, BF16), vmem(row), vmem(row), vmem(row, BF16), vmem((8, dim))]
         + [vmem((depth, 8, width)) for depth in (8, 8, 4, 3, 3)]

time: 717 us -> 686 us (0.957)
  matrix products: 155 us -> 124 us
  Pallas kernels: 506 us -> 481 us
  starting transfers between devices: 3.83 us -> 13.8 us
  waiting for transfers between devices: 15.4 us -> 24.9 us
    dot_general x19 -> x11, matrix products: 155 us -> 124 us  [mm(): lax.dot_general(left, right, dims, preferred_element_type=F32).astype(kind)]
    pallas_call x4, Pallas kernels: 475 us -> 450 us  [call(): pl.pallas_call(kernel, in_specs=specs, out_specs=out_specs, out_shape=[ja...]
    ppermute x4 -> x10, starting transfers between devices: 3.83 us -> 13.8 us  [send(): return lax.ppermute(value, 'dp', self.perm(stride, size, shift % size))]
    ppermute x4 -> x10, waiting for transfers between devices: 15.4 us -> 24.9 us  [send(): return lax.ppermute(value, 'dp', self.perm(stride, size, shift % size))]
    unnamed x79 -> x61, local copies, waits for them, and re-layouts: 14.6 us -> 15.3 us
  transfers between devices with their start and end apart: 4 -> 10, of which waited for: 2 -> 4; matrix products, arithmetic and copies ran while one was open for 13% -> 12% of each run, Pallas kernels for 4% -> 5%
where the time goes in v5:
time: 686 us; the launch traced here: 675 us
  Pallas kernels  481 us (70%)
  matrix products  124 us (18%)
  waiting for transfers between devices  24.9 us (4%)
  local copies, waits for them, and re-layouts  24.5 us (4%)
  starting transfers between devices  13.8 us (2%)
    pallas_call x4, Pallas kernels, call(): pl.pallas_call(kernel, in_specs=specs, out_specs=out_specs, out_shape=[ja...  450 us
    dot_general x11, matrix products, mm(): lax.dot_general(left, right, dims, preferred_element_type=F32).astype(kind)  124 us
    ppermute x10, waiting for transfers between devices, send(): return lax.ppermute(value, 'dp', self.perm(stride, size, shift % size))  24.9 us
    pallas_call x1, Pallas kernels, mixer_backward(): pl.pallas_call(backward_kernel, grid=(rows // SEQ_LEN,), in_specs=IN_SPEC...  18.6 us
    unnamed x61, local copies, waits for them, and re-layouts  15.3 us
    ppermute x10, starting transfers between devices, send(): return lax.ppermute(value, 'dp', self.perm(stride, size, shift % size))  13.8 us
  transfers between devices with their start and end apart: 10, of which 4 were waited for; matrix products, arithmetic and copies ran while one was open for 12% of the time, Pallas kernels for 5%

profile of v5, /device:TPU:0, one launch (start us, length us, event | category | flops | bytes accessed | tf_op | source)
XLA Modules:
  0.0 675.4 jit_solution(14503619895273606578)
XLA Ops:
  8.0 103.7 %gather_first.1 = (bf16[8,256,1664]{2,1,0:T(8,128)(2,1)}, bf16[8,256,512]{2,1,0:T(8,128)(2,1)}, bf16[256,4224]{1,0:T(8,128)(2,1)}, bf16[256,2048]{1,0:T(8,128)(2...) custom-call(bf16[512,2048]{1,0:T(8,128)(2,1)} %tokens.1, ...), custom_call_target="tpu_custom_call" | custom-call | tf_op jit(solution)/shard_map/gather_first/pallas_call | solution.py:1122
  111.7 1.4 collective-permute-start.1
  113.5 13.3 %fusion.5.q_ref.k_ref.v_ref.f_ref = f32[1024,1664]{1,0:T(8,128)} fusion(bf16[1024,2048]{1,0:T(8,128)(2,1)} %bitcast.76, bf16[2048,1664]{1,0:T(8,128)(2,1)} %bitcast.72), kind=kOutput, calls=%fused_computation.21 | convolution fusion | flops 6979321856 | bytes 17825792 | tf_op jit(solution)/shard_map/dot_general | solution.py:1241
  126.8 12.8 %mixer_forward.1 = (bf16[1024,512]{1,0:T(8,128)(2,1)S(1)}, f32[1024,128]{1,0:T(8,128)S(1)}, f32[1024,128]{1,0:T(8,128)S(1)}, f32[1024,256]{1,0:T(8,128)S(1)}, f32[1024,256]{1,0:T(8,128)S(1)}) custom-call(f32[1024,1664]{1,0:T(8,128)} %fusion.5.q_ref.k_ref.v_ref.f_ref, f32[1024,1664]{1,0:T(8,128)} %fusion.5.q_ref.k_ref.v_ref.f_ref, ...), custom_call_target="tpu_custom_call" | custom-call | flops 3072000000 | bytes 10240000 | tf_op jit(solution)/shard_map/mixer_forward/pallas_call | solution.py:251
  139.7 5.6 fusion.6.terms
  145.3 14.5 %collective-permute-done.1.b4 = bf16[256,4224]{1,0:T(8,128)(2,1)S(1)} collective-permute-done((bf16[256,4224]{1,0:T(8,128)(2,1)}, bf16[256,4224]{1,0:T(8,128)(2,1)S(1)}, u32[]{:S(2)}, u32[]{:S(2)}) %collective-permute-start.1) | collective-permute-done | bytes 2162720 | tf_op jit(solution)/shard_map/ppermute | solution.py:1157
  159.8 1.4 copy-done.10
  162.1 1.3 copy-done.11
  163.4 123.3 %gather_ffn.1 = (bf16[8,256,2816]{2,1,0:T(8,128)(2,1)}, bf16[8,256,1408]{2,1,0:T(8,128)(2,1)}, f32[256,2048]{1,0:T(8,128)}, bf16[4,256,2048]{2,1,0:T(8,128)(2,1)}) custom-call(bf16[256,4224]{1,0:T(8,128)(2,1)} %get-tuple-element.50.b0, bf16[256,4224]{1,0:T(8,128)(2,1)} %copy-done.11, bf16[256,4224]{1,0:T(8,128)(2,1)} %copy-done.10, ...), custom_call_target="tpu_custom_call" | custom-call | tf_op jit(solution)/shard_map/gather_ffn/pallas_call | solution.py:1122
  286.7 18.9 %fusion.7 = f32[1024,2816]{1,0:T(8,128)} fusion(bf16[1024,2048]{1,0:T(8,128)(2,1)} %bitcast.63, bf16[2048,2816]{1,0:T(8,128)(2,1)} %bitcast.70), kind=kOutput, calls=%fused_computation.23 | convolution fusion | flops 11811160064 | bytes 27262976 | tf_op jit(solution)/shard_map/dot_general | solution.py:1241
  305.6 13.1 %multiply_convert_fusion = (bf16[1024,1408]{1,0:T(8,128)(2,1)S(1)}, bf16[1024,1408]{1,0:T(8,128)(2,1)S(1)}, bf16[1024,1408]{1,0:T(8,128)(2,1)S(1)}) fusion(f32[1024,2816]{1,0:T(8,128)} %fusion.7, bf16[1024,2048]{1,0:T(8,128)(2,1)} %bitcast.80, bf16[2048,1408]{1,0:T(8,128)(2,1)S(1)} %bitcast.61), kind=kOutput, calls=%fused_computation.4 | convolution fusion | flops 5927206912 | bytes 30146560 | tf_op jit(solution)/shard_map/dot_general | solution.py:1241
  318.7 11.5 %convolution_convert_fusion.1 = bf16[2048,1408]{1,0:T(8,128)(2,1)S(1)} fusion(bf16[1024,2048]{1,0:T(8,128)(2,1)} %bitcast.81, bf16[1024,1408]{1,0:T(8,128)(2,1)S(1)} %get-tuple-element.90.hidden), kind=kOutput, calls=%fused_computation.1 | convolution fusion | flops 5908463616 | bytes 12845056 | tf_op jit(solution)/shard_map/dot_general | solution.py:1241
  330.3 1.5 slice.77
  331.9 1.4 pad_maximum_fusion.1
  334.2 1.3 collective-permute-start.4
  336.3 2.5 collective-permute-start.5
  340.0 19.7 %fusion.8.terms = f32[4,256,2048]{2,1,0:T(8,128)} fusion(bf16[4,256,2816]{2,1,0:T(8,128)(2,1)S(1)} %bitcast.56, bf16[2048,2816,1]{1,0,2:T(8,128)(2,1)} %bitcast.71), kind=kOutput, calls=%fused_computation.24 | convolution fusion | flops 11811160064 | bytes 25690112 | tf_op jit(solution)/shard_map/dot_general | solution.py:1241
  359.7 10.5 %convolution_convert_fusion.2 = bf16[2048,1408]{1,0:T(8,128)(2,1)} fusion(bf16[1024,2048]{1,0:T(8,128)(2,1)S(1)} %bitcast.65, bf16[1024,1408]{1,0:T(8,128)(2,1)} %copy-done.9), kind=kOutput, calls=%fused_computation.2 | convolution fusion | flops 5908463616 | bytes 12845056 | tf_op jit(solution)/shard_map/dot_general | solution.py:1241
  371.1 8.6 %collective-permute-done.2 = bf16[1024,896]{1,0:T(8,128)(2,1)} collective-permute-done((bf16[1024,896]{1,0:T(8,128)(2,1)}, bf16[1024,896]{1,0:T(8,128)(2,1)}, u32[]{:S(2)}, u32[]{:S(2)}) %collective-permute-start.2) | collective-permute-done | bytes 1835040 | tf_op jit(solution)/shard_map/ppermute | solution.py:1157
  379.7 100.6 %sum_ffn.1 = (f32[128,2816]{1,0:T(8,128)}, f32[128,2816]{1,0:T(8,128)}, f32[256,2048]{1,0:T(8,128)}, bf16[4,256,2048]{2,1,0:T(8,128)(2,1)}, f32[8,2048]{1,0:T(8,...) custom-call(bf16[8,256,1408]{2,1,0:T(8,128)(2,1)} %bitcast.62, ...), custom_call_target="tpu_custom_call" | custom-call | tf_op jit(solution)/shard_map/sum_ffn/pallas_call | solution.py:1122
  480.3 2.1 collective-permute-start.7
  482.4 2.5 collective-permute-start.8
  484.8 2.8 collective-permute-start.9
  487.7 5.2 fusion.9.d_ref
  492.9 18.6 %mixer_backward.1 = bf16[1024,1664]{1,0:T(8,128)(2,1)} custom-call(f32[1024,1664]{1,0:T(8,128)} %fusion.5.q_ref.k_ref.v_ref.f_ref, f32[1024,1664]{1,0:T(8,128)} %fusion.5.q_ref.k_ref.v_ref.f_ref, f32[1024,1664]{1,0:T(8,128)} %fusion.5.q_ref.k_ref.v_ref.f_ref, f32[1024,1664]{1,0:T(8,128)} %fusion.5.q_ref.k_ref.v_ref.f_ref, ...), custom_call_target="tpu_custom_call" | custom-call | flops 9216000000 | bytes 16384000 | tf_op jit(solution)/shard_map/mixer_backward/pallas_call | solution.py:266
  511.5 11.9 %convolution_convert_fusion = bf16[2048,1664]{1,0:T(8,128)(2,1)} fusion(bf16[1024,2048]{1,0:T(8,128)(2,1)S(1)} %bitcast.77, bf16[1024,1664]{1,0:T(8,128)(2,1)} %mixer_backward.1), kind=kOutput, calls=%fused_computation | convolution fusion | flops 6982729728 | bytes 14417920 | tf_op jit(solution)/shard_map/dot_general | solution.py:1241
  523.5 10.3 %fusion.10.terms = f32[4,256,2048]{2,1,0:T(8,128)} fusion(bf16[4,256,1664]{2,1,0:T(8,128)(2,1)S(1)} %bitcast.66, bf16[2048,1664,1]{1,0,2:T(8,128)(2,1)S(1)} %bitcast.75), kind=kOutput, calls=%fused_computation.26 | convolution fusion | flops 6979321856 | bytes 18612224 | tf_op jit(solution)/shard_map/dot_general | solution.py:1241
  533.8 3.8 convolution_convert_fusion.3
  538.4 122.1 %sum_last.1 = (f32[128,2816]{1,0:T(8,128)}, f32[128,1024]{1,0:T(8,128)}, f32[128,1024]{1,0:T(8,128)}, f32[128,1024]{1,0:T(8,128)}, f32[128,1024]{1,0:T(8,128)}, ...) custom-call(bf16[4,256,896]{2,1,0:T(8,128)(2,1)} %get-tuple-element.63.up, ...), custom_call_target="tpu_custom_call" | custom-call | tf_op jit(solution)/shard_map/sum_last/pallas_call | solution.py:1122
  660.4 1.4 slice_bitcast_fusion
  663.4 3.2 copy.40
  666.6 2.1 copy.41
  (84 shorter events, 19.5 us)
Async XLA Ops:
  111.7 48.1 %collective-permute-start.1 = (bf16[256,4224]{1,0:T(8,128)(2,1)}, bf16[256,4224]{1,0:T(8,128)(2,1)S(1)}, u32[]{:S(2)}, u32[]{:S(2)}) collective-permute-start(bf16[256,4224]{1,0:T(8,128)(2,1)} %get-tuple-element.50.b0), channel_id=1, source_target_pairs={{0,4},{2,6},{4,0},{6,2},{8,12},{10,14},{12,8},{14,10},{16,20},{18,... | collective-permute-start | bytes 6488072 | tf_op jit(solution)/shard_map/ppermute | solution.py:1157
  113.0 49.0 %collective-permute-start = (bf16[256,4224]{1,0:T(8,128)(2,1)}, bf16[256,4224]{1,0:T(8,128)(2,1)S(1)}, u32[]{:S(2)}, u32[]{:S(2)}) collective-permute-start(bf16[256,4224]{1,0:T(8,128)(2,1)} %get-tuple-element.50.b0), channel_id=1, source_target_pairs={{0,8},{2,10},{4,12},{6,14},{8,16},{10,18},{12,20},{14,22},{16,24},... | collective-permute-start | bytes 6488072 | tf_op jit(solution)/shard_map/ppermute | solution.py:1157
  126.8 12.8 %copy-start.23 = (bf16[8,256,512]{2,1,0:T(8,128)(2,1)S(1)}, bf16[8,256,512]{2,1,0:T(8,128)(2,1)}, u32[]{:S(2)}) copy-start(bf16[8,256,512]{2,1,0:T(8,128)(2,1)} %get-tuple-element.54) | copy-start | bytes 6291460
  139.7 5.7 copy-start
  286.7 18.9 %copy-start.4 = (bf16[8,256,1408]{2,1,0:T(8,128)(2,1)S(1)}, bf16[8,256,1408]{2,1,0:T(8,128)(2,1)}, u32[]{:S(2)}) copy-start(bf16[8,256,1408]{2,1,0:T(8,128)(2,1)} %get-tuple-element.59.w_down) | copy-start | bytes 17301508
  318.7 11.5 %copy-start.8 = (bf16[1024,1408]{1,0:T(8,128)(2,1)}, bf16[1024,1408]{1,0:T(8,128)(2,1)S(1)}, u32[]{:S(2)}) copy-start(bf16[1024,1408]{1,0:T(8,128)(2,1)S(1)} %get-tuple-element.90.hidden) | copy-start | bytes 8650756
  318.7 20.8 %copy-start.9 = (bf16[1024,1408]{1,0:T(8,128)(2,1)}, bf16[1024,1408]{1,0:T(8,128)(2,1)S(1)}, u32[]{:S(2)}) copy-start(bf16[1024,1408]{1,0:T(8,128)(2,1)S(1)} %get-tuple-element.89) | copy-start | bytes 8650756
  330.2 3.9 copy-start.3
  333.3 36.9 %collective-permute-start.3 = (bf16[2,256,512]{2,1,0:T(8,128)(2,1)}, bf16[2,256,512]{2,1,0:T(8,128)(2,1)S(1)}, u32[]{:S(2)}, u32[]{:S(2)}) collective-permute-start(bf16[2,256,512]{2,1,0:T(8,128)(2,1)} %pad_maximum_fusion.1), channel_id=1, source_target_pairs={{0,8},{2,10},{4,12},{6,14},{8,16},{10,18},{12,20},{14,22},{16,24},... | collective-permute-start | bytes 1572872 | tf_op jit(solution)/shard_map/ppermute | solution.py:1157
  334.2 36.9 %collective-permute-start.4 = (bf16[2,256,512]{2,1,0:T(8,128)(2,1)}, bf16[2,256,512]{2,1,0:T(8,128)(2,1)}, u32[]{:S(2)}, u32[]{:S(2)}) collective-permute-start(bf16[2,256,512]{2,1,0:T(8,128)(2,1)} %pad_maximum_fusion.2), channel_id=1, source_target_pairs={{0,16},{2,18},{4,20},{6,22},{8,24},{10,26},{12,28},{14,30},{16,0},... | collective-permute-start | bytes 1572872 | tf_op jit(solution)/shard_map/ppermute | solution.py:1157
  336.3 34.8 %collective-permute-start.5 = (bf16[2,256,512]{2,1,0:T(8,128)(2,1)}, bf16[2,256,512]{2,1,0:T(8,128)(2,1)}, u32[]{:S(2)}, u32[]{:S(2)}) collective-permute-start(bf16[2,256,512]{2,1,0:T(8,128)(2,1)} %pad_maximum_fusion.3), channel_id=1, source_target_pairs={{0,24},{2,26},{4,28},{6,30},{8,0},{10,2},{12,4},{14,6},{16,8},{18,... | collective-permute-start | bytes 1572872 | tf_op jit(solution)/shard_map/ppermute | solution.py:1157
  338.8 40.9 %collective-permute-start.2 = (bf16[1024,896]{1,0:T(8,128)(2,1)}, bf16[1024,896]{1,0:T(8,128)(2,1)}, u32[]{:S(2)}, u32[]{:S(2)}) collective-permute-start(bf16[1024,896]{1,0:T(8,128)(2,1)} %slice.77), channel_id=1, source_target_pairs={{0,4},{2,6},{4,0},{6,2},{8,12},{10,14},{12,8},{14,10},{16,20},{18,... | collective-permute-start | bytes 5505032 | tf_op jit(solution)/shard_map/ppermute | solution.py:1157
  340.0 19.8 %copy-start.2 = (bf16[1024,2816]{1,0:T(8,128)(2,1)}, bf16[1024,2816]{1,0:T(8,128)(2,1)S(1)}, u32[]{:S(2)}) copy-start(bf16[1024,2816]{1,0:T(8,128)(2,1)S(1)} %pad_maximum_fusion.d_wide) | copy-start | bytes 17301508
  340.0 19.8 %copy-start.6 = (bf16[4,256,2048]{2,1,0:T(8,128)(2,1)S(1)}, bf16[4,256,2048]{2,1,0:T(8,128)(2,1)}, u32[]{:S(2)}) copy-start(bf16[4,256,2048]{2,1,0:T(8,128)(2,1)} %get-tuple-element.57) | copy-start | bytes 12582916
  370.2 9.5 %copy-start.16 = (bf16[2,256,512]{2,1,0:T(8,128)(2,1)}, bf16[2,256,512]{2,1,0:T(8,128)(2,1)S(1)}, u32[]{:S(2)}) copy-start(bf16[2,256,512]{2,1,0:T(8,128)(2,1)S(1)} %collective-permute-done.3.given1) | copy-start | bytes 1572868
  480.3 57.3 %collective-permute-start.7 = (bf16[2,256,512]{2,1,0:T(8,128)(2,1)}, bf16[2,256,512]{2,1,0:T(8,128)(2,1)S(1)}, u32[]{:S(2)}, u32[]{:S(2)}) collective-permute-start(bf16[2,256,512]{2,1,0:T(8,128)(2,1)} %get-tuple-element.66), channel_id=1, source_target_pairs={{0,8},{2,10},{4,12},{6,14},{8,16},{10,18},{12,20},{14,22},{16,24},... | collective-permute-start | bytes 1572872 | tf_op jit(solution)/shard_map/ppermute | solution.py:1157
  482.4 55.2 %collective-permute-start.8 = (bf16[2,256,512]{2,1,0:T(8,128)(2,1)}, bf16[2,256,512]{2,1,0:T(8,128)(2,1)}, u32[]{:S(2)}, u32[]{:S(2)}) collective-permute-start(bf16[2,256,512]{2,1,0:T(8,128)(2,1)} %get-tuple-element.67), channel_id=1, source_target_pairs={{0,16},{2,18},{4,20},{6,22},{8,24},{10,26},{12,28},{14,30},{16,0},... | collective-permute-start | bytes 1572872 | tf_op jit(solution)/shard_map/ppermute | solution.py:1157
  484.8 52.7 %collective-permute-start.9 = (bf16[2,256,512]{2,1,0:T(8,128)(2,1)}, bf16[2,256,512]{2,1,0:T(8,128)(2,1)}, u32[]{:S(2)}, u32[]{:S(2)}) collective-permute-start(bf16[2,256,512]{2,1,0:T(8,128)(2,1)} %get-tuple-element.68), channel_id=1, source_target_pairs={{0,24},{2,26},{4,28},{6,30},{8,0},{10,2},{12,4},{14,6},{16,8},{18,... | collective-permute-start | bytes 1572872 | tf_op jit(solution)/shard_map/ppermute | solution.py:1157
  487.7 49.9 %collective-permute-start.6 = (bf16[4,256,896]{2,1,0:T(8,128)(2,1)}, bf16[4,256,896]{2,1,0:T(8,128)(2,1)}, u32[]{:S(2)}, u32[]{:S(2)}) collective-permute-start(bf16[4,256,896]{2,1,0:T(8,128)(2,1)} %get-tuple-element.64), channel_id=1, source_target_pairs={{0,4},{2,6},{4,0},{6,2},{8,12},{10,14},{12,8},{14,10},{16,20},{18,... | collective-permute-start | bytes 5505032 | tf_op jit(solution)/shard_map/ppermute | solution.py:1157
  492.9 18.6 %copy-start.21 = (bf16[4,256,2048]{2,1,0:T(8,128)(2,1)S(1)}, bf16[4,256,2048]{2,1,0:T(8,128)(2,1)}, u32[]{:S(2)}) copy-start(bf16[4,256,2048]{2,1,0:T(8,128)(2,1)} %get-tuple-element.51) | copy-start | bytes 12582916
  492.9 30.6 %slice-start = ((s8[6815744]{0:T(1024)(128)(4,1)}), s8[2621440]{0:T(1024)(128)(4,1)S(1)}, s32[]{:S(2)}) async-start(s8[6815744]{0:T(1024)(128)(4,1)} %bitcast.73), calls=%async_computation | async-start | bytes 5242880
  511.5 12.0 %copy-start.7 = (bf16[1024,1664]{1,0:T(8,128)(2,1)S(1)}, bf16[1024,1664]{1,0:T(8,128)(2,1)}, u32[]{:S(2)}) copy-start(bf16[1024,1664]{1,0:T(8,128)(2,1)} %mixer_backward.1) | copy-start | bytes 10223620
  511.5 11.9 %slice-start.1 = ((s8[6815744]{0:T(1024)(128)(4,1)}), s8[4194304]{0:T(1024)(128)(4,1)S(1)}, s32[]{:S(2)}) async-start(s8[6815744]{0:T(1024)(128)(4,1)} %bitcast.73), calls=%async_computation.1 | async-start | bytes 8388608
  523.5 10.3 %copy-start.1 = (bf16[1024,512]{1,0:T(8,128)(2,1)S(1)}, bf16[1024,512]{1,0:T(8,128)(2,1)}, u32[]{:S(2)}) copy-start(bf16[1024,512]{1,0:T(8,128)(2,1)} %copy-done) | copy-start | bytes 3145732
  523.5 10.3 %copy-start.22 = (bf16[4,256,2048]{2,1,0:T(8,128)(2,1)S(1)}, bf16[4,256,2048]{2,1,0:T(8,128)(2,1)}, u32[]{:S(2)}) copy-start(bf16[4,256,2048]{2,1,0:T(8,128)(2,1)} %get-tuple-element.69) | copy-start | bytes 12582916
  660.4 6.1 copy-start.5
  666.6 2.9 copy-start.19
  666.6 3.7 copy-start.18
  666.6 4.5 copy-start.17
  668.7 3.2 copy-start.13
  668.7 4.3 copy-start.14
  670.3 3.8 copy-start.12
  (4 other events, 5.6 us)

commit v6 on v5

--- a/solution.py
+++ b/solution.py
@@ -363,12 +363,11 @@
 
 
 class Quad:
-    def __init__(self, place, sems, source, target):
-        near = [pltpu.make_async_copy(source, target.at[0], sems.one())]
-        self.swap = place.copy("x", source, target.at[1], sems.two())
-        self.core = place.copy("core", source, target.at[2], sems.two())
-        self.last = place.copy("core", target.at[1], target.at[3], sems.two())
-        self.near = near
+    def __init__(self, place, sems, source, slots):
+        self.near = [] if slots[0] is None else [pltpu.make_async_copy(source, slots[0], sems.one())]
+        self.swap = place.copy("x", source, slots[1], sems.two())
+        self.core = place.copy("core", source, slots[2], sems.two())
+        self.last = place.copy("core", slots[1], slots[3], sems.two())
 
     def start(self):
         self.swap.start()
@@ -503,7 +502,7 @@
             pltpu.make_async_copy(cot.at[mine, place.columns(index, width)], grads.at[:, cols], sems.one())
         )
     last = place.copy("core", seqs.at[1], seqs.at[3], sems.two())
-    quad = Quad(place, sems, low, d_ffn)
+    quad = Quad(place, sems, low, [d_ffn.at[i] for i in range(4)])
     save_own = pltpu.make_async_copy(seqs.at[0], own, sems.one())
     save_res = pltpu.make_async_copy(grads, d_res, sems.one())
     save_in = [pltpu.make_async_copy(normed.at[i], attn_in.at[i], sems.one()) for i in range(4)]
@@ -607,104 +606,193 @@
     quad.finish()
 
 
+class WideMatmul:
+    def __init__(self, sems, acts, weight, stage, bufs, lows, wide, hidden):
+        self.acts, self.weight, self.stage, self.bufs, self.lows = acts, weight, stage, bufs, lows
+        self.wide, self.hidden = wide, hidden
+        self.hid = hidden.shape[1]
+        self.count = self.hid // 128
+        self.loads = [sems.some(2) for _ in range(2)]
+        self.stores = [sems.some(2) for _ in range(3)]
+
+    def columns(self, i, side):
+        return pl.ds(pl.multiple_of(side * self.hid + i * 128, 128), 128)
+
+    def fetch(self, i):
+        return [
+            pltpu.make_async_copy(
+                self.weight.at[:, self.columns(i, side)],
+                self.stage.at[i % 2, :, pl.ds(side * 128, 128)],
+                self.loads[side](i % 2),
+            )
+            for side in range(2)
+        ]
+
+    def leave(self, i):
+        copies = [
+            pltpu.make_async_copy(
+                self.bufs.at[i % 2, :, pl.ds(side * 128, 128)],
+                self.wide.at[:, self.columns(i, side)],
+                self.stores[side](i % 2),
+            )
+            for side in range(2)
+        ]
+        return copies + [
+            pltpu.make_async_copy(self.lows.at[i % 2], self.hidden.at[:, self.columns(i, 0)], self.stores[2](i % 2))
+        ]
+
+    def begin(self):
+        for copy in self.fetch(0):
+            copy.start()
+
+    def run(self, start, stop):
+        def step(i, carry):
+            for copy in self.fetch(i):
+                copy.wait()
+
+            @pl.when(i + 1 < self.count)
+            def _():
+                for copy in self.fetch(i + 1):
+                    copy.start()
+
+            @pl.when(i >= 2)
+            def _():
+                for copy in self.leave(i):
+                    copy.wait()
+
+            both = mm(self.acts[...], self.stage[i % 2])
+            gate = both[:, :128]
+            self.bufs[i % 2] = both
+            self.lows[i % 2] = (gate / (1.0 + jnp.exp(-gate)) * both[:, 128:]).astype(BF16)
+            for copy in self.leave(i):
+                copy.start()
+            return carry
+
+        lax.fori_loop(start, stop, step, 0)
+
+    def finish(self):
+        for i in (self.count - 2, self.count - 1):
+            for copy in self.leave(i):
+                copy.wait()
+
+
 def gather_ffn_kernel(
-    hid, cut, b0, b3, b4, terms, tokens, gains, w_wide, w_down, resid, ffn_in, s0, s1, s2, s3, kept, normed, inputs, stage, sem
+    hid, cut, b0, b3, b4, terms, tokens, gains, w_wide, w_down, resid, ffn_in, wide, hidden,
+    s0, s1, s2, s3, kept, acts, inputs, stage, tiles, bufs, lows, sem
 ):
     place, sems = Place(), Sems(sem)
-    chunks = [
-        (0, hid, w_wide, 0, False),
-        (hid, hid, w_wide, hid, False),
-        (2 * hid, cut, w_down, 0, False),
-        (2 * hid + cut, hid - cut, w_down, cut, True),
-    ]
-    keeps, rises, crosses = [], [], []
-    for first, width, target, start, y_first in chunks:
-        cols, source = pl.ds(start, width), pl.ds(first, width)
-
-        def block(index, target=target, cols=cols):
-            return target.at[index, :, cols]
-
-        keeps += [
-            Keep(sems, b.at[:, source], block(i), stage.at[at, :, source])
-            for at, (b, i) in enumerate(((b0, 0), (b3, 3), (b4, 4)))
+    rows = b0.shape[0]
+    keeps = []
+
+    def block(target, index, start, width):
+        return target.at[pl.ds(index * rows, rows), pl.ds(start, width)]
+
+    def chunk(first, width, target, start, y_first):
+        source = pl.ds(first, width)
+        at = lambda index: block(target, index, start, width)
+        for i, (b, index) in enumerate(((b0, 0), (b3, 3), (b4, 4))):
+            keeps.append(Keep(sems, b.at[:, source], at(index), stage.at[i, :, source]))
+        low = [
+            place.copy("up", b3.at[:, source], at(2), sems.two()),
+            place.copy("up", at(2), at(1), sems.two()),
         ]
-        lower = [
-            place.copy("up", b3.at[:, source], block(2), sems.two()),
-            place.copy("up", block(2), block(1), sems.two()),
-        ]
-        high = []
         if y_first:
-            high = [
-                place.copy("up", b4.at[:, source], block(7), sems.two()),
-                place.copy("up", block(7), block(6), sems.two()),
-                place.copy("up", block(6), block(5), sems.two()),
-            ]
-            crosses.append([])
-        else:
-            crosses.append(
+            return (
+                low,
                 [
-                    place.copy("y", b3.at[:, source], block(7), sems.two()),
-                    place.copy("y", block(2), block(6), sems.two()),
-                    place.copy("y", block(1), block(5), sems.two()),
-                ]
+                    place.copy("up", b4.at[:, source], at(7), sems.two()),
+                    place.copy("up", at(7), at(6), sems.two()),
+                    place.copy("up", at(6), at(5), sems.two()),
+                ],
+                [],
             )
-        rises.append((lower, high))
+        return (
+            low,
+            [],
+            [
+                place.copy("y", b3.at[:, source], at(7), sems.two()),
+                place.copy("y", at(2), at(6), sems.two()),
+                place.copy("y", at(1), at(5), sems.two()),
+            ],
+        )
+
+    gate = chunk(0, hid, w_wide, 0, False)
+    up = chunk(hid, hid, w_wide, hid, False)
+    down = chunk(2 * hid, cut, w_down, 0, False)
+    rest = chunk(2 * hid + cut, hid - cut, w_down, cut, True)
     total = QuadSum(place, sems, terms, (s0, s1, s2, s3))
-    out = Quad(place, sems, normed, ffn_in)
+    slots = [acts.at[pl.ds(i * SEQ_LEN, SEQ_LEN)] for i in range(4)]
+    out = Quad(place, sems, slots[0], [None] + slots[1:])
     fetch = pltpu.make_async_copy(tokens, inputs, sems.one())
     save = pltpu.make_async_copy(kept, resid, sems.one())
+    save_in = pltpu.make_async_copy(acts, ffn_in, sems.one())
+    matmul = WideMatmul(sems, acts, w_wide, tiles, bufs, lows, wide, hidden)
     place.greet()
     total.start()
     fetch.start()
-    for (lower, high), cross in zip(rises, crosses):
-        lower[0].start()
-        for copy in high[:1] + cross[:1]:
-            copy.start()
+    for low, _, cross in (gate, up):
+        low[0].start()
+        cross[0].start()
     for copy in keeps:
         copy.start()
     total.middle()
     for copy in keeps:
         copy.turn()
     fetch.wait()
-    for c, ((lower, high), cross) in enumerate(zip(rises, crosses)):
-        if c == 2:
-            total.ready()
-
-            def norm(part):
-                value = total.read(part) + inputs[part].astype(F32)
-                kept[part] = value
-                normed[part] = (value * rms(value) * gains[1:2, :]).astype(BF16)
-
-            pieces(SEQ_LEN, norm)
-            out.start()
-            save.start()
-        lower[0].wait_recv()
-        lower[1].start()
-        for copy in cross[1:2]:
-            copy.start()
-        if high:
-            high[0].wait_recv()
-            high[1].start()
-    for c, ((lower, high), cross) in enumerate(zip(rises, crosses)):
-        lower[1].wait_recv()
-        for copy in cross[2:]:
-            copy.start()
-        if high:
-            high[1].wait_recv()
-            high[2].start()
-        if c == 1:
-            out.forward()
-    for (lower, high), cross in zip(rises, crosses):
-        for copy in cross:
-            copy.wait()
-        for copy in high[2:]:
-            copy.wait_recv()
-        for copy in lower + high:
+    for low, _, cross in (gate, up):
+        low[0].wait_recv()
+        low[1].start()
+        cross[1].start()
+    rest[1][0].start()
+    down[0][0].start()
+    rest[0][0].start()
+    total.ready()
+
+    def norm(part):
+        value = total.read(part) + inputs[part].astype(F32)
+        kept[part] = value
+        acts[part] = (value * rms(value) * gains[1:2, :]).astype(BF16)
+
+    pieces(SEQ_LEN, norm)
+    out.start()
+    save.start()
+    for low, _, cross in (gate, up):
+        low[1].wait_recv()
+        cross[2].start()
+    down[2][0].start()
+    rest[1][0].wait_recv()
+    rest[1][1].start()
+    out.forward()
+    down[0][0].wait_recv()
+    down[0][1].start()
+    down[2][1].start()
+    rest[0][0].wait_recv()
+    rest[0][1].start()
+    out.finish()
+    save_in.start()
+    for copy in keeps[:6]:
+        copy.wait()
+    for copy in gate[2] + up[2]:
+        copy.wait_recv()
+    matmul.begin()
+    rest[1][1].wait_recv()
+    rest[1][2].start()
+    matmul.run(0, 4)
+    down[0][1].wait_recv()
+    down[2][2].start()
+    matmul.run(4, matmul.count)
+    for copy in down[2]:
+        copy.wait_recv()
+    rest[0][1].wait_recv()
+    rest[1][2].wait_recv()
+    for low, high, cross in (gate, up, down, rest):
+        for copy in low + high + cross:
             copy.wait_send()
-    for copy in keeps:
+    for copy in keeps[6:]:
         copy.wait()
-    out.finish()
+    matmul.finish()
     save.wait()
+    save_in.wait()
 
 
 class Sum:
@@ -941,7 +1029,7 @@
     ]
     back = QuadSum(place, sems, terms, scratch[20:24])
     value, res, low, acts, ups, up_bufs, hid_v, stage, out_bufs = scratch[24:33]
-    quad = Quad(place, sems, low, d_attn)
+    quad = Quad(place, sems, low, [d_attn.at[i] for i in range(4)])
     up = UpTerms(sems, acts, ups, up_bufs, up_over, up_own, (up0, up1, up2, up3))
     out = OutTerms(sems, hid_v, w_down, stage, out_bufs, out_terms)
     ready = [
@@ -1471,18 +1559,27 @@
     mixed, *saved = mixer_forward(proj)
     attn_terms = mm(mixed, w_out, NT).reshape(rows4)
     cut = hid // 256 * 128 + 128
-    w_wide, w_down, resid, ffn_in = call(
+    tokens4 = 4 * SEQ_LEN
+    w_wide, w_down, resid, ffn_in, wide, hidden = call(
         functools.partial(gather_ffn_kernel, hid, cut),
         "gather_ffn",
         1,
         (part0, part3, part4, attn_terms, own, gain_rows),
         [ANY] * 5 + [VMEM],
-        [((8, width, 2 * hid), BF16), ((8, width, hid), BF16), (row, F32), (rows4, BF16)],
-        [ANY] * 4,
-        quad_scratch(dim) + [vmem(row), vmem(row, BF16), vmem(row, BF16), vmem((3, width, 3 * hid), BF16)],
+        [
+            ((dim, 2 * hid), BF16),
+            ((dim, hid), BF16),
+            (row, F32),
+            ((tokens4, dim), BF16),
+            ((tokens4, 2 * hid), F32),
+            ((tokens4, hid), BF16),
+        ],
+        [ANY] * 6,
+        quad_scratch(dim)
+        + [vmem(row), vmem((tokens4, dim), BF16), vmem(row, BF16), vmem((3, width, 3 * hid), BF16)]
+        + [vmem((2, dim, 256), BF16), vmem((2, tokens4, 256)), vmem((2, tokens4, 128), BF16)],
         160,
     )
-    w_wide, w_down, ffn_in = map(flat, (w_wide, w_down, ffn_in))
 
     def early_terms(terms, start):
         over = over_y(terms[half:, start : start + EARLY])
@@ -1490,10 +1587,8 @@
         given = [ring.send(jnp.stack([rest[d], rest[4 + d]]), ring.stages[0], d) for d in (1, 2, 3)]
         return [blocks(over), *given]
 
-    wide = mm(ffn_in, w_wide)
     gate, up_vals = wide[:, :hid], wide[:, hid:]
     sig = jax.nn.sigmoid(gate)
-    hidden = (gate * sig * up_vals).astype(BF16)
     down_terms = mm(d_ffn, hidden, TN, BF16)
     down_given = early_terms(down_terms, 0)
     d_hidden = mm(d_ffn, w_down)

time: 686 us -> 652 us (0.950)
  matrix products: 124 us -> 101 us
  waiting for transfers between devices: 24.9 us -> 15.5 us
    dot_general x11 -> x10, matrix products: 124 us -> 101 us  [mm(): lax.dot_general(left, right, dims, preferred_element_type=F32).astype(kind)]
    ppermute x10, waiting for transfers between devices: 24.9 us -> 15.5 us  [send(): return lax.ppermute(value, 'dp', self.perm(stride, size, shift % size))]
  transfers between devices with their start and end apart: 10 -> 10, of which waited for: 4 -> 2; matrix products, arithmetic and copies ran while one was open for 12% -> 15% of each run, Pallas kernels for 5% -> 5%
where the time goes in v6:
time: 652 us; the launch traced here: 642 us
  Pallas kernels  481 us (74%)
  matrix products  101 us (15%)
  local copies, waits for them, and re-layouts  26.3 us (4%)
  waiting for transfers between devices  15.5 us (2%)
  starting transfers between devices  9.65 us (1%)
    pallas_call x4, Pallas kernels, call(): pl.pallas_call(kernel, in_specs=specs, out_specs=out_specs, out_shape=[ja...  450 us
    dot_general x10, matrix products, mm(): lax.dot_general(left, right, dims, preferred_element_type=F32).astype(kind)  101 us
    pallas_call x1, Pallas kernels, mixer_backward(): pl.pallas_call(backward_kernel, grid=(rows // SEQ_LEN,), in_specs=IN_SPEC...  18.4 us
    unnamed x61, local copies, waits for them, and re-layouts  17.2 us
    ppermute x10, waiting for transfers between devices, send(): return lax.ppermute(value, 'dp', self.perm(stride, size, shift % size))  15.5 us
  transfers between devices with their start and end apart: 10, of which 2 were waited for; matrix products, arithmetic and copies ran while one was open for 15% of the time, Pallas kernels for 5%

profile of v6, /device:TPU:0, one launch (start us, length us, event | category | flops | bytes accessed | tf_op | source)
XLA Modules:
  0.0 642.4 jit_solution(15243203218347381058)
XLA Ops:
  1.3 1.3 fusion.4
  8.0 103.7 %gather_first.1 = (bf16[8,256,1664]{2,1,0:T(8,128)(2,1)}, bf16[8,256,512]{2,1,0:T(8,128)(2,1)}, bf16[256,4224]{1,0:T(8,128)(2,1)}, bf16[256,2048]{1,0:T(8,128)(2...) custom-call(bf16[512,2048]{1,0:T(8,128)(2,1)} %tokens.1, ...), custom_call_target="tpu_custom_call" | custom-call | tf_op jit(solution)/shard_map/gather_first/pallas_call | solution.py:1210
  111.7 1.4 collective-permute-start.1
  113.5 13.3 %fusion.5.q_ref.k_ref.v_ref.f_ref = f32[1024,1664]{1,0:T(8,128)} fusion(bf16[1024,2048]{1,0:T(8,128)(2,1)} %bitcast.66, bf16[2048,1664]{1,0:T(8,128)(2,1)} %bitcast.62), kind=kOutput, calls=%fused_computation.20 | convolution fusion | flops 6979321856 | bytes 17825792 | tf_op jit(solution)/shard_map/dot_general | solution.py:1329
  126.8 12.8 %mixer_forward.1 = (bf16[1024,512]{1,0:T(8,128)(2,1)S(1)}, f32[1024,128]{1,0:T(8,128)S(1)}, f32[1024,128]{1,0:T(8,128)S(1)}, f32[1024,256]{1,0:T(8,128)S(1)}, f32[1024,256]{1,0:T(8,128)S(1)}) custom-call(f32[1024,1664]{1,0:T(8,128)} %fusion.5.q_ref.k_ref.v_ref.f_ref, f32[1024,1664]{1,0:T(8,128)} %fusion.5.q_ref.k_ref.v_ref.f_ref, ...), custom_call_target="tpu_custom_call" | custom-call | flops 3072000000 | bytes 10240000 | tf_op jit(solution)/shard_map/mixer_forward/pallas_call | solution.py:251
  139.7 5.6 fusion.6.terms
  145.3 14.6 %collective-permute-done.1.b4 = bf16[256,4224]{1,0:T(8,128)(2,1)S(1)} collective-permute-done((bf16[256,4224]{1,0:T(8,128)(2,1)}, bf16[256,4224]{1,0:T(8,128)(2,1)S(1)}, u32[]{:S(2)}, u32[]{:S(2)}) %collective-permute-start.1) | collective-permute-done | bytes 2162720 | tf_op jit(solution)/shard_map/ppermute | solution.py:1245
  159.8 1.4 copy-done.7
  162.1 1.3 copy-done.8
  163.4 123.3 %gather_ffn.1 = (bf16[2048,2816]{1,0:T(8,128)(2,1)}, bf16[2048,1408]{1,0:T(8,128)(2,1)}, f32[256,2048]{1,0:T(8,128)}, bf16[1024,2048]{1,0:T(8,128)(2,1)}, f32[10...) custom-call(bf16[256,4224]{1,0:T(8,128)(2,1)} %get-tuple-element.52.b0, bf16[256,4224]{1,0:T(8,128)(2,1)} %copy-done.8, ...), custom_call_target="tpu_custom_call" | custom-call | tf_op jit(solution)/shard_map/gather_ffn/pallas_call | solution.py:1210
  286.8 9.8 %convolution_convert_fusion.1 = bf16[2048,1408]{1,0:T(8,128)(2,1)S(1)} fusion(bf16[1024,2048]{1,0:T(8,128)(2,1)} %bitcast.68, bf16[1024,1408]{1,0:T(8,128)(2,1)} %get-tuple-element.63.hidden), kind=kOutput, calls=%fused_computation.1 | convolution fusion | flops 5908463616 | bytes 12845056 | tf_op jit(solution)/shard_map/dot_general | solution.py:1329
  296.6 1.4 slice.75
  302.0 2.5 collective-permute-start.5
  305.2 12.1 %multiply_convert_fusion = (bf16[1024,1408]{1,0:T(8,128)(2,1)S(1)}, bf16[1024,1408]{1,0:T(8,128)(2,1)}) fusion(f32[1024,2816]{1,0:T(8,128)} %get-tuple-element.62, bf16[1024,2048]{1,0:T(8,128)(2,1)S(1)} %bitcast.69, bf16[2048,1408]{1,0:T(8,128)(2,1)S(1)} %bitcast.56), kind=kOutput, calls=%fused_computation.4 | convolution fusion | flops 5924323328 | bytes 27262976 | tf_op jit(solution)/shard_map/dot_general | solution.py:1329
  317.4 18.0 %fusion = f32[1024,2048]{1,0:T(8,128)} fusion(bf16[2048,2816]{1,0:T(8,128)(2,1)} %get-tuple-element.64, bf16[1024,1408]{1,0:T(8,128)(2,1)S(1)} %get-tuple-element.92, bf16[1024,1408]{1,0:T(8,128)(2,1)} %get-tuple-element.93), kind=kOutput, calls=%fused_computation.15 | convolution fusion | flops 11822694400 | bytes 25690112 | tf_op jit(solution)/shard_map/dot_general | solution.py:1329
  335.3 10.6 %convolution_convert_fusion.2 = bf16[2048,1408]{1,0:T(8,128)(2,1)} fusion(bf16[1024,2048]{1,0:T(8,128)(2,1)S(1)} %copy-done.4, bf16[1024,1408]{1,0:T(8,128)(2,1)} %get-tuple-element.93), kind=kOutput, calls=%fused_computation.2 | convolution fusion | flops 5908463616 | bytes 12845056 | tf_op jit(solution)/shard_map/dot_general | solution.py:1329
  345.9 2.9 pad_maximum_fusion.d_wide
  349.6 100.9 %sum_ffn.1 = (f32[128,2816]{1,0:T(8,128)}, f32[128,2816]{1,0:T(8,128)}, f32[256,2048]{1,0:T(8,128)}, bf16[4,256,2048]{2,1,0:T(8,128)(2,1)}, f32[8,2048]{1,0:T(8,...) custom-call(bf16[8,256,1408]{2,1,0:T(8,128)(2,1)} %bitcast.57, ...), custom_call_target="tpu_custom_call" | custom-call | tf_op jit(solution)/shard_map/sum_ffn/pallas_call | solution.py:1210
  451.1 2.2 collective-permute-start.8
  453.3 1.2 collective-permute-start.9
  454.9 5.2 fusion.7.d_ref
  460.1 18.4 %mixer_backward.1 = bf16[1024,1664]{1,0:T(8,128)(2,1)} custom-call(f32[1024,1664]{1,0:T(8,128)} %fusion.5.q_ref.k_ref.v_ref.f_ref, f32[1024,1664]{1,0:T(8,128)} %fusion.5.q_ref.k_ref.v_ref.f_ref, f32[1024,1664]{1,0:T(8,128)} %fusion.5.q_ref.k_ref.v_ref.f_ref, f32[1024,1664]{1,0:T(8,128)} %fusion.5.q_ref.k_ref.v_ref.f_ref, ...), custom_call_target="tpu_custom_call" | custom-call | flops 9216000000 | bytes 16384000 | tf_op jit(solution)/shard_map/mixer_backward/pallas_call | solution.py:266
  478.5 11.9 %convolution_convert_fusion = bf16[2048,1664]{1,0:T(8,128)(2,1)} fusion(bf16[1024,2048]{1,0:T(8,128)(2,1)S(1)} %bitcast.67, bf16[1024,1664]{1,0:T(8,128)(2,1)} %mixer_backward.1), kind=kOutput, calls=%fused_computation | convolution fusion | flops 6982729728 | bytes 14417920 | tf_op jit(solution)/shard_map/dot_general | solution.py:1329
  490.5 10.3 %fusion.8.terms = f32[4,256,2048]{2,1,0:T(8,128)} fusion(bf16[4,256,1664]{2,1,0:T(8,128)(2,1)S(1)} %bitcast.58, bf16[2048,1664,1]{1,0,2:T(8,128)(2,1)S(1)} %bitcast.65), kind=kOutput, calls=%fused_computation.23 | convolution fusion | flops 6979321856 | bytes 18612224 | tf_op jit(solution)/shard_map/dot_general | solution.py:1329
  500.8 3.8 convolution_convert_fusion.3
  505.4 122.0 %sum_last.1 = (f32[128,2816]{1,0:T(8,128)}, f32[128,1024]{1,0:T(8,128)}, f32[128,1024]{1,0:T(8,128)}, f32[128,1024]{1,0:T(8,128)}, f32[128,1024]{1,0:T(8,128)}, ...) custom-call(bf16[4,256,896]{2,1,0:T(8,128)(2,1)} %get-tuple-element.67.up, ...), custom_call_target="tpu_custom_call" | custom-call | tf_op jit(solution)/shard_map/sum_last/pallas_call | solution.py:1210
  627.4 1.4 slice_bitcast_fusion
  630.4 3.2 copy.40
  633.6 2.1 copy.41
  638.9 1.1 copy.46
  640.0 1.1 copy.47
  641.1 1.1 copy.48
  (84 shorter events, 17.5 us)
Async XLA Ops:
  111.7 48.1 %collective-permute-start.1 = (bf16[256,4224]{1,0:T(8,128)(2,1)}, bf16[256,4224]{1,0:T(8,128)(2,1)S(1)}, u32[]{:S(2)}, u32[]{:S(2)}) collective-permute-start(bf16[256,4224]{1,0:T(8,128)(2,1)} %get-tuple-element.52.b0), channel_id=1, source_target_pairs={{0,4},{2,6},{4,0},{6,2},{8,12},{10,14},{12,8},{14,10},{16,20},{18,... | collective-permute-start | bytes 6488072 | tf_op jit(solution)/shard_map/ppermute | solution.py:1245
  113.0 49.0 %collective-permute-start = (bf16[256,4224]{1,0:T(8,128)(2,1)}, bf16[256,4224]{1,0:T(8,128)(2,1)S(1)}, u32[]{:S(2)}, u32[]{:S(2)}) collective-permute-start(bf16[256,4224]{1,0:T(8,128)(2,1)} %get-tuple-element.52.b0), channel_id=1, source_target_pairs={{0,8},{2,10},{4,12},{6,14},{8,16},{10,18},{12,20},{14,22},{16,24},... | collective-permute-start | bytes 6488072 | tf_op jit(solution)/shard_map/ppermute | solution.py:1245
  126.8 12.8 %copy-start.21 = (bf16[8,256,512]{2,1,0:T(8,128)(2,1)S(1)}, bf16[8,256,512]{2,1,0:T(8,128)(2,1)}, u32[]{:S(2)}) copy-start(bf16[8,256,512]{2,1,0:T(8,128)(2,1)} %get-tuple-element.56) | copy-start | bytes 6291460
  139.6 5.6 copy-start
  286.7 18.5 %slice-start = ((s8[5767168]{0:T(1024)(128)(4,1)}), s8[4194304]{0:T(1024)(128)(4,1)S(1)}, s32[]{:S(2)}) async-start(s8[5767168]{0:T(1024)(128)(4,1)} %bitcast.55), calls=%async_computation | async-start | bytes 8388608
  286.7 18.5 %slice-start.1 = ((s8[5767168]{0:T(1024)(128)(4,1)}), s8[1572864]{0:T(1024)(128)(4,1)S(1)}, s32[]{:S(2)}) async-start(s8[5767168]{0:T(1024)(128)(4,1)} %bitcast.55), calls=%async_computation.1 | async-start | bytes 3145728
  296.6 4.3 copy-start.2
  296.6 8.6 %copy-start.19 = (bf16[4,256,2048]{2,1,0:T(8,128)(2,1)S(1)}, bf16[4,256,2048]{2,1,0:T(8,128)(2,1)}, u32[]{:S(2)}) copy-start(bf16[4,256,2048]{2,1,0:T(8,128)(2,1)} %get-tuple-element.60) | copy-start | bytes 12582916
  299.0 49.9 %collective-permute-start.3 = (bf16[2,256,512]{2,1,0:T(8,128)(2,1)}, bf16[2,256,512]{2,1,0:T(8,128)(2,1)S(1)}, u32[]{:S(2)}, u32[]{:S(2)}) collective-permute-start(bf16[2,256,512]{2,1,0:T(8,128)(2,1)} %pad_maximum_fusion.1), channel_id=1, source_target_pairs={{0,8},{2,10},{4,12},{6,14},{8,16},{10,18},{12,20},{14,22},{16,24},... | collective-permute-start | bytes 1572872 | tf_op jit(solution)/shard_map/ppermute | solution.py:1245
  300.9 47.9 %collective-permute-start.4 = (bf16[2,256,512]{2,1,0:T(8,128)(2,1)}, bf16[2,256,512]{2,1,0:T(8,128)(2,1)}, u32[]{:S(2)}, u32[]{:S(2)}) collective-permute-start(bf16[2,256,512]{2,1,0:T(8,128)(2,1)} %pad_maximum_fusion.2), channel_id=1, source_target_pairs={{0,16},{2,18},{4,20},{6,22},{8,24},{10,26},{12,28},{14,30},{16,0},... | collective-permute-start | bytes 1572872 | tf_op jit(solution)/shard_map/ppermute | solution.py:1245
  302.0 46.9 %collective-permute-start.5 = (bf16[2,256,512]{2,1,0:T(8,128)(2,1)}, bf16[2,256,512]{2,1,0:T(8,128)(2,1)}, u32[]{:S(2)}, u32[]{:S(2)}) collective-permute-start(bf16[2,256,512]{2,1,0:T(8,128)(2,1)} %pad_maximum_fusion.3), channel_id=1, source_target_pairs={{0,24},{2,26},{4,28},{6,30},{8,0},{10,2},{12,4},{14,6},{16,8},{18,... | collective-permute-start | bytes 1572872 | tf_op jit(solution)/shard_map/ppermute | solution.py:1245
  304.5 44.4 %collective-permute-start.2 = (bf16[1024,896]{1,0:T(8,128)(2,1)}, bf16[1024,896]{1,0:T(8,128)(2,1)}, u32[]{:S(2)}, u32[]{:S(2)}) collective-permute-start(bf16[1024,896]{1,0:T(8,128)(2,1)} %slice.75), channel_id=1, source_target_pairs={{0,4},{2,6},{4,0},{6,2},{8,12},{10,14},{12,8},{14,10},{16,20},{18,... | collective-permute-start | bytes 5505032 | tf_op jit(solution)/shard_map/ppermute | solution.py:1245
  317.4 18.0 %copy-start.4 = (bf16[1024,2048]{1,0:T(8,128)(2,1)S(1)}, bf16[1024,2048]{1,0:T(8,128)(2,1)}, u32[]{:S(2)}) copy-start(bf16[1024,2048]{1,0:T(8,128)(2,1)} %get-tuple-element.59.ffn_in) | copy-start | bytes 12582916
  335.3 10.6 %copy-start.6 = (bf16[1024,1408]{1,0:T(8,128)(2,1)S(1)}, bf16[1024,1408]{1,0:T(8,128)(2,1)}, u32[]{:S(2)}) copy-start(bf16[1024,1408]{1,0:T(8,128)(2,1)} %get-tuple-element.93) | copy-start | bytes 8650756
  450.6 54.0 %collective-permute-start.7 = (bf16[2,256,512]{2,1,0:T(8,128)(2,1)}, bf16[2,256,512]{2,1,0:T(8,128)(2,1)S(1)}, u32[]{:S(2)}, u32[]{:S(2)}) collective-permute-start(bf16[2,256,512]{2,1,0:T(8,128)(2,1)} %get-tuple-element.70), channel_id=1, source_target_pairs={{0,8},{2,10},{4,12},{6,14},{8,16},{10,18},{12,20},{14,22},{16,24},... | collective-permute-start | bytes 1572872 | tf_op jit(solution)/shard_map/ppermute | solution.py:1245
  451.1 53.5 %collective-permute-start.8 = (bf16[2,256,512]{2,1,0:T(8,128)(2,1)}, bf16[2,256,512]{2,1,0:T(8,128)(2,1)}, u32[]{:S(2)}, u32[]{:S(2)}) collective-permute-start(bf16[2,256,512]{2,1,0:T(8,128)(2,1)} %get-tuple-element.71), channel_id=1, source_target_pairs={{0,16},{2,18},{4,20},{6,22},{8,24},{10,26},{12,28},{14,30},{16,0},... | collective-permute-start | bytes 1572872 | tf_op jit(solution)/shard_map/ppermute | solution.py:1245
  453.3 51.3 %collective-permute-start.9 = (bf16[2,256,512]{2,1,0:T(8,128)(2,1)}, bf16[2,256,512]{2,1,0:T(8,128)(2,1)}, u32[]{:S(2)}, u32[]{:S(2)}) collective-permute-start(bf16[2,256,512]{2,1,0:T(8,128)(2,1)} %get-tuple-element.72), channel_id=1, source_target_pairs={{0,24},{2,26},{4,28},{6,30},{8,0},{10,2},{12,4},{14,6},{16,8},{18,... | collective-permute-start | bytes 1572872 | tf_op jit(solution)/shard_map/ppermute | solution.py:1245
  454.4 50.2 %collective-permute-start.6 = (bf16[4,256,896]{2,1,0:T(8,128)(2,1)}, bf16[4,256,896]{2,1,0:T(8,128)(2,1)}, u32[]{:S(2)}, u32[]{:S(2)}) collective-permute-start(bf16[4,256,896]{2,1,0:T(8,128)(2,1)} %get-tuple-element.68), channel_id=1, source_target_pairs={{0,4},{2,6},{4,0},{6,2},{8,12},{10,14},{12,8},{14,10},{16,20},{18,... | collective-permute-start | bytes 5505032 | tf_op jit(solution)/shard_map/ppermute | solution.py:1245
  460.1 18.5 %copy-start.18 = (bf16[4,256,2048]{2,1,0:T(8,128)(2,1)S(1)}, bf16[4,256,2048]{2,1,0:T(8,128)(2,1)}, u32[]{:S(2)}) copy-start(bf16[4,256,2048]{2,1,0:T(8,128)(2,1)} %get-tuple-element.53) | copy-start | bytes 12582916
  460.1 30.4 %slice-start.2 = ((s8[6815744]{0:T(1024)(128)(4,1)}), s8[2621440]{0:T(1024)(128)(4,1)S(1)}, s32[]{:S(2)}) async-start(s8[6815744]{0:T(1024)(128)(4,1)} %bitcast.63), calls=%async_computation.2 | async-start | bytes 5242880
  478.5 12.0 %copy-start.5 = (bf16[1024,1664]{1,0:T(8,128)(2,1)S(1)}, bf16[1024,1664]{1,0:T(8,128)(2,1)}, u32[]{:S(2)}) copy-start(bf16[1024,1664]{1,0:T(8,128)(2,1)} %mixer_backward.1) | copy-start | bytes 10223620
  478.5 12.0 %slice-start.3 = ((s8[6815744]{0:T(1024)(128)(4,1)}), s8[4194304]{0:T(1024)(128)(4,1)S(1)}, s32[]{:S(2)}) async-start(s8[6815744]{0:T(1024)(128)(4,1)} %bitcast.63), calls=%async_computation.3 | async-start | bytes 8388608
  490.5 10.3 %copy-start.1 = (bf16[1024,512]{1,0:T(8,128)(2,1)S(1)}, bf16[1024,512]{1,0:T(8,128)(2,1)}, u32[]{:S(2)}) copy-start(bf16[1024,512]{1,0:T(8,128)(2,1)} %copy-done) | copy-start | bytes 3145732
  490.5 10.3 %copy-start.20 = (bf16[4,256,2048]{2,1,0:T(8,128)(2,1)S(1)}, bf16[4,256,2048]{2,1,0:T(8,128)(2,1)}, u32[]{:S(2)}) copy-start(bf16[4,256,2048]{2,1,0:T(8,128)(2,1)} %get-tuple-element.73) | copy-start | bytes 12582916
  627.4 6.1 copy-start.3
  633.6 2.1 copy-start.17
  633.6 2.9 copy-start.16
  633.6 3.7 copy-start.15
  633.6 4.5 copy-start.14
  635.7 3.2 copy-start.10
  635.7 4.3 copy-start.11
  637.3 3.8 copy-start.9
  (4 other events, 4.3 us)

commit v7 on v6

--- a/solution.py
+++ b/solution.py
@@ -278,12 +278,13 @@
 MESH = pl.DeviceIdType.MESH
 ANY = pl.BlockSpec(memory_space=pl.ANY)
 VMEM = pl.BlockSpec(memory_space=pltpu.VMEM)
+SMEM = pl.BlockSpec(memory_space=pltpu.SMEM)
 DMA = pltpu.SemaphoreType.DMA
 PIECE = 32
 
 
 class Place:
-    def __init__(self):
+    def __init__(self, all_z=False):
         dp = lax.axis_index("dp")
         self.core = lax.axis_index("head")
         self.x, self.y, self.z = dp % 2, dp // 2 % 2, dp // 4
@@ -295,6 +296,8 @@
             "down": ((self.z + 3) % 4 * 4 + rest, self.core),
             "core": (dp, 1 - self.core),
         }
+        if all_z:
+            self.peers["two"] = ((self.z + 2) % 4 * 4 + rest, self.core)
 
     def greet(self):
         ready = pltpu.get_barrier_semaphore()
@@ -413,6 +416,12 @@
 
     def read(self, part):
         return self.near[0, part] + self.theirs[0, part] + self.swapped[part].astype(F32)
+
+
+def live_rows(place, seq_count, valid_len, part):
+    rows = lax.broadcasted_iota(jnp.int32, (PIECE, 128), 0) + part.start
+    length = jnp.where(place.core == 0, valid_len[0], valid_len[1])
+    return ((rows < length) & (place.core < seq_count[0])).astype(F32)[:, :1]
 
 
 def quad_scratch(width):
@@ -445,8 +454,8 @@
 
 
 def gather_first_kernel(
-    tokens, cot, live, q_w, k_w, v_w, small, out_w, gate_w, up_w, down_w, w_in, w_out, ffn, own, attn_in, d_res, d_ffn, gains,
-    stage, seqs, normed, scales, turned, grads, low, sem
+    tokens, cot, seq_count, valid_len, gain0, gain1, q_w, k_w, v_w, forget_w, out_w, gate_w, up_w, down_w, w_in, w_out, ffn, own, attn_in, d_res, d_ffn, gains,
+    stage, seqs, normed, scales, turned, grads, low, small, sem
 ):
     place, sems = Place(), Sems(sem)
     shard = q_w.shape[0]
@@ -507,6 +516,13 @@
     save_res = pltpu.make_async_copy(grads, d_res, sems.one())
     save_in = [pltpu.make_async_copy(normed.at[i], attn_in.at[i], sems.one()) for i in range(4)]
     load_gains = [pltpu.make_async_copy(w_in.at[i, :, pl.ds(3 * KDIM, 128)], turned.at[i], sems.one()) for i in range(8)]
+    lane = lax.broadcasted_iota(jnp.int32, (shard, 128), 1)
+    column = jnp.concatenate([gain0[...].astype(F32).reshape(1, shard), gain1[...].astype(F32).reshape(1, shard)], axis=0)
+    column = jnp.concatenate([column, jnp.zeros((6, shard), F32)], axis=0).T
+    beside = jnp.where(lane == SLOTS, column[:, 0:1], jnp.where(lane == SLOTS + 1, column[:, 1:2], 0.0))
+    heads = forget_w[...].astype(F32)
+    small[:, :128] = jnp.where(lane < SLOTS, heads, beside).astype(BF16)
+    small[:, 128:] = jnp.where(lane < SLOTS, pltpu.roll(heads, SLOTS, 1), beside).astype(BF16)
     place.greet()
     for swap, keep in zip(swaps[:full], keeps[:full]):
         swap.start()
@@ -528,7 +544,7 @@
     save_own.start()
 
     def mask(part):
-        value = grads[part] * live[part, :1]
+        value = grads[part] * live_rows(place, seq_count, valid_len, part)
         grads[part] = value
         low[part] = value.astype(BF16)
 
@@ -606,22 +622,76 @@
     quad.finish()
 
 
+class BlockTerms:
+    def __init__(self, sems, acts, grads, bufs, over, own, parts):
+        self.acts, self.grads, self.bufs = acts, grads, bufs
+        self.over, self.own, self.parts = over, own, parts
+        self.early = over.shape[2]
+        self.left, self.right = sems.some(2), sems.some(2)
+
+    def copies(self, slot, left, right):
+        early, rest = self.early, self.bufs.shape[2] - self.early
+        return (
+            pltpu.make_async_copy(self.bufs.at[slot, :, pl.ds(0, early)], left, self.left(slot)),
+            pltpu.make_async_copy(self.bufs.at[slot, :, pl.ds(early, rest)], right, self.right(slot)),
+        )
+
+    def wait(self, slot):
+        for copy in self.copies(slot, self.own.at[0], self.parts[0].at[0]):
+            copy.wait()
+
+    def run(self, start, stop):
+        width = self.bufs.shape[1]
+
+        def step(i, carry):
+            slot, side, away = i % 2, i // 4, i % 4
+
+            @pl.when(i >= 2)
+            def _():
+                self.wait(slot)
+
+            cols = pl.ds(pl.multiple_of(i * width, width), width)
+            self.bufs[slot] = mm(self.acts[:, cols], self.grads[...], TN, BF16)
+
+            @pl.when(side == 0)
+            def _():
+                self.copies(slot, self.own.at[away], self.parts[0].at[0])[0].start()
+
+            @pl.when(side == 1)
+            def _():
+                self.copies(slot, self.over.at[away], self.parts[0].at[0])[0].start()
+
+            for place in range(4):
+
+                @pl.when(away == place)
+                def _(place=place):
+                    self.copies(slot, self.own.at[0], self.parts[place].at[side])[1].start()
+
+            return carry
+
+        lax.fori_loop(start, stop, step, 0)
+
+    def finish(self):
+        self.wait(0)
+        self.wait(1)
+
+
 class WideMatmul:
-    def __init__(self, sems, acts, weight, stage, bufs, lows, wide, hidden):
-        self.acts, self.weight, self.stage, self.bufs, self.lows = acts, weight, stage, bufs, lows
-        self.wide, self.hidden = wide, hidden
+    def __init__(self, sems, acts, weight, stage, sums, hidden, wide):
+        self.acts, self.weight, self.stage, self.sums, self.hidden, self.wide = acts, weight, stage, sums, hidden, wide
         self.hid = hidden.shape[1]
+        self.half = acts.shape[1] // 2
         self.count = self.hid // 128
         self.loads = [sems.some(2) for _ in range(2)]
-        self.stores = [sems.some(2) for _ in range(3)]
+        self.stores = [sems.some(2) for _ in range(2)]
 
     def columns(self, i, side):
         return pl.ds(pl.multiple_of(side * self.hid + i * 128, 128), 128)
 
-    def fetch(self, i):
+    def fetch(self, i, phase):
         return [
             pltpu.make_async_copy(
-                self.weight.at[:, self.columns(i, side)],
+                self.weight.at[pl.ds(phase * self.half, self.half), self.columns(i, side)],
                 self.stage.at[i % 2, :, pl.ds(side * 128, 128)],
                 self.loads[side](i % 2),
             )
@@ -629,41 +699,41 @@
         ]
 
     def leave(self, i):
-        copies = [
+        return [
             pltpu.make_async_copy(
-                self.bufs.at[i % 2, :, pl.ds(side * 128, 128)],
-                self.wide.at[:, self.columns(i, side)],
-                self.stores[side](i % 2),
+                self.sums.at[i, :, pl.ds(side * 128, 128)], self.wide.at[:, self.columns(i, side)], self.stores[side](i % 2)
             )
             for side in range(2)
         ]
-        return copies + [
-            pltpu.make_async_copy(self.lows.at[i % 2], self.hidden.at[:, self.columns(i, 0)], self.stores[2](i % 2))
-        ]
-
-    def begin(self):
-        for copy in self.fetch(0):
+
+    def begin(self, phase):
+        for copy in self.fetch(0, phase):
             copy.start()
 
-    def run(self, start, stop):
+    def run(self, phase, start, stop):
         def step(i, carry):
-            for copy in self.fetch(i):
+            for copy in self.fetch(i, phase):
                 copy.wait()
 
             @pl.when(i + 1 < self.count)
             def _():
-                for copy in self.fetch(i + 1):
+                for copy in self.fetch(i + 1, phase):
                     copy.start()
+
+            both = mm(self.acts[:, phase * self.half : (phase + 1) * self.half], self.stage[i % 2])
+            if phase == 0:
+                self.sums[i] = both
+                return carry
 
             @pl.when(i >= 2)
             def _():
-                for copy in self.leave(i):
+                for copy in self.leave(i - 2):
                     copy.wait()
 
-            both = mm(self.acts[...], self.stage[i % 2])
+            both = both + self.sums[i]
+            self.sums[i] = both
             gate = both[:, :128]
-            self.bufs[i % 2] = both
-            self.lows[i % 2] = (gate / (1.0 + jnp.exp(-gate)) * both[:, 128:]).astype(BF16)
+            self.hidden[:, self.columns(i, 0)] = (gate / (1.0 + jnp.exp(-gate)) * both[:, 128:]).astype(BF16)
             for copy in self.leave(i):
                 copy.start()
             return carry
@@ -677,8 +747,9 @@
 
 
 def gather_ffn_kernel(
-    hid, cut, b0, b3, b4, terms, tokens, gains, w_wide, w_down, resid, ffn_in, wide, hidden,
-    s0, s1, s2, s3, kept, acts, inputs, stage, tiles, bufs, lows, sem
+    hid, cut, b0, b3, b4, terms, tokens, gains, d_ffn,
+    w_wide, w_down, resid, ffn_in, wide, hidden, down_over, down_own, down0, down1, down2, down3,
+    s0, s1, s2, s3, kept, acts, inputs, stage, tiles, sums, hid_v, cots, bufs, sem
 ):
     place, sems = Place(), Sems(sem)
     rows = b0.shape[0]
@@ -726,7 +797,10 @@
     fetch = pltpu.make_async_copy(tokens, inputs, sems.one())
     save = pltpu.make_async_copy(kept, resid, sems.one())
     save_in = pltpu.make_async_copy(acts, ffn_in, sems.one())
-    matmul = WideMatmul(sems, acts, w_wide, tiles, bufs, lows, wide, hidden)
+    save_hidden = pltpu.make_async_copy(hid_v, hidden, sems.one())
+    fetch_cots = pltpu.make_async_copy(d_ffn, cots, sems.one())
+    matmul = WideMatmul(sems, acts, w_wide, tiles, sums, hid_v, wide)
+    grad = BlockTerms(sems, cots, hid_v, bufs, down_over, down_own, (down0, down1, down2, down3))
     place.greet()
     total.start()
     fetch.start()
@@ -760,27 +834,34 @@
         low[1].wait_recv()
         cross[2].start()
     down[2][0].start()
+    fetch_cots.start()
     rest[1][0].wait_recv()
     rest[1][1].start()
     out.forward()
+    for copy in keeps[:6]:
+        copy.wait()
+    out.finish()
+    save_in.start()
+    matmul.begin(0)
+    matmul.run(0, 0, matmul.count // 2)
     down[0][0].wait_recv()
     down[0][1].start()
     down[2][1].start()
+    matmul.run(0, matmul.count // 2, matmul.count)
     rest[0][0].wait_recv()
     rest[0][1].start()
-    out.finish()
-    save_in.start()
-    for copy in keeps[:6]:
-        copy.wait()
     for copy in gate[2] + up[2]:
         copy.wait_recv()
-    matmul.begin()
     rest[1][1].wait_recv()
     rest[1][2].start()
-    matmul.run(0, 4)
+    matmul.begin(1)
+    matmul.run(1, 0, matmul.count // 2)
     down[0][1].wait_recv()
     down[2][2].start()
-    matmul.run(4, matmul.count)
+    matmul.run(1, matmul.count // 2, matmul.count)
+    save_hidden.start()
+    fetch_cots.wait()
+    grad.run(0, 8)
     for copy in down[2]:
         copy.wait_recv()
     rest[0][1].wait_recv()
@@ -791,8 +872,10 @@
     for copy in keeps[6:]:
         copy.wait()
     matmul.finish()
+    grad.finish()
     save.wait()
     save_in.wait()
+    save_hidden.wait()
 
 
 class Sum:
@@ -916,60 +999,6 @@
     return [pltpu.VMEM((depth, rows, width), BF16) for depth in (4, 4, 3, 3)] + [pltpu.VMEM((rows, width), F32)]
 
 
-class UpTerms:
-    def __init__(self, sems, acts, grads, bufs, over, own, parts):
-        self.acts, self.grads, self.bufs = acts, grads, bufs
-        self.over, self.own, self.parts = over, own, parts
-        self.early = over.shape[2]
-        self.left, self.right = sems.some(2), sems.some(2)
-
-    def copies(self, slot, left, right):
-        early, rest = self.early, self.bufs.shape[2] - self.early
-        return (
-            pltpu.make_async_copy(self.bufs.at[slot, :, pl.ds(0, early)], left, self.left(slot)),
-            pltpu.make_async_copy(self.bufs.at[slot, :, pl.ds(early, rest)], right, self.right(slot)),
-        )
-
-    def wait(self, slot):
-        for copy in self.copies(slot, self.own.at[0], self.parts[0].at[0]):
-            copy.wait()
-
-    def run(self, start, stop):
-        width = self.bufs.shape[1]
-
-        def step(i, carry):
-            slot, side, away = i % 2, i // 4, i % 4
-
-            @pl.when(i >= 2)
-            def _():
-                self.wait(slot)
-
-            cols = pl.ds(pl.multiple_of(i * width, width), width)
-            self.bufs[slot] = mm(self.acts[:, cols], self.grads[...], TN, BF16)
-
-            @pl.when(side == 0)
-            def _():
-                self.copies(slot, self.own.at[away], self.parts[0].at[0])[0].start()
-
-            @pl.when(side == 1)
-            def _():
-                self.copies(slot, self.over.at[away], self.parts[0].at[0])[0].start()
-
-            for place in range(4):
-
-                @pl.when(away == place)
-                def _(place=place):
-                    self.copies(slot, self.own.at[0], self.parts[place].at[side])[1].start()
-
-            return carry
-
-        lax.fori_loop(start, stop, step, 0)
-
-    def finish(self):
-        self.wait(0)
-        self.wait(1)
-
-
 class OutTerms:
     def __init__(self, sems, hidden, weight, stage, bufs, target):
         self.hidden, self.weight, self.stage, self.bufs, self.target = hidden, weight, stage, bufs, target
@@ -1014,23 +1043,29 @@
     return scale * scaled - value * (scale * scale * scale * inner), jnp.sum(gains, axis=0)
 
 
+def thirds(columns):
+    tiles = columns // 128
+    wide = (tiles + 2) // 3 * 128
+    return ((0, wide), (wide, wide), (2 * wide, columns - 2 * wide))
+
+
 def sum_ffn_kernel(
-    hid, early, gate_t, down, given, given1, given2, given3, terms, resid, gains, d_res, ffn_in, d_wide, hidden, w_down,
+    hid, early, gate_t, down, given, down_rest, given1, given2, given3, terms, resid, gains, d_res, ffn_in, d_wide, hidden, w_down,
     gate_sum, down_sum, d_h, d_attn, gain_sum, up_over, up_own, up0, up1, up2, up3, out_terms, *scratch
 ):
     *scratch, sem = scratch
     place, sems = Place(), Sems(sem)
     rest = hid - early
     down_y = Sum(place, sems, down, given, down_sum, 0, early, scratch[0:5], hid)
-    down_z = SumGiven(place, sems, down, (given1, given2, given3), down_sum, early, rest, scratch[5:10], hid, early)
+    down_z = SumGiven(place, sems, down_rest, (given1, given2, given3), down_sum, 0, rest, scratch[5:10], hid, early)
     gate = [
-        Sum(place, sems, gate_t, None, gate_sum, 0, early, scratch[10:15], hid),
-        Sum(place, sems, gate_t, None, gate_sum, early, rest, scratch[15:20], hid, early),
+        Sum(place, sems, gate_t, None, gate_sum, first, width, scratch[10 + 5 * i : 15 + 5 * i], hid, first)
+        for i, (first, width) in enumerate(thirds(hid))
     ]
-    back = QuadSum(place, sems, terms, scratch[20:24])
-    value, res, low, acts, ups, up_bufs, hid_v, stage, out_bufs = scratch[24:33]
+    back = QuadSum(place, sems, terms, scratch[25:29])
+    value, res, low, acts, ups, up_bufs, hid_v, stage, out_bufs = scratch[29:38]
     quad = Quad(place, sems, low, [d_attn.at[i] for i in range(4)])
-    up = UpTerms(sems, acts, ups, up_bufs, up_over, up_own, (up0, up1, up2, up3))
+    up = BlockTerms(sems, acts, ups, up_bufs, up_over, up_own, (up0, up1, up2, up3))
     out = OutTerms(sems, hid_v, w_down, stage, out_bufs, out_terms)
     ready = [
         pltpu.make_async_copy(ffn_in, acts, sems.one()),
@@ -1080,11 +1115,11 @@
         one.step(1)
     down_y.step(2)
     up.run(4, 8)
+    down_z.second()
     for one in gate:
         one.step(2)
     down_y.step(3)
     out.run(0, 8)
-    down_z.second()
     quad.forward()
     for one in gate:
         one.step(3)
@@ -1097,11 +1132,11 @@
 
 
 def sum_last_kernel(
-    hid, early, up, given, up_rest, given1, given2, given3, out_t, in_t, terms, tokens, gain_rows, d_h, ffn_gains, out_terms, resid, live,
+    hid, early, up, given, up_rest, given1, given2, given3, out_t, in_t, terms, tokens, gain_rows, d_h, ffn_gains, out_terms, resid, seq_count, valid_len,
     up_sum, out_sum, q_sum, k_sum, v_sum, f_sum, grad, block_out, gain_sum, *scratch
 ):
     *scratch, sem = scratch
-    place, sems = Place(), Sems(sem)
+    place, sems = Place(True), Sems(sem)
     sums = []
     for terms_in, given_in, result, first, width, span, start in (
         (up, given, up_sum, 0, early, hid, 0),
@@ -1117,14 +1152,16 @@
     scratch = scratch[5:]
     back = QuadSum(place, sems, terms, scratch[0:4])
     ahead = QuadSum(place, sems, out_terms, scratch[4:8])
-    value, res, kept, shown, gains, parts, met, crossed, risen, rising, last, swapped = scratch[8:]
+    value, res, kept, shown, gains, parts, met, crossed, risen, last, swapped = scratch[8:]
     leave = Leave(place, sems, res, grad)
     leave_out = Leave(place, sems, shown, block_out)
     fetch = [pltpu.make_async_copy(tokens, value, sems.one()), pltpu.make_async_copy(d_h, res, sems.one())]
     fetch.append(pltpu.make_async_copy(resid, kept, sems.one()))
     meet = place.copy("core", parts, met, sems.two())
     cross = place.copy("y", parts.at[pl.ds(4, 4)], crossed, sems.two())
-    rise = [place.copy("up", rising.at[i], risen.at[i], sems.two()) for i in range(3)]
+    spread = [
+        place.copy(name, parts.at[i + 1], risen.at[i], sems.two()) for i, name in enumerate(("up", "two", "down"))
+    ]
     swap = place.copy("x", last.at[1 - place.x], swapped, sems.two())
     place.greet()
     back.start()
@@ -1175,29 +1212,28 @@
     for one in sums:
         one.step(2)
     cross.wait()
-    rising[0] = parts[3] + crossed[3]
-    rise[0].start()
+    parts[pl.ds(0, 4)] = parts[pl.ds(0, 4)] + crossed[...]
+    for copy in spread:
+        copy.start()
     ahead.ready()
 
     def show(part):
-        shown[part] = (live[part, :1] * (kept[part] + ahead.read(part))).astype(BF16)
+        alive = live_rows(place, seq_count, valid_len, part)
+        shown[part] = (alive * (kept[part] + ahead.read(part))).astype(BF16)
 
     pieces(SEQ_LEN, show)
     leave_out.start()
     for one in sums:
         one.step(3)
-    for step in (1, 2):
-        rise[step - 1].wait_recv()
-        rising[step] = parts[3 - step] + crossed[3 - step] + risen[step - 1]
-        rise[step].start()
-    rise[2].wait_recv()
-    total = parts[0] + crossed[0] + risen[2]
+    for copy in spread:
+        copy.wait_recv()
+    total = parts[0] + risen[0] + risen[1] + risen[2]
     last[0] = total[:, : width // 2]
     last[1] = total[:, width // 2 :]
     swap.start()
     swap.wait()
     gain_sum[...] = last[place.x] + swapped[...]
-    for copy in rise:
+    for copy in spread:
         copy.wait_send()
     leave.finish()
     leave_out.finish()
@@ -1510,27 +1546,35 @@
 ):
     shard, dim = q_weight.shape[0], tokens.shape[1]
     width, hid = 2 * shard, gate_weight.shape[1] // 2
-    core = lax.axis_index("head")
-    first = core == 0
     up_z, over_y = (lambda value: ring.send(value, ring.stages[0], 1)), (lambda value: ring.send(value, ring.stages[1], 1))
     rows4 = (4, SEQ_LEN, dim)
     blocks = lambda value: value.reshape(-1, width, value.shape[-1])
     flat = lambda value: value.reshape(-1, value.shape[-1])
     half = dim // 2
 
-    gains = jnp.concatenate([attn_gain[:, None], ffn_gain[:, None], jnp.zeros((shard, PAD - 2), BF16)], axis=1)
-    small = jnp.concatenate([forget_weight[:, :SLOTS], gains, forget_weight[:, SLOTS:], gains], axis=1)
-    places = lax.broadcasted_iota(jnp.int32, (SEQ_LEN, 128), 0)
-    length = jnp.where(first, valid_len[0], valid_len[1])
-    live = ((core < seq_count[0]) & (places < length)).astype(F32)
     row = (SEQ_LEN, dim)
     vmem = lambda shape, kind=F32: pltpu.VMEM(shape, kind)
     w_in, w_out, part0, own, attn_in, d_res, d_ffn, gain_rows = call(
         gather_first_kernel,
         "gather_first",
         0,
-        (tokens, cotangent, live, q_weight, k_weight, v_weight, small, out_weight, gate_weight, up_weight, down_weight),
-        [ANY, ANY, VMEM] + [ANY] * 8,
+        (
+            tokens,
+            cotangent,
+            seq_count,
+            valid_len,
+            attn_gain,
+            ffn_gain,
+            q_weight,
+            k_weight,
+            v_weight,
+            forget_weight,
+            out_weight,
+            gate_weight,
+            up_weight,
+            down_weight,
+        ),
+        [ANY, ANY, SMEM, SMEM, VMEM, VMEM, ANY, ANY, ANY, VMEM] + [ANY] * 4,
         [
             ((8, width, WIDE), BF16),
             ((8, width, KDIM), BF16),
@@ -1550,6 +1594,7 @@
             vmem((8, width, 128), BF16),
             vmem(row),
             vmem(row, BF16),
+            vmem((shard, 256), BF16),
         ],
         240,
     )
@@ -1560,12 +1605,13 @@
     attn_terms = mm(mixed, w_out, NT).reshape(rows4)
     cut = hid // 256 * 128 + 128
     tokens4 = 4 * SEQ_LEN
-    w_wide, w_down, resid, ffn_in, wide, hidden = call(
+    early, rest = [((4, width, EARLY), BF16)] * 2, [((2, width, hid - EARLY), BF16)] * 4
+    w_wide, w_down, resid, ffn_in, wide, hidden, down_over, down_own, *down_parts = call(
         functools.partial(gather_ffn_kernel, hid, cut),
         "gather_ffn",
         1,
-        (part0, part3, part4, attn_terms, own, gain_rows),
-        [ANY] * 5 + [VMEM],
+        (part0, part3, part4, attn_terms, own, gain_rows, d_ffn),
+        [ANY] * 5 + [VMEM, ANY],
         [
             ((dim, 2 * hid), BF16),
             ((dim, hid), BF16),
@@ -1573,39 +1619,39 @@
             ((tokens4, dim), BF16),
             ((tokens4, 2 * hid), F32),
             ((tokens4, hid), BF16),
-        ],
-        [ANY] * 6,
+        ]
+        + early
+        + rest,
+        [ANY] * 12,
         quad_scratch(dim)
         + [vmem(row), vmem((tokens4, dim), BF16), vmem(row, BF16), vmem((3, width, 3 * hid), BF16)]
-        + [vmem((2, dim, 256), BF16), vmem((2, tokens4, 256)), vmem((2, tokens4, 128), BF16)],
-        160,
+        + [vmem((2, dim // 2, 256), BF16), vmem((hid // 128, tokens4, 256)), vmem((tokens4, hid), BF16)]
+        + [vmem((tokens4, dim), BF16), vmem((2, width, hid), BF16)],
+        180,
     )
 
-    def early_terms(terms, start):
-        over = over_y(terms[half:, start : start + EARLY])
-        rest = blocks(terms)[:, :, start + EARLY : start + hid]
-        given = [ring.send(jnp.stack([rest[d], rest[4 + d]]), ring.stages[0], d) for d in (1, 2, 3)]
-        return [blocks(over), *given]
-
+    def exchange(over, parts):
+        return [over_y(over)] + [ring.send(parts[d], ring.stages[0], d) for d in (1, 2, 3)]
+
+    down_given = exchange(down_over, down_parts)
     gate, up_vals = wide[:, :hid], wide[:, hid:]
     sig = jax.nn.sigmoid(gate)
-    down_terms = mm(d_ffn, hidden, TN, BF16)
-    down_given = early_terms(down_terms, 0)
     d_hidden = mm(d_ffn, w_down)
     d_gate = (d_hidden * up_vals * (sig * (1.0 + gate * (1.0 - sig)))).astype(BF16)
     d_up = (d_hidden * (gate * sig)).astype(BF16)
     d_wide = jnp.concatenate([d_gate, d_up], axis=1)
     gate_terms = mm(ffn_in, d_wide[:, :hid], TN, BF16)
     d_ffn_terms = mm(d_wide, w_wide, NT).reshape(rows4)
-    rest = hid - EARLY
     gate_sum, down_sum, d_h, d_attn, ffn_gains, up_over, up_own, *up_parts, ffn_terms = call(
         functools.partial(sum_ffn_kernel, hid, EARLY),
         "sum_ffn",
         2,
         (
             blocks(gate_terms),
-            blocks(down_terms),
-            *down_given,
+            down_own,
+            down_given[0],
+            down_parts[0],
+            *down_given[1:],
             d_ffn_terms,
             resid,
             gain_rows,
@@ -1615,16 +1661,15 @@
             hidden,
             blocks(w_down),
         ),
-        [ANY] * 8 + [VMEM] + [ANY] * 5,
+        [ANY] * 9 + [VMEM] + [ANY] * 5,
         [((shard, 2 * hid), F32), ((shard, 2 * hid), F32), (row, F32), (rows4, BF16), ((8, dim), F32)]
-        + [((4, width, EARLY), BF16)] * 2
-        + [((2, width, rest), BF16)] * 4
+        + early
+        + rest
         + [((4 * SEQ_LEN, dim), F32)],
         [ANY] * 4 + [VMEM] + [ANY] * 7,
         sum_scratch(width, EARLY)
-        + given_scratch(width, rest)
-        + sum_scratch(width, EARLY)
-        + sum_scratch(width, rest)
+        + given_scratch(width, hid - EARLY)
+        + [one for _, columns in thirds(hid) for one in sum_scratch(width, columns)]
         + quad_scratch(dim)
         + [vmem(row), vmem(row), vmem(row, BF16)]
         + [vmem((4 * SEQ_LEN, dim), BF16), vmem((4 * SEQ_LEN, hid), BF16), vmem((2, width, hid), BF16)]
@@ -1632,7 +1677,7 @@
         220,
     )
     d_attn = flat(d_attn)
-    up_given = [over_y(up_over)] + [ring.send(up_parts[d], ring.stages[0], d) for d in (1, 2, 3)]
+    up_given = exchange(up_over, up_parts)
     d_proj = mixer_backward(proj, saved, mm(d_attn, w_out))
     d_attn_terms = mm(d_proj, w_in, NT).reshape(rows4)
     ffn_terms = ffn_terms.reshape(rows4)
@@ -1655,9 +1700,10 @@
             ffn_gains,
             ffn_terms,
             resid,
-            live,
+            seq_count,
+            valid_len,
         ),
-        [ANY] * 10 + [VMEM, ANY, VMEM, ANY, ANY, VMEM],
+        [ANY] * 10 + [VMEM, ANY, VMEM, ANY, ANY, SMEM, SMEM],
         [((shard, 2 * hid), F32)]
         + [((shard, 2 * KDIM), F32)] * 4
         + [((shard, 256), F32), ((2 * SEQ_LEN, dim), F32), ((2 * SEQ_LEN, dim), BF16), ((8, tail), F32)],
@@ -1665,10 +1711,10 @@
         sum_scratch(width, EARLY)
         + sum_scratch(width, KDIM) * 4
         + sum_scratch(width, 128)
-        + given_scratch(width, rest)
+        + given_scratch(width, hid - EARLY)
         + quad_scratch(dim) * 2
         + [vmem(row, BF16), vmem(row), vmem(row), vmem(row, BF16), vmem((8, dim))]
-        + [vmem((depth, 8, width)) for depth in (8, 8, 4, 3, 3)]
+        + [vmem((depth, 8, width)) for depth in (8, 8, 4, 3)]
         + [vmem((2, 8, tail)), vmem((8, tail))],
         280,
     )

time: 652 us -> 631 us (0.968)
  local copies, waits for them, and re-layouts: 26.3 us -> 18.3 us
  matrix products: 101 us -> 93.8 us
    dot_general x10 -> x9, matrix products: 101 us -> 93.8 us  [mm(): lax.dot_general(left, right, dims, preferred_element_type=F32).astype(kind)]
    unnamed x61 -> x53, local copies, waits for them, and re-layouts: 17.2 us -> 16 us
  transfers between devices with their start and end apart: 10 -> 10, of which waited for: 2 -> 2; matrix products, arithmetic and copies ran while one was open for 15% -> 16% of each run, Pallas kernels for 5% -> 5%
where the time goes in v7:
time: 631 us; the launch traced here: 621 us
  Pallas kernels  475 us (75%)
  matrix products  93.8 us (15%)
  local copies, waits for them, and re-layouts  18.3 us (3%)
  waiting for transfers between devices  15.4 us (2%)
  starting transfers between devices  12.8 us (2%)
    pallas_call x4, Pallas kernels, call(): pl.pallas_call(kernel, in_specs=specs, out_specs=out_specs, out_shape=[ja...  444 us
    dot_general x9, matrix products, mm(): lax.dot_general(left, right, dims, preferred_element_type=F32).astype(kind)  93.8 us
    pallas_call x1, Pallas kernels, mixer_backward(): pl.pallas_call(backward_kernel, grid=(rows // SEQ_LEN,), in_specs=IN_SPEC...  18.4 us
    unnamed x53, local copies, waits for them, and re-layouts  16 us
    ppermute x10, waiting for transfers between devices, send(): return lax.ppermute(value, 'dp', self.perm(stride, size, shift % size))  15.4 us
    ppermute x10, starting transfers between devices, send(): return lax.ppermute(value, 'dp', self.perm(stride, size, shift % size))  12.8 us
    pallas_call x1, Pallas kernels, mixer_forward(): pl.pallas_call(forward_kernel, grid=(rows // SEQ_LEN,), in_specs=IN_SPECS...  12.8 us
  transfers between devices with their start and end apart: 10, of which 2 were waited for; matrix products, arithmetic and copies ran while one was open for 16% of the time, Pallas kernels for 5%

profile of v7, /device:TPU:0, one launch (start us, length us, event | category | flops | bytes accessed | tf_op | source)
XLA Modules:
  0.0 620.7 jit_solution(2249519998337759119)
XLA Ops:
  1.3 103.6 %gather_first.1 = (bf16[8,256,1664]{2,1,0:T(8,128)(2,1)}, bf16[8,256,512]{2,1,0:T(8,128)(2,1)}, bf16[256,4224]{1,0:T(8,128)(2,1)}, bf16[256,2048]{1,0:T(8,128)(2...) custom-call(bf16[512,2048]{1,0:T(8,128)(2,1)} %tokens.1, ...), custom_call_target="tpu_custom_call" | custom-call | tf_op jit(solution)/shard_map/gather_first/pallas_call | solution.py:1246
  104.9 1.3 collective-permute-start.1
  106.8 13.3 %fusion.2.q_ref.k_ref.v_ref.f_ref = f32[1024,1664]{1,0:T(8,128)} fusion(bf16[1024,2048]{1,0:T(8,128)(2,1)} %bitcast.52, bf16[2048,1664]{1,0:T(8,128)(2,1)} %bitcast.48), kind=kOutput, calls=%fused_computation.12 | convolution fusion | flops 6979321856 | bytes 17825792 | tf_op jit(solution)/shard_map/dot_general | solution.py:1365
  120.0 12.8 %mixer_forward.1 = (bf16[1024,512]{1,0:T(8,128)(2,1)S(1)}, f32[1024,128]{1,0:T(8,128)S(1)}, f32[1024,128]{1,0:T(8,128)S(1)}, f32[1024,256]{1,0:T(8,128)S(1)}, f32[1024,256]{1,0:T(8,128)S(1)}) custom-call(f32[1024,1664]{1,0:T(8,128)} %fusion.2.q_ref.k_ref.v_ref.f_ref, f32[1024,1664]{1,0:T(8,128)} %fusion.2.q_ref.k_ref.v_ref.f_ref, ...), custom_call_target="tpu_custom_call" | custom-call | flops 3072000000 | bytes 10240000 | tf_op jit(solution)/shard_map/mixer_forward/pallas_call | solution.py:251
  132.9 5.7 fusion.3.terms
  138.6 14.5 %collective-permute-done.1.b4 = bf16[256,4224]{1,0:T(8,128)(2,1)S(1)} collective-permute-done((bf16[256,4224]{1,0:T(8,128)(2,1)}, bf16[256,4224]{1,0:T(8,128)(2,1)S(1)}, u32[]{:S(2)}, u32[]{:S(2)}) %collective-permute-start.1) | collective-permute-done | bytes 2162720 | tf_op jit(solution)/shard_map/ppermute | solution.py:1281
  153.1 1.3 copy-done.6
  155.3 1.3 copy-done.7
  156.7 123.7 %gather_ffn.1 = (bf16[2048,2816]{1,0:T(8,128)(2,1)}, bf16[2048,1408]{1,0:T(8,128)(2,1)}, f32[256,2048]{1,0:T(8,128)}, bf16[1024,2048]{1,0:T(8,128)(2,1)}, f32[10...) custom-call(bf16[256,4224]{1,0:T(8,128)(2,1)} %get-tuple-element.58., ...), custom_call_target="tpu_custom_call" | custom-call | tf_op jit(solution)/shard_map/gather_ffn/pallas_call | solution.py:1246
  280.4 1.7 collective-permute-start.4
  282.1 2.4 collective-permute-start.5
  284.5 1.3 collective-permute-start.2
  285.7 15.2 %multiply_convert_fusion = (bf16[1024,1408]{1,0:T(8,128)(2,1)S(1)}, bf16[1024,1408]{1,0:T(8,128)(2,1)}) fusion(f32[1024,2816]{1,0:T(8,128)} %get-tuple-element.68, bf16[1024,2048]{1,0:T(8,128)(2,1)} %bitcast.45, bf16[2048,1408]{1,0:T(8,128)(2,1)} %get-tuple-element.67), kind=kOutput, calls=%fused_computation.3 | convolution fusion | flops 5924323328 | bytes 27262976 | tf_op jit(solution)/shard_map/dot_general | solution.py:1365
  300.9 17.9 %fusion = f32[1024,2048]{1,0:T(8,128)} fusion(bf16[2048,2816]{1,0:T(8,128)(2,1)} %get-tuple-element.75, bf16[1024,1408]{1,0:T(8,128)(2,1)S(1)} %get-tuple-element.104, bf16[1024,1408]{1,0:T(8,128)(2,1)} %get-tuple-element.105), kind=kOutput, calls=%fused_computation.10 | convolution fusion | flops 11822694400 | bytes 25690112 | tf_op jit(solution)/shard_map/dot_general | solution.py:1365
  318.8 10.8 %convolution_convert_fusion.1 = bf16[2048,1408]{1,0:T(8,128)(2,1)} fusion(bf16[1024,2048]{1,0:T(8,128)(2,1)S(1)} %copy-done.3, bf16[1024,1408]{1,0:T(8,128)(2,1)} %get-tuple-element.105), kind=kOutput, calls=%fused_computation.1 | convolution fusion | flops 5908463616 | bytes 12845056 | tf_op jit(solution)/shard_map/dot_general | solution.py:1365
  329.6 2.9 pad_maximum_fusion.d_wide
  333.2 94.4 %sum_ffn.1 = (f32[128,2816]{1,0:T(8,128)}, f32[128,2816]{1,0:T(8,128)}, f32[256,2048]{1,0:T(8,128)}, bf16[4,256,2048]{2,1,0:T(8,128)(2,1)}, f32[8,2048]{1,0:T(8,...) custom-call(bf16[8,256,1408]{2,1,0:T(8,128)(2,1)} %bitcast.43, ...), custom_call_target="tpu_custom_call" | custom-call | tf_op jit(solution)/shard_map/sum_ffn/pallas_call | solution.py:1246
  427.7 1.0 collective-permute-start.7
  428.6 2.0 collective-permute-start.8
  431.6 1.7 collective-permute-start.6
  433.3 5.2 fusion.4.d_ref
  438.5 18.4 %mixer_backward.1 = bf16[1024,1664]{1,0:T(8,128)(2,1)} custom-call(f32[1024,1664]{1,0:T(8,128)} %fusion.2.q_ref.k_ref.v_ref.f_ref, f32[1024,1664]{1,0:T(8,128)} %fusion.2.q_ref.k_ref.v_ref.f_ref, f32[1024,1664]{1,0:T(8,128)} %fusion.2.q_ref.k_ref.v_ref.f_ref, f32[1024,1664]{1,0:T(8,128)} %fusion.2.q_ref.k_ref.v_ref.f_ref, ...), custom_call_target="tpu_custom_call" | custom-call | flops 9216000000 | bytes 16384000 | tf_op jit(solution)/shard_map/mixer_backward/pallas_call | solution.py:266
  456.9 11.9 %convolution_convert_fusion = bf16[2048,1664]{1,0:T(8,128)(2,1)} fusion(bf16[1024,2048]{1,0:T(8,128)(2,1)S(1)} %bitcast.53, bf16[1024,1664]{1,0:T(8,128)(2,1)} %mixer_backward.1), kind=kOutput, calls=%fused_computation | convolution fusion | flops 6982729728 | bytes 14417920 | tf_op jit(solution)/shard_map/dot_general | solution.py:1365
  468.9 10.1 %fusion.5.terms = f32[4,256,2048]{2,1,0:T(8,128)} fusion(bf16[4,256,1664]{2,1,0:T(8,128)(2,1)S(1)} %bitcast.46, bf16[2048,1664,1]{1,0,2:T(8,128)(2,1)S(1)} %bitcast.51), kind=kOutput, calls=%fused_computation.15 | convolution fusion | flops 6979321856 | bytes 18612224 | tf_op jit(solution)/shard_map/dot_general | solution.py:1365
  479.1 3.8 convolution_convert_fusion.2
  483.6 122.1 %sum_last.1 = (f32[128,2816]{1,0:T(8,128)}, f32[128,1024]{1,0:T(8,128)}, f32[128,1024]{1,0:T(8,128)}, f32[128,1024]{1,0:T(8,128)}, f32[128,1024]{1,0:T(8,128)}, ...) custom-call(bf16[4,256,896]{2,1,0:T(8,128)(2,1)} %get-tuple-element.79.up, ...), custom_call_target="tpu_custom_call" | custom-call | tf_op jit(solution)/shard_map/sum_last/pallas_call | solution.py:1246
  605.7 1.4 slice_bitcast_fusion
  608.7 3.2 copy.36
  611.9 2.1 copy.37
  617.2 1.1 copy.42
  618.3 1.1 copy.43
  619.4 1.1 copy.44
  (61 shorter events, 8.8 us)
Async XLA Ops:
  104.9 48.1 %collective-permute-start.1 = (bf16[256,4224]{1,0:T(8,128)(2,1)}, bf16[256,4224]{1,0:T(8,128)(2,1)S(1)}, u32[]{:S(2)}, u32[]{:S(2)}) collective-permute-start(bf16[256,4224]{1,0:T(8,128)(2,1)} %get-tuple-element.58.b0), channel_id=1, source_target_pairs={{0,4},{2,6},{4,0},{6,2},{8,12},{10,14},{12,8},{14,10},{16,20},{18,... | collective-permute-start | bytes 6488072 | tf_op jit(solution)/shard_map/ppermute | solution.py:1281
  106.3 49.1 %collective-permute-start = (bf16[256,4224]{1,0:T(8,128)(2,1)}, bf16[256,4224]{1,0:T(8,128)(2,1)S(1)}, u32[]{:S(2)}, u32[]{:S(2)}) collective-permute-start(bf16[256,4224]{1,0:T(8,128)(2,1)} %get-tuple-element.58.b0), channel_id=1, source_target_pairs={{0,8},{2,10},{4,12},{6,14},{8,16},{10,18},{12,20},{14,22},{16,24},... | collective-permute-start | bytes 6488072 | tf_op jit(solution)/shard_map/ppermute | solution.py:1281
  120.0 12.8 %copy-start.19 = (bf16[8,256,512]{2,1,0:T(8,128)(2,1)S(1)}, bf16[8,256,512]{2,1,0:T(8,128)(2,1)}, u32[]{:S(2)}) copy-start(bf16[8,256,512]{2,1,0:T(8,128)(2,1)} %get-tuple-element.62) | copy-start | bytes 6291460
  132.9 5.7 copy-start
  153.1 1.3 copy-start.6
  155.3 1.3 copy-start.7
  280.3 52.1 %collective-permute-start.3 = (bf16[2,256,512]{2,1,0:T(8,128)(2,1)}, bf16[2,256,512]{2,1,0:T(8,128)(2,1)S(1)}, u32[]{:S(2)}, u32[]{:S(2)}) collective-permute-start(bf16[2,256,512]{2,1,0:T(8,128)(2,1)} %get-tuple-element.72), channel_id=1, source_target_pairs={{0,8},{2,10},{4,12},{6,14},{8,16},{10,18},{12,20},{14,22},{16,24},... | collective-permute-start | bytes 1572872 | tf_op jit(solution)/shard_map/ppermute | solution.py:1281
  280.4 52.0 %collective-permute-start.4 = (bf16[2,256,512]{2,1,0:T(8,128)(2,1)}, bf16[2,256,512]{2,1,0:T(8,128)(2,1)}, u32[]{:S(2)}, u32[]{:S(2)}) collective-permute-start(bf16[2,256,512]{2,1,0:T(8,128)(2,1)} %get-tuple-element.73), channel_id=1, source_target_pairs={{0,16},{2,18},{4,20},{6,22},{8,24},{10,26},{12,28},{14,30},{16,0},... | collective-permute-start | bytes 1572872 | tf_op jit(solution)/shard_map/ppermute | solution.py:1281
  282.1 50.4 %collective-permute-start.5 = (bf16[2,256,512]{2,1,0:T(8,128)(2,1)}, bf16[2,256,512]{2,1,0:T(8,128)(2,1)}, u32[]{:S(2)}, u32[]{:S(2)}) collective-permute-start(bf16[2,256,512]{2,1,0:T(8,128)(2,1)} %get-tuple-element.74), channel_id=1, source_target_pairs={{0,24},{2,26},{4,28},{6,30},{8,0},{10,2},{12,4},{14,6},{16,8},{18,... | collective-permute-start | bytes 1572872 | tf_op jit(solution)/shard_map/ppermute | solution.py:1281
  284.5 48.0 %collective-permute-start.2 = (bf16[4,256,896]{2,1,0:T(8,128)(2,1)}, bf16[4,256,896]{2,1,0:T(8,128)(2,1)}, u32[]{:S(2)}, u32[]{:S(2)}) collective-permute-start(bf16[4,256,896]{2,1,0:T(8,128)(2,1)} %get-tuple-element.70), channel_id=1, source_target_pairs={{0,4},{2,6},{4,0},{6,2},{8,12},{10,14},{12,8},{14,10},{16,20},{18,... | collective-permute-start | bytes 5505032 | tf_op jit(solution)/shard_map/ppermute | solution.py:1281
  300.9 17.9 %copy-start.3 = (bf16[1024,2048]{1,0:T(8,128)(2,1)S(1)}, bf16[1024,2048]{1,0:T(8,128)(2,1)}, u32[]{:S(2)}) copy-start(bf16[1024,2048]{1,0:T(8,128)(2,1)} %get-tuple-element.66.ffn_in) | copy-start | bytes 12582916
  318.8 10.8 %copy-start.5 = (bf16[1024,1408]{1,0:T(8,128)(2,1)S(1)}, bf16[1024,1408]{1,0:T(8,128)(2,1)}, u32[]{:S(2)}) copy-start(bf16[1024,1408]{1,0:T(8,128)(2,1)} %get-tuple-element.105) | copy-start | bytes 8650756
  332.5 0.8 copy-start.16
  427.7 55.2 %collective-permute-start.7 = (bf16[2,256,512]{2,1,0:T(8,128)(2,1)}, bf16[2,256,512]{2,1,0:T(8,128)(2,1)S(1)}, u32[]{:S(2)}, u32[]{:S(2)}) collective-permute-start(bf16[2,256,512]{2,1,0:T(8,128)(2,1)} %get-tuple-element.82), channel_id=1, source_target_pairs={{0,8},{2,10},{4,12},{6,14},{8,16},{10,18},{12,20},{14,22},{16,24},... | collective-permute-start | bytes 1572872 | tf_op jit(solution)/shard_map/ppermute | solution.py:1281
  428.6 54.2 %collective-permute-start.8 = (bf16[2,256,512]{2,1,0:T(8,128)(2,1)}, bf16[2,256,512]{2,1,0:T(8,128)(2,1)}, u32[]{:S(2)}, u32[]{:S(2)}) collective-permute-start(bf16[2,256,512]{2,1,0:T(8,128)(2,1)} %get-tuple-element.83), channel_id=1, source_target_pairs={{0,16},{2,18},{4,20},{6,22},{8,24},{10,26},{12,28},{14,30},{16,0},... | collective-permute-start | bytes 1572872 | tf_op jit(solution)/shard_map/ppermute | solution.py:1281
  430.7 52.2 %collective-permute-start.9 = (bf16[2,256,512]{2,1,0:T(8,128)(2,1)}, bf16[2,256,512]{2,1,0:T(8,128)(2,1)}, u32[]{:S(2)}, u32[]{:S(2)}) collective-permute-start(bf16[2,256,512]{2,1,0:T(8,128)(2,1)} %get-tuple-element.84), channel_id=1, source_target_pairs={{0,24},{2,26},{4,28},{6,30},{8,0},{10,2},{12,4},{14,6},{16,8},{18,... | collective-permute-start | bytes 1572872 | tf_op jit(solution)/shard_map/ppermute | solution.py:1281
  431.6 51.3 %collective-permute-start.6 = (bf16[4,256,896]{2,1,0:T(8,128)(2,1)}, bf16[4,256,896]{2,1,0:T(8,128)(2,1)}, u32[]{:S(2)}, u32[]{:S(2)}) collective-permute-start(bf16[4,256,896]{2,1,0:T(8,128)(2,1)} %get-tuple-element.80), channel_id=1, source_target_pairs={{0,4},{2,6},{4,0},{6,2},{8,12},{10,14},{12,8},{14,10},{16,20},{18,... | collective-permute-start | bytes 5505032 | tf_op jit(solution)/shard_map/ppermute | solution.py:1281
  438.5 18.4 %copy-start.17 = (bf16[4,256,2048]{2,1,0:T(8,128)(2,1)S(1)}, bf16[4,256,2048]{2,1,0:T(8,128)(2,1)}, u32[]{:S(2)}) copy-start(bf16[4,256,2048]{2,1,0:T(8,128)(2,1)} %get-tuple-element.59) | copy-start | bytes 12582916
  438.5 30.4 %slice-start = ((s8[6815744]{0:T(1024)(128)(4,1)}), s8[2621440]{0:T(1024)(128)(4,1)S(1)}, s32[]{:S(2)}) async-start(s8[6815744]{0:T(1024)(128)(4,1)} %bitcast.49), calls=%async_computation | async-start | bytes 5242880
  456.9 11.9 %copy-start.4 = (bf16[1024,1664]{1,0:T(8,128)(2,1)S(1)}, bf16[1024,1664]{1,0:T(8,128)(2,1)}, u32[]{:S(2)}) copy-start(bf16[1024,1664]{1,0:T(8,128)(2,1)} %mixer_backward.1) | copy-start | bytes 10223620
  456.9 11.9 %slice-start.1 = ((s8[6815744]{0:T(1024)(128)(4,1)}), s8[4194304]{0:T(1024)(128)(4,1)S(1)}, s32[]{:S(2)}) async-start(s8[6815744]{0:T(1024)(128)(4,1)} %bitcast.49), calls=%async_computation.1 | async-start | bytes 8388608
  468.9 10.2 %copy-start.1 = (bf16[1024,512]{1,0:T(8,128)(2,1)S(1)}, bf16[1024,512]{1,0:T(8,128)(2,1)}, u32[]{:S(2)}) copy-start(bf16[1024,512]{1,0:T(8,128)(2,1)} %copy-done) | copy-start | bytes 3145732
  468.9 10.2 %copy-start.18 = (bf16[4,256,2048]{2,1,0:T(8,128)(2,1)S(1)}, bf16[4,256,2048]{2,1,0:T(8,128)(2,1)}, u32[]{:S(2)}) copy-start(bf16[4,256,2048]{2,1,0:T(8,128)(2,1)} %get-tuple-element.85) | copy-start | bytes 12582916
  482.8 0.8 copy-start.11
  605.7 6.1 copy-start.2
  611.9 2.1 copy-start.15
  611.9 2.9 copy-start.14
  611.9 3.7 copy-start.13
  611.9 4.5 copy-start.12
  614.0 3.2 copy-start.9
  614.0 4.3 copy-start.10
  615.6 3.8 copy-start.8

commit v8 on v7

--- a/solution.py
+++ b/solution.py
@@ -453,69 +453,341 @@
             copy.wait()
 
 
-def gather_first_kernel(
-    tokens, cot, seq_count, valid_len, gain0, gain1, q_w, k_w, v_w, forget_w, out_w, gate_w, up_w, down_w, w_in, w_out, ffn, own, attn_in, d_res, d_ffn, gains,
-    stage, seqs, normed, scales, turned, grads, low, small, sem
+class BlockTerms:
+    def __init__(self, sems, acts, grads, bufs, over, own, parts):
+        self.acts, self.grads, self.bufs = acts, grads, bufs
+        self.over, self.own, self.parts = over, own, parts
+        self.early = over.shape[2]
+        self.left, self.right = sems.some(2), sems.some(2)
+
+    def copies(self, slot, left, right):
+        early, rest = self.early, self.bufs.shape[2] - self.early
+        return (
+            pltpu.make_async_copy(self.bufs.at[slot, :, pl.ds(0, early)], left, self.left(slot)),
+            pltpu.make_async_copy(self.bufs.at[slot, :, pl.ds(early, rest)], right, self.right(slot)),
+        )
+
+    def wait(self, slot):
+        for copy in self.copies(slot, self.own.at[0], self.parts[0].at[0]):
+            copy.wait()
+
+    def run(self, start, stop):
+        width = self.bufs.shape[1]
+
+        def step(i, carry):
+            slot, side, away = i % 2, i // 4, i % 4
+
+            @pl.when(i >= 2)
+            def _():
+                self.wait(slot)
+
+            cols = pl.ds(pl.multiple_of(i * width, width), width)
+            self.bufs[slot] = mm(self.acts[:, cols], self.grads[...], TN, BF16)
+
+            @pl.when(side == 0)
+            def _():
+                self.copies(slot, self.own.at[away], self.parts[0].at[0])[0].start()
+
+            @pl.when(side == 1)
+            def _():
+                self.copies(slot, self.over.at[away], self.parts[0].at[0])[0].start()
+
+            for place in range(4):
+
+                @pl.when(away == place)
+                def _(place=place):
+                    self.copies(slot, self.own.at[0], self.parts[place].at[side])[1].start()
+
+            return carry
+
+        lax.fori_loop(start, stop, step, 0)
+
+    def finish(self):
+        self.wait(0)
+        self.wait(1)
+
+
+class WideMatmul:
+    def __init__(self, sems, acts, weight, stage, sums, hidden, wide):
+        self.acts, self.weight, self.stage, self.sums, self.hidden, self.wide = acts, weight, stage, sums, hidden, wide
+        self.hid = hidden.shape[1]
+        self.half = acts.shape[1] // 2
+        self.count = self.hid // 128
+        self.loads = [sems.some(2) for _ in range(2)]
+        self.stores = [sems.some(2) for _ in range(2)]
+
+    def columns(self, i, side):
+        return pl.ds(pl.multiple_of(side * self.hid + i * 128, 128), 128)
+
+    def fetch(self, i, phase):
+        return [
+            pltpu.make_async_copy(
+                self.weight.at[pl.ds(phase * self.half, self.half), self.columns(i, side)],
+                self.stage.at[i % 2, pl.ds(0, self.half), pl.ds(side * 128, 128)],
+                self.loads[side](i % 2),
+            )
+            for side in range(2)
+        ]
+
+    def leave(self, i):
+        return [
+            pltpu.make_async_copy(
+                self.sums.at[i, :, pl.ds(side * 128, 128)], self.wide.at[:, self.columns(i, side)], self.stores[side](i % 2)
+            )
+            for side in range(2)
+        ]
+
+    def begin(self, phase):
+        for copy in self.fetch(0, phase):
+            copy.start()
+
+    def run(self, phase):
+        def step(i, carry):
+            for copy in self.fetch(i, phase):
+                copy.wait()
+
+            @pl.when(i + 1 < self.count)
+            def _():
+                for copy in self.fetch(i + 1, phase):
+                    copy.start()
+
+            both = mm(self.acts[:, phase * self.half : (phase + 1) * self.half], self.stage[i % 2, : self.half])
+            if phase == 0:
+                self.sums[i] = both
+                return carry
+
+            @pl.when(i >= 2)
+            def _():
+                for copy in self.leave(i - 2):
+                    copy.wait()
+
+            both = both + self.sums[i]
+            self.sums[i] = both
+            gate = both[:, :128]
+            self.hidden[:, self.columns(i, 0)] = (gate / (1.0 + jnp.exp(-gate)) * both[:, 128:]).astype(BF16)
+            for copy in self.leave(i):
+                copy.start()
+            return carry
+
+        lax.fori_loop(0, self.count, step, 0)
+
+    def finish(self):
+        for i in (self.count - 2, self.count - 1):
+            for copy in self.leave(i):
+                copy.wait()
+
+
+class Chunk:
+    def __init__(self, place, sems, source, offset, width, target, first, y_first, stage):
+        shard = source.shape[0]
+        cols, span = pl.ds(first, width), source.shape[1] // 2
+        here, there = (pl.ds(pl.multiple_of(at * span + offset, 128), width) for at in (place.x, 1 - place.x))
+        where = target.at[place.half(shard), cols]
+        at = lambda index: target.at[pl.ds(index * 2 * shard, 2 * shard), cols]
+        self.y_first = y_first
+        self.swap = place.copy("x", source.at[:, there], where, sems.two())
+        self.keep = Keep(sems, source.at[:, here], where, stage)
+        ring = lambda side: [
+            place.copy("up", at((4 - i) % 4 + 4 * side), at(3 - i + 4 * side), sems.two()) for i in range(3)
+        ]
+        self.low = ring(0)
+        self.high = ring(1) if y_first else []
+        self.cross = [place.copy("y", at(i), at(4 + i), sems.two()) for i in ((0,) if y_first else (0, 3, 2, 1))]
+
+    def enter(self):
+        self.swap.start()
+        self.keep.start()
+
+    def launch(self):
+        self.keep.wait()
+        self.swap.wait_recv()
+
+    def pass_low(self, step, cross=True):
+        self.low[step].wait_recv()
+        if step < 2:
+            self.low[step + 1].start()
+        if cross and not self.y_first:
+            self.cross[step + 1].start()
+
+    def turn(self):
+        self.cross[0].wait_recv()
+        self.high[0].start()
+
+    def pass_high(self, step):
+        self.high[step].wait_recv()
+        if step < 2:
+            self.high[step + 1].start()
+
+    def crossed(self):
+        if not self.y_first:
+            for copy in self.cross:
+                copy.wait_recv()
+
+    def sent(self):
+        for copy in [self.swap] + self.low + self.high + self.cross:
+            copy.wait_send()
+
+
+class Loaded:
+    def __init__(self, value):
+        self.value = value
+
+    def __getitem__(self, index):
+        return self.value
+
+
+class Projections:
+    def __init__(self, sems, acts, weight, stage, sums, target):
+        self.acts, self.weight, self.stage, self.sums, self.target = acts, weight, stage, sums, target
+        self.loads, self.stores = sems.some(2), sems.some(7)
+
+    def fetch(self, i):
+        cols = pl.ds(pl.multiple_of(i * 256, 256), 256)
+        return pltpu.make_async_copy(self.weight.at[:, cols], self.stage.at[i % 2], self.loads(i % 2))
+
+    def fetch_last(self):
+        return pltpu.make_async_copy(
+            self.weight.at[:, pl.ds(3 * KDIM, 128)], self.stage.at[0, :, pl.ds(0, 128)], self.loads(0)
+        )
+
+    def leave(self, i, width=256):
+        cols = pl.ds(i * 256, width)
+        return pltpu.make_async_copy(self.sums.at[i, :, pl.ds(0, width)], self.target.at[:, cols], self.stores(i))
+
+    def run(self):
+        self.fetch(0).start()
+
+        def step(i, carry):
+            self.fetch(i).wait()
+
+            @pl.when(i < 5)
+            def _():
+                self.fetch(i + 1).start()
+
+            self.sums[i] = mm(self.acts[...], self.stage[i % 2])
+            return carry
+
+        lax.fori_loop(0, 6, step, 0)
+        last = self.fetch_last()
+        last.start()
+        last.wait()
+        self.sums[6, :, :128] = mm(self.acts[...], self.stage[0, :, :128])
+        for i in range(6):
+            self.leave(i).start()
+        self.leave(6, 128).start()
+
+    def mix(self, outs):
+        def step(i, carry):
+            rows = pl.ds(pl.multiple_of(i * SEQ_LEN, SEQ_LEN), SEQ_LEN)
+            pair = lambda j: Loaded(jnp.concatenate([self.sums[j, rows, :], self.sums[j + 1, rows, :]], axis=1))
+            forget = Loaded(self.sums[6, rows, :128])
+            forward_kernel(pair(0), pair(2), pair(4), forget, *(out.at[rows] for out in outs))
+            return carry
+
+        lax.fori_loop(0, 4, step, 0)
+
+    def finish(self):
+        for i in range(6):
+            self.leave(i).wait()
+        self.leave(6, 128).wait()
+
+
+class AttnTerms:
+    def __init__(self, sems, mixed, weight, bufs, target):
+        self.mixed, self.weight, self.bufs, self.target = mixed, weight, bufs, target
+        self.stores = sems.some(2)
+
+    def store(self, i):
+        width = self.bufs.shape[3]
+        cols = pl.ds(pl.multiple_of(i * width, width), width)
+        return pltpu.make_async_copy(self.bufs.at[i % 2], self.target.at[:, :, cols], self.stores(i % 2))
+
+    def run(self):
+        width = self.bufs.shape[3]
+
+        def step(i, carry):
+            @pl.when(i >= 2)
+            def _():
+                self.store(i).wait()
+
+            block = self.weight[pl.ds(pl.multiple_of(i * width, width), width), :]
+            self.bufs[i % 2] = mm(self.mixed[...], block, NT).reshape(4, SEQ_LEN, width)
+            self.store(i).start()
+            return carry
+
+        lax.fori_loop(0, 8, step, 0)
+        self.store(6).wait()
+        self.store(7).wait()
+
+
+def forward_all_kernel(
+    hid, cut, tokens, cot, seq_count, valid_len, gain0, gain1, q_w, k_w, v_w, forget_w, out_w, gate_w, up_w, down_w,
+    w_in, w_out, own, attn_in, d_res, d_ffn, gains, proj, save_p, save_s, save_a, save_b, save_mixed, terms,
+    w_wide, w_down, resid, ffn_in, wide, hidden, down_over, down_own, down0, down1, down2, down3,
+    stage, seqs, acts, scales, turned, grads, low, small, p_v, s_v, a_v, b_v, mixed_v, out_v, term_bufs,
+    s0, s1, s2, s3, kept, inputs, tiles, sums, hid_v, bufs, sem
 ):
     place, sems = Place(), Sems(sem)
     shard = q_w.shape[0]
-    rows = place.half(shard)
-    hid = gate_w.shape[1] // 2
-    chunks = [
-        (small, 0, 128, w_in, 3 * KDIM, True),
-        (q_w, 0, KDIM, w_in, 0, False),
-        (k_w, 0, KDIM, w_in, KDIM, False),
-        (v_w, 0, KDIM, w_in, 2 * KDIM, False),
-        (out_w, 0, KDIM // 2, w_out, 0, True),
-        (out_w, KDIM // 2, KDIM // 2, w_out, KDIM // 2, False),
-        (gate_w, 0, hid, ffn, 0, False),
-        (up_w, 0, hid, ffn, hid, False),
-        (down_w, 0, hid, ffn, 2 * hid, False),
+    used = 0
+
+    def chunk(source, offset, width, target, first, y_first):
+        nonlocal used
+        used += width
+        return Chunk(place, sems, source, offset, width, target, first, y_first, stage.at[:, pl.ds(used - width, width)])
+
+    first_chunks = [
+        chunk(small, 0, 128, w_in, 3 * KDIM, True),
+        chunk(q_w, 0, KDIM, w_in, 0, False),
+        chunk(k_w, 0, KDIM, w_in, KDIM, False),
+        chunk(v_w, 0, KDIM, w_in, 2 * KDIM, False),
+        chunk(out_w, 0, KDIM // 2, w_out, 0, True),
+        chunk(out_w, KDIM // 2, KDIM // 2, w_out, KDIM // 2, False),
     ]
-    full = len(chunks) - 3
-    swaps, keeps, rises, crosses = [], [], [], []
-    used = 0
-    for c, (source, offset, width, target, first, y_first) in enumerate(chunks):
-        cols = pl.ds(first, width)
-        where = target.at[0, rows, cols] if c < full else target.at[rows, cols]
-        span = source.shape[1] // 2
-        here, there = (pl.ds(pl.multiple_of(at * span + offset, 128), width) for at in (place.x, 1 - place.x))
-        swaps.append(place.copy("x", source.at[:, there], where, sems.two()))
-        keeps.append(Keep(sems, source.at[:, here], where, stage.at[:, pl.ds(used, width)]))
-        used += width
-        if c >= full:
-            continue
-
-        def block(index, target=target, cols=cols):
-            return target.at[index, :, cols]
-
-        rises.append(
-            [
-                [place.copy("up", block((4 - step) % 4 + 4 * u), block(3 - step + 4 * u), sems.two()) for step in range(3)]
-                for u in range(2 if y_first else 1)
-            ]
-        )
-        crosses.append(
-            [place.copy("y", block(i), block(4 + i), sems.two()) for i in range(1 if y_first else 4)]
-        )
+    gate = chunk(gate_w, 0, hid, w_wide, 0, False)
+    up = chunk(up_w, 0, hid, w_wide, hid, False)
+    down = chunk(down_w, 0, cut, w_down, 0, False)
+    rest = chunk(down_w, cut, hid - cut, w_down, cut, True)
+    ffn_chunks = [gate, up, down, rest]
     width = tokens.shape[1] // 8
     mine = pl.ds(pl.multiple_of(place.core * SEQ_LEN, SEQ_LEN), SEQ_LEN)
+    slot = [pl.ds(i * SEQ_LEN, SEQ_LEN) for i in range(4)]
     far, side, fetch, fetch_cot = [], [], [], []
     for index in range(8):
         part = tokens.at[mine, place.columns(index, width)]
         cols = pl.ds(index * width, width)
-        far.append(place.copy("x", part, seqs.at[1, :, cols], sems.two()))
-        side.append(place.copy("core", part, seqs.at[2, :, cols], sems.two()))
-        fetch.append(pltpu.make_async_copy(part, seqs.at[0, :, cols], sems.one()))
+        far.append(place.copy("x", part, seqs.at[slot[1], cols], sems.two()))
+        side.append(place.copy("core", part, seqs.at[slot[2], cols], sems.two()))
+        fetch.append(pltpu.make_async_copy(part, seqs.at[slot[0], cols], sems.one()))
         fetch_cot.append(
             pltpu.make_async_copy(cot.at[mine, place.columns(index, width)], grads.at[:, cols], sems.one())
         )
-    last = place.copy("core", seqs.at[1], seqs.at[3], sems.two())
-    quad = Quad(place, sems, low, [d_ffn.at[i] for i in range(4)])
-    save_own = pltpu.make_async_copy(seqs.at[0], own, sems.one())
+    last = place.copy("core", seqs.at[slot[1]], seqs.at[slot[3]], sems.two())
+    quad = Quad(place, sems, low, [d_ffn.at[one] for one in slot])
+    save_own = pltpu.make_async_copy(seqs.at[slot[0]], own, sems.one())
+    keep_own = pltpu.make_async_copy(seqs.at[slot[0]], inputs, sems.one())
     save_res = pltpu.make_async_copy(grads, d_res, sems.one())
-    save_in = [pltpu.make_async_copy(normed.at[i], attn_in.at[i], sems.one()) for i in range(4)]
-    load_gains = [pltpu.make_async_copy(w_in.at[i, :, pl.ds(3 * KDIM, 128)], turned.at[i], sems.one()) for i in range(8)]
+    save_attn = pltpu.make_async_copy(acts, attn_in, sems.one())
+    load_gains = [
+        pltpu.make_async_copy(w_in.at[pl.ds(i * width, width), pl.ds(3 * KDIM, 128)], turned.at[i], sems.one())
+        for i in range(8)
+    ]
+    load_out = pltpu.make_async_copy(w_out, out_v, sems.one())
+    projections = Projections(sems, acts, w_in, tiles, sums, proj)
+    saves = [
+        pltpu.make_async_copy(a, b, sems.one())
+        for a, b in ((p_v, save_p), (s_v, save_s), (a_v, save_a), (b_v, save_b), (mixed_v, save_mixed))
+    ]
+    attn_terms = AttnTerms(sems, mixed_v, out_v, term_bufs, terms)
+    total = QuadSum(place, sems, terms, (s0, s1, s2, s3))
+    slots = [acts.at[one] for one in slot]
+    out = Quad(place, sems, slots[0], [None] + slots[1:])
+    save = pltpu.make_async_copy(kept, resid, sems.one())
+    save_in = pltpu.make_async_copy(acts, ffn_in, sems.one())
+    save_hidden = pltpu.make_async_copy(hid_v, hidden, sems.one())
+    fetch_cots = pltpu.make_async_copy(d_ffn, seqs, sems.one())
+    matmul = WideMatmul(sems, acts, w_wide, tiles, sums, hid_v, wide)
+    grad = BlockTerms(sems, seqs, hid_v, bufs, down_over, down_own, (down0, down1, down2, down3))
     lane = lax.broadcasted_iota(jnp.int32, (shard, 128), 1)
     column = jnp.concatenate([gain0[...].astype(F32).reshape(1, shard), gain1[...].astype(F32).reshape(1, shard)], axis=0)
     column = jnp.concatenate([column, jnp.zeros((6, shard), F32)], axis=0).T
@@ -524,24 +796,22 @@
     small[:, :128] = jnp.where(lane < SLOTS, heads, beside).astype(BF16)
     small[:, 128:] = jnp.where(lane < SLOTS, pltpu.roll(heads, SLOTS, 1), beside).astype(BF16)
     place.greet()
-    for swap, keep in zip(swaps[:full], keeps[:full]):
-        swap.start()
-        keep.start()
+    for one in first_chunks:
+        one.enter()
     for copy in far + side + fetch + fetch_cot:
         copy.start()
-    for swap, keep in zip(swaps[full:], keeps[full:]):
-        swap.start()
-        keep.start()
-    for keep in keeps:
-        keep.turn()
-    for c in range(full):
-        keeps[c].wait()
-        swaps[c].wait_recv()
-        rises[c][0][0].start()
-        crosses[c][0].start()
+    for one in ffn_chunks:
+        one.enter()
+    for one in first_chunks + ffn_chunks:
+        one.keep.turn()
+    for one in first_chunks:
+        one.launch()
+        one.low[0].start()
+        one.cross[0].start()
     for copy in fetch + fetch_cot:
         copy.wait()
     save_own.start()
+    keep_own.start()
 
     def mask(part):
         value = grads[part] * live_rows(place, seq_count, valid_len, part)
@@ -551,36 +821,32 @@
     pieces(SEQ_LEN, mask)
     save_res.start()
     quad.start()
-    for c in range(full):
-        if chunks[c][5]:
-            crosses[c][0].wait_recv()
-            rises[c][1][0].start()
-
-    def measure(slot):
-        def one(part):
-            scales[slot, part] = jnp.broadcast_to(rms(seqs[slot, part].astype(F32)), (PIECE, 128))
-
-        pieces(SEQ_LEN, one)
-
-    def norm(slot):
-        def one(part):
-            value = seqs[slot, part].astype(F32) * scales[slot, part, :1] * gains[0:1, :]
-            normed[slot, part] = value.astype(BF16)
-
-        pieces(SEQ_LEN, one)
-        save_in[slot].start()
+    for one in first_chunks:
+        if one.y_first:
+            one.turn()
+
+    def measure(index):
+        def work(part):
+            rows = pl.ds(index * SEQ_LEN + part.start, PIECE)
+            scales[rows] = jnp.broadcast_to(rms(seqs[rows].astype(F32)), (PIECE, 128))
+
+        pieces(SEQ_LEN, work)
+
+    def norm_first(index):
+        def work(part):
+            rows = pl.ds(index * SEQ_LEN + part.start, PIECE)
+            acts[rows] = (seqs[rows].astype(F32) * scales[rows, :1] * gains[0:1, :]).astype(BF16)
+
+        pieces(SEQ_LEN, work)
 
     for step in range(3):
-        for c in range(full):
-            for rise in rises[c]:
-                rise[step].wait_recv()
-                if step < 2:
-                    rise[step + 1].start()
-            if not chunks[c][5]:
-                crosses[c][3 - step].start()
+        for c, one in enumerate(first_chunks):
+            one.pass_low(step)
+            if one.y_first:
+                one.pass_high(step)
             if step == 0 and c == 1:
                 measure(0)
-            if step == 0 and c == full - 1:
+            if step == 0 and c == 5:
                 for copy in far:
                     copy.wait_recv()
                 last.start()
@@ -600,226 +866,41 @@
                         flipped = turned[index].astype(F32).T
                         gains[0:8, index * width : (index + 1) * width] = flipped[SLOTS : SLOTS + 8]
                 if 1 <= c <= 4:
-                    norm(c - 1)
+                    norm_first(c - 1)
+        if step == 1:
+            for one in ffn_chunks:
+                one.launch()
+                one.low[0].start()
+    for one in (gate, up, rest):
+        one.cross[0].start()
+    save_attn.start()
     quad.forward()
-    for c in range(full):
-        for cross in crosses[c]:
-            cross.wait_send()
-            if not chunks[c][5]:
-                cross.wait_recv()
-        for rise in rises[c]:
-            for copy in rise:
-                copy.wait_send()
-    for swap in swaps[:full]:
-        swap.wait_send()
-    for swap, keep in zip(swaps[full:], keeps[full:]):
-        swap.wait()
-        keep.wait()
-    for copy in far + side + [last]:
+    for one in first_chunks:
+        one.crossed()
+    load_out.start()
+    projections.run()
+    gate.pass_low(0)
+    projections.mix((mixed_v, p_v, s_v, a_v, b_v))
+    for copy in saves:
+        copy.start()
+    up.pass_low(0)
+    load_out.wait()
+    attn_terms.run()
+    save_attn.wait()
+    total.start()
+    rest.turn()
+    total.middle()
+    quad.finish()
+    save_own.wait()
+    keep_own.wait()
+    for copy in side + [last]:
         copy.wait_send()
-    for copy in save_in + [save_own, save_res]:
-        copy.wait()
-    quad.finish()
-
-
-class BlockTerms:
-    def __init__(self, sems, acts, grads, bufs, over, own, parts):
-        self.acts, self.grads, self.bufs = acts, grads, bufs
-        self.over, self.own, self.parts = over, own, parts
-        self.early = over.shape[2]
-        self.left, self.right = sems.some(2), sems.some(2)
-
-    def copies(self, slot, left, right):
-        early, rest = self.early, self.bufs.shape[2] - self.early
-        return (
-            pltpu.make_async_copy(self.bufs.at[slot, :, pl.ds(0, early)], left, self.left(slot)),
-            pltpu.make_async_copy(self.bufs.at[slot, :, pl.ds(early, rest)], right, self.right(slot)),
-        )
-
-    def wait(self, slot):
-        for copy in self.copies(slot, self.own.at[0], self.parts[0].at[0]):
-            copy.wait()
-
-    def run(self, start, stop):
-        width = self.bufs.shape[1]
-
-        def step(i, carry):
-            slot, side, away = i % 2, i // 4, i % 4
-
-            @pl.when(i >= 2)
-            def _():
-                self.wait(slot)
-
-            cols = pl.ds(pl.multiple_of(i * width, width), width)
-            self.bufs[slot] = mm(self.acts[:, cols], self.grads[...], TN, BF16)
-
-            @pl.when(side == 0)
-            def _():
-                self.copies(slot, self.own.at[away], self.parts[0].at[0])[0].start()
-
-            @pl.when(side == 1)
-            def _():
-                self.copies(slot, self.over.at[away], self.parts[0].at[0])[0].start()
-
-            for place in range(4):
-
-                @pl.when(away == place)
-                def _(place=place):
-                    self.copies(slot, self.own.at[0], self.parts[place].at[side])[1].start()
-
-            return carry
-
-        lax.fori_loop(start, stop, step, 0)
-
-    def finish(self):
-        self.wait(0)
-        self.wait(1)
-
-
-class WideMatmul:
-    def __init__(self, sems, acts, weight, stage, sums, hidden, wide):
-        self.acts, self.weight, self.stage, self.sums, self.hidden, self.wide = acts, weight, stage, sums, hidden, wide
-        self.hid = hidden.shape[1]
-        self.half = acts.shape[1] // 2
-        self.count = self.hid // 128
-        self.loads = [sems.some(2) for _ in range(2)]
-        self.stores = [sems.some(2) for _ in range(2)]
-
-    def columns(self, i, side):
-        return pl.ds(pl.multiple_of(side * self.hid + i * 128, 128), 128)
-
-    def fetch(self, i, phase):
-        return [
-            pltpu.make_async_copy(
-                self.weight.at[pl.ds(phase * self.half, self.half), self.columns(i, side)],
-                self.stage.at[i % 2, :, pl.ds(side * 128, 128)],
-                self.loads[side](i % 2),
-            )
-            for side in range(2)
-        ]
-
-    def leave(self, i):
-        return [
-            pltpu.make_async_copy(
-                self.sums.at[i, :, pl.ds(side * 128, 128)], self.wide.at[:, self.columns(i, side)], self.stores[side](i % 2)
-            )
-            for side in range(2)
-        ]
-
-    def begin(self, phase):
-        for copy in self.fetch(0, phase):
-            copy.start()
-
-    def run(self, phase, start, stop):
-        def step(i, carry):
-            for copy in self.fetch(i, phase):
-                copy.wait()
-
-            @pl.when(i + 1 < self.count)
-            def _():
-                for copy in self.fetch(i + 1, phase):
-                    copy.start()
-
-            both = mm(self.acts[:, phase * self.half : (phase + 1) * self.half], self.stage[i % 2])
-            if phase == 0:
-                self.sums[i] = both
-                return carry
-
-            @pl.when(i >= 2)
-            def _():
-                for copy in self.leave(i - 2):
-                    copy.wait()
-
-            both = both + self.sums[i]
-            self.sums[i] = both
-            gate = both[:, :128]
-            self.hidden[:, self.columns(i, 0)] = (gate / (1.0 + jnp.exp(-gate)) * both[:, 128:]).astype(BF16)
-            for copy in self.leave(i):
-                copy.start()
-            return carry
-
-        lax.fori_loop(start, stop, step, 0)
-
-    def finish(self):
-        for i in (self.count - 2, self.count - 1):
-            for copy in self.leave(i):
-                copy.wait()
-
-
-def gather_ffn_kernel(
-    hid, cut, b0, b3, b4, terms, tokens, gains, d_ffn,
-    w_wide, w_down, resid, ffn_in, wide, hidden, down_over, down_own, down0, down1, down2, down3,
-    s0, s1, s2, s3, kept, acts, inputs, stage, tiles, sums, hid_v, cots, bufs, sem
-):
-    place, sems = Place(), Sems(sem)
-    rows = b0.shape[0]
-    keeps = []
-
-    def block(target, index, start, width):
-        return target.at[pl.ds(index * rows, rows), pl.ds(start, width)]
-
-    def chunk(first, width, target, start, y_first):
-        source = pl.ds(first, width)
-        at = lambda index: block(target, index, start, width)
-        for i, (b, index) in enumerate(((b0, 0), (b3, 3), (b4, 4))):
-            keeps.append(Keep(sems, b.at[:, source], at(index), stage.at[i, :, source]))
-        low = [
-            place.copy("up", b3.at[:, source], at(2), sems.two()),
-            place.copy("up", at(2), at(1), sems.two()),
-        ]
-        if y_first:
-            return (
-                low,
-                [
-                    place.copy("up", b4.at[:, source], at(7), sems.two()),
-                    place.copy("up", at(7), at(6), sems.two()),
-                    place.copy("up", at(6), at(5), sems.two()),
-                ],
-                [],
-            )
-        return (
-            low,
-            [],
-            [
-                place.copy("y", b3.at[:, source], at(7), sems.two()),
-                place.copy("y", at(2), at(6), sems.two()),
-                place.copy("y", at(1), at(5), sems.two()),
-            ],
-        )
-
-    gate = chunk(0, hid, w_wide, 0, False)
-    up = chunk(hid, hid, w_wide, hid, False)
-    down = chunk(2 * hid, cut, w_down, 0, False)
-    rest = chunk(2 * hid + cut, hid - cut, w_down, cut, True)
-    total = QuadSum(place, sems, terms, (s0, s1, s2, s3))
-    slots = [acts.at[pl.ds(i * SEQ_LEN, SEQ_LEN)] for i in range(4)]
-    out = Quad(place, sems, slots[0], [None] + slots[1:])
-    fetch = pltpu.make_async_copy(tokens, inputs, sems.one())
-    save = pltpu.make_async_copy(kept, resid, sems.one())
-    save_in = pltpu.make_async_copy(acts, ffn_in, sems.one())
-    save_hidden = pltpu.make_async_copy(hid_v, hidden, sems.one())
-    fetch_cots = pltpu.make_async_copy(d_ffn, cots, sems.one())
-    matmul = WideMatmul(sems, acts, w_wide, tiles, sums, hid_v, wide)
-    grad = BlockTerms(sems, cots, hid_v, bufs, down_over, down_own, (down0, down1, down2, down3))
-    place.greet()
-    total.start()
-    fetch.start()
-    for low, _, cross in (gate, up):
-        low[0].start()
-        cross[0].start()
-    for copy in keeps:
-        copy.start()
-    total.middle()
-    for copy in keeps:
-        copy.turn()
-    fetch.wait()
-    for low, _, cross in (gate, up):
-        low[0].wait_recv()
-        low[1].start()
-        cross[1].start()
-    rest[1][0].start()
-    down[0][0].start()
-    rest[0][0].start()
+    fetch_cots.start()
+    gate.pass_low(1)
+    up.pass_low(1)
+    down.pass_low(0, False)
+    rest.pass_low(0)
+    rest.pass_high(0)
     total.ready()
 
     def norm(part):
@@ -830,52 +911,38 @@
     pieces(SEQ_LEN, norm)
     out.start()
     save.start()
-    for low, _, cross in (gate, up):
-        low[1].wait_recv()
-        cross[2].start()
-    down[2][0].start()
-    fetch_cots.start()
-    rest[1][0].wait_recv()
-    rest[1][1].start()
+    gate.pass_low(2)
+    up.pass_low(2)
+    down.cross[0].start()
+    down.cross[1].start()
     out.forward()
-    for copy in keeps[:6]:
-        copy.wait()
     out.finish()
     save_in.start()
+    projections.finish()
     matmul.begin(0)
-    matmul.run(0, 0, matmul.count // 2)
-    down[0][0].wait_recv()
-    down[0][1].start()
-    down[2][1].start()
-    matmul.run(0, matmul.count // 2, matmul.count)
-    rest[0][0].wait_recv()
-    rest[0][1].start()
-    for copy in gate[2] + up[2]:
-        copy.wait_recv()
-    rest[1][1].wait_recv()
-    rest[1][2].start()
+    matmul.run(0)
+    down.pass_low(1)
+    rest.pass_low(1)
+    rest.pass_high(1)
+    gate.crossed()
+    up.crossed()
     matmul.begin(1)
-    matmul.run(1, 0, matmul.count // 2)
-    down[0][1].wait_recv()
-    down[2][2].start()
-    matmul.run(1, matmul.count // 2, matmul.count)
+    matmul.run(1)
+    down.pass_low(2)
     save_hidden.start()
     fetch_cots.wait()
     grad.run(0, 8)
-    for copy in down[2]:
-        copy.wait_recv()
-    rest[0][1].wait_recv()
-    rest[1][2].wait_recv()
-    for low, high, cross in (gate, up, down, rest):
-        for copy in low + high + cross:
-            copy.wait_send()
-    for copy in keeps[6:]:
+    rest.pass_low(2)
+    rest.pass_high(2)
+    down.crossed()
+    for one in first_chunks + ffn_chunks:
+        one.sent()
+    for copy in far:
+        copy.wait_send()
+    for copy in saves + [save_res, save, save_in, save_hidden]:
         copy.wait()
     matmul.finish()
     grad.finish()
-    save.wait()
-    save_in.wait()
-    save_hidden.wait()
 
 
 class Sum:
@@ -1097,7 +1164,6 @@
     for copy in fetch + ready:
         copy.wait()
     down_y.step(1)
-    up.run(0, 4)
     back.ready()
     gain_sum[...] = jnp.zeros_like(gain_sum)
 
@@ -1114,7 +1180,7 @@
     for one in gate:
         one.step(1)
     down_y.step(2)
-    up.run(4, 8)
+    up.run(0, 8)
     down_z.second()
     for one in gate:
         one.step(2)
@@ -1546,7 +1612,7 @@
 ):
     shard, dim = q_weight.shape[0], tokens.shape[1]
     width, hid = 2 * shard, gate_weight.shape[1] // 2
-    up_z, over_y = (lambda value: ring.send(value, ring.stages[0], 1)), (lambda value: ring.send(value, ring.stages[1], 1))
+    over_y = lambda value: ring.send(value, ring.stages[1], 1)
     rows4 = (4, SEQ_LEN, dim)
     blocks = lambda value: value.reshape(-1, width, value.shape[-1])
     flat = lambda value: value.reshape(-1, value.shape[-1])
@@ -1554,9 +1620,16 @@
 
     row = (SEQ_LEN, dim)
     vmem = lambda shape, kind=F32: pltpu.VMEM(shape, kind)
-    w_in, w_out, part0, own, attn_in, d_res, d_ffn, gain_rows = call(
-        gather_first_kernel,
-        "gather_first",
+    tokens4 = 4 * SEQ_LEN
+    cut = hid // 256 * 128 + 128
+    full = (tokens4, dim)
+    early, rest = [((4, width, EARLY), BF16)] * 2, [((2, width, hid - EARLY), BF16)] * 4
+    (
+        w_in, w_out, own, attn_in, d_res, d_ffn, gain_rows, proj, *saved, mixed, _,
+        w_wide, w_down, resid, ffn_in, wide, hidden, down_over, down_own, down0, down1, down2, down3,
+    ) = call(
+        functools.partial(forward_all_kernel, hid, cut),
+        "forward_all",
         0,
         (
             tokens,
@@ -1575,60 +1648,43 @@
             down_weight,
         ),
         [ANY, ANY, SMEM, SMEM, VMEM, VMEM, ANY, ANY, ANY, VMEM] + [ANY] * 4,
-        [
-            ((8, width, WIDE), BF16),
-            ((8, width, KDIM), BF16),
-            ((width, 3 * hid), BF16),
-            (row, BF16),
-            (rows4, BF16),
-            (row, F32),
-            (rows4, BF16),
-            ((8, dim), F32),
-        ],
-        [ANY] * 7 + [VMEM],
+        [((dim, WIDE), BF16), ((dim, KDIM), BF16), (row, BF16), (full, BF16), (row, F32), (full, BF16), ((8, dim), F32)]
+        + [((tokens4, WIDE), F32), ((tokens4, 128), F32), ((tokens4, 128), F32)]
+        + [((tokens4, SEQ_LEN), F32), ((tokens4, SEQ_LEN), F32), ((tokens4, KDIM), BF16), (rows4, F32)]
+        + [((dim, 2 * hid), BF16), ((dim, hid), BF16), (row, F32), (full, BF16)]
+        + [((tokens4, 2 * hid), F32), ((tokens4, hid), BF16)]
+        + early
+        + rest,
+        [ANY] * 6 + [VMEM] + [ANY] * 19,
         [
             vmem((shard, 4 * KDIM + 128 + 3 * hid), BF16),
-            vmem(rows4, BF16),
-            vmem(rows4, BF16),
-            vmem((4, SEQ_LEN, 128)),
+            vmem(full, BF16),
+            vmem(full, BF16),
+            vmem((tokens4, 128)),
             vmem((8, width, 128), BF16),
             vmem(row),
             vmem(row, BF16),
             vmem((shard, 256), BF16),
+            vmem((tokens4, 128)),
+            vmem((tokens4, 128)),
+            vmem((tokens4, SEQ_LEN)),
+            vmem((tokens4, SEQ_LEN)),
+            vmem((tokens4, KDIM), BF16),
+            vmem((dim, KDIM), BF16),
+            vmem((2, 4, SEQ_LEN, width)),
+        ]
+        + quad_scratch(dim)
+        + [
+            vmem(row),
+            vmem(row, BF16),
+            vmem((2, dim, 256), BF16),
+            vmem((hid // 128, tokens4, 256)),
+            vmem((tokens4, hid), BF16),
+            vmem((2, width, hid), BF16),
         ],
-        240,
+        360,
     )
-    part3, part4 = up_z(part0), over_y(part0)
-    w_in, w_out, attn_in, d_ffn = map(flat, (w_in, w_out, attn_in, d_ffn))
-    proj = mm(attn_in, w_in)
-    mixed, *saved = mixer_forward(proj)
-    attn_terms = mm(mixed, w_out, NT).reshape(rows4)
-    cut = hid // 256 * 128 + 128
-    tokens4 = 4 * SEQ_LEN
-    early, rest = [((4, width, EARLY), BF16)] * 2, [((2, width, hid - EARLY), BF16)] * 4
-    w_wide, w_down, resid, ffn_in, wide, hidden, down_over, down_own, *down_parts = call(
-        functools.partial(gather_ffn_kernel, hid, cut),
-        "gather_ffn",
-        1,
-        (part0, part3, part4, attn_terms, own, gain_rows, d_ffn),
-        [ANY] * 5 + [VMEM, ANY],
-        [
-            ((dim, 2 * hid), BF16),
-            ((dim, hid), BF16),
-            (row, F32),
-            ((tokens4, dim), BF16),
-            ((tokens4, 2 * hid), F32),
-            ((tokens4, hid), BF16),
-        ]
-        + early
-        + rest,
-        [ANY] * 12,
-        quad_scratch(dim)
-        + [vmem(row), vmem((tokens4, dim), BF16), vmem(row, BF16), vmem((3, width, 3 * hid), BF16)]
-        + [vmem((2, dim // 2, 256), BF16), vmem((hid // 128, tokens4, 256)), vmem((tokens4, hid), BF16)]
-        + [vmem((tokens4, dim), BF16), vmem((2, width, hid), BF16)],
-        180,
-    )
+    down_parts = [down0, down1, down2, down3]
 
     def exchange(over, parts):
         return [over_y(over)] + [ring.send(parts[d], ring.stages[0], d) for d in (1, 2, 3)]

time: 631 us -> 615 us (0.975)
  Pallas kernels: 475 us -> 503 us
  matrix products: 93.8 us -> 70.7 us
  waiting for transfers between devices: 15.4 us -> 0.02 us
    pallas_call x4 -> x3, Pallas kernels: 444 us -> 485 us  [call(): pl.pallas_call(kernel, in_specs=specs, out_specs=out_specs, out_shape=[ja...]
    dot_general x9 -> x7, matrix products: 93.8 us -> 70.7 us  [mm(): lax.dot_general(left, right, dims, preferred_element_type=F32).astype(kind)]
    ppermute x10 -> x8, waiting for transfers between devices: 15.4 us -> 0.02 us  [send(): return lax.ppermute(value, 'dp', self.perm(stride, size, shift % size))]
    pallas_call x1 -> x0, Pallas kernels: 12.8 us -> none  [mixer_forward(): pl.pallas_call(forward_kernel, grid=(rows // SEQ_LEN,), in_specs=IN_SPECS...]
    ppermute x10 -> x8, starting transfers between devices: 12.8 us -> 10.3 us  [send(): return lax.ppermute(value, 'dp', self.perm(stride, size, shift % size))]
    unnamed x53 -> x59, local copies, waits for them, and re-layouts: 16 us -> 14.5 us
  transfers between devices with their start and end apart: 10 -> 8, of which waited for: 2 -> 0; matrix products, arithmetic and copies ran while one was open for 16% -> 12% of each run, Pallas kernels for 5% -> 3%
where the time goes in v8:
time: 615 us; the launch traced here: 607 us
  Pallas kernels  503 us (82%)
  matrix products  70.7 us (11%)
  local copies, waits for them, and re-layouts  16.7 us (3%)
  starting transfers between devices  10.3 us (2%)
    pallas_call x3, Pallas kernels, call(): pl.pallas_call(kernel, in_specs=specs, out_specs=out_specs, out_shape=[ja...  485 us
    dot_general x7, matrix products, mm(): lax.dot_general(left, right, dims, preferred_element_type=F32).astype(kind)  70.7 us
    pallas_call x1, Pallas kernels, mixer_backward(): pl.pallas_call(backward_kernel, grid=(rows // SEQ_LEN,), in_specs=IN_SPEC...  18.4 us
    unnamed x59, local copies, waits for them, and re-layouts  14.5 us
  transfers between devices with their start and end apart: 8, of which 0 were waited for; matrix products, arithmetic and copies ran while one was open for 12% of the time, Pallas kernels for 3%

profile of v8, /device:TPU:0, one launch (start us, length us, event | category | flops | bytes accessed | tf_op | source)
XLA Modules:
  0.0 606.6 jit_solution(3500979364255628592)
XLA Ops:
  1.3 268.0 %forward_all.1 = (bf16[2048,1664]{1,0:T(8,128)(2,1)}, bf16[2048,512]{1,0:T(8,128)(2,1)}, bf16[256,2048]{1,0:T(8,128)(2,1)}, bf16[1024,2048]{1,0:T(8,128)(2,1)}, ...) custom-call(bf16[512,2048]{1,0:T(8,128)(2,1)} %tokens.1, ...), custom_call_target="tpu_custom_call" | custom-call | tf_op jit(solution)/shard_map/forward_all/pallas_call | solution.py:1312
  269.3 1.1 collective-permute-start.1
  270.9 2.4 collective-permute-start.3
  273.4 1.0 collective-permute-start
  274.4 14.1 %multiply_convert_fusion = (bf16[1024,1408]{1,0:T(8,128)(2,1)S(1)}, bf16[1024,1408]{1,0:T(8,128)(2,1)S(1)}) fusion(f32[1024,2816]{1,0:T(8,128)} %get-tuple-element.61, bf16[1024,2048]{1,0:T(8,128)(2,1)} %get-tuple-element.59, bf16[2048,1408]{1,0:T(8,128)(2,1)} %get-tuple-element.60), kind=kOutput, calls=%fused_computation.3 | convolution fusion | flops 5924323328 | bytes 27262976 | tf_op jit(solution)/shard_map/dot_general | solution.py:1431
  288.4 17.1 %fusion = f32[1024,2048]{1,0:T(8,128)} fusion(bf16[2048,2816]{1,0:T(8,128)(2,1)} %get-tuple-element.68, bf16[1024,1408]{1,0:T(8,128)(2,1)S(1)} %get-tuple-element.104, bf16[1024,1408]{1,0:T(8,128)(2,1)S(1)} %get-tuple-element.105), kind=kOutput, calls=%fused_computation.10 | convolution fusion | flops 11822694400 | bytes 25690112 | tf_op jit(solution)/shard_map/dot_general | solution.py:1431
  305.6 8.6 %convolution_convert_fusion.1 = bf16[2048,1408]{1,0:T(8,128)(2,1)} fusion(bf16[1024,2048]{1,0:T(8,128)(2,1)S(1)} %copy-done.5, bf16[1024,1408]{1,0:T(8,128)(2,1)S(1)} %get-tuple-element.105), kind=kOutput, calls=%fused_computation.1 | convolution fusion | flops 5908463616 | bytes 12845056 | tf_op jit(solution)/shard_map/dot_general | solution.py:1431
  314.2 2.9 pad_maximum_fusion.d_wide
  317.2 0.8 copy-done.18
  318.1 94.5 %sum_ffn.1 = (f32[128,2816]{1,0:T(8,128)}, f32[128,2816]{1,0:T(8,128)}, f32[256,2048]{1,0:T(8,128)}, bf16[4,256,2048]{2,1,0:T(8,128)(2,1)}, f32[8,2048]{1,0:T(8,...) custom-call(bf16[8,256,1408]{2,1,0:T(8,128)(2,1)} %bitcast.30, ...), custom_call_target="tpu_custom_call" | custom-call | tf_op jit(solution)/shard_map/sum_ffn/pallas_call | solution.py:1312
  412.6 0.9 collective-permute-start.5
  413.5 2.1 collective-permute-start.6
  415.6 0.9 collective-permute-start.7
  416.5 1.4 collective-permute-start.4
  417.9 5.3 fusion.2.d_ref
  423.3 18.4 %mixer_backward.1 = bf16[1024,1664]{1,0:T(8,128)(2,1)} custom-call(f32[1024,1664]{1,0:T(8,128)} %get-tuple-element.82.q_ref.k_ref.v_ref.f_ref, f32[1024,1664]{1,0:T(8,128)} %get-tuple-element.82.q_ref.k_ref.v_ref.f_ref, f32[1024,1664]{1,0:T(8,128)} %get-tuple-element.82.q_ref.k_ref.v_ref.f_ref, f32[1024,1664]{1,0:T(8,128)} %get-tuple-element.82.q_ref.k_ref.v_ref.f_ref, ...), custom_call_target="tpu_custom_call" | custom-call | flops 9216000000 | bytes 16384000 | tf_op jit(solution)/shard_map/mixer_backward/pallas_call | solution.py:266
  441.8 11.5 %fusion.3 = f32[1024,2048]{1,0:T(8,128)} fusion(bf16[1024,1664]{1,0:T(8,128)(2,1)} %mixer_backward.1, bf16[2048,1664]{1,0:T(8,128)(2,1)S(1)} %bitcast.33), kind=kOutput, calls=%fused_computation.13 | convolution fusion | flops 6979321856 | bytes 18612224 | tf_op jit(solution)/shard_map/dot_general | solution.py:1431
  453.3 10.3 %convolution_convert_fusion = bf16[2048,1664]{1,0:T(8,128)(2,1)} fusion(bf16[1024,2048]{1,0:T(8,128)(2,1)S(1)} %copy-done.20, bf16[1024,1664]{1,0:T(8,128)(2,1)S(1)} %copy-done.6), kind=kOutput, calls=%fused_computation | convolution fusion | flops 6982729728 | bytes 14417920 | tf_op jit(solution)/shard_map/dot_general | solution.py:1431
  463.6 3.8 convolution_convert_fusion.2
  467.5 0.7 copy-done.11
  469.2 122.2 %sum_last.1 = (f32[128,2816]{1,0:T(8,128)}, f32[128,1024]{1,0:T(8,128)}, f32[128,1024]{1,0:T(8,128)}, f32[128,1024]{1,0:T(8,128)}, f32[128,1024]{1,0:T(8,128)}, ...) custom-call(bf16[4,256,896]{2,1,0:T(8,128)(2,1)} %get-tuple-element.73.up, ...), custom_call_target="tpu_custom_call" | custom-call | tf_op jit(solution)/shard_map/sum_last/pallas_call | solution.py:1312
  591.4 1.3 slice_bitcast_fusion
  592.8 0.9 fusion.1
  594.4 3.2 copy.36
  597.6 2.1 copy.37
  599.7 0.8 copy.38
  600.5 0.8 copy.39
  601.3 0.8 copy.40
  602.1 0.8 copy.41
  602.9 1.1 copy.42
  604.0 1.1 copy.43
  605.1 1.1 copy.44
  (59 shorter events, 2.5 us)
Async XLA Ops:
  269.3 47.8 %collective-permute-start.1 = (bf16[2,256,512]{2,1,0:T(8,128)(2,1)}, bf16[2,256,512]{2,1,0:T(8,128)(2,1)S(1)}, u32[]{:S(2)}, u32[]{:S(2)}) collective-permute-start(bf16[2,256,512]{2,1,0:T(8,128)(2,1)} %get-tuple-element.65), channel_id=1, source_target_pairs={{0,8},{2,10},{4,12},{6,14},{8,16},{10,18},{12,20},{14,22},{16,24},... | collective-permute-start | bytes 1572872 | tf_op jit(solution)/shard_map/ppermute | solution.py:1347
  270.4 46.8 %collective-permute-start.2 = (bf16[2,256,512]{2,1,0:T(8,128)(2,1)}, bf16[2,256,512]{2,1,0:T(8,128)(2,1)S(1)}, u32[]{:S(2)}, u32[]{:S(2)}) collective-permute-start(bf16[2,256,512]{2,1,0:T(8,128)(2,1)} %get-tuple-element.66), channel_id=1, source_target_pairs={{0,16},{2,18},{4,20},{6,22},{8,24},{10,26},{12,28},{14,30},{16,0},... | collective-permute-start | bytes 1572872 | tf_op jit(solution)/shard_map/ppermute | solution.py:1347
  270.9 46.2 %collective-permute-start.3 = (bf16[2,256,512]{2,1,0:T(8,128)(2,1)}, bf16[2,256,512]{2,1,0:T(8,128)(2,1)}, u32[]{:S(2)}, u32[]{:S(2)}) collective-permute-start(bf16[2,256,512]{2,1,0:T(8,128)(2,1)} %get-tuple-element.67), channel_id=1, source_target_pairs={{0,24},{2,26},{4,28},{6,30},{8,0},{10,2},{12,4},{14,6},{16,8},{18,... | collective-permute-start | bytes 1572872 | tf_op jit(solution)/shard_map/ppermute | solution.py:1347
  273.4 43.8 %collective-permute-start = (bf16[4,256,896]{2,1,0:T(8,128)(2,1)}, bf16[4,256,896]{2,1,0:T(8,128)(2,1)}, u32[]{:S(2)}, u32[]{:S(2)}) collective-permute-start(bf16[4,256,896]{2,1,0:T(8,128)(2,1)} %get-tuple-element.63), channel_id=1, source_target_pairs={{0,4},{2,6},{4,0},{6,2},{8,12},{10,14},{12,8},{14,10},{16,20},{18,... | collective-permute-start | bytes 5505032 | tf_op jit(solution)/shard_map/ppermute | solution.py:1347
  288.4 17.1 %copy-start.5 = (bf16[1024,2048]{1,0:T(8,128)(2,1)S(1)}, bf16[1024,2048]{1,0:T(8,128)(2,1)}, u32[]{:S(2)}) copy-start(bf16[1024,2048]{1,0:T(8,128)(2,1)} %get-tuple-element.58.ffn_in) | copy-start | bytes 12582916
  317.1 0.8 copy-start.18
  317.2 1.0 copy-start.19
  412.6 54.8 %collective-permute-start.5 = (bf16[2,256,512]{2,1,0:T(8,128)(2,1)}, bf16[2,256,512]{2,1,0:T(8,128)(2,1)S(1)}, u32[]{:S(2)}, u32[]{:S(2)}) collective-permute-start(bf16[2,256,512]{2,1,0:T(8,128)(2,1)} %get-tuple-element.76), channel_id=1, source_target_pairs={{0,8},{2,10},{4,12},{6,14},{8,16},{10,18},{12,20},{14,22},{16,24},... | collective-permute-start | bytes 1572872 | tf_op jit(solution)/shard_map/ppermute | solution.py:1347
  413.5 53.9 %collective-permute-start.6 = (bf16[2,256,512]{2,1,0:T(8,128)(2,1)}, bf16[2,256,512]{2,1,0:T(8,128)(2,1)S(1)}, u32[]{:S(2)}, u32[]{:S(2)}) collective-permute-start(bf16[2,256,512]{2,1,0:T(8,128)(2,1)} %get-tuple-element.77), channel_id=1, source_target_pairs={{0,16},{2,18},{4,20},{6,22},{8,24},{10,26},{12,28},{14,30},{16,0},... | collective-permute-start | bytes 1572872 | tf_op jit(solution)/shard_map/ppermute | solution.py:1347
  415.6 51.8 %collective-permute-start.7 = (bf16[2,256,512]{2,1,0:T(8,128)(2,1)}, bf16[2,256,512]{2,1,0:T(8,128)(2,1)S(1)}, u32[]{:S(2)}, u32[]{:S(2)}) collective-permute-start(bf16[2,256,512]{2,1,0:T(8,128)(2,1)} %get-tuple-element.78), channel_id=1, source_target_pairs={{0,24},{2,26},{4,28},{6,30},{8,0},{10,2},{12,4},{14,6},{16,8},{18,... | collective-permute-start | bytes 1572872 | tf_op jit(solution)/shard_map/ppermute | solution.py:1347
  416.5 51.0 %collective-permute-start.4 = (bf16[4,256,896]{2,1,0:T(8,128)(2,1)}, bf16[4,256,896]{2,1,0:T(8,128)(2,1)S(1)}, u32[]{:S(2)}, u32[]{:S(2)}) collective-permute-start(bf16[4,256,896]{2,1,0:T(8,128)(2,1)} %get-tuple-element.74), channel_id=1, source_target_pairs={{0,4},{2,6},{4,0},{6,2},{8,12},{10,14},{12,8},{14,10},{16,20},{18,... | collective-permute-start | bytes 5505032 | tf_op jit(solution)/shard_map/ppermute | solution.py:1347
  417.9 5.4 copy-start
  417.9 5.4 copy-start.1
  417.9 5.4 copy-start.2
  417.9 5.4 copy-start.3
  417.9 23.8 %slice-start = ((s8[6815744]{0:T(1024)(128)(4,1)}), s8[4194304]{0:T(1024)(128)(4,1)S(1)}, s32[]{:S(2)}) async-start(s8[6815744]{0:T(1024)(128)(4,1)} %bitcast.32), calls=%async_computation | async-start | bytes 8388608
  423.3 18.4 %slice-start.1 = ((s8[6815744]{0:T(1024)(128)(4,1)}), s8[2621440]{0:T(1024)(128)(4,1)S(1)}, s32[]{:S(2)}) async-start(s8[6815744]{0:T(1024)(128)(4,1)} %bitcast.32), calls=%async_computation.1 | async-start | bytes 5242880
  441.8 11.5 %copy-start.6 = (bf16[1024,1664]{1,0:T(8,128)(2,1)S(1)}, bf16[1024,1664]{1,0:T(8,128)(2,1)}, u32[]{:S(2)}) copy-start(bf16[1024,1664]{1,0:T(8,128)(2,1)} %mixer_backward.1) | copy-start | bytes 10223620
  441.8 11.5 %copy-start.20 = (bf16[1024,2048]{1,0:T(8,128)(2,1)S(1)}, bf16[1024,2048]{1,0:T(8,128)(2,1)}, u32[]{:S(2)}) copy-start(bf16[1024,2048]{1,0:T(8,128)(2,1)} %get-tuple-element.81) | copy-start | bytes 12582916
  453.3 10.3 %copy-start.21 = (bf16[4,256,2048]{2,1,0:T(8,128)(2,1)S(1)}, bf16[4,256,2048]{2,1,0:T(8,128)(2,1)}, u32[]{:S(2)}) copy-start(bf16[4,256,2048]{2,1,0:T(8,128)(2,1)} %get-tuple-element.79) | copy-start | bytes 12582916
  453.3 10.3 %copy-start.22 = (bf16[1024,512]{1,0:T(8,128)(2,1)S(1)}, bf16[1024,512]{1,0:T(8,128)(2,1)}, u32[]{:S(2)}) copy-start(bf16[1024,512]{1,0:T(8,128)(2,1)} %get-tuple-element.80) | copy-start | bytes 3145732
  467.4 1.0 copy-start.12
  467.5 1.1 copy-start.13
  467.5 1.7 copy-start.7
  591.4 6.1 %copy-start.4 = (f32[512,2048]{1,0:T(8,128)S(1)}, f32[512,2048]{1,0:T(8,128)}, u32[]{:S(2)}) copy-start(f32[512,2048]{1,0:T(8,128)} %get-tuple-element.123) | copy-start | bytes 12582916
  597.5 2.1 copy-start.17
  597.5 2.9 copy-start.16
  597.6 3.7 copy-start.15
  597.6 4.5 copy-start.14
  599.7 3.2 copy-start.9
  599.7 4.3 copy-start.10
  601.3 3.8 copy-start.8
  (1 other events, 0.8 us)

commit v9 on v8

--- a/solution.py
+++ b/solution.py
@@ -1621,7 +1621,7 @@
     row = (SEQ_LEN, dim)
     vmem = lambda shape, kind=F32: pltpu.VMEM(shape, kind)
     tokens4 = 4 * SEQ_LEN
-    cut = hid // 256 * 128 + 128
+    cut = hid // 256 * 128
     full = (tokens4, dim)
     early, rest = [((4, width, EARLY), BF16)] * 2, [((2, width, hid - EARLY), BF16)] * 4
     (

time: 615 us -> 612 us (level)
  no operation moved by 1% of the time
where the time goes in v9:
time: 612 us; the launch traced here: 604 us
  Pallas kernels  501 us (82%)
  matrix products  70.8 us (12%)
  local copies, waits for them, and re-layouts  16.7 us (3%)
  starting transfers between devices  9.59 us (2%)
    pallas_call x3, Pallas kernels, call(): pl.pallas_call(kernel, in_specs=specs, out_specs=out_specs, out_shape=[ja...  483 us
    dot_general x7, matrix products, mm(): lax.dot_general(left, right, dims, preferred_element_type=F32).astype(kind)  70.8 us
    pallas_call x1, Pallas kernels, mixer_backward(): pl.pallas_call(backward_kernel, grid=(rows // SEQ_LEN,), in_specs=IN_SPEC...  18.4 us
    unnamed x59, local copies, waits for them, and re-layouts  14.5 us
  transfers between devices with their start and end apart: 8, of which 0 were waited for; matrix products, arithmetic and copies ran while one was open for 12% of the time, Pallas kernels for 3%

profile of v9, /device:TPU:0, one launch (start us, length us, event | category | flops | bytes accessed | tf_op | source)
XLA Modules:
  0.0 604.1 jit_solution(11640224305770076875)
XLA Ops:
  1.3 266.0 %forward_all.1 = (bf16[2048,1664]{1,0:T(8,128)(2,1)}, bf16[2048,512]{1,0:T(8,128)(2,1)}, bf16[256,2048]{1,0:T(8,128)(2,1)}, bf16[1024,2048]{1,0:T(8,128)(2,1)}, ...) custom-call(bf16[512,2048]{1,0:T(8,128)(2,1)} %tokens.1, ...), custom_call_target="tpu_custom_call" | custom-call | tf_op jit(solution)/shard_map/forward_all/pallas_call | solution.py:1312
  267.3 0.6 collective-permute-start.1
  268.4 2.9 collective-permute-start.3
  271.3 0.6 collective-permute-start
  271.9 14.1 %multiply_convert_fusion = (bf16[1024,1408]{1,0:T(8,128)(2,1)S(1)}, bf16[1024,1408]{1,0:T(8,128)(2,1)S(1)}) fusion(f32[1024,2816]{1,0:T(8,128)} %get-tuple-element.61, bf16[1024,2048]{1,0:T(8,128)(2,1)} %get-tuple-element.59, bf16[2048,1408]{1,0:T(8,128)(2,1)} %get-tuple-element.60), kind=kOutput, calls=%fused_computation.3 | convolution fusion | flops 5924323328 | bytes 27262976 | tf_op jit(solution)/shard_map/dot_general | solution.py:1431
  286.0 17.1 %fusion = f32[1024,2048]{1,0:T(8,128)} fusion(bf16[2048,2816]{1,0:T(8,128)(2,1)} %get-tuple-element.68, bf16[1024,1408]{1,0:T(8,128)(2,1)S(1)} %get-tuple-element.104, bf16[1024,1408]{1,0:T(8,128)(2,1)S(1)} %get-tuple-element.105), kind=kOutput, calls=%fused_computation.10 | convolution fusion | flops 11822694400 | bytes 25690112 | tf_op jit(solution)/shard_map/dot_general | solution.py:1431
  303.1 8.6 %convolution_convert_fusion.1 = bf16[2048,1408]{1,0:T(8,128)(2,1)} fusion(bf16[1024,2048]{1,0:T(8,128)(2,1)S(1)} %copy-done.5, bf16[1024,1408]{1,0:T(8,128)(2,1)S(1)} %get-tuple-element.105), kind=kOutput, calls=%fused_computation.1 | convolution fusion | flops 5908463616 | bytes 12845056 | tf_op jit(solution)/shard_map/dot_general | solution.py:1431
  311.8 2.9 pad_maximum_fusion.d_wide
  314.8 0.8 copy-done.18
  315.7 94.9 %sum_ffn.1 = (f32[128,2816]{1,0:T(8,128)}, f32[128,2816]{1,0:T(8,128)}, f32[256,2048]{1,0:T(8,128)}, bf16[4,256,2048]{2,1,0:T(8,128)(2,1)}, f32[8,2048]{1,0:T(8,...) custom-call(bf16[8,256,1408]{2,1,0:T(8,128)(2,1)} %bitcast.30, ...), custom_call_target="tpu_custom_call" | custom-call | tf_op jit(solution)/shard_map/sum_ffn/pallas_call | solution.py:1312
  410.6 1.8 collective-permute-start.5
  412.4 2.6 collective-permute-start.6
  415.5 5.3 fusion.2.d_ref
  420.9 18.4 %mixer_backward.1 = bf16[1024,1664]{1,0:T(8,128)(2,1)} custom-call(f32[1024,1664]{1,0:T(8,128)} %get-tuple-element.82.q_ref.k_ref.v_ref.f_ref, f32[1024,1664]{1,0:T(8,128)} %get-tuple-element.82.q_ref.k_ref.v_ref.f_ref, f32[1024,1664]{1,0:T(8,128)} %get-tuple-element.82.q_ref.k_ref.v_ref.f_ref, f32[1024,1664]{1,0:T(8,128)} %get-tuple-element.82.q_ref.k_ref.v_ref.f_ref, ...), custom_call_target="tpu_custom_call" | custom-call | flops 9216000000 | bytes 16384000 | tf_op jit(solution)/shard_map/mixer_backward/pallas_call | solution.py:266
  439.4 11.5 %fusion.3 = f32[1024,2048]{1,0:T(8,128)} fusion(bf16[1024,1664]{1,0:T(8,128)(2,1)} %mixer_backward.1, bf16[2048,1664]{1,0:T(8,128)(2,1)S(1)} %bitcast.33), kind=kOutput, calls=%fused_computation.13 | convolution fusion | flops 6979321856 | bytes 18612224 | tf_op jit(solution)/shard_map/dot_general | solution.py:1431
  450.9 10.3 %convolution_convert_fusion = bf16[2048,1664]{1,0:T(8,128)(2,1)} fusion(bf16[1024,2048]{1,0:T(8,128)(2,1)S(1)} %copy-done.20, bf16[1024,1664]{1,0:T(8,128)(2,1)S(1)} %copy-done.6), kind=kOutput, calls=%fused_computation | convolution fusion | flops 6982729728 | bytes 14417920 | tf_op jit(solution)/shard_map/dot_general | solution.py:1431
  461.2 3.8 convolution_convert_fusion.2
  465.1 0.7 copy-done.11
  466.1 0.6 copy-done.7
  466.8 122.1 %sum_last.1 = (f32[128,2816]{1,0:T(8,128)}, f32[128,1024]{1,0:T(8,128)}, f32[128,1024]{1,0:T(8,128)}, f32[128,1024]{1,0:T(8,128)}, f32[128,1024]{1,0:T(8,128)}, ...) custom-call(bf16[4,256,896]{2,1,0:T(8,128)(2,1)} %get-tuple-element.73.up, ...), custom_call_target="tpu_custom_call" | custom-call | tf_op jit(solution)/shard_map/sum_last/pallas_call | solution.py:1312
  588.9 1.3 slice_bitcast_fusion
  590.2 0.9 fusion.1
  591.1 0.7 pad_maximum_fusion.1
  591.8 3.2 copy.36
  595.0 2.1 copy.37
  597.1 0.8 copy.38
  597.9 0.8 copy.39
  598.7 0.8 copy.40
  599.5 0.8 copy.41
  600.3 1.1 copy.42
  601.4 1.1 copy.43
  602.5 1.1 copy.44
  (59 shorter events, 1.7 us)
Async XLA Ops:
  267.3 47.5 %collective-permute-start.1 = (bf16[2,256,512]{2,1,0:T(8,128)(2,1)}, bf16[2,256,512]{2,1,0:T(8,128)(2,1)S(1)}, u32[]{:S(2)}, u32[]{:S(2)}) collective-permute-start(bf16[2,256,512]{2,1,0:T(8,128)(2,1)} %get-tuple-element.65), channel_id=1, source_target_pairs={{0,8},{2,10},{4,12},{6,14},{8,16},{10,18},{12,20},{14,22},{16,24},... | collective-permute-start | bytes 1572872 | tf_op jit(solution)/shard_map/ppermute | solution.py:1347
  267.8 46.9 %collective-permute-start.2 = (bf16[2,256,512]{2,1,0:T(8,128)(2,1)}, bf16[2,256,512]{2,1,0:T(8,128)(2,1)S(1)}, u32[]{:S(2)}, u32[]{:S(2)}) collective-permute-start(bf16[2,256,512]{2,1,0:T(8,128)(2,1)} %get-tuple-element.66), channel_id=1, source_target_pairs={{0,16},{2,18},{4,20},{6,22},{8,24},{10,26},{12,28},{14,30},{16,0},... | collective-permute-start | bytes 1572872 | tf_op jit(solution)/shard_map/ppermute | solution.py:1347
  268.4 46.4 %collective-permute-start.3 = (bf16[2,256,512]{2,1,0:T(8,128)(2,1)}, bf16[2,256,512]{2,1,0:T(8,128)(2,1)}, u32[]{:S(2)}, u32[]{:S(2)}) collective-permute-start(bf16[2,256,512]{2,1,0:T(8,128)(2,1)} %get-tuple-element.67), channel_id=1, source_target_pairs={{0,24},{2,26},{4,28},{6,30},{8,0},{10,2},{12,4},{14,6},{16,8},{18,... | collective-permute-start | bytes 1572872 | tf_op jit(solution)/shard_map/ppermute | solution.py:1347
  271.3 43.5 %collective-permute-start = (bf16[4,256,896]{2,1,0:T(8,128)(2,1)}, bf16[4,256,896]{2,1,0:T(8,128)(2,1)}, u32[]{:S(2)}, u32[]{:S(2)}) collective-permute-start(bf16[4,256,896]{2,1,0:T(8,128)(2,1)} %get-tuple-element.63), channel_id=1, source_target_pairs={{0,4},{2,6},{4,0},{6,2},{8,12},{10,14},{12,8},{14,10},{16,20},{18,... | collective-permute-start | bytes 5505032 | tf_op jit(solution)/shard_map/ppermute | solution.py:1347
  286.0 17.1 %copy-start.5 = (bf16[1024,2048]{1,0:T(8,128)(2,1)S(1)}, bf16[1024,2048]{1,0:T(8,128)(2,1)}, u32[]{:S(2)}) copy-start(bf16[1024,2048]{1,0:T(8,128)(2,1)} %get-tuple-element.58.ffn_in) | copy-start | bytes 12582916
  314.7 0.8 copy-start.18
  314.7 1.0 copy-start.19
  410.6 54.4 %collective-permute-start.5 = (bf16[2,256,512]{2,1,0:T(8,128)(2,1)}, bf16[2,256,512]{2,1,0:T(8,128)(2,1)S(1)}, u32[]{:S(2)}, u32[]{:S(2)}) collective-permute-start(bf16[2,256,512]{2,1,0:T(8,128)(2,1)} %get-tuple-element.76), channel_id=1, source_target_pairs={{0,8},{2,10},{4,12},{6,14},{8,16},{10,18},{12,20},{14,22},{16,24},... | collective-permute-start | bytes 1572872 | tf_op jit(solution)/shard_map/ppermute | solution.py:1347
  412.4 52.6 %collective-permute-start.6 = (bf16[2,256,512]{2,1,0:T(8,128)(2,1)}, bf16[2,256,512]{2,1,0:T(8,128)(2,1)S(1)}, u32[]{:S(2)}, u32[]{:S(2)}) collective-permute-start(bf16[2,256,512]{2,1,0:T(8,128)(2,1)} %get-tuple-element.77), channel_id=1, source_target_pairs={{0,16},{2,18},{4,20},{6,22},{8,24},{10,26},{12,28},{14,30},{16,0},... | collective-permute-start | bytes 1572872 | tf_op jit(solution)/shard_map/ppermute | solution.py:1347
  415.0 50.0 %collective-permute-start.7 = (bf16[2,256,512]{2,1,0:T(8,128)(2,1)}, bf16[2,256,512]{2,1,0:T(8,128)(2,1)S(1)}, u32[]{:S(2)}, u32[]{:S(2)}) collective-permute-start(bf16[2,256,512]{2,1,0:T(8,128)(2,1)} %get-tuple-element.78), channel_id=1, source_target_pairs={{0,24},{2,26},{4,28},{6,30},{8,0},{10,2},{12,4},{14,6},{16,8},{18,... | collective-permute-start | bytes 1572872 | tf_op jit(solution)/shard_map/ppermute | solution.py:1347
  415.0 50.1 %collective-permute-start.4 = (bf16[4,256,896]{2,1,0:T(8,128)(2,1)}, bf16[4,256,896]{2,1,0:T(8,128)(2,1)S(1)}, u32[]{:S(2)}, u32[]{:S(2)}) collective-permute-start(bf16[4,256,896]{2,1,0:T(8,128)(2,1)} %get-tuple-element.74), channel_id=1, source_target_pairs={{0,4},{2,6},{4,0},{6,2},{8,12},{10,14},{12,8},{14,10},{16,20},{18,... | collective-permute-start | bytes 5505032 | tf_op jit(solution)/shard_map/ppermute | solution.py:1347
  415.5 5.4 copy-start
  415.5 5.4 copy-start.1
  415.5 5.4 copy-start.2
  415.5 5.4 copy-start.3
  415.5 23.8 %slice-start = ((s8[6815744]{0:T(1024)(128)(4,1)}), s8[4194304]{0:T(1024)(128)(4,1)S(1)}, s32[]{:S(2)}) async-start(s8[6815744]{0:T(1024)(128)(4,1)} %bitcast.32), calls=%async_computation | async-start | bytes 8388608
  420.9 18.4 %slice-start.1 = ((s8[6815744]{0:T(1024)(128)(4,1)}), s8[2621440]{0:T(1024)(128)(4,1)S(1)}, s32[]{:S(2)}) async-start(s8[6815744]{0:T(1024)(128)(4,1)} %bitcast.32), calls=%async_computation.1 | async-start | bytes 5242880
  439.3 11.5 %copy-start.6 = (bf16[1024,1664]{1,0:T(8,128)(2,1)S(1)}, bf16[1024,1664]{1,0:T(8,128)(2,1)}, u32[]{:S(2)}) copy-start(bf16[1024,1664]{1,0:T(8,128)(2,1)} %mixer_backward.1) | copy-start | bytes 10223620
  439.4 11.5 %copy-start.20 = (bf16[1024,2048]{1,0:T(8,128)(2,1)S(1)}, bf16[1024,2048]{1,0:T(8,128)(2,1)}, u32[]{:S(2)}) copy-start(bf16[1024,2048]{1,0:T(8,128)(2,1)} %get-tuple-element.81) | copy-start | bytes 12582916
  450.9 10.3 %copy-start.21 = (bf16[4,256,2048]{2,1,0:T(8,128)(2,1)S(1)}, bf16[4,256,2048]{2,1,0:T(8,128)(2,1)}, u32[]{:S(2)}) copy-start(bf16[4,256,2048]{2,1,0:T(8,128)(2,1)} %get-tuple-element.79) | copy-start | bytes 12582916
  450.9 10.3 %copy-start.22 = (bf16[1024,512]{1,0:T(8,128)(2,1)S(1)}, bf16[1024,512]{1,0:T(8,128)(2,1)}, u32[]{:S(2)}) copy-start(bf16[1024,512]{1,0:T(8,128)(2,1)} %get-tuple-element.80) | copy-start | bytes 3145732
  465.0 1.0 copy-start.12
  465.0 1.1 copy-start.13
  465.1 1.7 copy-start.7
  588.9 6.1 %copy-start.4 = (f32[512,2048]{1,0:T(8,128)S(1)}, f32[512,2048]{1,0:T(8,128)}, u32[]{:S(2)}) copy-start(f32[512,2048]{1,0:T(8,128)} %get-tuple-element.123) | copy-start | bytes 12582916
  595.0 2.1 copy-start.17
  595.0 2.9 copy-start.16
  595.0 3.7 copy-start.15
  595.0 4.5 copy-start.14
  597.1 3.2 copy-start.9
  597.1 4.3 copy-start.10
  598.7 3.8 copy-start.8
  (1 other events, 0.8 us)

commit v10 on v9

--- a/solution.py
+++ b/solution.py
@@ -1142,10 +1142,10 @@
     fetch = [pltpu.make_async_copy(resid, value, sems.one()), pltpu.make_async_copy(d_res, res, sems.one())]
     save = pltpu.make_async_copy(res, d_h, sems.one())
     place.greet()
-    back.start()
     for one in (down_y, *gate):
         one.start(0)
     down_z.start()
+    back.start()
     for copy in fetch:
         copy.start()
     for one in (down_y, *gate):
@@ -1230,10 +1230,11 @@
     ]
     swap = place.copy("x", last.at[1 - place.x], swapped, sems.two())
     place.greet()
-    back.start()
-    for one in sums:
+    sums[0].start(0)
+    for one in sums[1:]:
         one.start(0)
     up_z.start()
+    back.start()
     for copy in fetch:
         copy.start()
     for one in sums:

time: 612 us -> 611 us (level)
  no operation moved by 1% of the time
where the time goes in v10:
time: 611 us; the launch traced here: 603 us
  Pallas kernels  500 us (82%)
  matrix products  70.8 us (12%)
  local copies, waits for them, and re-layouts  16.7 us (3%)
  starting transfers between devices  9.67 us (2%)
    pallas_call x3, Pallas kernels, call(): pl.pallas_call(kernel, in_specs=specs, out_specs=out_specs, out_shape=[ja...  482 us
    dot_general x7, matrix products, mm(): lax.dot_general(left, right, dims, preferred_element_type=F32).astype(kind)  70.8 us
    pallas_call x1, Pallas kernels, mixer_backward(): pl.pallas_call(backward_kernel, grid=(rows // SEQ_LEN,), in_specs=IN_SPEC...  18.4 us
    unnamed x59, local copies, waits for them, and re-layouts  14.5 us
  transfers between devices with their start and end apart: 8, of which 0 were waited for; matrix products, arithmetic and copies ran while one was open for 12% of the time, Pallas kernels for 3%

profile of v10, /device:TPU:0, one launch (start us, length us, event | category | flops | bytes accessed | tf_op | source)
XLA Modules:
  0.0 602.8 jit_solution(15820391295471316678)
XLA Ops:
  1.3 266.0 %forward_all.1 = (bf16[2048,1664]{1,0:T(8,128)(2,1)}, bf16[2048,512]{1,0:T(8,128)(2,1)}, bf16[256,2048]{1,0:T(8,128)(2,1)}, bf16[1024,2048]{1,0:T(8,128)(2,1)}, ...) custom-call(bf16[512,2048]{1,0:T(8,128)(2,1)} %tokens.1, ...), custom_call_target="tpu_custom_call" | custom-call | tf_op jit(solution)/shard_map/forward_all/pallas_call | solution.py:1313
  268.4 2.9 collective-permute-start.3
  271.3 0.6 collective-permute-start
  271.9 14.1 %multiply_convert_fusion = (bf16[1024,1408]{1,0:T(8,128)(2,1)S(1)}, bf16[1024,1408]{1,0:T(8,128)(2,1)S(1)}) fusion(f32[1024,2816]{1,0:T(8,128)} %get-tuple-element.61, bf16[1024,2048]{1,0:T(8,128)(2,1)} %get-tuple-element.59, bf16[2048,1408]{1,0:T(8,128)(2,1)} %get-tuple-element.60), kind=kOutput, calls=%fused_computation.3 | convolution fusion | flops 5924323328 | bytes 27262976 | tf_op jit(solution)/shard_map/dot_general | solution.py:1432
  286.0 17.1 %fusion = f32[1024,2048]{1,0:T(8,128)} fusion(bf16[2048,2816]{1,0:T(8,128)(2,1)} %get-tuple-element.68, bf16[1024,1408]{1,0:T(8,128)(2,1)S(1)} %get-tuple-element.104, bf16[1024,1408]{1,0:T(8,128)(2,1)S(1)} %get-tuple-element.105), kind=kOutput, calls=%fused_computation.10 | convolution fusion | flops 11822694400 | bytes 25690112 | tf_op jit(solution)/shard_map/dot_general | solution.py:1432
  303.1 8.6 %convolution_convert_fusion.1 = bf16[2048,1408]{1,0:T(8,128)(2,1)} fusion(bf16[1024,2048]{1,0:T(8,128)(2,1)S(1)} %copy-done.5, bf16[1024,1408]{1,0:T(8,128)(2,1)S(1)} %get-tuple-element.105), kind=kOutput, calls=%fused_computation.1 | convolution fusion | flops 5908463616 | bytes 12845056 | tf_op jit(solution)/shard_map/dot_general | solution.py:1432
  311.8 2.9 pad_maximum_fusion.d_wide
  314.8 0.8 copy-done.18
  315.7 94.5 %sum_ffn.1 = (f32[128,2816]{1,0:T(8,128)}, f32[128,2816]{1,0:T(8,128)}, f32[256,2048]{1,0:T(8,128)}, bf16[4,256,2048]{2,1,0:T(8,128)(2,1)}, f32[8,2048]{1,0:T(8,...) custom-call(bf16[8,256,1408]{2,1,0:T(8,128)(2,1)} %bitcast.30, ...), custom_call_target="tpu_custom_call" | custom-call | tf_op jit(solution)/shard_map/sum_ffn/pallas_call | solution.py:1313
  410.2 0.9 collective-permute-start.5
  411.1 2.7 collective-permute-start.6
  414.1 1.1 collective-permute-start.4
  415.2 5.3 fusion.2.d_ref
  420.6 18.4 %mixer_backward.1 = bf16[1024,1664]{1,0:T(8,128)(2,1)} custom-call(f32[1024,1664]{1,0:T(8,128)} %get-tuple-element.82.q_ref.k_ref.v_ref.f_ref, f32[1024,1664]{1,0:T(8,128)} %get-tuple-element.82.q_ref.k_ref.v_ref.f_ref, f32[1024,1664]{1,0:T(8,128)} %get-tuple-element.82.q_ref.k_ref.v_ref.f_ref, f32[1024,1664]{1,0:T(8,128)} %get-tuple-element.82.q_ref.k_ref.v_ref.f_ref, ...), custom_call_target="tpu_custom_call" | custom-call | flops 9216000000 | bytes 16384000 | tf_op jit(solution)/shard_map/mixer_backward/pallas_call | solution.py:266
  439.1 11.5 %fusion.3 = f32[1024,2048]{1,0:T(8,128)} fusion(bf16[1024,1664]{1,0:T(8,128)(2,1)} %mixer_backward.1, bf16[2048,1664]{1,0:T(8,128)(2,1)S(1)} %bitcast.33), kind=kOutput, calls=%fused_computation.13 | convolution fusion | flops 6979321856 | bytes 18612224 | tf_op jit(solution)/shard_map/dot_general | solution.py:1432
  450.6 10.3 %convolution_convert_fusion = bf16[2048,1664]{1,0:T(8,128)(2,1)} fusion(bf16[1024,2048]{1,0:T(8,128)(2,1)S(1)} %copy-done.20, bf16[1024,1664]{1,0:T(8,128)(2,1)S(1)} %copy-done.6), kind=kOutput, calls=%fused_computation | convolution fusion | flops 6982729728 | bytes 14417920 | tf_op jit(solution)/shard_map/dot_general | solution.py:1432
  461.0 3.8 convolution_convert_fusion.2
  464.8 0.7 copy-done.11
  465.9 0.6 copy-done.7
  466.5 121.1 %sum_last.1 = (f32[128,2816]{1,0:T(8,128)}, f32[128,1024]{1,0:T(8,128)}, f32[128,1024]{1,0:T(8,128)}, f32[128,1024]{1,0:T(8,128)}, f32[128,1024]{1,0:T(8,128)}, ...) custom-call(bf16[4,256,896]{2,1,0:T(8,128)(2,1)} %get-tuple-element.73.up, ...), custom_call_target="tpu_custom_call" | custom-call | tf_op jit(solution)/shard_map/sum_last/pallas_call | solution.py:1313
  587.6 1.3 slice_bitcast_fusion
  588.9 0.9 fusion.1
  589.8 0.7 pad_maximum_fusion.1
  590.5 3.2 copy.36
  593.7 2.1 copy.37
  595.8 0.8 copy.38
  596.6 0.8 copy.39
  597.4 0.8 copy.40
  598.2 0.8 copy.41
  599.0 1.1 copy.42
  600.1 1.1 copy.43
  601.2 1.1 copy.44
  (59 shorter events, 2.0 us)
Async XLA Ops:
  267.3 47.5 %collective-permute-start.1 = (bf16[2,256,512]{2,1,0:T(8,128)(2,1)}, bf16[2,256,512]{2,1,0:T(8,128)(2,1)S(1)}, u32[]{:S(2)}, u32[]{:S(2)}) collective-permute-start(bf16[2,256,512]{2,1,0:T(8,128)(2,1)} %get-tuple-element.65), channel_id=1, source_target_pairs={{0,8},{2,10},{4,12},{6,14},{8,16},{10,18},{12,20},{14,22},{16,24},... | collective-permute-start | bytes 1572872 | tf_op jit(solution)/shard_map/ppermute | solution.py:1348
  267.8 46.9 %collective-permute-start.2 = (bf16[2,256,512]{2,1,0:T(8,128)(2,1)}, bf16[2,256,512]{2,1,0:T(8,128)(2,1)S(1)}, u32[]{:S(2)}, u32[]{:S(2)}) collective-permute-start(bf16[2,256,512]{2,1,0:T(8,128)(2,1)} %get-tuple-element.66), channel_id=1, source_target_pairs={{0,16},{2,18},{4,20},{6,22},{8,24},{10,26},{12,28},{14,30},{16,0},... | collective-permute-start | bytes 1572872 | tf_op jit(solution)/shard_map/ppermute | solution.py:1348
  268.4 46.4 %collective-permute-start.3 = (bf16[2,256,512]{2,1,0:T(8,128)(2,1)}, bf16[2,256,512]{2,1,0:T(8,128)(2,1)}, u32[]{:S(2)}, u32[]{:S(2)}) collective-permute-start(bf16[2,256,512]{2,1,0:T(8,128)(2,1)} %get-tuple-element.67), channel_id=1, source_target_pairs={{0,24},{2,26},{4,28},{6,30},{8,0},{10,2},{12,4},{14,6},{16,8},{18,... | collective-permute-start | bytes 1572872 | tf_op jit(solution)/shard_map/ppermute | solution.py:1348
  271.3 43.5 %collective-permute-start = (bf16[4,256,896]{2,1,0:T(8,128)(2,1)}, bf16[4,256,896]{2,1,0:T(8,128)(2,1)}, u32[]{:S(2)}, u32[]{:S(2)}) collective-permute-start(bf16[4,256,896]{2,1,0:T(8,128)(2,1)} %get-tuple-element.63), channel_id=1, source_target_pairs={{0,4},{2,6},{4,0},{6,2},{8,12},{10,14},{12,8},{14,10},{16,20},{18,... | collective-permute-start | bytes 5505032 | tf_op jit(solution)/shard_map/ppermute | solution.py:1348
  286.0 17.1 %copy-start.5 = (bf16[1024,2048]{1,0:T(8,128)(2,1)S(1)}, bf16[1024,2048]{1,0:T(8,128)(2,1)}, u32[]{:S(2)}) copy-start(bf16[1024,2048]{1,0:T(8,128)(2,1)} %get-tuple-element.58.ffn_in) | copy-start | bytes 12582916
  314.7 0.8 copy-start.18
  314.7 1.0 copy-start.19
  410.2 54.5 %collective-permute-start.5 = (bf16[2,256,512]{2,1,0:T(8,128)(2,1)}, bf16[2,256,512]{2,1,0:T(8,128)(2,1)S(1)}, u32[]{:S(2)}, u32[]{:S(2)}) collective-permute-start(bf16[2,256,512]{2,1,0:T(8,128)(2,1)} %get-tuple-element.76), channel_id=1, source_target_pairs={{0,8},{2,10},{4,12},{6,14},{8,16},{10,18},{12,20},{14,22},{16,24},... | collective-permute-start | bytes 1572872 | tf_op jit(solution)/shard_map/ppermute | solution.py:1348
  411.1 53.6 %collective-permute-start.6 = (bf16[2,256,512]{2,1,0:T(8,128)(2,1)}, bf16[2,256,512]{2,1,0:T(8,128)(2,1)S(1)}, u32[]{:S(2)}, u32[]{:S(2)}) collective-permute-start(bf16[2,256,512]{2,1,0:T(8,128)(2,1)} %get-tuple-element.77), channel_id=1, source_target_pairs={{0,16},{2,18},{4,20},{6,22},{8,24},{10,26},{12,28},{14,30},{16,0},... | collective-permute-start | bytes 1572872 | tf_op jit(solution)/shard_map/ppermute | solution.py:1348
  413.8 50.9 %collective-permute-start.7 = (bf16[2,256,512]{2,1,0:T(8,128)(2,1)}, bf16[2,256,512]{2,1,0:T(8,128)(2,1)S(1)}, u32[]{:S(2)}, u32[]{:S(2)}) collective-permute-start(bf16[2,256,512]{2,1,0:T(8,128)(2,1)} %get-tuple-element.78), channel_id=1, source_target_pairs={{0,24},{2,26},{4,28},{6,30},{8,0},{10,2},{12,4},{14,6},{16,8},{18,... | collective-permute-start | bytes 1572872 | tf_op jit(solution)/shard_map/ppermute | solution.py:1348
  414.1 50.7 %collective-permute-start.4 = (bf16[4,256,896]{2,1,0:T(8,128)(2,1)}, bf16[4,256,896]{2,1,0:T(8,128)(2,1)S(1)}, u32[]{:S(2)}, u32[]{:S(2)}) collective-permute-start(bf16[4,256,896]{2,1,0:T(8,128)(2,1)} %get-tuple-element.74), channel_id=1, source_target_pairs={{0,4},{2,6},{4,0},{6,2},{8,12},{10,14},{12,8},{14,10},{16,20},{18,... | collective-permute-start | bytes 5505032 | tf_op jit(solution)/shard_map/ppermute | solution.py:1348
  415.2 5.4 copy-start
  415.2 5.4 copy-start.1
  415.2 5.4 copy-start.2
  415.2 5.4 copy-start.3
  415.2 23.8 %slice-start = ((s8[6815744]{0:T(1024)(128)(4,1)}), s8[4194304]{0:T(1024)(128)(4,1)S(1)}, s32[]{:S(2)}) async-start(s8[6815744]{0:T(1024)(128)(4,1)} %bitcast.32), calls=%async_computation | async-start | bytes 8388608
  420.6 18.4 %slice-start.1 = ((s8[6815744]{0:T(1024)(128)(4,1)}), s8[2621440]{0:T(1024)(128)(4,1)S(1)}, s32[]{:S(2)}) async-start(s8[6815744]{0:T(1024)(128)(4,1)} %bitcast.32), calls=%async_computation.1 | async-start | bytes 5242880
  439.1 11.5 %copy-start.6 = (bf16[1024,1664]{1,0:T(8,128)(2,1)S(1)}, bf16[1024,1664]{1,0:T(8,128)(2,1)}, u32[]{:S(2)}) copy-start(bf16[1024,1664]{1,0:T(8,128)(2,1)} %mixer_backward.1) | copy-start | bytes 10223620
  439.1 11.5 %copy-start.20 = (bf16[1024,2048]{1,0:T(8,128)(2,1)S(1)}, bf16[1024,2048]{1,0:T(8,128)(2,1)}, u32[]{:S(2)}) copy-start(bf16[1024,2048]{1,0:T(8,128)(2,1)} %get-tuple-element.81) | copy-start | bytes 12582916
  450.6 10.3 %copy-start.21 = (bf16[4,256,2048]{2,1,0:T(8,128)(2,1)S(1)}, bf16[4,256,2048]{2,1,0:T(8,128)(2,1)}, u32[]{:S(2)}) copy-start(bf16[4,256,2048]{2,1,0:T(8,128)(2,1)} %get-tuple-element.79) | copy-start | bytes 12582916
  450.6 10.3 %copy-start.22 = (bf16[1024,512]{1,0:T(8,128)(2,1)S(1)}, bf16[1024,512]{1,0:T(8,128)(2,1)}, u32[]{:S(2)}) copy-start(bf16[1024,512]{1,0:T(8,128)(2,1)} %get-tuple-element.80) | copy-start | bytes 3145732
  464.7 1.0 copy-start.12
  464.8 1.1 copy-start.13
  464.8 1.7 copy-start.7
  587.6 6.1 %copy-start.4 = (f32[512,2048]{1,0:T(8,128)S(1)}, f32[512,2048]{1,0:T(8,128)}, u32[]{:S(2)}) copy-start(f32[512,2048]{1,0:T(8,128)} %get-tuple-element.123) | copy-start | bytes 12582916
  593.7 2.1 copy-start.17
  593.7 2.9 copy-start.16
  593.7 3.7 copy-start.15
  593.7 4.5 copy-start.14
  595.8 3.2 copy-start.9
  595.8 4.3 copy-start.10
  597.4 3.8 copy-start.8
  (1 other events, 0.8 us)
